TPU v7x, 32 devices: a whole 2x2x4 slice. The times are simulated.
32 devices in a mesh: fsdp: 4 (over y, x), context: 2 (over core), tensor: 4 (over z).
Axes of the slice: x: 2, y: 2, z: 4, core: 2. Of those that a mesh axis runs over, the one named last changes fastest.
Arguments:
- block_input: bfloat16 [4, 2048, 2048], P('fsdp', 'context'), may hold values from -6 to 6
- doc_ids: int32 [4, 2048], P('fsdp'), may hold values from 0 to 7, never falling along the last dimension, each value on 1 to 1536 neighbouring positions
- norm_gain: float32 [2048], replicated, may hold values from 0.25 to 1.75
- in_proj: bfloat16 [2, 2048, 4096], P(None, 'fsdp', 'tensor'), may hold values from -0.125 to 0.125
- conv_weight: float32 [4, 4096], P(None, 'tensor'), may hold values from -0.5 to 0.5
- conv_bias: float32 [4096], P('tensor'), may hold values from -0.5 to 0.5
- x_proj: bfloat16 [4096, 160], P('tensor', 'fsdp'), may hold values from -1 to 1
- dt_proj: bfloat16 [128, 4096], P('fsdp', 'tensor'), may hold values from -2 to 2
- dt_bias: float32 [4096], P('tensor'), may hold values from -6.5 to -2.5
- a_log: float32 [16, 4096], P(None, 'tensor'), may hold values from 0 to 2.77
- d_skip: float32 [4096], P('tensor'), may hold values from 0.5 to 1.5
- out_proj: bfloat16 [4096, 2048], P('tensor', 'fsdp'), may hold values from -0.1875 to 0.1875
- grad_output: bfloat16 [4, 2048, 2048], P('fsdp', 'context'), may hold values from -6 to 6
Outputs:
- block_output: bfloat16 [4, 2048, 2048], P('fsdp', 'context')
- grad_input: bfloat16 [4, 2048, 2048], P('fsdp', 'context')
- grad_norm_gain: float32 [2048], replicated
- grad_in_proj: float32 [2, 2048, 4096], P(None, 'fsdp', 'tensor')
- grad_conv_weight: float32 [4, 4096], P(None, 'tensor')
- grad_conv_bias: float32 [4096], P('tensor')
- grad_x_proj: float32 [4096, 160], P('tensor', 'fsdp')
- grad_dt_proj: float32 [128, 4096], P('fsdp', 'tensor')
- grad_dt_bias: float32 [4096], P('tensor')
- grad_a_log: float32 [16, 4096], P(None, 'tensor')
- grad_d_skip: float32 [4096], P('tensor')
- grad_out_proj: float32 [4096, 2048], P('tensor', 'fsdp')
Inputs may be any that keep to these rules, and one draw needn't show every extreme that they name: `doc_ids`: ids never fall along a sequence and start at 0 in each.
All inputs are finite; a program needn't handle non-finite values.
Results may differ from a plain program's by a relative error of at most 0.012.
The roundings to bfloat16 on the way count: a program that leaves them out, or rounds other values in their place, can miss the bound.
Values may be sent and summed in bfloat16 or wider, within the bound.
No kernel may reach another device: no remote copies, remote signals or barrier semaphores. Data moves between devices by JAX's collectives and lax.ppermute only.
A program may use at most 256 MiB of HBM per device.

v0:
```python
import math

import jax
import jax.numpy as jnp
from jax import lax
from jax.sharding import PartitionSpec as P

EPS = 1e-05


def from_behind(array, axis, by):
    size = lax.axis_size(axis)
    pairs = [(i, i + by) for i in range(size) if 0 <= i + by < size]
    return lax.ppermute(array, axis, pairs)


def prefix(array, axis, join, neutral, backward):
    count = lax.axis_size(axis)
    place = lax.axis_index(axis)
    ahead = count - 1 - place if backward else place
    gathered = jax.tree.map(
        lambda a, kind: lax.all_gather(a.astype(kind), axis), array, (jnp.bfloat16, jnp.bfloat16)
    )
    state = jax.tree.map(lambda a, e: jnp.zeros_like(a) + jnp.asarray(e, a.dtype), array, neutral)

    def one(turn, state):
        source = count - 1 - turn if backward else turn
        return join(
            state,
            jax.tree.map(
                lambda a, own: lax.dynamic_index_in_dim(a, source, 0, False).astype(own.dtype),
                gathered,
                array,
            ),
        )

    return lax.fori_loop(0, ahead, one, state)


def combine_pairs(earlier, later):
    return (earlier[0] * later[0], earlier[1] * later[0] + later[1])


def silu_slope(entries):
    sigmoid = jax.nn.sigmoid(entries)
    return sigmoid * (1.0 + entries * (1.0 - sigmoid))


def contract(left_side, right_side, left_dim, right_dim):
    return lax.dot_general(
        left_side,
        right_side,
        (((left_dim,), (right_dim,)), ((), ())),
        preferred_element_type=jnp.float32,
    )


def decay_factor(decay_rates, step_now, keep_now):
    return jnp.exp(step_now[:, None, :] * decay_rates) * keep_now[:, :, None]


def advance(state, decay_rates, step_now, value_now, in_now, keep_now):
    factor = decay_factor(decay_rates, step_now, keep_now)
    return factor * state + (step_now * value_now)[:, None, :] * in_now[:, :, None]


def norm_back(d_normed, norm_gain, inputs_f32, inv_rms, cotangent_f32, model_width):
    scaled_grad = d_normed * norm_gain
    row_inner = jnp.sum(scaled_grad * inputs_f32, axis=-1, keepdims=True)
    grad_rows = (
        cotangent_f32
        + inv_rms * scaled_grad
        - inputs_f32 * (inv_rms * inv_rms * inv_rms) * row_inner / model_width
    )
    gain_part = jnp.sum(d_normed * inputs_f32 * inv_rms, axis=0)
    return (grad_rows.astype(jnp.bfloat16), gain_part)


def shards(
    block_input,
    doc_ids,
    norm_gain,
    in_proj,
    conv_weight,
    conv_bias,
    x_proj,
    dt_proj,
    dt_bias,
    a_log,
    d_skip,
    out_proj,
    grad_output,
):
    seq_count, piece_len, model_width = block_input.shape
    row_count = seq_count * piece_len
    tap_count = conv_weight.shape[0]
    tail_len = tap_count - 1
    state_count = a_log.shape[0]
    in_gathered, xproj_gathered, dtproj_gathered, outproj_gathered = (
        lax.all_gather(in_proj, "fsdp", axis=1, tiled=True),
        lax.all_gather(x_proj, "fsdp", axis=1, tiled=True),
        lax.all_gather(dt_proj, "fsdp", axis=0, tiled=True),
        lax.all_gather(out_proj, "fsdp", axis=1, tiled=True),
    )
    inner_local = in_gathered.shape[2]
    rank_count = dtproj_gathered.shape[0]
    inputs_f32 = block_input.reshape(row_count, model_width).astype(jnp.float32)
    inv_rms = lax.rsqrt(jnp.mean(inputs_f32 * inputs_f32, axis=-1, keepdims=True) + EPS)
    normed = (inputs_f32 * inv_rms * norm_gain).astype(jnp.bfloat16)
    projected = jnp.einsum("td,kde->kte", normed, in_gathered, preferred_element_type=jnp.float32)
    conv_input = projected[0].astype(jnp.bfloat16).reshape(seq_count, piece_len, inner_local)
    gate_input = projected[1]
    previous_tail = from_behind(conv_input[:, piece_len - tail_len :], "context", 1)
    extended = jnp.concatenate([previous_tail, conv_input], axis=1).astype(jnp.float32)
    offset_rows = lax.axis_index("context") * piece_len
    padded_ids = jnp.concatenate([jnp.full((seq_count, tail_len), -1, jnp.int32), doc_ids], axis=1)
    id_window = lax.dynamic_slice_in_dim(padded_ids, offset_rows, piece_len + tail_len, 1)
    current_ids = id_window[:, tail_len:]
    same_doc = []
    conv_output = conv_bias
    for shift_by in range(tap_count):
        lower_edge = tail_len - shift_by
        match_now = (id_window[:, lower_edge : lower_edge + piece_len] == current_ids).astype(
            jnp.float32
        )[..., None]
        same_doc.append(match_now)
        conv_output = (
            conv_output
            + conv_weight[shift_by] * extended[:, lower_edge : lower_edge + piece_len] * match_now
        )
    conv_flat = conv_output.reshape(row_count, inner_local)
    activated = jax.nn.silu(conv_flat).astype(jnp.bfloat16)
    activated_f32 = activated.astype(jnp.float32)
    projections = lax.psum(
        jnp.dot(activated, xproj_gathered, preferred_element_type=jnp.float32), "tensor"
    )
    proj_bf16 = projections.astype(jnp.bfloat16)
    dt_input = proj_bf16[:, :rank_count]
    in_coef = proj_bf16[:, rank_count : rank_count + state_count].astype(jnp.float32)
    out_coef = proj_bf16[:, rank_count + state_count :].astype(jnp.float32)
    dt_logits = jnp.dot(dt_input, dtproj_gathered, preferred_element_type=jnp.float32) + dt_bias
    step_sizes = jax.nn.softplus(dt_logits)
    decay_rates = -jnp.exp(a_log)
    block_len = math.gcd(piece_len, 16)
    block_count = piece_len // block_len
    total_blocks = seq_count * block_count

    def to_blocks(array):
        return jnp.swapaxes(array.reshape(total_blocks, block_len, array.shape[-1]), 0, 1)

    def per_seq(array):
        return array.reshape(seq_count, block_count, state_count, inner_local)

    step_blocks = to_blocks(step_sizes)
    value_blocks = to_blocks(activated_f32)
    in_blocks = to_blocks(in_coef)
    out_blocks = to_blocks(out_coef)
    keep_blocks = to_blocks(same_doc[1].reshape(row_count, 1))

    def first_pass(state, token):
        return (advance(state, decay_rates, token[0], token[1], token[2], token[3]), None)

    zero_state = jnp.zeros((total_blocks, state_count, inner_local), jnp.float32)
    block_ends, _ = lax.scan(
        first_pass, zero_state, (step_blocks, value_blocks, in_blocks, keep_blocks)
    )
    block_fades = (
        jnp.exp(jnp.sum(step_blocks, axis=0)[:, None, :] * decay_rates)
        * jnp.prod(keep_blocks, axis=0)[:, :, None]
    )
    inclusive = lax.associative_scan(
        combine_pairs, (per_seq(block_fades), per_seq(block_ends)), axis=1
    )
    seq_ones = jnp.ones((seq_count, state_count, inner_local), jnp.float32)
    seq_zeros = jnp.zeros((seq_count, state_count, inner_local), jnp.float32)
    earlier_pieces = prefix(
        (inclusive[0][:, -1], inclusive[1][:, -1]),
        "context",
        combine_pairs,
        (seq_ones, seq_zeros),
        False,
    )
    entry_fade = jnp.concatenate([seq_ones[:, None], inclusive[0][:, :-1]], axis=1)
    entry_part = jnp.concatenate([seq_zeros[:, None], inclusive[1][:, :-1]], axis=1)
    entry_states = (entry_fade * earlier_pieces[1][:, None] + entry_part).reshape(
        total_blocks, state_count, inner_local
    )

    def second_pass(state, token):
        state = advance(state, decay_rates, token[0], token[1], token[2], token[3])
        return (state, jnp.sum(token[4][:, :, None] * state, axis=1))

    _, scan_blocks = lax.scan(
        second_pass, entry_states, (step_blocks, value_blocks, in_blocks, keep_blocks, out_blocks)
    )
    scanned = jnp.swapaxes(scan_blocks, 0, 1).reshape(row_count, inner_local)
    mixed = scanned + d_skip * activated_f32
    gate_value = jax.nn.silu(gate_input)
    gated = (mixed * gate_value).astype(jnp.bfloat16)
    partial_branch = jnp.dot(gated, outproj_gathered, preferred_element_type=jnp.float32)
    branch = lax.psum(partial_branch, "tensor")
    output_flat = (inputs_f32 + branch).astype(jnp.bfloat16)
    block_output = output_flat.reshape(seq_count, piece_len, model_width)
    cotangent = grad_output.reshape(row_count, model_width)
    d_gated = contract(cotangent, outproj_gathered, 1, 1)
    grad_out_local = contract(gated, cotangent, 0, 0)
    d_mixed = d_gated * gate_value
    d_gate = (d_gated * mixed * silu_slope(gate_input)).astype(jnp.bfloat16)
    grad_skip_local = jnp.sum(d_mixed * activated_f32, axis=0)
    upstream_blocks = to_blocks(d_mixed)

    def back_first(flow, token):
        factor = decay_factor(decay_rates, token[0], token[1])
        adjoint = token[2][:, :, None] * token[3][:, None, :] + flow
        return (factor * adjoint, None)

    leaving, _ = lax.scan(
        back_first,
        zero_state,
        (step_blocks, keep_blocks, out_blocks, upstream_blocks),
        reverse=True,
    )
    backward_incl = lax.associative_scan(
        combine_pairs, (per_seq(block_fades), per_seq(leaving)), axis=1, reverse=True
    )
    later_pieces = prefix(
        (backward_incl[0][:, 0], backward_incl[1][:, 0]),
        "context",
        combine_pairs,
        (seq_ones, seq_zeros),
        True,
    )
    exit_fade = jnp.concatenate([backward_incl[0][:, 1:], seq_ones[:, None]], axis=1)
    exit_part = jnp.concatenate([backward_incl[1][:, 1:], seq_zeros[:, None]], axis=1)
    exit_flows = (exit_fade * later_pieces[1][:, None] + exit_part).reshape(
        total_blocks, state_count, inner_local
    )
    group_size = math.gcd(total_blocks, 8)
    team_count = total_blocks // group_size

    def grouped(array):
        return jnp.swapaxes(
            array.reshape(array.shape[0], team_count, group_size, array.shape[-1]), 0, 1
        )

    def grouped_states(array):
        return array.reshape(team_count, group_size, state_count, inner_local)

    def flatten_rows(array):
        merged = jnp.swapaxes(array, 0, 1).reshape(array.shape[1], total_blocks, array.shape[-1])
        return jnp.swapaxes(merged, 0, 1).reshape(row_count, array.shape[-1])

    def team_pass(decay_total, item):
        (
            step_team,
            value_team,
            in_team,
            keep_team,
            out_team,
            upstream_team,
            start_state,
            exit_flow,
        ) = item

        def forward_step(state, token):
            fresh = advance(state, decay_rates, token[0], token[1], token[2], token[3])
            return (fresh, fresh)

        _, kept_states = lax.scan(
            forward_step, start_state, (step_team, value_team, in_team, keep_team)
        )
        prior_states = jnp.concatenate([start_state[None], kept_states[:-1]], axis=0)

        def backward_step(carry, token):
            flow, accumulated = carry
            (
                step_now,
                value_now,
                in_now,
                keep_now,
                out_now,
                upstream_now,
                state_now,
                state_before,
            ) = token
            factor = decay_factor(decay_rates, step_now, keep_now)
            adjoint = out_now[:, :, None] * upstream_now[:, None, :] + flow
            pulled = adjoint * factor * state_before
            in_weighted = jnp.sum(adjoint * in_now[:, :, None], axis=1)
            d_step = jnp.sum(pulled * decay_rates, axis=1) + value_now * in_weighted
            d_value = step_now * in_weighted
            d_in = jnp.sum(adjoint * (step_now * value_now)[:, None, :], axis=2)
            d_out = jnp.sum(state_now * upstream_now[:, None, :], axis=2)
            accumulated = accumulated + jnp.sum(pulled * step_now[:, None, :], axis=0)
            return ((factor * adjoint, accumulated), (d_step, d_value, d_in, d_out))

        (_, decay_total), results = lax.scan(
            backward_step,
            (exit_flow, decay_total),
            (
                step_team,
                value_team,
                in_team,
                keep_team,
                out_team,
                upstream_team,
                kept_states,
                prior_states,
            ),
            reverse=True,
        )
        return (decay_total, results)

    team_inputs = (
        grouped(step_blocks),
        grouped(value_blocks),
        grouped(in_blocks),
        grouped(keep_blocks),
        grouped(out_blocks),
        grouped(upstream_blocks),
        grouped_states(entry_states),
        grouped_states(exit_flows),
    )
    decay_sum, team_results = lax.scan(
        team_pass, jnp.zeros((state_count, inner_local), jnp.float32), team_inputs
    )
    d_step_sizes = flatten_rows(team_results[0])
    d_act_scan = flatten_rows(team_results[1])
    d_in_coef = flatten_rows(team_results[2])
    d_out_coef = flatten_rows(team_results[3])
    grad_decay_local = decay_sum * decay_rates
    d_logits = (d_step_sizes * jax.nn.sigmoid(dt_logits)).astype(jnp.bfloat16)
    grad_dt_bias_local = jnp.sum(d_logits.astype(jnp.float32), axis=0)
    grad_dt_local = contract(dt_input, d_logits, 0, 0)
    d_dt_input = contract(d_logits, dtproj_gathered, 1, 1)
    d_projections = lax.psum(
        jnp.concatenate([d_dt_input, d_in_coef, d_out_coef], axis=1), "tensor"
    ).astype(jnp.bfloat16)
    grad_xproj_local = contract(activated, d_projections, 0, 0)
    d_act = d_mixed * d_skip + d_act_scan + contract(d_projections, xproj_gathered, 1, 1)
    d_conv = (d_act * silu_slope(conv_flat)).reshape(seq_count, piece_len, inner_local)
    d_extended = jnp.zeros((seq_count, piece_len + tail_len, inner_local), jnp.float32)
    tap_grads = []
    for shift_by in range(tap_count):
        lower_edge = tail_len - shift_by
        masked = d_conv * same_doc[shift_by]
        d_extended = d_extended + jnp.pad(
            conv_weight[shift_by] * masked, ((0, 0), (lower_edge, shift_by), (0, 0))
        )
        tap_grads.append(
            jnp.sum(masked * extended[:, lower_edge : lower_edge + piece_len], axis=(0, 1))
        )
    grad_taps_local = jnp.stack(tap_grads)
    grad_conv_bias_local = jnp.sum(d_conv, axis=(0, 1))
    returned_tail = from_behind(d_extended[:, :tail_len], "context", -1)
    d_conv_input = d_extended[:, tail_len:] + jnp.pad(
        returned_tail, ((0, 0), (piece_len - tail_len, 0), (0, 0))
    )
    d_conv_input = d_conv_input.reshape(row_count, inner_local).astype(jnp.bfloat16)
    d_both = jnp.stack([d_conv_input, d_gate])
    grad_in_local = jnp.einsum("td,kte->kde", normed, d_both, preferred_element_type=jnp.float32)
    d_normed_part = jnp.einsum(
        "kte,kde->td", d_both, in_gathered, preferred_element_type=jnp.float32
    )
    cotangent_f32 = cotangent.astype(jnp.float32)
    d_normed = lax.psum(d_normed_part, "tensor")
    grad_flat, grad_gain_local = norm_back(
        d_normed, norm_gain, inputs_f32, inv_rms, cotangent_f32, model_width
    )
    grad_input = grad_flat.reshape(seq_count, piece_len, model_width)
    large_grads = (grad_in_local, grad_xproj_local, grad_dt_local, grad_out_local)
    owned = (
        lax.psum_scatter(large_grads[0], "fsdp", scatter_dimension=1, tiled=True),
        lax.psum_scatter(large_grads[1], "fsdp", scatter_dimension=1, tiled=True),
        lax.psum_scatter(large_grads[2], "fsdp", scatter_dimension=0, tiled=True),
        lax.psum_scatter(large_grads[3], "fsdp", scatter_dimension=1, tiled=True),
    )
    owned = lax.psum((owned[0], owned[1], owned[2], owned[3]), "context")
    smaller = lax.psum(
        (
            grad_gain_local,
            grad_taps_local,
            grad_conv_bias_local,
            grad_dt_bias_local,
            grad_decay_local,
            grad_skip_local,
        ),
        ("fsdp", "context"),
    )
    return (
        block_output,
        grad_input,
        smaller[0],
        owned[0],
        smaller[1],
        smaller[2],
        owned[1],
        owned[2],
        smaller[3],
        smaller[4],
        smaller[5],
        owned[3],
    )


def solution(mesh):
    placed = (
        P("fsdp", "context", None),
        P("fsdp", None),
        P(),
        P(None, "fsdp", "tensor"),
        P(None, "tensor"),
        P("tensor"),
        P("tensor", "fsdp"),
        P("fsdp", "tensor"),
        P("tensor"),
        P(None, "tensor"),
        P("tensor"),
        P("tensor", "fsdp"),
        P("fsdp", "context", None),
    )
    return jax.shard_map(
        shards,
        mesh=mesh,
        in_specs=placed,
        out_specs=(
            P("fsdp", "context", None),
            P("fsdp", "context", None),
            P(),
            P(None, "fsdp", "tensor"),
            P(None, "tensor"),
            P("tensor"),
            P("tensor", "fsdp"),
            P("fsdp", "tensor"),
            P("tensor"),
            P(None, "tensor"),
            P("tensor"),
            P("tensor", "fsdp"),
        ),
        check_vma=False,
    )
```

profile of v0, /device:TPU:0, one launch (start us, length us, event | category | flops | bytes accessed | tf_op | source)
XLA Modules:
  0.0 2823.4 jit_solution(12022358136798212450)
XLA Ops:
  8.7 11.0 all_gather.29
  27.2 73.1 %all-gather.3.cloned.1.call-done = bf16[2,2048,1024]{2,1,0:T(8,128)(2,1)} async-done(((bf16[2,512,1024]{2,1,0:T(8,128)(2,1)}), bf16[2,2048,1024]{2,1,0:T(8,128)(2,1)}) %all-gather.3.cloned.1.call-update) | async-done | bytes 8388624 | tf_op jit(solution)/shard_map/all_gather | solution.py:100
  100.2 14.7 fusion.96
  137.9 17.7 all-gather.5.cloned.1.call-done
  155.7 20.2 fusion.23
  176.8 32.5 %all-reduce.73 = bf16[1024,160]{0,1:T(8,128)(2,1)S(1)} all-reduce(f32[1024,160]{0,1:T(8,128)S(1)} %fusion.97), channel_id=1, replica_groups=mesh['fsdp'=4,'context'=2,'tensor'=4] {'tensor'}, use_global_device_ids=true, to_apply=%region_1.2 | all-reduce | flops 163840 | bytes 983040 | tf_op jit(solution)/shard_map/psum | solution.py:134
  227.8 111.6 %while.172 = (s32[]{:T(128)}, f32[64,16,1024]{2,1,0:T(8,128)}, f32[16,64,1024]{2,1,0:T(8,128)}, f32[16,1024]{1,0:T(8,128)S(1)}, f32[16,64,1]{1,2,0:T(1,128)S(1)}...) while((s32[]{:T(128)}, f32[64,16,1024]{2,1,0:T(8,128)}, ...), condition=%wide.region_5.6_spmd.clone, body=%wide.region_4.5_spmd.clone.sunk | while | flops 6356995 | bytes 10302335 | solution.py:164
  481.0 96.2 %while.173 = (s32[]{:T(128)}, f32[64,16,1024]{2,1,0:T(8,128)}, f32[16,64,1024]{2,1,0:T(8,128)}, f32[16,1024]{1,0:T(8,128)S(1)}, f32[16,64,1]{1,2,0:T(1,128)S(1)}...) while((s32[]{:T(128)}, f32[64,16,1024]{2,1,0:T(8,128)}, ...), condition=%wide.region_13.14_spmd.clone, body=%wide.region_12.13_spmd.clone.sunk | while | flops 6291460 | bytes 10040207 | solution.py:217
  719.0 12.0 pad.184
  731.0 12.0 pad.407
  743.0 18.4 pad.410
  765.9 12.0 pad.285
  777.9 12.2 pad.195
  790.0 18.5 pad.405
  819.7 12.0 pad.183
  840.9 223.8 %while.167 = (s32[]{:T(128)}, f32[64,16,1024]{2,1,0:T(8,128)}, f32[16,64,1024]{2,0,1:T(8,128)}, f32[16,64,1024]{2,1,0:T(8,128)}, f32[16,1024]{1,0:T(8,128)S(1)},...) while((s32[]{:T(128)}, f32[64,16,1024]{2,1,0:T(8,128)}, ...), condition=%wide.region_10.11_spmd, body=%wide.region_8.10_spmd.sunk | while | flops 7340034 | bytes 11625353 | solution.py:193
  1066.5 11.9 pad.289
  1078.4 18.5 pad.408
  1108.5 11.9 pad.208
  1122.1 12.0 pad.207
  1147.8 11.9 pad.219
  1176.5 14.1 copy_bitcast_fusion
  1193.6 645.2 %while.171 = (s32[]{:T(128)}, f32[16,1024]{1,0:T(8,128)S(1)}, f32[8,16,8,1024]{3,2,0,1:T(8,128)}, f32[8,16,8,1024]{3,2,0,1:T(8,128)}, f32[8,16,8,16]{3,2,1,0:T(8...) while((s32[]{:T(128)}, f32[16,1024]{1,0:T(8,128)S(1)}, ...), condition=%wide.region_26.27_spmd, body=%wide.region_16.26_spmd.sunk | while | flops 4873991 | bytes 47047160 | solution.py:324
  1202.4 17.9 while.174
  1229.7 43.0 %while.175 = (s32[]{:T(128)}, f32[8,16,1024]{2,1,0:T(8,128)S(1)}, f32[16,1024]{1,0:T(8,128)S(1)}, f32[16,8,1024]{2,1,0:T(8,128)S(1)}, f32[16,8,1024]{2,1,0:T(8,1...) while((s32[]{:T(128)}, f32[8,16,1024]{2,1,0:T(8,128)S(1)}, ...), condition=%wide.region_25.25_spmd, body=%wide.region_19.24_spmd.sunk | while | flops 2113283 | bytes 3035449 | solution.py:297
  1283.0 17.9 while.174
  1310.3 43.0 %while.175 = (s32[]{:T(128)}, f32[8,16,1024]{2,1,0:T(8,128)S(1)}, f32[16,1024]{1,0:T(8,128)S(1)}, f32[16,8,1024]{2,1,0:T(8,128)S(1)}, f32[16,8,1024]{2,1,0:T(8,1...) while((s32[]{:T(128)}, f32[8,16,1024]{2,1,0:T(8,128)S(1)}, ...), condition=%wide.region_25.25_spmd, body=%wide.region_19.24_spmd.sunk | while | flops 2113283 | bytes 3035449 | solution.py:297
  1363.6 17.9 while.174
  1390.9 43.0 %while.175 = (s32[]{:T(128)}, f32[8,16,1024]{2,1,0:T(8,128)S(1)}, f32[16,1024]{1,0:T(8,128)S(1)}, f32[16,8,1024]{2,1,0:T(8,128)S(1)}, f32[16,8,1024]{2,1,0:T(8,1...) while((s32[]{:T(128)}, f32[8,16,1024]{2,1,0:T(8,128)S(1)}, ...), condition=%wide.region_25.25_spmd, body=%wide.region_19.24_spmd.sunk | while | flops 2113283 | bytes 3035449 | solution.py:297
  1444.2 17.9 while.174
  1471.5 43.0 %while.175 = (s32[]{:T(128)}, f32[8,16,1024]{2,1,0:T(8,128)S(1)}, f32[16,1024]{1,0:T(8,128)S(1)}, f32[16,8,1024]{2,1,0:T(8,128)S(1)}, f32[16,8,1024]{2,1,0:T(8,1...) while((s32[]{:T(128)}, f32[8,16,1024]{2,1,0:T(8,128)S(1)}, ...), condition=%wide.region_25.25_spmd, body=%wide.region_19.24_spmd.sunk | while | flops 2113283 | bytes 3035449 | solution.py:297
  1524.9 17.9 while.174
  1552.2 43.0 %while.175 = (s32[]{:T(128)}, f32[8,16,1024]{2,1,0:T(8,128)S(1)}, f32[16,1024]{1,0:T(8,128)S(1)}, f32[16,8,1024]{2,1,0:T(8,128)S(1)}, f32[16,8,1024]{2,1,0:T(8,1...) while((s32[]{:T(128)}, f32[8,16,1024]{2,1,0:T(8,128)S(1)}, ...), condition=%wide.region_25.25_spmd, body=%wide.region_19.24_spmd.sunk | while | flops 2113283 | bytes 3035449 | solution.py:297
  1605.5 17.9 while.174
  1632.8 43.0 %while.175 = (s32[]{:T(128)}, f32[8,16,1024]{2,1,0:T(8,128)S(1)}, f32[16,1024]{1,0:T(8,128)S(1)}, f32[16,8,1024]{2,1,0:T(8,128)S(1)}, f32[16,8,1024]{2,1,0:T(8,1...) while((s32[]{:T(128)}, f32[8,16,1024]{2,1,0:T(8,128)S(1)}, ...), condition=%wide.region_25.25_spmd, body=%wide.region_19.24_spmd.sunk | while | flops 2113283 | bytes 3035449 | solution.py:297
  1686.1 17.9 while.174
  1713.4 43.0 %while.175 = (s32[]{:T(128)}, f32[8,16,1024]{2,1,0:T(8,128)S(1)}, f32[16,1024]{1,0:T(8,128)S(1)}, f32[16,8,1024]{2,1,0:T(8,128)S(1)}, f32[16,8,1024]{2,1,0:T(8,1...) while((s32[]{:T(128)}, f32[8,16,1024]{2,1,0:T(8,128)S(1)}, ...), condition=%wide.region_25.25_spmd, body=%wide.region_19.24_spmd.sunk | while | flops 2113283 | bytes 3035449 | solution.py:297
  1766.8 17.9 while.174
  1794.1 43.0 %while.175 = (s32[]{:T(128)}, f32[8,16,1024]{2,1,0:T(8,128)S(1)}, f32[16,1024]{1,0:T(8,128)S(1)}, f32[16,8,1024]{2,1,0:T(8,128)S(1)}, f32[16,8,1024]{2,1,0:T(8,1...) while((s32[]{:T(128)}, f32[8,16,1024]{2,1,0:T(8,128)S(1)}, ...), condition=%wide.region_25.25_spmd, body=%wide.region_19.24_spmd.sunk | while | flops 2113283 | bytes 3035449 | solution.py:297
  1851.7 31.8 %all-reduce.74 = bf16[1024,160]{0,1:T(8,128)(2,1)S(1)} all-reduce(f32[1024,160]{0,1:T(8,128)S(1)} %pad_maximum_fusion.12), channel_id=1, replica_groups=mesh['fsdp'=4,'context'=2,'tensor'=4] {'tensor'}, use_global_device_ids=true, to_apply=%region_27.28 | all-reduce | flops 163840 | bytes 983040 | tf_op jit(solution)/shard_map/psum | solution.py:336
  1901.1 12.6 fusion.31
  1939.9 12.4 convolution_bitcast_fusion
  1963.6 13.2 convolution_bitcast_fusion.1
  1977.0 20.3 reduce-scatter.11.cloned.1.call-done
  1997.3 157.0 %reduce-scatter.7.cloned.1.call-done = f32[2,512,1024]{1,2,0:T(8,128)} async-done(((f32[2,2048,1024]{1,2,0:T(8,128)}), f32[2,512,1024]{1,2,0:T(8,128)}) %reduce-scatter.7.cloned.1.call-update) | async-done | bytes 4194320 | tf_op jit(solution)/shard_map/reduce_scatter | solution.py:373
  2155.1 565.3 %all-reduce.70.cloned.1.call-done = (f32[1024,2048]{1,0:T(8,128)}, f32[1024,2048]{1,0:T(8,128)}) async-done(((f32[1024,2048]{1,0:T(8,128)}, f32[1024,2048]{1,0:T(8,128)}), (f32[1024,2048]{1,0:T(8,128)}, f32[1024,2048]{1,0:T(8,128)})) %all-reduce.70.cloned.1.call-update) | async-done | bytes 16777232 | tf_op jit(solution)/shard_map/psum | solution.py:201
  2739.9 25.1 all-reduce.59
  2770.5 42.0 %all-reduce.68.cloned.1.call-done = f32[16,1024]{1,0:T(8,128)} async-done(((f32[16,1024]{1,0:T(8,128)}), f32[16,1024]{1,0:T(8,128)}) %all-reduce.68.cloned.1.call-update) | async-done | bytes 65552 | tf_op jit(solution)/shard_map/psum | solution.py:379
  (2614 shorter events, 1558.2 us)
Async XLA Ops:
  7.2 19.9 copy-start.89
  7.2 19.9 copy-start.62
  7.2 93.0 %copy-start.71 = (f32[2048]{0:T(1024)S(1)}, f32[2048]{0:T(1024)}, u32[]{:S(2)}) copy-start(f32[2048]{0:T(1024)} %param.31) | copy-start | bytes 24580
  7.2 93.0 %all-gather.3.cloned.1.call-start = ((), (), s32[]{:S(2)}) async-start(), calls=%async_computation.4 | async-start | bytes 10485760 | tf_op jit(solution)/shard_map/all_gather | solution.py:100
  7.9 147.7 %all-gather.5.cloned.1.call-start = ((), (), s32[]{:S(2)}) async-start(), calls=%async_computation.5 | async-start | bytes 5242880 | tf_op jit(solution)/shard_map/all_gather | solution.py:103
  8.7 1968.2 %reduce-scatter.9.cloned.1.call-start = ((), (), s32[]{:S(2)}) async-start(), calls=%async_computation.7 | async-start | bytes 655360 | tf_op jit(solution)/shard_map/reduce_scatter | solution.py:375
  19.8 156.1 %copy-start.52 = (bf16[1024,160]{0,1:T(8,128)(2,1)}, bf16[1024,160]{0,1:T(8,128)(2,1)S(1)}, u32[]{:S(2)}) copy-start(bf16[1024,160]{0,1:T(8,128)(2,1)S(1)} %all_gather.29) | copy-start | bytes 983044
  21.8 133.8 %copy-start.75 = (f32[1,1024]{1,0:T(1,128)}, f32[1,1024]{1,0:T(1,128)S(1)}, u32[]{:S(2)}) copy-start(f32[1,1024]{1,0:T(1,128)S(1)} %get-tuple-element.1497) | copy-start | bytes 12292
  22.8 132.8 %copy-start.77 = (f32[1,1024]{1,0:T(1,128)}, f32[1,1024]{1,0:T(1,128)S(1)}, u32[]{:S(2)}) copy-start(f32[1,1024]{1,0:T(1,128)S(1)} %get-tuple-element.1586) | copy-start | bytes 12292
  22.8 132.8 %copy-start.79 = (f32[1,1024]{1,0:T(1,128)}, f32[1,1024]{1,0:T(1,128)S(1)}, u32[]{:S(2)}) copy-start(f32[1,1024]{1,0:T(1,128)S(1)} %get-tuple-element.1587) | copy-start | bytes 12292
  27.1 87.9 %copy-start.69 = (f32[1024]{0:T(1024)}, f32[1024]{0:T(1024)S(1)}, u32[]{:S(2)}) copy-start(f32[1024]{0:T(1024)S(1)} %get-tuple-element.1589) | copy-start | bytes 12292
  27.1 128.6 %copy-start.81 = (f32[1,1024]{1,0:T(1,128)}, f32[1,1024]{1,0:T(1,128)S(1)}, u32[]{:S(2)}) copy-start(f32[1,1024]{1,0:T(1,128)S(1)} %get-tuple-element.1582) | copy-start | bytes 12292
  27.1 128.6 %copy-start.83 = (f32[1,1024]{1,0:T(1,128)}, f32[1,1024]{1,0:T(1,128)S(1)}, u32[]{:S(2)}) copy-start(f32[1,1024]{1,0:T(1,128)S(1)} %get-tuple-element.1583) | copy-start | bytes 12292
  27.1 128.6 %copy-start.85 = (f32[1,1024]{1,0:T(1,128)}, f32[1,1024]{1,0:T(1,128)S(1)}, u32[]{:S(2)}) copy-start(f32[1,1024]{1,0:T(1,128)S(1)} %get-tuple-element.1584) | copy-start | bytes 12292
  27.1 128.6 %copy-start.87 = (f32[1,1024]{1,0:T(1,128)}, f32[1,1024]{1,0:T(1,128)S(1)}, u32[]{:S(2)}) copy-start(f32[1,1024]{1,0:T(1,128)S(1)} %get-tuple-element.1585) | copy-start | bytes 12292
  100.2 18.5 copy-start.68
  117.0 18.4 collective-permute-start
  128.4 81.0 %copy-start.57 = (bf16[128,1024]{1,0:T(8,128)(2,1)}, bf16[128,1024]{1,0:T(8,128)(2,1)S(1)}, u32[]{:S(2)}) copy-start(bf16[128,1024]{1,0:T(8,128)(2,1)S(1)} %all_gather.30) | copy-start | bytes 786436
  135.3 20.4 copy-start.93
  155.7 53.6 %copy-start.90 = (f32[1024]{0:T(1024)S(1)}, f32[1024]{0:T(1024)}, u32[]{:S(2)}) copy-start(f32[1024]{0:T(1024)} %param.37) | copy-start | bytes 12292
  175.9 37.8 %copy-start.14 = (bf16[1024,1024]{1,0:T(8,128)(2,1)}, bf16[1024,1024]{1,0:T(8,128)(2,1)S(1)}, u32[]{:S(2)}) copy-start(bf16[1024,1024]{1,0:T(8,128)(2,1)S(1)} %get-tuple-element.1492) | copy-start | bytes 6291460
  209.3 11.1 copy-start.54
  392.4 17.3 copy-start.65
  430.1 31.5 %copy-start.17 = (f32[1,32,16,1024]{3,2,1,0:T(8,128)}, f32[1,32,16,1024]{3,2,1,0:T(8,128)S(1)}, u32[]{:S(2)}) copy-start(f32[1,32,16,1024]{3,2,1,0:T(8,128)S(1)} %pad.182) | copy-start | bytes 6291460
  621.9 11.5 copy-start.64
  808.5 9.5 slice-start
  1066.5 30.5 %copy-start.12 = (f32[1,32,16,1024]{3,2,1,0:T(8,128)}, f32[1,32,16,1024]{3,2,1,0:T(8,128)S(1)}, u32[]{:S(2)}) copy-start(f32[1,32,16,1024]{3,2,1,0:T(8,128)S(1)} %pad_maximum_fusion.7) | copy-start | bytes 6291460
  1145.8 16.7 copy-start.73
  1176.5 14.1 copy-start.26
  1176.5 14.1 copy-start.27
  1847.7 35.9 %copy-start.15 = (bf16[1024,1024]{1,0:T(8,128)(2,1)S(1)}, bf16[1024,1024]{1,0:T(8,128)(2,1)}, u32[]{:S(2)}) copy-start(bf16[1024,1024]{1,0:T(8,128)(2,1)} %copy-done.14) | copy-start | bytes 6291460
  1850.6 126.4 %reduce-scatter.13.cloned.1.call-start = ((), (), s32[]{:S(2)}) async-start(), calls=%async_computation.10 | async-start | bytes 819200
  1884.9 112.3 %reduce-scatter.11.cloned.1.call-start = ((), (), s32[]{:S(2)}) async-start(), calls=%async_computation.9 | async-start | bytes 10485760 | tf_op jit(solution)/shard_map/reduce_scatter | solution.py:376
  1896.1 258.2 %reduce-scatter.7.cloned.1.call-start = ((), (), s32[]{:S(2)}) async-start(), calls=%async_computation.6 | async-start | bytes 20971520 | tf_op jit(solution)/shard_map/reduce_scatter | solution.py:373
  1901.0 12.6 copy-start.82
  1901.0 12.6 copy-start.84
  1901.0 12.6 copy-start.86
  1901.1 12.6 copy-start.88
  1919.1 15.5 collective-permute-start.1
  1952.3 768.1 %all-reduce.70.cloned.1.call-start = ((), (), s32[]{:S(2)}) async-start(), calls=%async_computation.11 | async-start | bytes 33554432 | tf_op jit(solution)/shard_map/psum | solution.py:201
  1952.6 11.0 copy-start.49
  1976.8 177.5 %copy-start.63 = (f32[16,1024]{1,0:T(8,128)S(1)}, f32[16,1024]{1,0:T(8,128)}, u32[]{:S(2)}) copy-start(f32[16,1024]{1,0:T(8,128)} %param.38) | copy-start | bytes 196612
  1976.9 788.1 %all-reduce.72.cloned.1.call-start = ((), (), s32[]{:S(2)}) async-start(), calls=%async_computation.12 | async-start | bytes 13172736 | tf_op jit(solution)/shard_map/psum | solution.py:378
  2154.3 658.2 %all-reduce.68.cloned.1.call-start = ((), (), s32[]{:S(2)}) async-start(), calls=%async_computation.8 | async-start | bytes 131072 | tf_op jit(solution)/shard_map/psum | solution.py:379
  2729.0 10.9 copy-start.92
  2765.0 47.5 %copy-start.66 = (f32[1024,40]{0,1:T(8,128)S(1)}, f32[1024,40]{0,1:T(8,128)}, u32[]{:S(2)}) copy-start(f32[1024,40]{0,1:T(8,128)} %get-tuple-element.2443) | copy-start | bytes 491524
  2765.0 48.2 %copy-start.67 = (f32[32,1024]{1,0:T(8,128)S(1)}, f32[32,1024]{1,0:T(8,128)}, u32[]{:S(2)}) copy-start(f32[32,1024]{1,0:T(8,128)} %get-tuple-element.2444) | copy-start | bytes 393220
  2765.0 50.3 %copy-start.50 = (f32[1024,512]{1,0:T(8,128)S(1)}, f32[1024,512]{1,0:T(8,128)}, u32[]{:S(2)}) copy-start(f32[1024,512]{1,0:T(8,128)} %get-tuple-element.2448) | copy-start | bytes 6291460
  (58 other events, 241.3 us)
Sparse Core Ops, SparseCore 0:
  9.9 90.2 all-gather.2
  102.1 53.5 all-gather.4
  1850.7 22.4 reduce-scatter.8
  1885.1 22.8 reduce-scatter.12
  1910.9 86.3 reduce-scatter.10
  2000.5 153.7 reduce-scatter.6
  2157.1 563.2 all-reduce.69
  2723.4 31.6 all-reduce.71
  2758.8 53.6 all-reduce.67
where the time goes:
time: 2860 us; the launch traced here: 2820 us
  waiting for transfers between devices  877 us (31%)
  other arithmetic  846 us (30%)
  local copies, waits for them, and re-layouts  836 us (29%)
  blocking collectives  118 us (4%)
  matrix products  104 us (4%)
    psum x1, waiting for transfers between devices, shards(): branch = lax.psum(partial_branch, 'tensor')  565 us
    reduce_sum x128, other arithmetic, backward_step(): d_in = jnp.sum(adjoint * (step_now * value_now)[:, None, :], axis=2)  228 us
    reduce_scatter x1, waiting for transfers between devices, shards(): lax.psum_scatter(large_grads[0], 'fsdp', scatter_dimension=1, tiled=True)  157 us
    dynamic_update_slice x128, other arithmetic, team_pass(): lax.scan(forward_step, start_state, (step_team, value_team, in_team, keep...  138 us
    pad x19, local copies, waits for them, and re-layouts, shards(): lax.associative_scan(combine_pairs, (per_seq(block_fades), per_seq(leavin...  113 us
    pad x19, local copies, waits for them, and re-layouts, shards(): lax.associative_scan(combine_pairs, (per_seq(block_fades), per_seq(block_...  110 us
    unnamed x201, local copies, waits for them, and re-layouts  105 us
    dynamic_update_slice x32, local copies, waits for them, and re-layouts, shards(): lax.scan(second_pass, entry_states, (step_blocks, value_blocks, in_blocks...  102 us
  transfers between devices with their start and end apart: 11, of which 6 were waited for; matrix products, arithmetic and copies ran while one was open for 5% of the time, Pallas kernels for 0%

commit v1 on v0

v1 whole, which is shorter than its diff:
```python
import functools

import jax
import jax.numpy as jnp
from jax import lax
from jax.experimental import pallas as pl
from jax.experimental.pallas import tpu as pltpu
from jax.sharding import PartitionSpec as P

LANES=128; GROUP=8

def fold(pending, value, level_masks):
    level=0
    while pending and pending[-1][0]==level:
        _, first = pending.pop()
        d = 1<<level
        if d < 4:
            value = jnp.where(level_masks[level], first + pltpu.roll(first, 8-d, 0), value + pltpu.roll(value, d, 0))
        else:
            x = jnp.where(level_masks[2], first, value); z = jnp.where(level_masks[2], value, first)
            value = x + pltpu.roll(z, 4, 0)
        level += 1
    pending.append((level,value))

def fold_down(pending, value, level_masks):
    level=0
    while pending and pending[-1][0]==level:
        _, later = pending.pop()
        d = 1<<level
        if d < 4:
            value = jnp.where(level_masks[level], value + pltpu.roll(value, 8-d, 0), later + pltpu.roll(later, d, 0))
        else:
            x = jnp.where(level_masks[2], value, later); z = jnp.where(level_masks[2], later, value)
            value = x + pltpu.roll(z, 4, 0)
        level += 1
    pending.append((level,value))

def masks():
    row = lax.broadcasted_iota(jnp.int32,(8,LANES),0)
    return [(row & d)==0 for d in (1,2,4)]

def tiles(ref, base, groups):
    return [ref[pl.ds(base, 8), g*LANES:(g+1)*LANES] for g in range(groups)]

def row(tile, r):
    return jnp.broadcast_to(tile[r:r+1, :], (8, LANES))

def fwd_kernel(dtf_ref, dtx_ref, bt_ref, ct_ref, a2_ref, y_ref, h_ref, last_ref, state_ref, *, halves, groups):
    chunk = dtf_ref.shape[0]
    @pl.when(pl.program_id(0)==0)
    def _(): state_ref[...] = jnp.zeros_like(state_ref)
    a2 = [[a2_ref[8*i:8*i+8, g*LANES:(g+1)*LANES] for g in range(groups)] for i in range(halves)]
    lane = lax.broadcasted_iota(jnp.int32,(8,LANES),1)
    lm = masks()
    def body(k, st):
        st = [list(s) for s in st]
        base = pl.multiple_of(k*8, 8)
        pend = [[] for _ in range(groups)]
        tf = tiles(dtf_ref, base, groups); tx = tiles(dtx_ref, base, groups)
        for r in range(8):
            t = base + r
            m = lane == t
            bc = [jnp.sum(jnp.where(m, bt_ref[8*i:8*i+8,:], 0.0), axis=1, keepdims=True) for i in range(halves)]
            cc = [jnp.sum(jnp.where(m, ct_ref[8*i:8*i+8,:], 0.0), axis=1, keepdims=True) for i in range(halves)]
            for g in range(groups):
                dtf = row(tf[g], r); dtx = row(tx[g], r)
                p = None
                for i in range(halves):
                    h_ref[pl.ds(pl.multiple_of(t*(8*halves)+8*i,8), 8), g*LANES:(g+1)*LANES] = st[i][g].astype(h_ref.dtype)
                    f = jnp.exp2(dtf*a2[i][g])
                    s = f*st[i][g] + dtx*bc[i]
                    st[i][g] = s
                    q = s*cc[i]
                    p = q if p is None else p+q
                fold(pend[g], p, lm)
        for g in range(groups):
            y_ref[pl.ds(base,8), g*LANES:(g+1)*LANES] = pend[g][0][1]
        return tuple(tuple(s) for s in st)
    st = tuple(tuple(state_ref[8*i:8*i+8, g*LANES:(g+1)*LANES] for g in range(groups)) for i in range(halves))
    st = lax.fori_loop(0, chunk//8, body, st)
    for i in range(halves):
        for g in range(groups):
            state_ref[8*i:8*i+8, g*LANES:(g+1)*LANES] = st[i][g]
            last_ref[8*i:8*i+8, g*LANES:(g+1)*LANES] = st[i][g]

def fwd(dtf, dtx, bt, ct, a2, h_dtype=jnp.float32, chunk=128):
    T,E = dtf.shape; N=a2.shape[0]
    halves, groups = N//8, E//LANES
    rows = lambda w: pl.BlockSpec((w,E), lambda c:(c,0))
    cols = pl.BlockSpec((N,chunk), lambda c:(0,c))
    whole = pl.BlockSpec((N,E), lambda c:(0,0))
    return pl.pallas_call(
        functools.partial(fwd_kernel, halves=halves, groups=groups),
        grid=(T//chunk,),
        in_specs=[rows(chunk), rows(chunk), cols, cols, whole],
        out_specs=[rows(chunk), rows(chunk*N), whole],
        out_shape=[jax.ShapeDtypeStruct((T,E),jnp.float32), jax.ShapeDtypeStruct((T*N,E),h_dtype), jax.ShapeDtypeStruct((N,E),jnp.float32)],
        scratch_shapes=[pltpu.VMEM((N,E),jnp.float32)],
        compiler_params=pltpu.CompilerParams(dimension_semantics=("arbitrary",), vmem_limit_bytes=40<<20),
    )(dtf,dtx,bt,ct,a2)

def bwd_kernel(dtf_ref, dtx_ref, u_ref, bt_ref, ct_ref, a2_ref, h_ref, last_ref,
               iw_ref, ds_ref, din_ref, dout_ref, da_ref, flow_ref, hcur_ref, *, halves, groups):
    chunk = dtf_ref.shape[0]
    @pl.when(pl.program_id(0)==0)
    def _():
        flow_ref[...] = jnp.zeros_like(flow_ref); da_ref[...] = jnp.zeros_like(da_ref)
        hcur_ref[...] = last_ref[...]
    sl = lambda g: slice(g*LANES,(g+1)*LANES)
    a2 = [[a2_ref[8*i:8*i+8, sl(g)] for g in range(groups)] for i in range(halves)]
    lane = lax.broadcasted_iota(jnp.int32,(8,LANES),1)
    lm = masks()
    grab = lambda ref: tuple(tuple(ref[8*i:8*i+8, sl(g)] for g in range(groups)) for i in range(halves))
    def body(k, carry):
        flow, da, hcur, din, dout = carry
        flow=[list(s) for s in flow]; da=[list(s) for s in da]; hcur=[list(s) for s in hcur]
        din=list(din); dout=list(dout)
        base = pl.multiple_of(chunk-8-k*8, 8)
        tf = tiles(dtf_ref, base, groups); tx = tiles(dtx_ref, base, groups); tu = tiles(u_ref, base, groups)
        piw = [[] for _ in range(groups)]; pds=[[] for _ in range(groups)]
        for r in range(7,-1,-1):
            t = base + r
            m = lane == t
            bc = [jnp.sum(jnp.where(m, bt_ref[8*i:8*i+8,:], 0.0), axis=1, keepdims=True) for i in range(halves)]
            cc = [jnp.sum(jnp.where(m, ct_ref[8*i:8*i+8,:], 0.0), axis=1, keepdims=True) for i in range(halves)]
            di=[None]*halves; do=[None]*halves
            for g in range(groups):
                dtf = row(tf[g],r); dtx=row(tx[g],r); u=row(tu[g],r)
                iw=None; ds=None
                for i in range(halves):
                    hp = h_ref[pl.ds(pl.multiple_of(t*(8*halves)+8*i,8),8), sl(g)].astype(jnp.float32)
                    f = jnp.exp2(dtf*a2[i][g])
                    adj = cc[i]*u + flow[i][g]
                    o = hcur[i][g]*u
                    do[i] = o if do[i] is None else do[i]+o
                    n_ = adj*dtx
                    di[i] = n_ if di[i] is None else di[i]+n_
                    fl = f*adj
                    flow[i][g]=fl
                    pulled = fl*hp
                    w = adj*bc[i]; iw = w if iw is None else iw+w
                    s = pulled*a2[i][g]; ds = s if ds is None else ds+s
                    da[i][g] = da[i][g] + pulled*dtf
                    hcur[i][g]=hp
                fold_down(piw[g], iw, lm); fold_down(pds[g], ds, lm)
            for i in range(halves):
                din[i] = jnp.where(m, jnp.sum(di[i],axis=1,keepdims=True), din[i])
                dout[i] = jnp.where(m, jnp.sum(do[i],axis=1,keepdims=True), dout[i])
        for g in range(groups):
            iw_ref[pl.ds(base,8), sl(g)] = piw[g][0][1]
            ds_ref[pl.ds(base,8), sl(g)] = pds[g][0][1]
        tt=lambda x: tuple(tuple(s) for s in x)
        return tt(flow),tt(da),tt(hcur),tuple(din),tuple(dout)
    z = tuple(jnp.zeros((8,LANES),jnp.float32) for _ in range(halves))
    flow,da,hcur,din,dout = lax.fori_loop(0, chunk//8, body, (grab(flow_ref),grab(da_ref),grab(hcur_ref),z,z))
    for i in range(halves):
        din_ref[8*i:8*i+8,:]=din[i]; dout_ref[8*i:8*i+8,:]=dout[i]
        for g in range(groups):
            flow_ref[8*i:8*i+8, sl(g)]=flow[i][g]; da_ref[8*i:8*i+8, sl(g)]=da[i][g]; hcur_ref[8*i:8*i+8, sl(g)]=hcur[i][g]

def bwd(dtf,dtx,u,bt,ct,a2,h,last,chunk=128):
    T,E=dtf.shape; N=a2.shape[0]
    halves, groups = N//8, E//LANES
    n=T//chunk
    rows=lambda w: pl.BlockSpec((w,E), lambda c:(n-1-c,0))
    cols=pl.BlockSpec((N,chunk), lambda c:(0,n-1-c))
    whole=pl.BlockSpec((N,E), lambda c:(0,0))
    f32=jnp.float32
    return pl.pallas_call(
        functools.partial(bwd_kernel, halves=halves, groups=groups),
        grid=(n,),
        in_specs=[rows(chunk)]*3+[cols,cols,whole,rows(chunk*N),whole],
        out_specs=[rows(chunk),rows(chunk),cols,cols,whole],
        out_shape=[jax.ShapeDtypeStruct((T,E),f32)]*2+[jax.ShapeDtypeStruct((N,T),f32)]*2+[jax.ShapeDtypeStruct((N,E),f32)],
        scratch_shapes=[pltpu.VMEM((N,E),f32)]*2,
        compiler_params=pltpu.CompilerParams(dimension_semantics=("arbitrary",), vmem_limit_bytes=40<<20),
    )(dtf,dtx,u,bt,ct,a2,h,last)


EPS = 1e-05
GONE = 1e4
LOG2E = 1.4426950408889634
BF16 = jnp.bfloat16
F32 = jnp.float32


def swap(array, axis, k):
    size = lax.axis_size(axis)
    return lax.ppermute(array, axis, [(i, i ^ k) for i in range(size)])


def gather(array, axis, dim):
    count, me, size = lax.axis_size(axis), lax.axis_index(axis), array.shape[dim]
    shape = array.shape[:dim] + (size * count,) + array.shape[dim + 1 :]
    out = jnp.zeros(shape, array.dtype)
    for k in range(count):
        piece = swap(array, axis, k) if k else array
        out = lax.dynamic_update_slice_in_dim(out, piece, (me ^ k) * size, dim)
    return out


def piece_of(array, axis, dim, index):
    size = array.shape[dim] // lax.axis_size(axis)
    return lax.dynamic_slice_in_dim(array, index * size, size, dim)


def scatter_sum(array, axis, dim, kind):
    me = lax.axis_index(axis)
    total = piece_of(array, axis, dim, me)
    for k in range(1, lax.axis_size(axis)):
        total = total + swap(piece_of(array, axis, dim, me ^ k).astype(kind), axis, k).astype(F32)
    return total


def doubling_sum(array, axes):
    for axis in axes:
        k = 1
        while k < lax.axis_size(axis):
            array = array + swap(array, axis, k)
            k *= 2
    return array


def dot(left, right, left_dim=1, right_dim=0):
    return lax.dot_general(left, right, (((left_dim,), (right_dim,)), ((), ())), preferred_element_type=F32)


def silu_slope(v):
    s = jax.nn.sigmoid(v)
    return s * (1.0 + v * (1.0 - s))


def inverse_rms(x):
    return lax.rsqrt(jnp.mean(x * x, axis=-1, keepdims=True) + EPS)


def shards(
    block_input,
    doc_ids,
    norm_gain,
    in_proj,
    conv_weight,
    conv_bias,
    x_proj,
    dt_proj,
    dt_bias,
    a_log,
    d_skip,
    out_proj,
    grad_output,
):
    seqs, piece, width = block_input.shape
    length = doc_ids.shape[1]
    ctx, ctxs = lax.axis_index("context"), lax.axis_size("context")
    taps, tail = conv_weight.shape[0], conv_weight.shape[0] - 1
    states = a_log.shape[0]
    rows = seqs * length
    inner = in_proj.shape[2] // ctxs
    rank = dt_proj.shape[0] * lax.axis_size("fsdp")

    def mine(array, dim):
        return piece_of(array, "context", dim, ctx)

    in_half = mine(in_proj, 2)
    w_conv = gather(in_half[0], "fsdp", 0)
    x_own = block_input.astype(F32)
    normed_own = (x_own * inverse_rms(x_own) * norm_gain).astype(BF16)
    normed = gather(normed_own, "context", 1).reshape(rows, width)
    small = jnp.concatenate([mine(x_proj, 0).T, mine(dt_proj, 1)], axis=0)
    xcols = x_proj.shape[1]
    small_all = gather(small[None], "fsdp", 0)
    w_x = small_all[:, :xcols].reshape(-1, inner)
    w_dt = small_all[:, xcols:].reshape(rank, inner)
    w_gate = gather(in_half[1], "fsdp", 0)
    w_out = gather(mine(out_proj, 0), "fsdp", 1)
    cotangent = gather(grad_output, "context", 1).reshape(rows, width)
    taps_w, bias, dt_b = mine(conv_weight, 1), mine(conv_bias, 0), mine(dt_bias, 0)
    rates = -jnp.exp(mine(a_log, 1))
    skip = mine(d_skip, 0)

    conv_input = dot(normed, w_conv).astype(BF16)
    padded_ids = jnp.concatenate([jnp.full((seqs, tail), -1, jnp.int32), doc_ids], axis=1)
    same = [
        (padded_ids[:, tail - k : tail - k + length] == doc_ids).astype(F32)[..., None]
        for k in range(taps)
    ]
    padded = jnp.pad(conv_input.reshape(seqs, length, inner), ((0, 0), (tail, 0), (0, 0))).astype(F32)
    shifted = [padded[:, tail - k : tail - k + length] for k in range(taps)]
    conv_output = bias
    for k in range(taps):
        conv_output = conv_output + taps_w[k] * shifted[k] * same[k]
    conv_flat = conv_output.reshape(rows, inner)
    activated = jax.nn.silu(conv_flat).astype(BF16)
    act = activated.astype(F32)

    def all_sum(part):
        part = scatter_sum(part, "context", 1, F32)
        part = scatter_sum(part, "tensor", 1, BF16).astype(BF16)
        return gather(gather(part, "tensor", 1), "context", 1)

    projections = all_sum(dot(w_x, activated, 1, 1))
    dt_input = projections[:rank]
    in_coef = projections[rank : rank + states].astype(F32)
    out_coef = projections[rank + states :].astype(F32)
    dt_logits = dot(dt_input, w_dt, 0, 0) + dt_b
    steps = jax.nn.softplus(dt_logits)
    keep = same[1].reshape(rows, 1)
    fading = jnp.where(keep > 0, steps, GONE)
    fed = steps * act
    rates2 = rates * LOG2E
    scanned, history, last = fwd(fading, fed, in_coef, out_coef, rates2)

    gate = dot(normed, w_gate)
    gate_value = jax.nn.silu(gate)
    mixed = scanned + skip * act
    gated = (mixed * gate_value).astype(BF16)
    d_gated = dot(cotangent, w_out, 1, 1)
    d_mixed = d_gated * gate_value
    d_gate = (d_gated * mixed * silu_slope(gate)).astype(BF16)

    def my_tokens(array):
        array = array.reshape(seqs, length, array.shape[-1])
        parts = [piece_of(array, "context", 1, ctx)]
        for k in range(1, ctxs):
            parts.append(swap(piece_of(array, "context", 1, ctx ^ k), "context", k))
        return [p.reshape(seqs * piece, p.shape[-1]) for p in parts]

    def all_halves(weight):
        return [weight] + [swap(weight, "context", k) for k in range(1, ctxs)]

    def over_tensor(part):
        return scatter_sum(part, "tensor", 0, BF16)

    zplace = lax.axis_index("tensor")

    def my_rows(array):
        return piece_of(array.reshape(seqs * piece, width), "tensor", 0, zplace).astype(F32)

    x_rows = my_rows(block_input)
    branch = dot(
        jnp.concatenate(my_tokens(gated), axis=1), jnp.concatenate(all_halves(w_out), axis=0)
    )
    branch = over_tensor(branch)
    block_output = gather((x_rows + branch).astype(BF16), "tensor", 0).reshape(block_input.shape)

    in_weighted, d_fade, d_in_coef, d_out_coef, d_rates = bwd(
        fading, fed, d_mixed, in_coef, out_coef, rates2, history, last
    )
    d_step = d_fade * (1.0 / LOG2E) + act * in_weighted
    d_logits = (d_step * jax.nn.sigmoid(dt_logits)).astype(BF16)
    d_part = jnp.concatenate([dot(w_dt, d_logits, 1, 1), d_in_coef, d_out_coef], axis=0)
    d_projections = all_sum(d_part)
    grad_out_part = dot(gated, cotangent, 0, 0)
    grad_gate_part = dot(normed, d_gate, 0, 0)
    grad_dt_part = dot(dt_input, d_logits)
    d_act = d_mixed * skip + steps * in_weighted + dot(d_projections, w_x, 0, 0)
    grad_x_part = dot(d_projections, activated)
    d_conv = (d_act * silu_slope(conv_flat)).reshape(seqs, length, inner)
    d_conv_input = jnp.zeros((seqs, length, inner), F32)
    tap_grads = []
    for k in range(taps):
        masked = d_conv * same[k]
        late = jnp.pad(masked, ((0, 0), (0, tail), (0, 0)))[:, k : k + length]
        d_conv_input = d_conv_input + taps_w[k] * late
        tap_grads.append(jnp.sum(masked * shifted[k], axis=(0, 1)))
    d_conv_input = d_conv_input.reshape(rows, inner).astype(BF16)
    grad_conv_part = dot(normed, d_conv_input, 0, 0)

    left = jnp.concatenate(my_tokens(d_gate) + my_tokens(d_conv_input), axis=1)
    right = jnp.concatenate(all_halves(w_gate) + all_halves(w_conv), axis=1)
    d_normed = over_tensor(dot(left, right, 1, 1))
    inv = inverse_rms(x_rows)
    scaled = d_normed * norm_gain
    inner_sum = jnp.sum(scaled * x_rows, axis=-1, keepdims=True)
    grad_rows = my_rows(grad_output) + inv * scaled - x_rows * (inv * inv * inv) * inner_sum / width
    grad_input = gather(grad_rows.astype(BF16), "tensor", 0).reshape(block_input.shape)
    grad_gain = doubling_sum(
        jnp.sum(d_normed * x_rows * inv, axis=0)[None], ("context", "fsdp", "tensor")
    )[0]

    def owned(part, dim, ctx_dim):
        return gather(scatter_sum(part, "fsdp", dim, BF16), "context", ctx_dim)

    grad_in = owned(jnp.stack([grad_conv_part, grad_gate_part]), 1, 2)
    grad_out = owned(grad_out_part, 1, 0)
    grad_x = owned(grad_x_part, 0, 1).T
    grad_dt = owned(grad_dt_part, 0, 1)
    thin = jnp.concatenate(
        [
            d_rates * rates,
            jnp.stack(tap_grads),
            jnp.sum(d_conv, axis=(0, 1))[None],
            jnp.sum(d_logits.astype(F32), axis=0)[None],
            jnp.sum(d_mixed * act, axis=0)[None],
        ],
        axis=0,
    )
    thin = gather(doubling_sum(thin, ("fsdp",)), "context", 1)
    return (
        block_output,
        grad_input,
        grad_gain,
        grad_in,
        thin[states : states + taps],
        thin[states + taps],
        grad_x,
        grad_dt,
        thin[states + taps + 1],
        thin[:states],
        thin[states + taps + 2],
        grad_out,
    )


def solution(mesh):
    placed = (
        P("fsdp", "context", None),
        P("fsdp", None),
        P(),
        P(None, "fsdp", "tensor"),
        P(None, "tensor"),
        P("tensor"),
        P("tensor", "fsdp"),
        P("fsdp", "tensor"),
        P("tensor"),
        P(None, "tensor"),
        P("tensor"),
        P("tensor", "fsdp"),
        P("fsdp", "context", None),
    )
    return jax.shard_map(
        shards,
        mesh=mesh,
        in_specs=placed,
        out_specs=(
            P("fsdp", "context", None),
            P("fsdp", "context", None),
            P(),
            P(None, "fsdp", "tensor"),
            P(None, "tensor"),
            P("tensor"),
            P("tensor", "fsdp"),
            P("fsdp", "tensor"),
            P("tensor"),
            P(None, "tensor"),
            P("tensor"),
            P("tensor", "fsdp"),
        ),
        check_vma=False,
    )
```

time: 2860 us -> 790 us (0.28)
  other arithmetic: 846 us -> 44.2 us
  local copies, waits for them, and re-layouts: 836 us -> 63.3 us
  waiting for transfers between devices: 877 us -> 318 us
  starting transfers between devices: 4.43 us -> 139 us
  Pallas kernels: 0 us -> 119 us
  blocking collectives: 118 us -> 0 us
    psum x3 -> x0, waiting for transfers between devices: 607 us -> none  [the longest x1 565 us: shards(): branch = lax.psum(partial_branch, 'tensor')]
    ppermute x2 -> x72, waiting for transfers between devices: 0.01 us -> 318 us  [swap(): return lax.ppermute(array, axis, [(i, i ^ k) for i in range(size)])]
    reduce_sum x149 -> x4, other arithmetic: 322 us -> 12.1 us  [the longest x1 4.63 us: shards(): tap_grads.append(jnp.sum(masked * shifted[k], axis=(0, 1)))]
    pad x38 -> x0, local copies, waits for them, and re-layouts: 223 us -> none  [the longest x19 113 us: shards(): lax.associative_scan(combine_pairs, (per_seq(block_fades), per_seq(leavin...]
    reduce_scatter x3 -> x0, waiting for transfers between devices: 177 us -> none  [the longest x1 157 us: shards(): lax.psum_scatter(large_grads[0], 'fsdp', scatter_dimension=1, tiled=True)]
    mul x912 -> x0, local copies, waits for them, and re-layouts: 175 us -> none  [the longest x128 98.6 us: backward_step(): adjoint = out_now[:, :, None] * upstream_now[:, None, :] + flow]
    mul x329 -> x4, other arithmetic: 145 us -> 2.12 us  [the longest x1 0.77 us: shards(): rates2 = rates * LOG2E]
    add x171 -> x8, other arithmetic: 139 us -> 2.11 us  [the longest x2 1.45 us: scatter_sum(): total + swap(piece_of(array, axis, dim, me ^ k).astype(kind), axis, k).as...]
  transfers between devices with their start and end apart: 11 -> 72, of which waited for: 6 -> 30; matrix products, arithmetic and copies ran while one was open for 5% -> 19% of each run, Pallas kernels for 0% -> 15%
where the time goes in v1:
time: 790 us; the launch traced here: 781 us
  waiting for transfers between devices  318 us (40%)
  starting transfers between devices  139 us (18%)
  Pallas kernels  119 us (15%)
  matrix products  95.4 us (12%)
  local copies, waits for them, and re-layouts  63.3 us (8%)
  other arithmetic  44.2 us (6%)
    ppermute x72, waiting for transfers between devices, swap(): return lax.ppermute(array, axis, [(i, i ^ k) for i in range(size)])  318 us
    ppermute x72, starting transfers between devices, swap(): return lax.ppermute(array, axis, [(i, i ^ k) for i in range(size)])  139 us
    dot_general x14, matrix products, dot(): lax.dot_general(left, right, (((left_dim,), (right_dim,)), ((), ())), pre...  95.4 us
    pallas_call x1, Pallas kernels, bwd(): pl.pallas_call(functools.partial(bwd_kernel, halves=halves, groups=groups...  78.3 us
    pallas_call x1, Pallas kernels, fwd(): pl.pallas_call(functools.partial(fwd_kernel, halves=halves, groups=groups...  40.9 us
    dynamic_update_slice x39, local copies, waits for them, and re-layouts, gather(): out = lax.dynamic_update_slice_in_dim(out, piece, (me ^ k) * size, dim)  24.8 us
  transfers between devices with their start and end apart: 72, of which 30 were waited for; matrix products, arithmetic and copies ran while one was open for 19% of the time, Pallas kernels for 15%

profile of v1, /device:TPU:0, one launch (start us, length us, event | category | flops | bytes accessed | tf_op | source)
XLA Modules:
  0.0 781.2 jit_solution(5239250350766866453)
XLA Ops:
  0.7 3.1 fusion
  8.7 3.3 copy-done.10
  20.7 4.5 reshape.215.clone.1
  33.2 2.9 collective-permute-start.2
  39.3 2.9 collective-permute-start.6
  46.2 4.8 collective-permute-done.15
  52.6 9.7 %collective-permute-done.6 = bf16[512,512]{1,0:T(8,128)(2,1)S(1)} collective-permute-done((bf16[512,512]{1,0:T(8,128)(2,1)}, bf16[512,512]{1,0:T(8,128)(2,1)S(1)}, u32[]{:S(2)}, u32[]{:S(2)}) %collective-permute-start.6) | collective-permute-done | bytes 524320 | tf_op jit(solution)/shard_map/ppermute | solution.py:189
  63.9 14.8 %collective-permute-done.16 = bf16[512,512]{1,0:T(8,128)(2,1)S(1)} collective-permute-done((bf16[512,512]{1,0:T(8,128)(2,1)S(1)}, bf16[512,512]{1,0:T(8,128)(2,1)S(1)}, u32[]{:S(2)}, u32[]{:S(2)}) %collective-permute-start.16) | collective-permute-done | bytes 524320 | tf_op jit(solution)/shard_map/ppermute | solution.py:189
  85.0 12.9 %collective-permute-done.20 = bf16[512,512]{1,0:T(8,128)(2,1)S(1)} collective-permute-done((bf16[512,512]{1,0:T(8,128)(2,1)S(1)}, bf16[512,512]{1,0:T(8,128)(2,1)S(1)}, u32[]{:S(2)}, u32[]{:S(2)}) %collective-permute-start.20) | collective-permute-done | bytes 524320 | tf_op jit(solution)/shard_map/ppermute | solution.py:189
  99.6 4.8 bitcast_dynamic-update-slice_fusion.2
  104.4 8.6 %fusion.43 = bf16[1,2048,512]{2,1,0:T(8,128)(2,1)S(1)} fusion(bf16[2048,2048]{1,0:T(8,128)(2,1)} %bitcast_dynamic-update-slice_fusion.2, bf16[2048,512]{1,0:T(8,128)(2,1)} %constant_dynamic-update-slice_fusion.30), kind=kOutput, calls=%fused_computation.89 | convolution fusion | flops 4296015872 | bytes 12582912 | tf_op jit(solution)/shard_map/dot_general | solution.py:225
  113.0 2.7 pad_convert_fusion
  115.8 6.0 fusion.89
  124.1 22.1 %fusion.22 = (f32[512]{0:T(512)}, f32[2048,512]{1,0:T(8,128)}, bf16[2048,512]{1,0:T(8,128)(2,1)S(1)}, f32[1,2048,512]{2,1,0:T(8,128)}, f32[2048,512]{1,0:T(8,128)}) fusion(f32[2048,512]{1,0:T(8,128)} %fusion.89, f32[2048]{0:T(1024)S(1)} %bitcast.167, f32[1,2051,512]{2,1,0:T(8,128)} %pad_convert_fusion, f32[512]{0:T(512)S(1)} %bitcast.175, ...), kind=kOutput, calls=%fused_computation.40 | convolution fusion | flops 4320132608 | bytes 46174208 | tf_op jit(solution)/shard_map/dot_general | solution.py:225
  146.2 3.6 fusion.67
  154.6 3.7 collective-permute-start.10
  167.6 3.1 collective-permute-start.12
  171.8 3.6 collective-permute-done.12
  178.8 4.5 convert_multiply_fusion.5
  183.3 40.9 %shard_map.220 = (f32[2048,512]{1,0:T(8,128)S(1)}, f32[32768,512]{1,0:T(8,128)}, f32[16,512]{1,0:T(8,128)S(1)}) custom-call(f32[2048,512]{1,0:T(8,128)S(1)} %get-tuple-element.84.dtf_ref, f32[2048,512]{1,0:T(8,128)S(1)} %get-tuple-element.83.dtx_ref, f32[16,2048]{1,0:T(8,128)S(1)} %get-tuple-element.100.bt_ref, f32[16,2048]{1,0:T(8,128)S(1)} %get-tuple-element.99.ct_ref, ...), custom_call_target="tpu_custom_call" | custom-call | tf_op jit(solution)/shard_map/pallas_call | solution.py:92
  226.2 78.3 %shard_map.221 = (f32[2048,512]{1,0:T(8,128)S(1)}, f32[2048,512]{1,0:T(8,128)S(1)}, f32[16,2048]{1,0:T(8,128)S(1)}, f32[16,2048]{1,0:T(8,128)S(1)}, f32[16,512]{1,0:T(8,128)S(1)}) custom-call(f32[2048,512]{1,0:T(8,128)S(1)} %get-tuple-element.84.dtf_ref, f32[2048,512]{1,0:T(8,128)} %copy-done.2, f32[2048,512]{1,0:T(8,128)} %get-tuple-element.43.u_ref, ...), custom_call_target="tpu_custom_call" | custom-call | tf_op jit(solution)/shard_map/pallas_call | solution.py:169
  304.5 8.2 %multiply_convert_fusion = (bf16[2048,512]{1,0:T(8,128)(2,1)}, bf16[2048,512]{1,0:T(8,128)(2,1)S(1)}, f32[512]{0:T(512)}, bf16[2048,512]{1,0:T(8,128)(2,1)S(1)}) fusion(f32[2048,512]{1,0:T(8,128)} %fusion.89, f32[2048,512]{1,0:T(8,128)} %get-tuple-element.122, f32[2048,512]{1,0:T(8,128)S(1)} %copy-done.4, bf16[2048,512]{1,0:T(8,128)(2,1)S(1)} %get-tuple-element.44, ...), kind=kLoop, calls=%fused_computation.80 | loop fusion | flops 28311040 | bytes 33560576 | tf_op jit(solution)/shard_map/convert_element_type | solution.py:319
  314.0 7.2 fusion.92
  324.5 6.1 convolution_bitcast_fusion
  342.4 3.9 collective-permute-done.33
  349.0 3.9 collective-permute-done.35
  354.6 4.6 collective-permute-done.36
  361.6 3.8 collective-permute-done.37
  370.6 6.9 fusion.82
  379.3 4.6 multiply_reduce_fusion
  383.9 3.7 fusion.15
  393.4 7.1 fusion.23
  414.3 14.1 %fusion.3 = f32[1024,2048]{1,0:T(8,128)} fusion(bf16[2048,512]{1,0:T(8,128)(2,1)} %collective-permute-done.41, bf16[2048,512]{1,0:T(8,128)(2,1)} %constant_dynamic-update-slice_fusion.30, bf16[2048,512]{1,0:T(8,128)(2,1)} %collective-permute-done.40, bf16[2048,512]{1,0:T(8,128)(2,1)} %copy-done.22, bf16[1024,512]{1,0:T(8,128)(2,1)} %bitcast.189, ...), kind=kOutput, calls=%fused_computation.14 | convolution fusion | flops 8640266240 | bytes 20971520 | tf_op jit(solution)/shard_map/dot_general | solution.py:225
  428.4 3.4 dynamic-slice_convert_fusion.2
  433.3 7.3 convolution_bitcast_fusion.1
  441.1 2.9 collective-permute-start.43
  444.0 14.2 %collective-permute-done.23 = bf16[256,2048]{1,0:T(8,128)(2,1)} collective-permute-done((bf16[256,2048]{1,0:T(8,128)(2,1)}, bf16[256,2048]{1,0:T(8,128)(2,1)}, u32[]{:S(2)}, u32[]{:S(2)}) %collective-permute-start.23) | collective-permute-done | bytes 1048608 | tf_op jit(solution)/shard_map/ppermute | solution.py:189
  461.9 20.7 %collective-permute-done.24 = bf16[256,2048]{1,0:T(8,128)(2,1)} collective-permute-done((bf16[256,2048]{1,0:T(8,128)(2,1)}, bf16[256,2048]{1,0:T(8,128)(2,1)}, u32[]{:S(2)}, u32[]{:S(2)}) %collective-permute-start.24) | collective-permute-done | bytes 1048608 | tf_op jit(solution)/shard_map/ppermute | solution.py:189
  484.4 18.7 %collective-permute-done.42 = bf16[256,2048]{1,0:T(8,128)(2,1)S(1)} collective-permute-done((bf16[256,2048]{1,0:T(8,128)(2,1)S(1)}, bf16[256,2048]{1,0:T(8,128)(2,1)S(1)}, u32[]{:S(2)}, u32[]{:S(2)}) %collective-permute-start.42) | collective-permute-done | bytes 1048608 | tf_op jit(solution)/shard_map/ppermute | solution.py:189
  506.3 3.3 bitcast_dynamic-update-slice_fusion.11
  509.6 62.7 %collective-permute-done.43 = bf16[256,2048]{1,0:T(8,128)(2,1)S(1)} collective-permute-done((bf16[256,2048]{1,0:T(8,128)(2,1)S(1)}, bf16[256,2048]{1,0:T(8,128)(2,1)S(1)}, u32[]{:S(2)}, u32[]{:S(2)}) %collective-permute-start.43) | collective-permute-done | bytes 1048608 | tf_op jit(solution)/shard_map/ppermute | solution.py:189
  572.4 23.3 %collective-permute-start.27 = (bf16[256,2048]{1,0:T(8,128)(2,1)S(1)}, bf16[256,2048]{1,0:T(8,128)(2,1)S(1)}, u32[]{:S(2)}, u32[]{:S(2)}) collective-permute-start(bf16[256,2048]{1,0:T(8,128)(2,1)S(1)} %get-tuple-element.61), channel_id=1, source_target_pairs={{0,2},{1,3},{2,0},{3,1},{4,6},{5,7},{6,4},{7,5},{8,10},{9,11},{10,... | collective-permute-start | bytes 3145736 | tf_op jit(solution)/shard_map/ppermute | solution.py:189
  595.6 2.9 fusion.52
  609.3 3.0 collective-permute-start.46
  612.3 53.8 %collective-permute-done.27 = bf16[256,2048]{1,0:T(8,128)(2,1)S(1)} collective-permute-done((bf16[256,2048]{1,0:T(8,128)(2,1)S(1)}, bf16[256,2048]{1,0:T(8,128)(2,1)S(1)}, u32[]{:S(2)}, u32[]{:S(2)}) %collective-permute-start.27) | collective-permute-done | bytes 1048608 | tf_op jit(solution)/shard_map/ppermute | solution.py:189
  666.2 19.4 %collective-permute-done.51 = f32[1,2048]{1,0:T(1,128)S(1)} collective-permute-done((f32[1,2048]{1,0:T(1,128)S(1)}, f32[1,2048]{1,0:T(1,128)S(1)}, u32[]{:S(2)}, u32[]{:S(2)}) %collective-permute-start.51) | collective-permute-done | bytes 8224 | tf_op jit(solution)/shard_map/ppermute | solution.py:189
  686.8 45.7 %collective-permute-start.52 = (f32[1,2048]{1,0:T(1,128)S(1)}, f32[1,2048]{1,0:T(1,128)S(1)}, u32[]{:S(2)}, u32[]{:S(2)}) collective-permute-start(f32[1,2048]{1,0:T(1,128)S(1)} %add.421), channel_id=1, source_target_pairs={{0,2},{1,3},{2,0},{3,1},{4,6},{5,7},{6,4},{7,5},{8,10},{9,11},{10,... | collective-permute-start | bytes 24584 | tf_op jit(solution)/shard_map/ppermute | solution.py:189
  732.7 43.6 %collective-permute-done.52 = f32[1,2048]{1,0:T(1,128)S(1)} collective-permute-done((f32[1,2048]{1,0:T(1,128)S(1)}, f32[1,2048]{1,0:T(1,128)S(1)}, u32[]{:S(2)}, u32[]{:S(2)}) %collective-permute-start.52) | collective-permute-done | bytes 8224 | tf_op jit(solution)/shard_map/ppermute | solution.py:189
  (360 shorter events, 138.6 us)
Async XLA Ops:
  12.0 87.6 %collective-permute-start.3 = (bf16[1,1024,2048]{2,1,0:T(8,128)(2,1)}, bf16[1,1024,2048]{2,1,0:T(8,128)(2,1)}, u32[]{:S(2)}, u32[]{:S(2)}) collective-permute-start(bf16[1,1024,2048]{2,1,0:T(8,128)(2,1)} %get-tuple-element.69), channel_id=1, source_target_pairs={{0,4},{4,0},{1,5},{5,1},{2,6},{6,2},{3,7},{7,3},{8,12},{12,8},{9,1... | collective-permute-start | bytes 12582920 | tf_op jit(solution)/shard_map/ppermute | solution.py:189
  16.0 26.3 %collective-permute-start.4 = (bf16[512,512]{1,0:T(8,128)(2,1)}, bf16[512,512]{1,0:T(8,128)(2,1)}, u32[]{:S(2)}, u32[]{:S(2)}) collective-permute-start(bf16[512,512]{1,0:T(8,128)(2,1)} %get-tuple-element.67), channel_id=1, source_target_pairs={{0,8},{8,0},{16,24},{24,16},{1,9},{9,1},{17,25},{25,17},{2,10},{10... | collective-permute-start | bytes 1572872 | tf_op jit(solution)/shard_map/ppermute | solution.py:189
  18.5 24.3 %collective-permute-start.5 = (bf16[512,512]{1,0:T(8,128)(2,1)}, bf16[512,512]{1,0:T(8,128)(2,1)}, u32[]{:S(2)}, u32[]{:S(2)}) collective-permute-start(bf16[512,512]{1,0:T(8,128)(2,1)} %get-tuple-element.67), channel_id=1, source_target_pairs={{0,16},{8,24},{16,0},{24,8},{1,17},{9,25},{17,1},{25,9},{2,18},{10... | collective-permute-start | bytes 1572872 | tf_op jit(solution)/shard_map/ppermute | solution.py:189
  20.0 13.2 %collective-permute-start = (bf16[1,72,512]{2,1,0:T(8,128)(2,1)S(1)}, bf16[1,72,512]{2,1,0:T(8,128)(2,1)S(1)}, u32[]{:S(2)}, u32[]{:S(2)}) collective-permute-start(bf16[1,72,512]{2,1,0:T(8,128)(2,1)S(1)} %maximum_bitcast_fusion), channel_id=1, source_target_pairs={{0,8},{8,0},{16,24},{24,16},{1,9},{9,1},{17,25},{25,17},{2,10},{10... | collective-permute-start | bytes 221192 | tf_op jit(solution)/shard_map/ppermute | solution.py:189
  20.7 15.4 %collective-permute-start.1 = (bf16[1,72,512]{2,1,0:T(8,128)(2,1)S(1)}, bf16[1,72,512]{2,1,0:T(8,128)(2,1)S(1)}, u32[]{:S(2)}, u32[]{:S(2)}) collective-permute-start(bf16[1,72,512]{2,1,0:T(8,128)(2,1)S(1)} %maximum_bitcast_fusion), channel_id=1, source_target_pairs={{0,16},{8,24},{16,0},{24,8},{1,17},{9,25},{17,1},{25,9},{2,18},{10... | collective-permute-start | bytes 221192 | tf_op jit(solution)/shard_map/ppermute | solution.py:189
  36.2 14.9 %collective-permute-start.15 = (bf16[512,512]{1,0:T(8,128)(2,1)S(1)}, bf16[512,512]{1,0:T(8,128)(2,1)S(1)}, u32[]{:S(2)}, u32[]{:S(2)}) collective-permute-start(bf16[512,512]{1,0:T(8,128)(2,1)S(1)} %get-tuple-element.63), channel_id=1, source_target_pairs={{0,8},{8,0},{16,24},{24,16},{1,9},{9,1},{17,25},{25,17},{2,10},{10... | collective-permute-start | bytes 1572872 | tf_op jit(solution)/shard_map/ppermute | solution.py:189
  39.3 23.0 %collective-permute-start.6 = (bf16[512,512]{1,0:T(8,128)(2,1)}, bf16[512,512]{1,0:T(8,128)(2,1)S(1)}, u32[]{:S(2)}, u32[]{:S(2)}) collective-permute-start(bf16[512,512]{1,0:T(8,128)(2,1)} %get-tuple-element.67), channel_id=1, source_target_pairs={{0,24},{8,16},{16,8},{24,0},{1,25},{9,17},{17,9},{25,1},{2,26},{10... | collective-permute-start | bytes 1572872 | tf_op jit(solution)/shard_map/ppermute | solution.py:189
  42.3 36.4 %collective-permute-start.16 = (bf16[512,512]{1,0:T(8,128)(2,1)S(1)}, bf16[512,512]{1,0:T(8,128)(2,1)S(1)}, u32[]{:S(2)}, u32[]{:S(2)}) collective-permute-start(bf16[512,512]{1,0:T(8,128)(2,1)S(1)} %get-tuple-element.63), channel_id=1, source_target_pairs={{0,16},{8,24},{16,0},{24,8},{1,17},{9,25},{17,1},{25,9},{2,18},{10... | collective-permute-start | bytes 1572872 | tf_op jit(solution)/shard_map/ppermute | solution.py:189
  42.8 37.8 %collective-permute-start.17 = (bf16[512,512]{1,0:T(8,128)(2,1)S(1)}, bf16[512,512]{1,0:T(8,128)(2,1)S(1)}, u32[]{:S(2)}, u32[]{:S(2)}) collective-permute-start(bf16[512,512]{1,0:T(8,128)(2,1)S(1)} %get-tuple-element.63), channel_id=1, source_target_pairs={{0,24},{8,16},{16,8},{24,0},{1,25},{9,17},{17,9},{25,1},{2,26},{10... | collective-permute-start | bytes 1572872 | tf_op jit(solution)/shard_map/ppermute | solution.py:189
  51.1 33.1 %collective-permute-start.19 = (bf16[512,512]{1,0:T(8,128)(2,1)S(1)}, bf16[512,512]{1,0:T(8,128)(2,1)S(1)}, u32[]{:S(2)}, u32[]{:S(2)}) collective-permute-start(bf16[512,512]{1,0:T(8,128)(2,1)S(1)} %get-tuple-element.71), channel_id=1, source_target_pairs={{0,8},{8,0},{16,24},{24,16},{1,9},{9,1},{17,25},{25,17},{2,10},{10... | collective-permute-start | bytes 1572872 | tf_op jit(solution)/shard_map/ppermute | solution.py:189
  62.3 35.6 %collective-permute-start.20 = (bf16[512,512]{1,0:T(8,128)(2,1)S(1)}, bf16[512,512]{1,0:T(8,128)(2,1)S(1)}, u32[]{:S(2)}, u32[]{:S(2)}) collective-permute-start(bf16[512,512]{1,0:T(8,128)(2,1)S(1)} %get-tuple-element.71), channel_id=1, source_target_pairs={{0,16},{8,24},{16,0},{24,8},{1,17},{9,25},{17,1},{25,9},{2,18},{10... | collective-permute-start | bytes 1572872 | tf_op jit(solution)/shard_map/ppermute | solution.py:189
  78.7 43.1 %collective-permute-start.29 = (bf16[1,1024,2048]{2,1,0:T(8,128)(2,1)S(1)}, bf16[1,1024,2048]{2,1,0:T(8,128)(2,1)S(1)}, u32[]{:S(2)}, u32[]{:S(2)}) collective-permute-start(bf16[1,1024,2048]{2,1,0:T(8,128)(2,1)S(1)} %copy-done.13), channel_id=1, source_target_pairs={{0,4},{4,0},{1,5},{5,1},{2,6},{6,2},{3,7},{7,3},{8,12},{12,8},{9,1... | collective-permute-start | bytes 12582920 | tf_op jit(solution)/shard_map/ppermute | solution.py:189
  80.6 18.2 %collective-permute-start.21 = (bf16[512,512]{1,0:T(8,128)(2,1)S(1)}, bf16[512,512]{1,0:T(8,128)(2,1)S(1)}, u32[]{:S(2)}, u32[]{:S(2)}) collective-permute-start(bf16[512,512]{1,0:T(8,128)(2,1)S(1)} %get-tuple-element.71), channel_id=1, source_target_pairs={{0,24},{8,16},{16,8},{24,0},{1,25},{9,17},{17,9},{25,1},{2,26},{10... | collective-permute-start | bytes 1572872 | tf_op jit(solution)/shard_map/ppermute | solution.py:189
  177.8 232.1 %collective-permute-start.40 = (bf16[2048,512]{1,0:T(8,128)(2,1)}, bf16[2048,512]{1,0:T(8,128)(2,1)}, u32[]{:S(2)}, u32[]{:S(2)}) collective-permute-start(bf16[2048,512]{1,0:T(8,128)(2,1)} %copy-done.22), channel_id=1, source_target_pairs={{0,4},{4,0},{1,5},{5,1},{2,6},{6,2},{3,7},{7,3},{8,12},{12,8},{9,1... | collective-permute-start | bytes 6291464 | tf_op jit(solution)/shard_map/ppermute | solution.py:189
  321.5 43.9 %collective-permute-start.68 = (bf16[512,512]{1,0:T(8,128)(2,1)S(1)}, bf16[512,512]{1,0:T(8,128)(2,1)S(1)}, u32[]{:S(2)}, u32[]{:S(2)}) collective-permute-start(bf16[512,512]{1,0:T(8,128)(2,1)S(1)} %get-tuple-element.85), channel_id=1, source_target_pairs={{0,8},{8,0},{16,24},{24,16},{1,9},{9,1},{17,25},{25,17},{2,10},{10... | collective-permute-start | bytes 1572872 | tf_op jit(solution)/shard_map/ppermute | solution.py:189
  322.2 14.0 %collective-permute-start.64 = (bf16[32,512]{1,0:T(8,128)(2,1)S(1)}, bf16[32,512]{1,0:T(8,128)(2,1)S(1)}, u32[]{:S(2)}, u32[]{:S(2)}) collective-permute-start(bf16[32,512]{1,0:T(8,128)(2,1)S(1)} %get-tuple-element.107), channel_id=1, source_target_pairs={{0,8},{8,0},{16,24},{24,16},{1,9},{9,1},{17,25},{25,17},{2,10},{10... | collective-permute-start | bytes 98312 | tf_op jit(solution)/shard_map/ppermute | solution.py:189
  323.7 13.3 %collective-permute-start.65 = (bf16[32,512]{1,0:T(8,128)(2,1)S(1)}, bf16[32,512]{1,0:T(8,128)(2,1)S(1)}, u32[]{:S(2)}, u32[]{:S(2)}) collective-permute-start(bf16[32,512]{1,0:T(8,128)(2,1)S(1)} %get-tuple-element.109), channel_id=1, source_target_pairs={{0,16},{8,24},{16,0},{24,8},{1,17},{9,25},{17,1},{25,9},{2,18},{10... | collective-permute-start | bytes 98312 | tf_op jit(solution)/shard_map/ppermute | solution.py:189
  324.4 9.5 %collective-permute-start.31 = (f32[160,1024]{1,0:T(8,128)S(1)}, f32[160,1024]{1,0:T(8,128)S(1)}, u32[]{:S(2)}, u32[]{:S(2)}) collective-permute-start(f32[160,1024]{1,0:T(8,128)S(1)} %constant_dynamic-slice_fusion.2), channel_id=1, source_target_pairs={{0,4},{4,0},{1,5},{5,1},{2,6},{6,2},{3,7},{7,3},{8,12},{12,8},{9,1... | collective-permute-start | bytes 1966088 | tf_op jit(solution)/shard_map/ppermute | solution.py:189
  337.0 9.2 %collective-permute-start.33 = (bf16[160,256]{1,0:T(8,128)(2,1)S(1)}, bf16[160,256]{1,0:T(8,128)(2,1)S(1)}, u32[]{:S(2)}, u32[]{:S(2)}) collective-permute-start(bf16[160,256]{1,0:T(8,128)(2,1)S(1)} %get-tuple-element.98), channel_id=1, source_target_pairs={{0,2},{1,3},{2,0},{3,1},{4,6},{5,7},{6,4},{7,5},{8,10},{9,11},{10,... | collective-permute-start | bytes 245768 | tf_op jit(solution)/shard_map/ppermute | solution.py:189
  341.6 24.4 %collective-permute-start.69 = (bf16[512,512]{1,0:T(8,128)(2,1)S(1)}, bf16[512,512]{1,0:T(8,128)(2,1)S(1)}, u32[]{:S(2)}, u32[]{:S(2)}) collective-permute-start(bf16[512,512]{1,0:T(8,128)(2,1)S(1)} %get-tuple-element.87), channel_id=1, source_target_pairs={{0,16},{8,24},{16,0},{24,8},{1,17},{9,25},{17,1},{25,9},{2,18},{10... | collective-permute-start | bytes 1572872 | tf_op jit(solution)/shard_map/ppermute | solution.py:189
  346.2 19.9 %collective-permute-start.70 = (bf16[512,512]{1,0:T(8,128)(2,1)S(1)}, bf16[512,512]{1,0:T(8,128)(2,1)S(1)}, u32[]{:S(2)}, u32[]{:S(2)}) collective-permute-start(bf16[512,512]{1,0:T(8,128)(2,1)S(1)} %get-tuple-element.86), channel_id=1, source_target_pairs={{0,24},{8,16},{16,8},{24,0},{1,25},{9,17},{17,9},{25,1},{2,26},{10... | collective-permute-start | bytes 1572872 | tf_op jit(solution)/shard_map/ppermute | solution.py:189
  365.4 44.9 %collective-permute-start.41 = (bf16[2048,512]{1,0:T(8,128)(2,1)}, bf16[2048,512]{1,0:T(8,128)(2,1)}, u32[]{:S(2)}, u32[]{:S(2)}) collective-permute-start(bf16[2048,512]{1,0:T(8,128)(2,1)} %constant_dynamic-update-slice_fusion.30), channel_id=1, source_target_pairs={{0,4},{4,0},{1,5},{5,1},{2,6},{6,2},{3,7},{7,3},{8,12},{12,8},{9,1... | collective-permute-start | bytes 6291464 | tf_op jit(solution)/shard_map/ppermute | solution.py:189
  365.4 22.3 %collective-permute-start.22 = (bf16[512,2048]{1,0:T(8,128)(2,1)}, bf16[512,2048]{1,0:T(8,128)(2,1)}, u32[]{:S(2)}, u32[]{:S(2)}) collective-permute-start(bf16[512,2048]{1,0:T(8,128)(2,1)} %constant_dynamic-update-slice_fusion.16), channel_id=1, source_target_pairs={{0,4},{4,0},{1,5},{5,1},{2,6},{6,2},{3,7},{7,3},{8,12},{12,8},{9,1... | collective-permute-start | bytes 6291464 | tf_op jit(solution)/shard_map/ppermute | solution.py:189
  366.0 26.1 %collective-permute-start.18 = (bf16[1,1024,512]{2,1,0:T(8,128)(2,1)}, bf16[1,1024,512]{2,1,0:T(8,128)(2,1)}, u32[]{:S(2)}, u32[]{:S(2)}) collective-permute-start(bf16[1,1024,512]{2,1,0:T(8,128)(2,1)} %get-tuple-element.95), channel_id=1, source_target_pairs={{0,4},{4,0},{1,5},{5,1},{2,6},{6,2},{3,7},{7,3},{8,12},{12,8},{9,1... | collective-permute-start | bytes 3145736 | tf_op jit(solution)/shard_map/ppermute | solution.py:189
  378.7 13.5 %collective-permute-start.60 = (bf16[40,512]{1,0:T(8,128)(2,1)}, bf16[40,512]{1,0:T(8,128)(2,1)}, u32[]{:S(2)}, u32[]{:S(2)}) collective-permute-start(bf16[40,512]{1,0:T(8,128)(2,1)} %get-tuple-element.104), channel_id=1, source_target_pairs={{0,8},{8,0},{16,24},{24,16},{1,9},{9,1},{17,25},{25,17},{2,10},{10... | collective-permute-start | bytes 122888 | tf_op jit(solution)/shard_map/ppermute | solution.py:189
  392.2 20.8 %collective-permute-start.30 = (bf16[1,1024,512]{2,1,0:T(8,128)(2,1)}, bf16[1,1024,512]{2,1,0:T(8,128)(2,1)S(1)}, u32[]{:S(2)}, u32[]{:S(2)}) collective-permute-start(bf16[1,1024,512]{2,1,0:T(8,128)(2,1)} %get-tuple-element.89), channel_id=1, source_target_pairs={{0,4},{4,0},{1,5},{5,1},{2,6},{6,2},{3,7},{7,3},{8,12},{12,8},{9,1... | collective-permute-start | bytes 3145736 | tf_op jit(solution)/shard_map/ppermute | solution.py:189
  393.2 19.7 %collective-permute-start.39 = (bf16[1,1024,512]{2,1,0:T(8,128)(2,1)}, bf16[1,1024,512]{2,1,0:T(8,128)(2,1)S(1)}, u32[]{:S(2)}, u32[]{:S(2)}) collective-permute-start(bf16[1,1024,512]{2,1,0:T(8,128)(2,1)} %get-tuple-element.93), channel_id=1, source_target_pairs={{0,4},{4,0},{1,5},{5,1},{2,6},{6,2},{3,7},{7,3},{8,12},{12,8},{9,1... | collective-permute-start | bytes 3145736 | tf_op jit(solution)/shard_map/ppermute | solution.py:189
  409.8 31.3 %collective-permute-start.71 = (f32[512,512]{1,0:T(8,128)}, f32[512,512]{1,0:T(8,128)}, u32[]{:S(2)}, u32[]{:S(2)}) collective-permute-start(f32[512,512]{1,0:T(8,128)} %get-tuple-element.35), channel_id=1, source_target_pairs={{0,4},{4,0},{1,5},{5,1},{2,6},{6,2},{3,7},{7,3},{8,12},{12,8},{9,1... | collective-permute-start | bytes 3145736 | tf_op jit(solution)/shard_map/ppermute | solution.py:189
  409.9 48.3 %collective-permute-start.23 = (bf16[256,2048]{1,0:T(8,128)(2,1)}, bf16[256,2048]{1,0:T(8,128)(2,1)}, u32[]{:S(2)}, u32[]{:S(2)}) collective-permute-start(bf16[256,2048]{1,0:T(8,128)(2,1)} %get-tuple-element.80), channel_id=1, source_target_pairs={{0,1},{1,0},{2,3},{3,2},{4,5},{5,4},{6,7},{7,6},{8,9},{9,8},{10,11... | collective-permute-start | bytes 3145736 | tf_op jit(solution)/shard_map/ppermute | solution.py:189
  410.3 72.2 %collective-permute-start.24 = (bf16[256,2048]{1,0:T(8,128)(2,1)}, bf16[256,2048]{1,0:T(8,128)(2,1)}, u32[]{:S(2)}, u32[]{:S(2)}) collective-permute-start(bf16[256,2048]{1,0:T(8,128)(2,1)} %get-tuple-element.82), channel_id=1, source_target_pairs={{0,2},{1,3},{2,0},{3,1},{4,6},{5,7},{6,4},{7,5},{8,10},{9,11},{10,... | collective-permute-start | bytes 3145736 | tf_op jit(solution)/shard_map/ppermute | solution.py:189
  412.9 18.9 %collective-permute-start.63 = (f32[40,512]{1,0:T(8,128)}, f32[40,512]{1,0:T(8,128)S(1)}, u32[]{:S(2)}, u32[]{:S(2)}) collective-permute-start(f32[40,512]{1,0:T(8,128)} %get-tuple-element.39), channel_id=1, source_target_pairs={{0,4},{4,0},{1,5},{5,1},{2,6},{6,2},{3,7},{7,3},{8,12},{12,8},{9,1... | collective-permute-start | bytes 245768 | tf_op jit(solution)/shard_map/ppermute | solution.py:189
  413.0 20.3 %collective-permute-start.59 = (f32[23,512]{1,0:T(8,128)S(1)}, f32[23,512]{1,0:T(8,128)S(1)}, u32[]{:S(2)}, u32[]{:S(2)}) collective-permute-start(f32[23,512]{1,0:T(8,128)S(1)} %get-tuple-element.41), channel_id=1, source_target_pairs={{0,4},{4,0},{1,5},{5,1},{2,6},{6,2},{3,7},{7,3},{8,12},{12,8},{9,1... | collective-permute-start | bytes 141320 | tf_op jit(solution)/shard_map/ppermute | solution.py:189
  431.8 51.6 %collective-permute-start.25 = (bf16[256,2048]{1,0:T(8,128)(2,1)S(1)}, bf16[256,2048]{1,0:T(8,128)(2,1)S(1)}, u32[]{:S(2)}, u32[]{:S(2)}) collective-permute-start(bf16[256,2048]{1,0:T(8,128)(2,1)S(1)} %copy-done.24), channel_id=1, source_target_pairs={{0,3},{1,2},{2,1},{3,0},{4,7},{5,6},{6,5},{7,4},{8,11},{9,10},{10,... | collective-permute-start | bytes 3145736 | tf_op jit(solution)/shard_map/ppermute | solution.py:189
  433.3 69.8 %collective-permute-start.42 = (bf16[256,2048]{1,0:T(8,128)(2,1)S(1)}, bf16[256,2048]{1,0:T(8,128)(2,1)S(1)}, u32[]{:S(2)}, u32[]{:S(2)}) collective-permute-start(bf16[256,2048]{1,0:T(8,128)(2,1)S(1)} %get-tuple-element.77), channel_id=1, source_target_pairs={{0,1},{1,0},{2,3},{3,2},{4,5},{5,4},{6,7},{7,6},{8,9},{9,8},{10,11... | collective-permute-start | bytes 3145736 | tf_op jit(solution)/shard_map/ppermute | solution.py:189
  441.1 131.2 %collective-permute-start.43 = (bf16[256,2048]{1,0:T(8,128)(2,1)S(1)}, bf16[256,2048]{1,0:T(8,128)(2,1)S(1)}, u32[]{:S(2)}, u32[]{:S(2)}) collective-permute-start(bf16[256,2048]{1,0:T(8,128)(2,1)S(1)} %get-tuple-element.79), channel_id=1, source_target_pairs={{0,2},{1,3},{2,0},{3,1},{4,6},{5,7},{6,4},{7,5},{8,10},{9,11},{10,... | collective-permute-start | bytes 3145736 | tf_op jit(solution)/shard_map/ppermute | solution.py:189
  458.2 114.2 %collective-permute-start.44 = (bf16[256,2048]{1,0:T(8,128)(2,1)S(1)}, bf16[256,2048]{1,0:T(8,128)(2,1)S(1)}, u32[]{:S(2)}, u32[]{:S(2)}) collective-permute-start(bf16[256,2048]{1,0:T(8,128)(2,1)S(1)} %get-tuple-element.78), channel_id=1, source_target_pairs={{0,3},{1,2},{2,1},{3,0},{4,7},{5,6},{6,5},{7,4},{8,11},{9,10},{10,... | collective-permute-start | bytes 3145736 | tf_op jit(solution)/shard_map/ppermute | solution.py:189
  482.6 115.9 %collective-permute-start.53 = (bf16[2,512,512]{2,1,0:T(8,128)(2,1)S(1)}, bf16[2,512,512]{2,1,0:T(8,128)(2,1)S(1)}, u32[]{:S(2)}, u32[]{:S(2)}) collective-permute-start(bf16[2,512,512]{2,1,0:T(8,128)(2,1)S(1)} %get-tuple-element.74), channel_id=1, source_target_pairs={{0,8},{8,0},{16,24},{24,16},{1,9},{9,1},{17,25},{25,17},{2,10},{10... | collective-permute-start | bytes 3145736 | tf_op jit(solution)/shard_map/ppermute | solution.py:189
  483.4 116.6 %collective-permute-start.54 = (bf16[2,512,512]{2,1,0:T(8,128)(2,1)S(1)}, bf16[2,512,512]{2,1,0:T(8,128)(2,1)S(1)}, u32[]{:S(2)}, u32[]{:S(2)}) collective-permute-start(bf16[2,512,512]{2,1,0:T(8,128)(2,1)S(1)} %get-tuple-element.75), channel_id=1, source_target_pairs={{0,16},{8,24},{16,0},{24,8},{1,17},{9,25},{17,1},{25,9},{2,18},{10... | collective-permute-start | bytes 3145736 | tf_op jit(solution)/shard_map/ppermute | solution.py:189
  503.1 96.9 %collective-permute-start.55 = (bf16[2,512,512]{2,1,0:T(8,128)(2,1)S(1)}, bf16[2,512,512]{2,1,0:T(8,128)(2,1)S(1)}, u32[]{:S(2)}, u32[]{:S(2)}) collective-permute-start(bf16[2,512,512]{2,1,0:T(8,128)(2,1)S(1)} %get-tuple-element.76), channel_id=1, source_target_pairs={{0,24},{8,16},{16,8},{24,0},{1,25},{9,17},{17,9},{25,1},{2,26},{10... | collective-permute-start | bytes 3145736 | tf_op jit(solution)/shard_map/ppermute | solution.py:189
  572.4 33.3 %collective-permute-start.26 = (bf16[256,2048]{1,0:T(8,128)(2,1)S(1)}, bf16[256,2048]{1,0:T(8,128)(2,1)S(1)}, u32[]{:S(2)}, u32[]{:S(2)}) collective-permute-start(bf16[256,2048]{1,0:T(8,128)(2,1)S(1)} %get-tuple-element.61), channel_id=1, source_target_pairs={{0,1},{1,0},{2,3},{3,2},{4,5},{5,4},{6,7},{7,6},{8,9},{9,8},{10,11... | collective-permute-start | bytes 3145736 | tf_op jit(solution)/shard_map/ppermute | solution.py:189
  572.4 93.7 %collective-permute-start.27 = (bf16[256,2048]{1,0:T(8,128)(2,1)S(1)}, bf16[256,2048]{1,0:T(8,128)(2,1)S(1)}, u32[]{:S(2)}, u32[]{:S(2)}) collective-permute-start(bf16[256,2048]{1,0:T(8,128)(2,1)S(1)} %get-tuple-element.61), channel_id=1, source_target_pairs={{0,2},{1,3},{2,0},{3,1},{4,6},{5,7},{6,4},{7,5},{8,10},{9,11},{10,... | collective-permute-start | bytes 3145736 | tf_op jit(solution)/shard_map/ppermute | solution.py:189
  598.5 88.3 %collective-permute-start.28 = (bf16[256,2048]{1,0:T(8,128)(2,1)S(1)}, bf16[256,2048]{1,0:T(8,128)(2,1)S(1)}, u32[]{:S(2)}, u32[]{:S(2)}) collective-permute-start(bf16[256,2048]{1,0:T(8,128)(2,1)S(1)} %get-tuple-element.61), channel_id=1, source_target_pairs={{0,3},{1,2},{2,1},{3,0},{4,7},{5,6},{6,5},{7,4},{8,11},{9,10},{10,... | collective-permute-start | bytes 3145736 | tf_op jit(solution)/shard_map/ppermute | solution.py:189
  601.2 176.2 %collective-permute-start.56 = (f32[2,512,512]{2,1,0:T(8,128)S(1)}, f32[2,512,512]{2,1,0:T(8,128)S(1)}, u32[]{:S(2)}, u32[]{:S(2)}) collective-permute-start(f32[2,512,512]{2,1,0:T(8,128)S(1)} %get-tuple-element.54), channel_id=1, source_target_pairs={{0,4},{4,0},{1,5},{5,1},{2,6},{6,2},{3,7},{7,3},{8,12},{12,8},{9,1... | collective-permute-start | bytes 6291464 | tf_op jit(solution)/shard_map/ppermute | solution.py:189
  605.5 171.4 %collective-permute-start.45 = (bf16[256,2048]{1,0:T(8,128)(2,1)S(1)}, bf16[256,2048]{1,0:T(8,128)(2,1)S(1)}, u32[]{:S(2)}, u32[]{:S(2)}) collective-permute-start(bf16[256,2048]{1,0:T(8,128)(2,1)S(1)} %get-tuple-element.56), channel_id=1, source_target_pairs={{0,1},{1,0},{2,3},{3,2},{4,5},{5,4},{6,7},{7,6},{8,9},{9,8},{10,11... | collective-permute-start | bytes 3145736 | tf_op jit(solution)/shard_map/ppermute | solution.py:189
  609.3 167.7 %collective-permute-start.46 = (bf16[256,2048]{1,0:T(8,128)(2,1)S(1)}, bf16[256,2048]{1,0:T(8,128)(2,1)S(1)}, u32[]{:S(2)}, u32[]{:S(2)}) collective-permute-start(bf16[256,2048]{1,0:T(8,128)(2,1)S(1)} %get-tuple-element.56), channel_id=1, source_target_pairs={{0,2},{1,3},{2,0},{3,1},{4,6},{5,7},{6,4},{7,5},{8,10},{9,11},{10,... | collective-permute-start | bytes 3145736 | tf_op jit(solution)/shard_map/ppermute | solution.py:189
  666.1 19.5 %collective-permute-start.51 = (f32[1,2048]{1,0:T(1,128)S(1)}, f32[1,2048]{1,0:T(1,128)S(1)}, u32[]{:S(2)}, u32[]{:S(2)}) collective-permute-start(f32[1,2048]{1,0:T(1,128)S(1)} %add.420), channel_id=1, source_target_pairs={{0,1},{1,0},{2,3},{3,2},{4,5},{5,4},{6,7},{7,6},{8,9},{9,8},{10,11... | collective-permute-start | bytes 24584 | tf_op jit(solution)/shard_map/ppermute | solution.py:189
  685.6 91.6 %collective-permute-start.47 = (bf16[256,2048]{1,0:T(8,128)(2,1)S(1)}, bf16[256,2048]{1,0:T(8,128)(2,1)S(1)}, u32[]{:S(2)}, u32[]{:S(2)}) collective-permute-start(bf16[256,2048]{1,0:T(8,128)(2,1)S(1)} %get-tuple-element.56), channel_id=1, source_target_pairs={{0,3},{1,2},{2,1},{3,0},{4,7},{5,6},{6,5},{7,4},{8,11},{9,10},{10,... | collective-permute-start | bytes 3145736 | tf_op jit(solution)/shard_map/ppermute | solution.py:189
  686.8 89.5 %collective-permute-start.52 = (f32[1,2048]{1,0:T(1,128)S(1)}, f32[1,2048]{1,0:T(1,128)S(1)}, u32[]{:S(2)}, u32[]{:S(2)}) collective-permute-start(f32[1,2048]{1,0:T(1,128)S(1)} %add.421), channel_id=1, source_target_pairs={{0,2},{1,3},{2,0},{3,1},{4,6},{5,7},{6,4},{7,5},{8,10},{9,11},{10,... | collective-permute-start | bytes 24584 | tf_op jit(solution)/shard_map/ppermute | solution.py:189
  (89 other events, 2064.7 us)

commit v2 on v1

v2 whole, which is shorter than its diff:
```python
import functools

import jax
import jax.numpy as jnp
from jax import lax
from jax.experimental import pallas as pl
from jax.experimental.layout import Layout, with_layout_constraint
from jax.experimental.pallas import tpu as pltpu
from jax.sharding import PartitionSpec as P

LANES = 128
SUB = 8
CHUNK = 128


def span(group):
    return slice(group * LANES, (group + 1) * LANES)


def blocks(ref, halves, groups):
    return [[ref[SUB * i : SUB * i + SUB, span(g)] for g in range(groups)] for i in range(halves)]


def put_blocks(ref, values):
    for i, line in enumerate(values):
        for g, value in enumerate(line):
            ref[SUB * i : SUB * i + SUB, span(g)] = value


def column(ref, halves, t):
    return [
        jnp.broadcast_to(ref[SUB * i : SUB * i + SUB, t : t + 1], (SUB, LANES))
        for i in range(halves)
    ]


def row(tile, r):
    return jnp.broadcast_to(tile[r : r + 1, :], (SUB, LANES))


def sublane_bits():
    index = lax.broadcasted_iota(jnp.int32, (SUB, LANES), 0)
    return [(index & d) == 0 for d in (1, 2, 4)]


def fold(pending, value, bits, falling):
    level = 0
    while pending and pending[-1][0] == level:
        _, other = pending.pop()
        early, late = (value, other) if falling else (other, value)
        d = 1 << level
        if d < 4:
            value = jnp.where(
                bits[level], early + pltpu.roll(early, SUB - d, 0), late + pltpu.roll(late, d, 0)
            )
        else:
            value = jnp.where(bits[level], early, late) + pltpu.roll(
                jnp.where(bits[level], late, early), d, 0
            )
        level += 1
    pending.append((level, value))


def total(values):
    return functools.reduce(lambda a, b: a + b, values)


def scan_kernel(fade_ref, fed_ref, in_ref, out_ref, rate_ref, y_ref, h_ref, last_ref, state_ref):
    chunk, width = fade_ref.shape
    halves, groups = rate_ref.shape[0] // SUB, width // LANES

    @pl.when(pl.program_id(0) == 0)
    def _():
        state_ref[...] = jnp.zeros_like(state_ref)

    rate = blocks(rate_ref, halves, groups)
    state = blocks(state_ref, halves, groups)
    bits = sublane_bits()
    for base in range(0, chunk, SUB):
        fade = [fade_ref[base : base + SUB, span(g)] for g in range(groups)]
        fed = [fed_ref[base : base + SUB, span(g)] for g in range(groups)]
        pending = [[] for _ in range(groups)]
        for r in range(SUB):
            t = base + r
            in_col, out_col = column(in_ref, halves, t), column(out_ref, halves, t)
            for g in range(groups):
                fade_row, fed_row = row(fade[g], r), row(fed[g], r)
                parts = []
                for i in range(halves):
                    place = (t * halves + i) * SUB
                    h_ref[place : place + SUB, span(g)] = state[i][g]
                    factor = jnp.exp2(fade_row * rate[i][g])
                    state[i][g] = factor * state[i][g] + fed_row * in_col[i]
                    parts.append(state[i][g] * out_col[i])
                fold(pending[g], total(parts), bits, False)
        for g in range(groups):
            y_ref[base : base + SUB, span(g)] = pending[g][0][1]
    put_blocks(state_ref, state)
    last_ref[...] = state_ref[...]


def lane_sums(products):
    ones = jnp.ones((SUB, LANES), jnp.bfloat16)
    high = products.astype(jnp.bfloat16)
    low = (products - high.astype(jnp.float32)).astype(jnp.bfloat16)
    across = (((1,), (1,)), ((), ()))
    return lax.dot_general(
        ones, high, across, preferred_element_type=jnp.float32
    ) + lax.dot_general(ones, low, across, preferred_element_type=jnp.float32)


def adjoint_kernel(
    fade_ref,
    fed_ref,
    up_ref,
    in_ref,
    out_ref,
    rate_ref,
    h_ref,
    last_ref,
    weighted_ref,
    pulled_ref,
    d_in_ref,
    d_out_ref,
    d_rate_ref,
    flow_ref,
    now_ref,
    in_part_ref,
    out_part_ref,
):
    chunk, width = fade_ref.shape
    halves, groups = rate_ref.shape[0] // SUB, width // LANES

    @pl.when(pl.program_id(0) == 0)
    def _():
        flow_ref[...] = jnp.zeros_like(flow_ref)
        d_rate_ref[...] = jnp.zeros_like(d_rate_ref)
        now_ref[...] = last_ref[...]

    rate = blocks(rate_ref, halves, groups)
    flow = blocks(flow_ref, halves, groups)
    d_rate = blocks(d_rate_ref, halves, groups)
    now = blocks(now_ref, halves, groups)
    bits = sublane_bits()
    for base in range(chunk - SUB, -SUB, -SUB):
        fade = [fade_ref[base : base + SUB, span(g)] for g in range(groups)]
        fed = [fed_ref[base : base + SUB, span(g)] for g in range(groups)]
        up = [up_ref[base : base + SUB, span(g)] for g in range(groups)]
        weighted = [[] for _ in range(groups)]
        slopes = [[] for _ in range(groups)]
        for r in range(SUB - 1, -1, -1):
            t = base + r
            in_col, out_col = column(in_ref, halves, t), column(out_ref, halves, t)
            in_parts = [[] for _ in range(halves)]
            out_parts = [[] for _ in range(halves)]
            for g in range(groups):
                fade_row, fed_row, up_row = row(fade[g], r), row(fed[g], r), row(up[g], r)
                by_in, by_rate = [], []
                for i in range(halves):
                    place = (t * halves + i) * SUB
                    before = h_ref[place : place + SUB, span(g)]
                    factor = jnp.exp2(fade_row * rate[i][g])
                    adjoint = out_col[i] * up_row + flow[i][g]
                    out_parts[i].append(now[i][g] * up_row)
                    in_parts[i].append(adjoint * fed_row)
                    flow[i][g] = factor * adjoint
                    pulled = flow[i][g] * before
                    by_in.append(adjoint * in_col[i])
                    by_rate.append(pulled * rate[i][g])
                    d_rate[i][g] = d_rate[i][g] + pulled * fade_row
                    now[i][g] = before
                fold(weighted[g], total(by_in), bits, True)
                fold(slopes[g], total(by_rate), bits, True)
            for i in range(halves):
                place = (t * halves + i) * SUB
                in_part_ref[place : place + SUB, :] = total(in_parts[i])
                out_part_ref[place : place + SUB, :] = total(out_parts[i])
        for g in range(groups):
            weighted_ref[base : base + SUB, span(g)] = weighted[g][0][1]
            pulled_ref[base : base + SUB, span(g)] = slopes[g][0][1]
    put_blocks(flow_ref, flow)
    put_blocks(d_rate_ref, d_rate)
    put_blocks(now_ref, now)
    d_in_ref[...] = lane_sums(in_part_ref[...])
    d_out_ref[...] = lane_sums(out_part_ref[...])


def fwd(fading, fed, in_coef, out_coef, rates, **unused):
    tokens, width = fading.shape
    states = rates.shape[0]
    by_row = lambda size: pl.BlockSpec((size, width), lambda c: (c, 0))
    cols = pl.BlockSpec((states, CHUNK), lambda c: (0, c))
    whole = pl.BlockSpec((states, width), lambda c: (0, 0))
    like = jax.ShapeDtypeStruct
    work = tokens * states * width
    return pl.pallas_call(
        scan_kernel,
        grid=(tokens // CHUNK,),
        in_specs=[by_row(CHUNK), by_row(CHUNK), cols, cols, whole],
        out_specs=[by_row(CHUNK), by_row(CHUNK * states), whole],
        out_shape=[
            like((tokens, width), jnp.float32),
            like((tokens * states, width), jnp.float32),
            like((states, width), jnp.float32),
        ],
        scratch_shapes=[pltpu.VMEM((states, width), jnp.float32)],
        compiler_params=pltpu.CompilerParams(
            dimension_semantics=("arbitrary",), vmem_limit_bytes=40 << 20
        ),
        cost_estimate=pl.CostEstimate(flops=2400 * work, bytes_accessed=6 * work, transcendentals=work),
        name="scan",
    )(fading, fed, in_coef, out_coef, rates)


def bwd(fading, fed, upstream, in_coef, out_coef, rates, history, last):
    tokens, width = fading.shape
    states = rates.shape[0]
    count = tokens // CHUNK
    by_row = lambda size: pl.BlockSpec((size, width), lambda c: (count - 1 - c, 0))
    cols = pl.BlockSpec((states, CHUNK), lambda c: (0, count - 1 - c))
    flat = pl.BlockSpec((SUB, CHUNK * states), lambda c: (0, count - 1 - c))
    whole = pl.BlockSpec((states, width), lambda c: (0, 0))
    like = jax.ShapeDtypeStruct
    work = tokens * states * width
    weighted, pulled, d_in, d_out, d_rate = pl.pallas_call(
        adjoint_kernel,
        grid=(count,),
        in_specs=[by_row(CHUNK)] * 3 + [cols, cols, whole, by_row(CHUNK * states), whole],
        out_specs=[by_row(CHUNK), by_row(CHUNK), flat, flat, whole],
        out_shape=[like((tokens, width), jnp.float32)] * 2
        + [like((SUB, tokens * states), jnp.float32)] * 2
        + [like((states, width), jnp.float32)],
        scratch_shapes=[pltpu.VMEM((states, width), jnp.float32)] * 2
        + [pltpu.VMEM((CHUNK * states, LANES), jnp.float32)] * 2,
        compiler_params=pltpu.CompilerParams(
            dimension_semantics=("arbitrary",), vmem_limit_bytes=40 << 20
        ),
        cost_estimate=pl.CostEstimate(flops=4800 * work, bytes_accessed=8 * work, transcendentals=work),
        name="adjoint",
    )(fading, fed, upstream, in_coef, out_coef, rates, history, last)
    by_state = lambda flat_sums: flat_sums[0].reshape(tokens, states).T
    return weighted, pulled, by_state(d_in), by_state(d_out), d_rate


EPS = 1e-05
GONE = 1e4
LOG2E = 1.4426950408889634
BF16 = jnp.bfloat16
F32 = jnp.float32


def swap(array, axis, k):
    size = lax.axis_size(axis)
    return lax.ppermute(array, axis, [(i, i ^ k) for i in range(size)])


def after(value, *others):
    return lax.optimization_barrier((value, others))[0]


def pieces_over(array, axis, hold=None):
    pieces = [array] + [swap(array, axis, k) for k in range(1, lax.axis_size(axis))]
    return pieces if hold is None else [after(piece, hold) for piece in pieces]


def assemble(pieces, axis, dim):
    me, size = lax.axis_index(axis), pieces[0].shape[dim]
    shape = pieces[0].shape[:dim] + (size * len(pieces),) + pieces[0].shape[dim + 1 :]
    out = jnp.zeros(shape, pieces[0].dtype)
    for k, piece in enumerate(pieces):
        out = lax.dynamic_update_slice_in_dim(out, piece, (me ^ k) * size, dim)
    return row_major(out)


def gather(array, axis, dim, hold=None):
    return assemble(pieces_over(array, axis, hold), axis, dim)


def row_major(array):
    return with_layout_constraint(array, Layout(major_to_minor=tuple(range(array.ndim))))


def piece_of(array, axis, dim, index):
    size = array.shape[dim] // lax.axis_size(axis)
    return lax.dynamic_slice_in_dim(array, index * size, size, dim)


def shares(array, axis, dim, kind):
    me = lax.axis_index(axis)
    own = piece_of(array, axis, dim, me).astype(F32)
    sent = [
        piece_of(array, axis, dim, me ^ k).astype(kind) for k in range(1, lax.axis_size(axis))
    ]
    return own, sent


def collect(own, sent, axis):
    return total([own] + [swap(part, axis, k + 1).astype(F32) for k, part in enumerate(sent)])


def scatter_sum(array, axis, dim, kind):
    return collect(*shares(array, axis, dim, kind), axis)


def doubling_sum(array, axes):
    for axis in axes:
        k = 1
        while k < lax.axis_size(axis):
            array = array + swap(array, axis, k)
            k *= 2
    return array


def dot(left, right, left_dim=1, right_dim=0):
    return lax.dot_general(left, right, (((left_dim,), (right_dim,)), ((), ())), preferred_element_type=F32)


def silu_slope(v):
    s = jax.nn.sigmoid(v)
    return s * (1.0 + v * (1.0 - s))


def inverse_rms(x):
    return lax.rsqrt(jnp.mean(x * x, axis=-1, keepdims=True) + EPS)


def shards(
    block_input,
    doc_ids,
    norm_gain,
    in_proj,
    conv_weight,
    conv_bias,
    x_proj,
    dt_proj,
    dt_bias,
    a_log,
    d_skip,
    out_proj,
    grad_output,
):
    seqs, piece, width = block_input.shape
    length = doc_ids.shape[1]
    ctx, ctxs = lax.axis_index("context"), lax.axis_size("context")
    taps, tail = conv_weight.shape[0], conv_weight.shape[0] - 1
    states = a_log.shape[0]
    rows = seqs * length
    inner = in_proj.shape[2] // ctxs
    rank = dt_proj.shape[0] * lax.axis_size("fsdp")

    def mine(array, dim):
        return piece_of(array, "context", dim, ctx)

    in_half = mine(in_proj, 2)
    xcols, dtrows, share = x_proj.shape[1], dt_proj.shape[0], in_proj.shape[1]
    x_own = block_input.reshape(seqs * piece, width).astype(F32)
    normed_own = (x_own * inverse_rms(x_own) * norm_gain).astype(BF16)
    first = pieces_over(
        jnp.concatenate([mine(x_proj, 0).T, mine(dt_proj, 1), in_half[0]], axis=0),
        "fsdp",
        normed_own,
    )
    w_x = assemble([p[:xcols] for p in first], "fsdp", 0)
    w_dt = assemble([p[xcols : xcols + dtrows] for p in first], "fsdp", 0)
    w_conv = assemble([p[xcols + dtrows :] for p in first], "fsdp", 0)
    normed = [normed_own] + [swap(normed_own, "context", k) for k in range(1, ctxs)]
    def whole_tokens(parts):
        out = jnp.zeros((seqs, length, parts[0].shape[-1]), parts[0].dtype)
        for k, part in enumerate(parts):
            part = part.reshape(seqs, piece, part.shape[-1])
            out = lax.dynamic_update_slice_in_dim(out, part, (ctx ^ k) * piece, 1)
        return out.reshape(rows, -1)

    def token_parts(array):
        array = array.reshape(seqs, length, array.shape[-1])
        parts = [piece_of(array, "context", 1, ctx ^ k) for k in range(ctxs)]
        return [part.reshape(seqs * piece, -1) for part in parts]

    def over_tokens(left, right):
        return total([dot(l, r, 0, 0) for l, r in zip(left, right)])

    taps_w, bias, dt_b = mine(conv_weight, 1), mine(conv_bias, 0), mine(dt_bias, 0)
    rates = -jnp.exp(mine(a_log, 1))
    skip = mine(d_skip, 0)

    conv_input = whole_tokens([dot(part, w_conv).astype(BF16) for part in normed])
    padded_ids = jnp.concatenate([jnp.full((seqs, tail), -1, jnp.int32), doc_ids], axis=1)
    same = [
        (padded_ids[:, tail - k : tail - k + length] == doc_ids).astype(F32)[..., None]
        for k in range(taps)
    ]
    padded = jnp.pad(conv_input.reshape(seqs, length, inner), ((0, 0), (tail, 0), (0, 0))).astype(F32)
    shifted = [padded[:, tail - k : tail - k + length] for k in range(taps)]
    conv_output = bias
    for k in range(taps):
        conv_output = conv_output + taps_w[k] * shifted[k] * same[k]
    conv_flat = conv_output.reshape(rows, inner)
    activated = jax.nn.silu(conv_flat).astype(BF16)
    act = activated.astype(F32)
    def all_sum(part):
        halved = scatter_sum(part, "context", 1, F32)
        summed = scatter_sum(halved, "tensor", 1, BF16).astype(BF16)
        return gather(gather(summed, "tensor", 1), "context", 1), halved

    projections, halved = all_sum(dot(w_x, activated, 1, 1))
    w_gate = after(
        lax.all_gather(after(in_half[1], first), "fsdp", axis=0, tiled=True), halved
    )
    w_out = lax.all_gather(after(mine(out_proj, 0).T, w_gate), "fsdp", axis=0, tiled=True)
    own_cotangent = grad_output.reshape(seqs * piece, width)
    cotangent = [own_cotangent] + [
        swap(after(own_cotangent, conv_input), "context", k) for k in range(1, ctxs)
    ]
    dt_input = projections[:rank]
    in_coef = projections[rank : rank + states].astype(F32)
    out_coef = projections[rank + states :].astype(F32)
    dt_logits = dot(dt_input, w_dt, 0, 0) + dt_b
    steps = jax.nn.softplus(dt_logits)
    keep = same[1].reshape(rows, 1)
    fading = jnp.where(keep > 0, steps, GONE)
    fed = steps * act
    rates2 = rates * LOG2E
    w_out = after(w_out, fading)
    scanned, history, last = fwd(fading, fed, in_coef, out_coef, rates2)

    gate = whole_tokens([dot(part, w_gate) for part in normed])
    gate_value = jax.nn.silu(gate)
    mixed = scanned + skip * act
    gated = (mixed * gate_value).astype(BF16)
    d_gated = whole_tokens([dot(part, w_out) for part in cotangent])
    d_mixed = d_gated * gate_value
    d_gate = (d_gated * mixed * silu_slope(gate)).astype(BF16)

    def my_tokens(parts):
        return [parts[0]] + [swap(parts[k], "context", k) for k in range(1, ctxs)]

    def all_halves(weight):
        return [weight] + [swap(weight, "context", k) for k in range(1, ctxs)]

    zplace = lax.axis_index("tensor")
    x_flat = block_input.reshape(seqs * piece, width)
    gated_parts = token_parts(gated)
    branch = dot(
        jnp.concatenate(my_tokens(gated_parts), axis=1),
        jnp.concatenate(all_halves(w_out), axis=1),
        1,
        1,
    ).astype(BF16)
    branch, d_mixed = after((branch, d_mixed))
    branch = lax.psum_scatter(branch, "tensor", scatter_dimension=0, tiled=True).astype(F32)

    in_weighted, d_fade, d_in_coef, d_out_coef, d_rates = bwd(
        fading, fed, d_mixed, in_coef, out_coef, rates2, history, last
    )
    in_weighted, d_fade, branch = after((in_weighted, d_fade, branch))
    x_rows = piece_of(x_flat, "tensor", 0, zplace).astype(F32)
    output_rows = (x_rows + branch).astype(BF16)
    d_step = d_fade * (1.0 / LOG2E) + act * in_weighted
    d_logits = (d_step * jax.nn.sigmoid(dt_logits)).astype(BF16)
    d_part = jnp.concatenate([dot(w_dt, d_logits, 1, 1), d_in_coef, d_out_coef], axis=0)
    d_part, output_rows = after((d_part, output_rows))
    block_output = lax.all_gather(output_rows[None], "tensor", axis=1, tiled=True)
    d_projections, halved = all_sum(d_part)
    gated_parts, d_gate = after((gated_parts, d_gate), halved)
    grad_out_part = over_tokens(cotangent, gated_parts)
    gate_parts = token_parts(d_gate)
    grad_gate_part = over_tokens(normed, gate_parts)
    grad_dt_part = dot(dt_input, d_logits)
    d_act = d_mixed * skip + steps * in_weighted + dot(d_projections, w_x, 0, 0)
    grad_x_part = dot(d_projections, activated)
    d_conv = (d_act * silu_slope(conv_flat)).reshape(seqs, length, inner)
    d_conv_input = jnp.zeros((seqs, length, inner), F32)
    tap_grads = []
    for k in range(taps):
        masked = d_conv * same[k]
        late = jnp.pad(masked, ((0, 0), (0, tail), (0, 0)))[:, k : k + length]
        d_conv_input = d_conv_input + taps_w[k] * late
        tap_grads.append(jnp.sum(masked * shifted[k], axis=(0, 1)))
    d_conv_input = d_conv_input.reshape(rows, inner).astype(BF16)
    conv_parts = token_parts(d_conv_input)
    left = jnp.concatenate(my_tokens(gate_parts) + my_tokens(conv_parts), axis=1)
    right = jnp.concatenate(all_halves(w_gate) + all_halves(w_conv), axis=1)
    partial = dot(left, right, 1, 1).astype(BF16)
    own_rows, sent_rows = shares(partial, "tensor", 0, BF16)
    grad_conv_part = over_tokens(normed, after(conv_parts, sent_rows))
    d_normed = collect(own_rows, sent_rows, "tensor")
    d_rows = piece_of(own_cotangent, "tensor", 0, zplace).astype(F32)
    inv = inverse_rms(x_rows)
    scaled = d_normed * norm_gain
    inner_sum = jnp.sum(scaled * x_rows, axis=-1, keepdims=True)
    grad_rows = d_rows + inv * scaled - x_rows * (inv * inv * inv) * inner_sum / width
    grad_rows, block_output = after((grad_rows.astype(BF16), block_output))
    gain = jnp.sum(d_normed * x_rows * inv, axis=0)
    devices = lax.axis_size("fsdp")

    def owned(*parts):
        pieces = [part.reshape(devices, -1, inner).astype(BF16) for part in parts]
        pieces = row_major(jnp.concatenate(pieces, axis=1).reshape(-1, inner))
        return lax.psum_scatter(pieces, "fsdp", scatter_dimension=0, tiled=True)

    early = owned(*after((grad_gate_part, grad_out_part), sent_rows, block_output))
    late = owned(grad_x_part, grad_dt_part, grad_conv_part)
    thin = jnp.concatenate(
        [
            d_rates * rates,
            jnp.stack(tap_grads),
            jnp.sum(d_conv, axis=(0, 1))[None],
            jnp.sum(d_logits.astype(F32), axis=0)[None],
            jnp.sum(d_mixed * act, axis=0)[None],
            gain.reshape(-1, inner),
        ],
        axis=0,
    )
    channels = states + taps + 3
    thin = doubling_sum(thin, ("fsdp",))
    others = [thin] + [swap(thin, "context", k) for k in range(1, ctxs)]
    gain = total([part[channels:] for part in others]).reshape(1, width)
    terms = []
    for _ in range(3):
        terms.append(gain.astype(BF16))
        gain = gain - terms[-1].astype(F32)
    half = grad_rows.shape[0] // 2
    fill = jnp.zeros((SUB * 2 - len(terms), width), BF16)
    early_rows = gather(grad_rows[:half], "tensor", 0).reshape(-1, half, width)
    late_rows = gather(jnp.concatenate([grad_rows[half:]] + terms + [fill]), "tensor", 0)
    late_rows = late_rows.reshape(-1, half + SUB * 2, width)
    grad_gain = total(
        [jnp.sum(late_rows[:, half + i].astype(F32), axis=0) for i in range(len(terms) - 1, -1, -1)]
    )
    grad_input = jnp.concatenate([early_rows, late_rows[:, :half]], axis=1).reshape(block_input.shape)

    def side_by_side(parts, dim):
        size = parts[0].shape[dim]
        shape = parts[0].shape[:dim] + (size * ctxs,) + parts[0].shape[dim + 1 :]
        out = jnp.zeros(shape, parts[0].dtype)
        for k, part in enumerate(parts):
            out = lax.dynamic_update_slice_in_dim(out, part, (ctx ^ k) * size, dim)
        return out

    thin = side_by_side([part[:channels] for part in others], 1)
    early, late = [
        [sums] + [swap(sums, "context", k) for k in range(1, ctxs)] for sums in (early, late)
    ]
    grad_in = jnp.stack(
        [
            side_by_side([part[xcols + dtrows :].astype(F32) for part in late], 1),
            side_by_side([part[:share].astype(F32) for part in early], 1),
        ]
    )
    grad_out = side_by_side([part[share:].T.astype(F32) for part in early], 0)
    grad_x = side_by_side([part[:xcols].T.astype(F32) for part in late], 0)
    grad_dt = side_by_side([part[xcols : xcols + dtrows].astype(F32) for part in late], 1)
    return (
        block_output.reshape(block_input.shape),
        grad_input,
        grad_gain,
        grad_in,
        thin[states : states + taps],
        thin[states + taps],
        grad_x,
        grad_dt,
        thin[states + taps + 1],
        thin[:states],
        thin[states + taps + 2],
        grad_out,
    )


def solution(mesh):
    placed = (
        P("fsdp", "context", None),
        P("fsdp", None),
        P(),
        P(None, "fsdp", "tensor"),
        P(None, "tensor"),
        P("tensor"),
        P("tensor", "fsdp"),
        P("fsdp", "tensor"),
        P("tensor"),
        P(None, "tensor"),
        P("tensor"),
        P("tensor", "fsdp"),
        P("fsdp", "context", None),
    )
    return jax.shard_map(
        shards,
        mesh=mesh,
        in_specs=placed,
        out_specs=(
            P("fsdp", "context", None),
            P("fsdp", "context", None),
            P(),
            P(None, "fsdp", "tensor"),
            P(None, "tensor"),
            P("tensor"),
            P("tensor", "fsdp"),
            P("fsdp", "tensor"),
            P("tensor"),
            P(None, "tensor"),
            P("tensor"),
            P("tensor", "fsdp"),
        ),
        check_vma=False,
    )
```

time: 790 us -> 618 us (0.78)
  the two profiles are of different devices: /device:TPU:0 before, /device:TPU:13 now
where the time goes in v2:
time: 618 us; the launch traced here: 610 us
  waiting for transfers between devices  245 us (40%)
  matrix products  90.1 us (15%)
  Pallas kernels  82.7 us (13%)
  other arithmetic  70 us (11%)
  local copies, waits for them, and re-layouts  68.7 us (11%)
  starting transfers between devices  36.6 us (6%)
  between operations  16.9 us (3%)
    ppermute x41, waiting for transfers between devices, swap(): return lax.ppermute(array, axis, [(i, i ^ k) for i in range(size)])  226 us
    dot_general x20, matrix products, dot(): lax.dot_general(left, right, (((left_dim,), (right_dim,)), ((), ())), pre...  90.1 us
    pallas_call x1, Pallas kernels, bwd(): pl.pallas_call(adjoint_kernel, grid=(count,), in_specs=[by_row(CHUNK)] *...  55.3 us
    ppermute x41, starting transfers between devices, swap(): return lax.ppermute(array, axis, [(i, i ^ k) for i in range(size)])  35.7 us
    pallas_call x1, Pallas kernels, fwd(): pl.pallas_call(scan_kernel, grid=(tokens // CHUNK,), in_specs=[by_row(CHU...  27.3 us
    unnamed x166, local copies, waits for them, and re-layouts  25.7 us
  transfers between devices with their start and end apart: 47, of which 22 were waited for; matrix products, arithmetic and copies ran while one was open for 28% of the time, Pallas kernels for 14%

profile of v2, /device:TPU:13, one launch (start us, length us, event | category | flops | bytes accessed | tf_op | source)
XLA Modules:
  0.0 609.7 jit_solution(16541319003190653838)
XLA Ops:
  7.3 3.2 fusion
  10.8 3.0 fusion.2
  22.3 8.5 %collective-permute-done = bf16[584,512]{1,0:T(8,128)(2,1)S(1)} collective-permute-done((bf16[584,512]{1,0:T(8,128)(2,1)S(1)}, bf16[584,512]{1,0:T(8,128)(2,1)S(1)}, u32[]{:S(2)}, u32[]{:S(2)}) %collective-permute-start) | collective-permute-done | bytes 598048 | tf_op jit(solution)/shard_map/ppermute | solution.py:254
  30.8 13.7 %collective-permute-done.1 = bf16[584,512]{1,0:T(8,128)(2,1)} collective-permute-done((bf16[584,512]{1,0:T(8,128)(2,1)S(1)}, bf16[584,512]{1,0:T(8,128)(2,1)}, u32[]{:S(2)}, u32[]{:S(2)}) %collective-permute-start.1) | collective-permute-done | bytes 598048 | tf_op jit(solution)/shard_map/ppermute | solution.py:254
  49.2 5.3 fusion.66
  54.6 4.5 fusion.68
  59.8 5.0 fusion.38
  72.4 8.3 %all-gather.5.cloned.1.call-done = bf16[2048,512]{1,0:T(8,128)(2,1)} async-done(((bf16[512,512]{1,0:T(8,128)(2,1)}), bf16[2048,512]{1,0:T(8,128)(2,1)}) %all-gather.5.cloned.1.call-update) | async-done | bytes 2097168 | tf_op jit(solution)/shard_map/all_gather | solution.py:407
  82.6 4.5 convolution_dynamic-update-slice_fusion.1
  89.3 5.3 collective-permute-done.9
  97.7 4.5 convolution_dynamic-update-slice_fusion
  104.3 4.5 convert_multiply_fusion.5
  108.8 27.3 %scan.1 = (f32[2048,512]{1,0:T(8,128)S(1)}, f32[32768,512]{1,0:T(8,128)}, f32[16,512]{1,0:T(8,128)S(1)}) custom-call(f32[2048,512]{1,0:T(8,128)S(1)} %get-tuple-element.100.fade_ref, f32[2048,512]{1,0:T(8,128)S(1)} %get-tuple-element.99.fed_ref, f32[16,2048]{1,0:T(8,128)S(1)} %get-tuple-element.122.in_ref, f32[16,2048]{1,0:T(8,128)S(1)} %get-tuple-element.121.out_ref, ...), custom_call_target="tpu_custom_call" | custom-call | flops 40265318400 | bytes 100663296 | tf_op jit(solution)/shard_map/scan/pallas_call | solution.py:196
  144.5 4.1 bitcast_dynamic-update-slice_fusion.1
  148.6 4.7 bitcast_dynamic-update-slice_fusion
  153.4 4.2 multiply_convert_fusion.1
  161.4 6.1 %fusion.48 = bf16[1024,2048]{1,0:T(8,128)(2,1)} fusion(bf16[2048,512]{0,1:T(8,128)(2,1)S(1)} %collective-permute-done.14, bf16[2048,512]{0,1:T(8,128)(2,1)S(1)} %copy-done.76, bf16[1024,512]{1,0:T(8,128)(2,1)S(1)} %collective-permute-done.13, bf16[1024,512]{1,0:T(8,128)(2,1)S(1)} %get-tuple-element.72), kind=kOutput, calls=%fused_computation.80 | convolution fusion | flops 4309647360 | bytes 10485760 | tf_op jit(solution)/shard_map/dot_general | solution.py:315
  167.6 55.3 %adjoint.1 = (f32[2048,512]{1,0:T(8,128)S(1)}, f32[2048,512]{1,0:T(8,128)S(1)}, f32[8,32768]{1,0:T(8,128)S(1)}, f32[8,32768]{1,0:T(8,128)S(1)}, f32[16,512]{1,0:T(8,128)S(1)}) custom-call(f32[2048,512]{1,0:T(8,128)} %copy-done.5, f32[2048,512]{1,0:T(8,128)} %copy-done.4, f32[2048,512]{1,0:T(8,128)} %get-tuple-element.53.up_ref, ...), custom_call_target="tpu_custom_call" | custom-call | flops 80530636800 | bytes 134217728 | tf_op jit(solution)/shard_map/adjoint/pallas_call | solution.py:225
  233.3 10.3 %reduce-scatter.3.cloned.1.call-done = bf16[256,2048]{1,0:T(8,128)(2,1)} async-done(((bf16[1024,2048]{1,0:T(8,128)(2,1)}), bf16[256,2048]{1,0:T(8,128)(2,1)}) %reduce-scatter.3.cloned.1.call-update) | async-done | bytes 1048592 | tf_op jit(solution)/shard_map/reduce_scatter | solution.py:450
  245.1 6.9 %convert_reduce_fusion = (f32[512]{0:T(512)S(1)}, bf16[2048,512]{1,0:T(8,128)(2,1)S(1)}, f32[512]{0:T(512)S(1)}) fusion(f32[2048,512]{1,0:T(8,128)} %get-tuple-element.140, f32[512]{0:T(512)S(1)} %copy-done.68, f32[2048,512]{1,0:T(8,128)} %copy-done.2, bf16[2048,512]{1,0:T(8,128)(2,1)S(1)} %get-tuple-element.94, f32[2048,512]{1,0:T(8,128)} %copy-done.6, ...), kind=kLoop, calls=%fused_computation.67 | loop fusion | flops 14679040 | bytes 20977664 | tf_op jit(solution)/shard_map/reduce_sum | solution.py:508
  265.5 4.5 collective-permute-done.18
  274.5 3.1 collective-permute-start.21
  277.6 7.7 %collective-permute-done.21 = bf16[160,256]{1,0:T(8,128)(2,1)S(1)} collective-permute-done((bf16[160,256]{1,0:T(8,128)(2,1)S(1)}, bf16[160,256]{1,0:T(8,128)(2,1)S(1)}, u32[]{:S(2)}, u32[]{:S(2)}) %collective-permute-start.21) | collective-permute-done | bytes 81952 | tf_op jit(solution)/shard_map/ppermute | solution.py:254
  285.3 11.7 %collective-permute-done.22 = bf16[160,256]{1,0:T(8,128)(2,1)S(1)} collective-permute-done((bf16[160,256]{1,0:T(8,128)(2,1)S(1)}, bf16[160,256]{1,0:T(8,128)(2,1)S(1)}, u32[]{:S(2)}, u32[]{:S(2)}) %collective-permute-start.22) | collective-permute-done | bytes 81952 | tf_op jit(solution)/shard_map/ppermute | solution.py:254
  297.4 5.2 fusion.96
  303.4 4.4 fusion.91
  307.9 5.2 multiply_reduce_fusion
  313.1 4.6 fusion.15
  325.7 14.1 %fusion.43 = bf16[1024,2048]{1,0:T(8,128)(2,1)} fusion(bf16[2048,512]{1,0:T(8,128)(2,1)} %collective-permute-done.26, bf16[2048,512]{1,0:T(8,128)(2,1)} %slice_dynamic-update-slice_fusion, bf16[2048,512]{1,0:T(8,128)(2,1)} %collective-permute-done.25, bf16[2048,512]{1,0:T(8,128)(2,1)} %all-gather.5.cloned.1.call-done, bf16[1024,512]{1,0:T(8,128)(2,1)} %copy-done.77, ...), kind=kOutput, calls=%fused_computation.79 | convolution fusion | flops 8642363392 | bytes 16777216 | tf_op jit(solution)/shard_map/dot_general | solution.py:315
  339.8 3.7 constant_dynamic-slice_fusion.3
  346.2 4.6 fusion.94
  350.8 4.6 add_convert_fusion
  357.4 4.9 fusion.95
  362.3 6.4 %convolution_add_fusion = bf16[2048,512]{1,0:T(8,128)(2,1)} fusion(f32[2048,512]{1,0:T(8,128)S(1)} %fusion.95, bf16[1024,2048]{1,0:T(8,128)(2,1)} %collective-permute-done.3, bf16[1024,512]{1,0:T(8,128)(2,1)} %get-tuple-element.108), kind=kOutput, calls=%fused_computation.81 | convolution fusion | flops 2149580800 | bytes 11534336 | tf_op jit(solution)/shard_map/dot_general | solution.py:315
  368.7 23.1 %collective-permute-done.27 = bf16[256,2048]{1,0:T(8,128)(2,1)} collective-permute-done((bf16[256,2048]{1,0:T(8,128)(2,1)}, bf16[256,2048]{1,0:T(8,128)(2,1)}, u32[]{:S(2)}, u32[]{:S(2)}) %collective-permute-start.27) | collective-permute-done | bytes 1048608 | tf_op jit(solution)/shard_map/ppermute | solution.py:254
  391.8 25.6 %collective-permute-done.28 = bf16[256,2048]{1,0:T(8,128)(2,1)} collective-permute-done((bf16[256,2048]{1,0:T(8,128)(2,1)}, bf16[256,2048]{1,0:T(8,128)(2,1)}, u32[]{:S(2)}, u32[]{:S(2)}) %collective-permute-start.28) | collective-permute-done | bytes 1048608 | tf_op jit(solution)/shard_map/ppermute | solution.py:254
  417.4 24.8 %collective-permute-done.29 = bf16[256,2048]{1,0:T(8,128)(2,1)} collective-permute-done((bf16[256,2048]{1,0:T(8,128)(2,1)}, bf16[256,2048]{1,0:T(8,128)(2,1)}, u32[]{:S(2)}, u32[]{:S(2)}) %collective-permute-start.29) | collective-permute-done | bytes 1048608 | tf_op jit(solution)/shard_map/ppermute | solution.py:254
  442.2 3.3 fusion.59
  445.4 4.3 fusion.56
  449.7 2.8 copy.54
  452.5 4.5 pad_maximum_fusion.1
  462.9 2.9 collective-permute-done.34
  465.7 3.2 collective-permute-start.35
  487.3 16.2 %collective-permute-done.30 = bf16[128,2048]{1,0:T(8,128)(2,1)} collective-permute-done((bf16[128,2048]{1,0:T(8,128)(2,1)}, bf16[128,2048]{1,0:T(8,128)(2,1)}, u32[]{:S(2)}, u32[]{:S(2)}) %collective-permute-start.30) | collective-permute-done | bytes 524320 | tf_op jit(solution)/shard_map/ppermute | solution.py:254
  509.2 59.6 %collective-permute-done.32 = bf16[128,2048]{1,0:T(8,128)(2,1)S(1)} collective-permute-done((bf16[128,2048]{1,0:T(8,128)(2,1)}, bf16[128,2048]{1,0:T(8,128)(2,1)S(1)}, u32[]{:S(2)}, u32[]{:S(2)}) %collective-permute-start.32) | collective-permute-done | bytes 524320 | tf_op jit(solution)/shard_map/ppermute | solution.py:254
  569.8 11.6 %collective-permute-done.38 = bf16[144,2048]{1,0:T(8,128)(2,1)S(1)} collective-permute-done((bf16[144,2048]{1,0:T(8,128)(2,1)S(1)}, bf16[144,2048]{1,0:T(8,128)(2,1)S(1)}, u32[]{:S(2)}, u32[]{:S(2)}) %collective-permute-start.38) | collective-permute-done | bytes 589856 | tf_op jit(solution)/shard_map/ppermute | solution.py:254
  583.7 4.3 pad_maximum_fusion
  596.1 4.2 pad_maximum_fusion.2
  (371 shorter events, 128.3 us)
Async XLA Ops:
  7.2 73.5 %all-gather.5.cloned.1.call-start = ((), (), s32[]{:S(2)}) async-start(), calls=%async_computation.2 | async-start | bytes 2621440 | tf_op jit(solution)/shard_map/all_gather | solution.py:407
  13.8 40.7 %collective-permute-start.3 = (bf16[1024,2048]{1,0:T(8,128)(2,1)}, bf16[1024,2048]{1,0:T(8,128)(2,1)}, u32[]{:S(2)}, u32[]{:S(2)}) collective-permute-start(bf16[1024,2048]{1,0:T(8,128)(2,1)} %fusion.2), channel_id=1, source_target_pairs={{0,4},{4,0},{1,5},{5,1},{2,6},{6,2},{3,7},{7,3},{8,12},{12,8},{9,1... | collective-permute-start | bytes 12582920 | tf_op jit(solution)/shard_map/ppermute | solution.py:254
  15.6 15.3 %collective-permute-start = (bf16[584,512]{1,0:T(8,128)(2,1)S(1)}, bf16[584,512]{1,0:T(8,128)(2,1)S(1)}, u32[]{:S(2)}, u32[]{:S(2)}) collective-permute-start(bf16[584,512]{1,0:T(8,128)(2,1)S(1)} %pad_maximum_fusion.5), channel_id=1, source_target_pairs={{0,8},{8,0},{16,24},{24,16},{1,9},{9,1},{17,25},{25,17},{2,10},{10... | collective-permute-start | bytes 1794056 | tf_op jit(solution)/shard_map/ppermute | solution.py:254
  16.8 27.7 %collective-permute-start.1 = (bf16[584,512]{1,0:T(8,128)(2,1)S(1)}, bf16[584,512]{1,0:T(8,128)(2,1)}, u32[]{:S(2)}, u32[]{:S(2)}) collective-permute-start(bf16[584,512]{1,0:T(8,128)(2,1)S(1)} %pad_maximum_fusion.5), channel_id=1, source_target_pairs={{0,16},{8,24},{16,0},{24,8},{1,17},{9,25},{17,1},{25,9},{2,18},{10... | collective-permute-start | bytes 1794056 | tf_op jit(solution)/shard_map/ppermute | solution.py:254
  17.1 27.5 %collective-permute-start.2 = (bf16[584,512]{1,0:T(8,128)(2,1)S(1)}, bf16[584,512]{1,0:T(8,128)(2,1)S(1)}, u32[]{:S(2)}, u32[]{:S(2)}) collective-permute-start(bf16[584,512]{1,0:T(8,128)(2,1)S(1)} %pad_maximum_fusion.5), channel_id=1, source_target_pairs={{0,24},{8,16},{16,8},{24,0},{1,25},{9,17},{17,9},{25,1},{2,26},{10... | collective-permute-start | bytes 1794056 | tf_op jit(solution)/shard_map/ppermute | solution.py:254
  18.3 130.3 %collective-permute-start.12 = (bf16[1024,2048]{1,0:T(8,128)(2,1)}, bf16[1024,2048]{1,0:T(8,128)(2,1)}, u32[]{:S(2)}, u32[]{:S(2)}) collective-permute-start(bf16[1024,2048]{1,0:T(8,128)(2,1)} %bitcast.189), channel_id=1, source_target_pairs={{0,4},{4,0},{1,5},{5,1},{2,6},{6,2},{3,7},{7,3},{8,12},{12,8},{9,1... | collective-permute-start | bytes 12582920 | tf_op jit(solution)/shard_map/ppermute | solution.py:254
  44.6 97.7 %all-gather.7.cloned.1.call-start = ((), (), s32[]{:S(2)}) async-start(), calls=%async_computation.3 | async-start | bytes 2621440 | tf_op jit(solution)/shard_map/all_gather | solution.py:409
  65.7 3.0 collective-permute-start.4
  68.9 12.1 %collective-permute-start.5 = (bf16[160,256]{1,0:T(8,128)(2,1)S(1)}, bf16[160,256]{1,0:T(8,128)(2,1)S(1)}, u32[]{:S(2)}, u32[]{:S(2)}) collective-permute-start(bf16[160,256]{1,0:T(8,128)(2,1)S(1)} %get-tuple-element.123), channel_id=1, source_target_pairs={{0,1},{1,0},{2,3},{3,2},{4,5},{5,4},{6,7},{7,6},{8,9},{9,8},{10,11... | collective-permute-start | bytes 245768 | tf_op jit(solution)/shard_map/ppermute | solution.py:254
  69.1 11.9 %collective-permute-start.6 = (bf16[160,256]{1,0:T(8,128)(2,1)S(1)}, bf16[160,256]{1,0:T(8,128)(2,1)S(1)}, u32[]{:S(2)}, u32[]{:S(2)}) collective-permute-start(bf16[160,256]{1,0:T(8,128)(2,1)S(1)} %get-tuple-element.125), channel_id=1, source_target_pairs={{0,2},{1,3},{2,0},{3,1},{4,6},{5,7},{6,4},{7,5},{8,10},{9,11},{10,... | collective-permute-start | bytes 245768 | tf_op jit(solution)/shard_map/ppermute | solution.py:254
  71.5 9.5 %collective-permute-start.7 = (bf16[160,256]{1,0:T(8,128)(2,1)S(1)}, bf16[160,256]{1,0:T(8,128)(2,1)S(1)}, u32[]{:S(2)}, u32[]{:S(2)}) collective-permute-start(bf16[160,256]{1,0:T(8,128)(2,1)S(1)} %get-tuple-element.124), channel_id=1, source_target_pairs={{0,3},{1,2},{2,1},{3,0},{4,7},{5,6},{6,5},{7,4},{8,11},{9,10},{10,... | collective-permute-start | bytes 245768 | tf_op jit(solution)/shard_map/ppermute | solution.py:254
  80.8 162.9 %reduce-scatter.3.cloned.1.call-start = ((), (), s32[]{:S(2)}) async-start(), calls=%async_computation.4 | async-start | bytes 5242880 | tf_op jit(solution)/shard_map/reduce_scatter | solution.py:450
  81.1 8.1 %collective-permute-start.8 = (bf16[160,256]{1,0:T(8,128)(2,1)S(1)}, bf16[160,256]{1,0:T(8,128)(2,1)S(1)}, u32[]{:S(2)}, u32[]{:S(2)}) collective-permute-start(bf16[160,256]{1,0:T(8,128)(2,1)S(1)} %get-tuple-element.93), channel_id=1, source_target_pairs={{0,1},{1,0},{2,3},{3,2},{4,5},{5,4},{6,7},{7,6},{8,9},{9,8},{10,11... | collective-permute-start | bytes 245768 | tf_op jit(solution)/shard_map/ppermute | solution.py:254
  87.1 7.5 %collective-permute-start.9 = (bf16[160,256]{1,0:T(8,128)(2,1)S(1)}, bf16[160,256]{1,0:T(8,128)(2,1)S(1)}, u32[]{:S(2)}, u32[]{:S(2)}) collective-permute-start(bf16[160,256]{1,0:T(8,128)(2,1)S(1)} %get-tuple-element.93), channel_id=1, source_target_pairs={{0,2},{1,3},{2,0},{3,1},{4,6},{5,7},{6,4},{7,5},{8,10},{9,11},{10,... | collective-permute-start | bytes 245768 | tf_op jit(solution)/shard_map/ppermute | solution.py:254
  89.3 7.4 %collective-permute-start.10 = (bf16[160,256]{1,0:T(8,128)(2,1)S(1)}, bf16[160,256]{1,0:T(8,128)(2,1)S(1)}, u32[]{:S(2)}, u32[]{:S(2)}) collective-permute-start(bf16[160,256]{1,0:T(8,128)(2,1)S(1)} %get-tuple-element.93), channel_id=1, source_target_pairs={{0,3},{1,2},{2,1},{3,0},{4,7},{5,6},{6,5},{7,4},{8,11},{9,10},{10,... | collective-permute-start | bytes 245768 | tf_op jit(solution)/shard_map/ppermute | solution.py:254
  96.6 5.7 collective-permute-start.11
  142.3 19.1 %collective-permute-start.14 = (bf16[2048,512]{0,1:T(8,128)(2,1)}, bf16[2048,512]{0,1:T(8,128)(2,1)S(1)}, u32[]{:S(2)}, u32[]{:S(2)}) collective-permute-start(bf16[2048,512]{0,1:T(8,128)(2,1)} %all-gather.7.cloned.1.call-done), channel_id=1, source_target_pairs={{0,4},{4,0},{1,5},{5,1},{2,6},{6,2},{3,7},{7,3},{8,12},{12,8},{9,1... | collective-permute-start | bytes 6291464 | tf_op jit(solution)/shard_map/ppermute | solution.py:254
  158.7 2.7 collective-permute-start.13
  167.5 282.2 %all-gather.9.cloned.1.call-start = ((), (), s32[]{:S(2)}) async-start(), calls=%async_computation.6 | async-start | bytes 5242880 | tf_op jit(solution)/shard_map/all_gather | solution.py:462
  258.0 3.2 collective-permute-start.15
  258.7 66.0 %collective-permute-start.26 = (bf16[2048,512]{1,0:T(8,128)(2,1)}, bf16[2048,512]{1,0:T(8,128)(2,1)}, u32[]{:S(2)}, u32[]{:S(2)}) collective-permute-start(bf16[2048,512]{1,0:T(8,128)(2,1)} %slice_dynamic-update-slice_fusion), channel_id=1, source_target_pairs={{0,4},{4,0},{1,5},{5,1},{2,6},{6,2},{3,7},{7,3},{8,12},{12,8},{9,1... | collective-permute-start | bytes 6291464 | tf_op jit(solution)/shard_map/ppermute | solution.py:254
  258.8 66.0 %collective-permute-start.25 = (bf16[2048,512]{1,0:T(8,128)(2,1)}, bf16[2048,512]{1,0:T(8,128)(2,1)}, u32[]{:S(2)}, u32[]{:S(2)}) collective-permute-start(bf16[2048,512]{1,0:T(8,128)(2,1)} %all-gather.5.cloned.1.call-done), channel_id=1, source_target_pairs={{0,4},{4,0},{1,5},{5,1},{2,6},{6,2},{3,7},{7,3},{8,12},{12,8},{9,1... | collective-permute-start | bytes 6291464 | tf_op jit(solution)/shard_map/ppermute | solution.py:254
  261.4 4.1 collective-permute-start.17
  261.8 8.2 %collective-permute-start.18 = (bf16[160,256]{1,0:T(8,128)(2,1)S(1)}, bf16[160,256]{1,0:T(8,128)(2,1)S(1)}, u32[]{:S(2)}, u32[]{:S(2)}) collective-permute-start(bf16[160,256]{1,0:T(8,128)(2,1)S(1)} %get-tuple-element.120), channel_id=1, source_target_pairs={{0,2},{1,3},{2,0},{3,1},{4,6},{5,7},{6,4},{7,5},{8,10},{9,11},{10,... | collective-permute-start | bytes 245768 | tf_op jit(solution)/shard_map/ppermute | solution.py:254
  264.4 7.6 %collective-permute-start.19 = (bf16[160,256]{1,0:T(8,128)(2,1)S(1)}, bf16[160,256]{1,0:T(8,128)(2,1)S(1)}, u32[]{:S(2)}, u32[]{:S(2)}) collective-permute-start(bf16[160,256]{1,0:T(8,128)(2,1)S(1)} %get-tuple-element.119), channel_id=1, source_target_pairs={{0,3},{1,2},{2,1},{3,0},{4,7},{5,6},{6,5},{7,4},{8,11},{9,10},{10,... | collective-permute-start | bytes 245768 | tf_op jit(solution)/shard_map/ppermute | solution.py:254
  264.4 205.4 %all-reduce.8.cloned.1.call-start = ((), (), s32[]{:S(2)}) async-start(), calls=%async_computation.7 | async-start | bytes 4784128
  272.1 5.5 collective-permute-start.20
  273.7 51.0 %collective-permute-start.16 = (bf16[1024,512]{1,0:T(8,128)(2,1)}, bf16[1024,512]{1,0:T(8,128)(2,1)}, u32[]{:S(2)}, u32[]{:S(2)}) collective-permute-start(bf16[1024,512]{1,0:T(8,128)(2,1)} %get-tuple-element.108), channel_id=1, source_target_pairs={{0,4},{4,0},{1,5},{5,1},{2,6},{6,2},{3,7},{7,3},{8,12},{12,8},{9,1... | collective-permute-start | bytes 3145736 | tf_op jit(solution)/shard_map/ppermute | solution.py:254
  274.5 10.8 %collective-permute-start.21 = (bf16[160,256]{1,0:T(8,128)(2,1)S(1)}, bf16[160,256]{1,0:T(8,128)(2,1)S(1)}, u32[]{:S(2)}, u32[]{:S(2)}) collective-permute-start(bf16[160,256]{1,0:T(8,128)(2,1)S(1)} %get-tuple-element.91), channel_id=1, source_target_pairs={{0,2},{1,3},{2,0},{3,1},{4,6},{5,7},{6,4},{7,5},{8,10},{9,11},{10,... | collective-permute-start | bytes 245768 | tf_op jit(solution)/shard_map/ppermute | solution.py:254
  277.6 19.4 %collective-permute-start.22 = (bf16[160,256]{1,0:T(8,128)(2,1)S(1)}, bf16[160,256]{1,0:T(8,128)(2,1)S(1)}, u32[]{:S(2)}, u32[]{:S(2)}) collective-permute-start(bf16[160,256]{1,0:T(8,128)(2,1)S(1)} %get-tuple-element.91), channel_id=1, source_target_pairs={{0,3},{1,2},{2,1},{3,0},{4,7},{5,6},{6,5},{7,4},{8,11},{9,10},{10,... | collective-permute-start | bytes 245768 | tf_op jit(solution)/shard_map/ppermute | solution.py:254
  297.1 5.7 collective-permute-start.23
  318.8 5.9 collective-permute-start.24
  343.6 48.2 %collective-permute-start.27 = (bf16[256,2048]{1,0:T(8,128)(2,1)}, bf16[256,2048]{1,0:T(8,128)(2,1)}, u32[]{:S(2)}, u32[]{:S(2)}) collective-permute-start(bf16[256,2048]{1,0:T(8,128)(2,1)} %get-tuple-element.101), channel_id=1, source_target_pairs={{0,1},{1,0},{2,3},{3,2},{4,5},{5,4},{6,7},{7,6},{8,9},{9,8},{10,11... | collective-permute-start | bytes 3145736 | tf_op jit(solution)/shard_map/ppermute | solution.py:254
  343.6 73.8 %collective-permute-start.28 = (bf16[256,2048]{1,0:T(8,128)(2,1)}, bf16[256,2048]{1,0:T(8,128)(2,1)}, u32[]{:S(2)}, u32[]{:S(2)}) collective-permute-start(bf16[256,2048]{1,0:T(8,128)(2,1)} %get-tuple-element.103), channel_id=1, source_target_pairs={{0,2},{1,3},{2,0},{3,1},{4,6},{5,7},{6,4},{7,5},{8,10},{9,11},{10,... | collective-permute-start | bytes 3145736 | tf_op jit(solution)/shard_map/ppermute | solution.py:254
  344.9 97.3 %collective-permute-start.29 = (bf16[256,2048]{1,0:T(8,128)(2,1)}, bf16[256,2048]{1,0:T(8,128)(2,1)}, u32[]{:S(2)}, u32[]{:S(2)}) collective-permute-start(bf16[256,2048]{1,0:T(8,128)(2,1)} %get-tuple-element.102), channel_id=1, source_target_pairs={{0,3},{1,2},{2,1},{3,0},{4,7},{5,6},{6,5},{7,4},{8,11},{9,10},{10,... | collective-permute-start | bytes 3145736 | tf_op jit(solution)/shard_map/ppermute | solution.py:254
  357.1 224.5 %reduce-scatter.5.cloned.1.call-start = ((), (), s32[]{:S(2)}) async-start(), calls=%async_computation.5 | async-start | bytes 5242880 | tf_op jit(solution)/shard_map/reduce_scatter | solution.py:499
  458.0 3.2 collective-permute-start.33
  461.2 4.5 collective-permute-start.34
  465.7 4.1 collective-permute-start.35
  471.0 7.7 %collective-permute-start.39 = (bf16[584,512]{1,0:T(8,128)(2,1)S(1)}, bf16[584,512]{1,0:T(8,128)(2,1)S(1)}, u32[]{:S(2)}, u32[]{:S(2)}) collective-permute-start(bf16[584,512]{1,0:T(8,128)(2,1)S(1)} %constant_dynamic-slice_fusion.11), channel_id=1, source_target_pairs={{0,4},{4,0},{1,5},{5,1},{2,6},{6,2},{3,7},{7,3},{8,12},{12,8},{9,1... | collective-permute-start | bytes 1794056 | tf_op jit(solution)/shard_map/ppermute | solution.py:254
  482.5 21.0 %collective-permute-start.30 = (bf16[128,2048]{1,0:T(8,128)(2,1)}, bf16[128,2048]{1,0:T(8,128)(2,1)}, u32[]{:S(2)}, u32[]{:S(2)}) collective-permute-start(bf16[128,2048]{1,0:T(8,128)(2,1)} %get-tuple-element.115), channel_id=1, source_target_pairs={{0,1},{1,0},{2,3},{3,2},{4,5},{5,4},{6,7},{7,6},{8,9},{9,8},{10,11... | collective-permute-start | bytes 1572872 | tf_op jit(solution)/shard_map/ppermute | solution.py:254
  482.5 24.7 %collective-permute-start.31 = (bf16[128,2048]{1,0:T(8,128)(2,1)}, bf16[128,2048]{1,0:T(8,128)(2,1)}, u32[]{:S(2)}, u32[]{:S(2)}) collective-permute-start(bf16[128,2048]{1,0:T(8,128)(2,1)} %get-tuple-element.115), channel_id=1, source_target_pairs={{0,2},{1,3},{2,0},{3,1},{4,6},{5,7},{6,4},{7,5},{8,10},{9,11},{10,... | collective-permute-start | bytes 1572872 | tf_op jit(solution)/shard_map/ppermute | solution.py:254
  483.3 86.3 %copy-start.49 = (f32[32,1024]{1,0:T(8,128)}, f32[32,1024]{1,0:T(8,128)S(1)}, u32[]{:S(2)}) copy-start(f32[32,1024]{1,0:T(8,128)S(1)} %convert_dynamic-update-slice_fusion.4) | copy-start | bytes 393220
  483.8 85.8 %collective-permute-start.36 = (bf16[144,2048]{1,0:T(8,128)(2,1)S(1)}, bf16[144,2048]{1,0:T(8,128)(2,1)S(1)}, u32[]{:S(2)}, u32[]{:S(2)}) collective-permute-start(bf16[144,2048]{1,0:T(8,128)(2,1)S(1)} %concatenate.44), channel_id=1, source_target_pairs={{0,1},{1,0},{2,3},{3,2},{4,5},{5,4},{6,7},{7,6},{8,9},{9,8},{10,11... | collective-permute-start | bytes 1769480 | tf_op jit(solution)/shard_map/ppermute | solution.py:254
  485.1 84.6 %collective-permute-start.37 = (bf16[144,2048]{1,0:T(8,128)(2,1)S(1)}, bf16[144,2048]{1,0:T(8,128)(2,1)S(1)}, u32[]{:S(2)}, u32[]{:S(2)}) collective-permute-start(bf16[144,2048]{1,0:T(8,128)(2,1)S(1)} %concatenate.44), channel_id=1, source_target_pairs={{0,2},{1,3},{2,0},{3,1},{4,6},{5,7},{6,4},{7,5},{8,10},{9,11},{10,... | collective-permute-start | bytes 1769480 | tf_op jit(solution)/shard_map/ppermute | solution.py:254
  486.9 81.8 %collective-permute-start.32 = (bf16[128,2048]{1,0:T(8,128)(2,1)}, bf16[128,2048]{1,0:T(8,128)(2,1)S(1)}, u32[]{:S(2)}, u32[]{:S(2)}) collective-permute-start(bf16[128,2048]{1,0:T(8,128)(2,1)} %get-tuple-element.115), channel_id=1, source_target_pairs={{0,3},{1,2},{2,1},{3,0},{4,7},{5,6},{6,5},{7,4},{8,11},{9,10},{10,... | collective-permute-start | bytes 1572872 | tf_op jit(solution)/shard_map/ppermute | solution.py:254
  503.5 77.9 %collective-permute-start.38 = (bf16[144,2048]{1,0:T(8,128)(2,1)S(1)}, bf16[144,2048]{1,0:T(8,128)(2,1)S(1)}, u32[]{:S(2)}, u32[]{:S(2)}) collective-permute-start(bf16[144,2048]{1,0:T(8,128)(2,1)S(1)} %concatenate.44), channel_id=1, source_target_pairs={{0,3},{1,2},{2,1},{3,0},{4,7},{5,6},{6,5},{7,4},{8,11},{9,10},{10,... | collective-permute-start | bytes 1769480 | tf_op jit(solution)/shard_map/ppermute | solution.py:254
  581.6 8.2 %collective-permute-start.40 = (bf16[1024,512]{1,0:T(8,128)(2,1)}, bf16[1024,512]{1,0:T(8,128)(2,1)}, u32[]{:S(2)}, u32[]{:S(2)}) collective-permute-start(bf16[1024,512]{1,0:T(8,128)(2,1)} %reduce-scatter.5.cloned.1.call-done), channel_id=1, source_target_pairs={{0,4},{4,0},{1,5},{5,1},{2,6},{6,2},{3,7},{7,3},{8,12},{12,8},{9,1... | collective-permute-start | bytes 3145736 | tf_op jit(solution)/shard_map/ppermute | solution.py:254
  (80 other events, 1032.3 us)
Sparse Core Ops, SparseCore 0:
  44.7 36.0 all-gather.4
  82.5 35.1 all-gather.6
  167.6 75.9 reduce-scatter.2
  264.6 89.9 all-gather.8
  358.5 76.5 all-reduce.7
  457.2 51.7 reduce-scatter.4

commit v3 on v2

--- a/solution.py
+++ b/solution.py
@@ -11,6 +11,9 @@
 LANES = 128
 SUB = 8
 CHUNK = 128
+VMEM_LIMIT = 40 << 20
+GONE = 1e4
+LOG2E = 1.4426950408889634
 
 
 def span(group):
@@ -65,14 +68,61 @@
     return functools.reduce(lambda a, b: a + b, values)
 
 
-def scan_kernel(fade_ref, fed_ref, in_ref, out_ref, rate_ref, y_ref, h_ref, last_ref, state_ref):
-    chunk, width = fade_ref.shape
+def soft_step(v):
+    small = jnp.exp(-jnp.abs(v))
+    slope = jnp.where(v >= 0, 1.0, small) / (1.0 + small)
+    return jnp.maximum(v, 0.0) + jnp.log1p(small), slope
+
+
+def step_rows(steps, act, keep_ref, fade_ref, fed_ref):
+    for g in range(steps.shape[1] // LANES):
+        fade_ref[:, span(g)] = jnp.where(keep_ref[...] > 0, steps[:, span(g)], GONE)
+    fed_ref[...] = steps * act
+
+
+def scan_kernel(
+    proj_ref,
+    act_ref,
+    gate_ref,
+    keep_ref,
+    rate_ref,
+    w_dt_ref,
+    bias_ref,
+    skip_ref,
+    gated_ref,
+    sloped_ref,
+    steps_ref,
+    slope_ref,
+    h_ref,
+    last_ref,
+    state_ref,
+    fade_ref,
+    fed_ref,
+    y_ref,
+    coef_ref,
+):
+    chunk, width = act_ref.shape
     halves, groups = rate_ref.shape[0] // SUB, width // LANES
+    states, rank = rate_ref.shape[0], w_dt_ref.shape[0]
 
     @pl.when(pl.program_id(0) == 0)
     def _():
         state_ref[...] = jnp.zeros_like(state_ref)
 
+    logits = (
+        lax.dot_general(
+            proj_ref[:rank, :],
+            w_dt_ref[...],
+            (((0,), (0,)), ((), ())),
+            preferred_element_type=jnp.float32,
+        )
+        + bias_ref[...]
+    )
+    steps, slope_ref[...] = soft_step(logits)
+    steps_ref[...] = steps
+    step_rows(steps, act_ref[...].astype(jnp.float32), keep_ref, fade_ref, fed_ref)
+    coef_ref[...] = proj_ref[rank:, :].astype(jnp.float32)
+    in_ref, out_ref = coef_ref.at[:states], coef_ref.at[states:]
     rate = blocks(rate_ref, halves, groups)
     state = blocks(state_ref, halves, groups)
     bits = sublane_bits()
@@ -97,46 +147,66 @@
             y_ref[base : base + SUB, span(g)] = pending[g][0][1]
     put_blocks(state_ref, state)
     last_ref[...] = state_ref[...]
-
-
-def lane_sums(products):
-    ones = jnp.ones((SUB, LANES), jnp.bfloat16)
-    high = products.astype(jnp.bfloat16)
-    low = (products - high.astype(jnp.float32)).astype(jnp.bfloat16)
-    across = (((1,), (1,)), ((), ()))
-    return lax.dot_general(
-        ones, high, across, preferred_element_type=jnp.float32
-    ) + lax.dot_general(ones, low, across, preferred_element_type=jnp.float32)
+    mixed = y_ref[...] + skip_ref[...] * act_ref[...].astype(jnp.float32)
+    gate = gate_ref[...]
+    sigmoid = jax.nn.sigmoid(gate)
+    gated_ref[...] = (mixed * (gate * sigmoid)).astype(jnp.bfloat16)
+    sloped_ref[...] = mixed * (sigmoid * (1.0 + gate * (1.0 - sigmoid)))
+
+
+def lane_sums(products_ref, states):
+    ones = jnp.ones((LANES, LANES), jnp.bfloat16)
+    sums = jnp.dot(products_ref[...], ones, preferred_element_type=jnp.float32)
+    lane = lax.broadcasted_iota(jnp.int32, (states, LANES), 1)
+    result = jnp.zeros((states, LANES), jnp.float32)
+    for t in range(CHUNK):
+        result = jnp.where(lane == t, sums[t * states : (t + 1) * states], result)
+    return result
 
 
 def adjoint_kernel(
-    fade_ref,
-    fed_ref,
+    proj_ref,
+    act_ref,
+    steps_ref,
+    slope_ref,
     up_ref,
-    in_ref,
-    out_ref,
+    keep_ref,
     rate_ref,
+    w_dt_ref,
+    skip_ref,
     h_ref,
     last_ref,
-    weighted_ref,
-    pulled_ref,
-    d_in_ref,
-    d_out_ref,
+    d_logits_ref,
+    d_act_ref,
+    d_proj_ref,
     d_rate_ref,
+    d_bias_ref,
+    d_skip_ref,
     flow_ref,
     now_ref,
     in_part_ref,
     out_part_ref,
+    fade_ref,
+    fed_ref,
+    weighted_ref,
+    pulled_ref,
+    coef_ref,
 ):
-    chunk, width = fade_ref.shape
+    chunk, width = act_ref.shape
     halves, groups = rate_ref.shape[0] // SUB, width // LANES
+    states, rank = rate_ref.shape[0], w_dt_ref.shape[0]
 
     @pl.when(pl.program_id(0) == 0)
     def _():
         flow_ref[...] = jnp.zeros_like(flow_ref)
         d_rate_ref[...] = jnp.zeros_like(d_rate_ref)
+        d_bias_ref[...] = jnp.zeros_like(d_bias_ref)
+        d_skip_ref[...] = jnp.zeros_like(d_skip_ref)
         now_ref[...] = last_ref[...]
 
+    step_rows(steps_ref[...], act_ref[...].astype(jnp.float32), keep_ref, fade_ref, fed_ref)
+    coef_ref[...] = proj_ref[rank:, :].astype(jnp.float32)
+    in_ref, out_ref = coef_ref.at[:states], coef_ref.at[states:]
     rate = blocks(rate_ref, halves, groups)
     flow = blocks(flow_ref, halves, groups)
     d_rate = blocks(d_rate_ref, halves, groups)
@@ -171,80 +241,119 @@
                     now[i][g] = before
                 fold(weighted[g], total(by_in), bits, True)
                 fold(slopes[g], total(by_rate), bits, True)
-            for i in range(halves):
-                place = (t * halves + i) * SUB
-                in_part_ref[place : place + SUB, :] = total(in_parts[i])
-                out_part_ref[place : place + SUB, :] = total(out_parts[i])
+            place = slice(t * states, (t + 1) * states)
+            for ref, parts in ((in_part_ref, in_parts), (out_part_ref, out_parts)):
+                ref[place, :] = jnp.concatenate([total(part) for part in parts]).astype(jnp.bfloat16)
         for g in range(groups):
             weighted_ref[base : base + SUB, span(g)] = weighted[g][0][1]
             pulled_ref[base : base + SUB, span(g)] = slopes[g][0][1]
     put_blocks(flow_ref, flow)
     put_blocks(d_rate_ref, d_rate)
     put_blocks(now_ref, now)
-    d_in_ref[...] = lane_sums(in_part_ref[...])
-    d_out_ref[...] = lane_sums(out_part_ref[...])
-
-
-def fwd(fading, fed, in_coef, out_coef, rates, **unused):
-    tokens, width = fading.shape
+    d_proj_ref[rank : rank + states, :] = lane_sums(in_part_ref, states)
+    d_proj_ref[rank + states :, :] = lane_sums(out_part_ref, states)
+    act = act_ref[...].astype(jnp.float32)
+    d_step = pulled_ref[...] * (1.0 / LOG2E) + act * weighted_ref[...]
+    d_logits = (d_step * slope_ref[...]).astype(jnp.bfloat16)
+    d_logits_ref[...] = d_logits
+    d_bias_ref[...] += jnp.sum(d_logits.astype(jnp.float32), axis=0, keepdims=True)
+    d_skip_ref[...] += jnp.sum(up_ref[...] * act, axis=0, keepdims=True)
+    d_act_ref[...] = up_ref[...] * skip_ref[...] + steps_ref[...] * weighted_ref[...]
+    d_proj_ref[:rank, :] = lax.dot_general(
+        w_dt_ref[...],
+        d_logits,
+        (((1,), (1,)), ((), ())),
+        preferred_element_type=jnp.float32,
+    )
+
+
+def cost(scale, tokens, states, width):
+    work = tokens * states * width
+    return pl.CostEstimate(flops=scale * work, bytes_accessed=8 * work, transcendentals=work)
+
+
+def whole(array):
+    return pl.BlockSpec(array.shape, lambda c: (0,) * len(array.shape))
+
+
+def scan(proj, act, gate, keep, rates, w_dt, bias, skip):
+    tokens, width = act.shape
     states = rates.shape[0]
-    by_row = lambda size: pl.BlockSpec((size, width), lambda c: (c, 0))
-    cols = pl.BlockSpec((states, CHUNK), lambda c: (0, c))
-    whole = pl.BlockSpec((states, width), lambda c: (0, 0))
+    by_row = lambda size, wide: pl.BlockSpec((size, wide), lambda c: (c, 0))
     like = jax.ShapeDtypeStruct
-    work = tokens * states * width
+    scratch = lambda *shape: pltpu.VMEM(shape, jnp.float32)
+    state = like((states, width), jnp.float32)
     return pl.pallas_call(
         scan_kernel,
         grid=(tokens // CHUNK,),
-        in_specs=[by_row(CHUNK), by_row(CHUNK), cols, cols, whole],
-        out_specs=[by_row(CHUNK), by_row(CHUNK * states), whole],
+        in_specs=[
+            pl.BlockSpec((proj.shape[0], CHUNK), lambda c: (0, c)),
+            by_row(CHUNK, width),
+            by_row(CHUNK, width),
+            by_row(CHUNK, LANES),
+            whole(rates),
+            whole(w_dt),
+            whole(bias),
+            whole(skip),
+        ],
+        out_specs=[by_row(CHUNK, width)] * 4 + [by_row(CHUNK * states, width), whole(state)],
         out_shape=[
+            like((tokens, width), jnp.bfloat16),
+            like((tokens, width), jnp.float32),
+            like((tokens, width), jnp.float32),
             like((tokens, width), jnp.float32),
             like((tokens * states, width), jnp.float32),
-            like((states, width), jnp.float32),
+            state,
         ],
-        scratch_shapes=[pltpu.VMEM((states, width), jnp.float32)],
+        scratch_shapes=[scratch(states, width)]
+        + [scratch(CHUNK, width)] * 3
+        + [scratch(2 * states, CHUNK)],
         compiler_params=pltpu.CompilerParams(
-            dimension_semantics=("arbitrary",), vmem_limit_bytes=40 << 20
+            dimension_semantics=("arbitrary",), vmem_limit_bytes=VMEM_LIMIT
         ),
-        cost_estimate=pl.CostEstimate(flops=2400 * work, bytes_accessed=6 * work, transcendentals=work),
+        cost_estimate=cost(2400, tokens, states, width),
         name="scan",
-    )(fading, fed, in_coef, out_coef, rates)
-
-
-def bwd(fading, fed, upstream, in_coef, out_coef, rates, history, last):
-    tokens, width = fading.shape
+    )(proj, act, gate, keep, rates, w_dt, bias, skip)
+
+
+def adjoint(proj, act, steps, slope, upstream, keep, rates, w_dt, skip, history, last):
+    tokens, width = act.shape
     states = rates.shape[0]
     count = tokens // CHUNK
-    by_row = lambda size: pl.BlockSpec((size, width), lambda c: (count - 1 - c, 0))
-    cols = pl.BlockSpec((states, CHUNK), lambda c: (0, count - 1 - c))
-    flat = pl.BlockSpec((SUB, CHUNK * states), lambda c: (0, count - 1 - c))
-    whole = pl.BlockSpec((states, width), lambda c: (0, 0))
+    by_row = lambda size, wide: pl.BlockSpec((size, wide), lambda c: (count - 1 - c, 0))
+    cols = pl.BlockSpec((proj.shape[0], CHUNK), lambda c: (0, count - 1 - c))
     like = jax.ShapeDtypeStruct
-    work = tokens * states * width
-    weighted, pulled, d_in, d_out, d_rate = pl.pallas_call(
+    scratch = lambda *shape: pltpu.VMEM(shape, jnp.float32)
+    line = like((1, width), jnp.float32)
+    return pl.pallas_call(
         adjoint_kernel,
         grid=(count,),
-        in_specs=[by_row(CHUNK)] * 3 + [cols, cols, whole, by_row(CHUNK * states), whole],
-        out_specs=[by_row(CHUNK), by_row(CHUNK), flat, flat, whole],
-        out_shape=[like((tokens, width), jnp.float32)] * 2
-        + [like((SUB, tokens * states), jnp.float32)] * 2
-        + [like((states, width), jnp.float32)],
-        scratch_shapes=[pltpu.VMEM((states, width), jnp.float32)] * 2
-        + [pltpu.VMEM((CHUNK * states, LANES), jnp.float32)] * 2,
+        in_specs=[cols]
+        + [by_row(CHUNK, width)] * 4
+        + [by_row(CHUNK, LANES), whole(rates), whole(w_dt), whole(skip)]
+        + [by_row(CHUNK * states, width), whole(last)],
+        out_specs=[by_row(CHUNK, width)] * 2 + [cols, whole(last), whole(line), whole(line)],
+        out_shape=[
+            like((tokens, width), jnp.bfloat16),
+            like((tokens, width), jnp.float32),
+            like(proj.shape, jnp.float32),
+            like(last.shape, jnp.float32),
+            line,
+            line,
+        ],
+        scratch_shapes=[scratch(states, width)] * 2
+        + [pltpu.VMEM((CHUNK * states, LANES), jnp.bfloat16)] * 2
+        + [scratch(CHUNK, width)] * 4
+        + [scratch(2 * states, CHUNK)],
         compiler_params=pltpu.CompilerParams(
-            dimension_semantics=("arbitrary",), vmem_limit_bytes=40 << 20
+            dimension_semantics=("arbitrary",), vmem_limit_bytes=VMEM_LIMIT
         ),
-        cost_estimate=pl.CostEstimate(flops=4800 * work, bytes_accessed=8 * work, transcendentals=work),
+        cost_estimate=cost(4800, tokens, states, width),
         name="adjoint",
-    )(fading, fed, upstream, in_coef, out_coef, rates, history, last)
-    by_state = lambda flat_sums: flat_sums[0].reshape(tokens, states).T
-    return weighted, pulled, by_state(d_in), by_state(d_out), d_rate
+    )(proj, act, steps, slope, upstream, keep, rates, w_dt, skip, history, last)
 
 
 EPS = 1e-05
-GONE = 1e4
-LOG2E = 1.4426950408889634
 BF16 = jnp.bfloat16
 F32 = jnp.float32
 
@@ -300,6 +409,24 @@
 
 def scatter_sum(array, axis, dim, kind):
     return collect(*shares(array, axis, dim, kind), axis)
+
+
+def halving_sum(pieces, axis):
+    k = 1
+    while len(pieces) > 1:
+        came = [swap(piece.astype(BF16), axis, k) for piece in pieces[1::2]]
+        pieces = [own.astype(F32) + part.astype(F32) for own, part in zip(pieces[::2], came)]
+        k *= 2
+    return pieces[0]
+
+
+def doubling_pieces(array, axis):
+    k = lax.axis_size(axis) // 2
+    pieces = {0: array}
+    while k:
+        pieces.update({j ^ k: swap(piece, axis, k) for j, piece in pieces.items()})
+        k //= 2
+    return [pieces[j] for j in range(len(pieces))]
 
 
 def doubling_sum(array, axes):
@@ -396,7 +523,6 @@
         conv_output = conv_output + taps_w[k] * shifted[k] * same[k]
     conv_flat = conv_output.reshape(rows, inner)
     activated = jax.nn.silu(conv_flat).astype(BF16)
-    act = activated.astype(F32)
     def all_sum(part):
         halved = scatter_sum(part, "context", 1, F32)
         summed = scatter_sum(halved, "tensor", 1, BF16).astype(BF16)
@@ -412,24 +538,12 @@
         swap(after(own_cotangent, conv_input), "context", k) for k in range(1, ctxs)
     ]
     dt_input = projections[:rank]
-    in_coef = projections[rank : rank + states].astype(F32)
-    out_coef = projections[rank + states :].astype(F32)
-    dt_logits = dot(dt_input, w_dt, 0, 0) + dt_b
-    steps = jax.nn.softplus(dt_logits)
-    keep = same[1].reshape(rows, 1)
-    fading = jnp.where(keep > 0, steps, GONE)
-    fed = steps * act
-    rates2 = rates * LOG2E
-    w_out = after(w_out, fading)
-    scanned, history, last = fwd(fading, fed, in_coef, out_coef, rates2)
-
+    keep = jnp.broadcast_to(same[1].reshape(rows, 1), (rows, LANES))
+    w_out = after(w_out, projections)
     gate = whole_tokens([dot(part, w_gate) for part in normed])
-    gate_value = jax.nn.silu(gate)
-    mixed = scanned + skip * act
-    gated = (mixed * gate_value).astype(BF16)
-    d_gated = whole_tokens([dot(part, w_out) for part in cotangent])
-    d_mixed = d_gated * gate_value
-    d_gate = (d_gated * mixed * silu_slope(gate)).astype(BF16)
+    gated, sloped, steps, slope, history, last = scan(
+        projections, activated, gate, keep, rates * LOG2E, w_dt, dt_b[None], skip[None]
+    )
 
     def my_tokens(parts):
         return [parts[0]] + [swap(parts[k], "context", k) for k in range(1, ctxs)]
@@ -446,27 +560,26 @@
         1,
         1,
     ).astype(BF16)
-    branch, d_mixed = after((branch, d_mixed))
+    w_out_late = after(w_out, branch)
+    d_gated = whole_tokens([dot(part, w_out_late) for part in cotangent])
+    d_mixed = d_gated * jax.nn.silu(gate)
+    d_gate = (d_gated * sloped).astype(BF16)
     branch = lax.psum_scatter(branch, "tensor", scatter_dimension=0, tiled=True).astype(F32)
 
-    in_weighted, d_fade, d_in_coef, d_out_coef, d_rates = bwd(
-        fading, fed, d_mixed, in_coef, out_coef, rates2, history, last
-    )
-    in_weighted, d_fade, branch = after((in_weighted, d_fade, branch))
+    d_logits, d_act, d_part, d_rates, d_bias, d_skips = adjoint(
+        projections, activated, steps, slope, d_mixed, keep, rates * LOG2E, w_dt, skip[None],
+        history, last,
+    )
+    grad_out_part = over_tokens(cotangent, gated_parts)
+    d_part, branch, grad_out_part = after((d_part, branch, grad_out_part))
     x_rows = piece_of(x_flat, "tensor", 0, zplace).astype(F32)
     output_rows = (x_rows + branch).astype(BF16)
-    d_step = d_fade * (1.0 / LOG2E) + act * in_weighted
-    d_logits = (d_step * jax.nn.sigmoid(dt_logits)).astype(BF16)
-    d_part = jnp.concatenate([dot(w_dt, d_logits, 1, 1), d_in_coef, d_out_coef], axis=0)
     d_part, output_rows = after((d_part, output_rows))
     block_output = lax.all_gather(output_rows[None], "tensor", axis=1, tiled=True)
     d_projections, halved = all_sum(d_part)
-    gated_parts, d_gate = after((gated_parts, d_gate), halved)
-    grad_out_part = over_tokens(cotangent, gated_parts)
     gate_parts = token_parts(d_gate)
-    grad_gate_part = over_tokens(normed, gate_parts)
     grad_dt_part = dot(dt_input, d_logits)
-    d_act = d_mixed * skip + steps * in_weighted + dot(d_projections, w_x, 0, 0)
+    d_act = d_act + dot(d_projections, w_x, 0, 0)
     grad_x_part = dot(d_projections, activated)
     d_conv = (d_act * silu_slope(conv_flat)).reshape(seqs, length, inner)
     d_conv_input = jnp.zeros((seqs, length, inner), F32)
@@ -481,32 +594,37 @@
     left = jnp.concatenate(my_tokens(gate_parts) + my_tokens(conv_parts), axis=1)
     right = jnp.concatenate(all_halves(w_gate) + all_halves(w_conv), axis=1)
     partial = dot(left, right, 1, 1).astype(BF16)
-    own_rows, sent_rows = shares(partial, "tensor", 0, BF16)
-    grad_conv_part = over_tokens(normed, after(conv_parts, sent_rows))
-    d_normed = collect(own_rows, sent_rows, "tensor")
+    row_parts = [
+        piece_of(partial, "tensor", 0, zplace ^ k) for k in range(lax.axis_size("tensor"))
+    ]
+    row_parts, block_output = after((row_parts, block_output))
+    d_normed = halving_sum(row_parts, "tensor")
+    grad_conv_part = over_tokens(normed, conv_parts)
+    grad_gate_part = over_tokens(normed, gate_parts)
     d_rows = piece_of(own_cotangent, "tensor", 0, zplace).astype(F32)
     inv = inverse_rms(x_rows)
     scaled = d_normed * norm_gain
     inner_sum = jnp.sum(scaled * x_rows, axis=-1, keepdims=True)
     grad_rows = d_rows + inv * scaled - x_rows * (inv * inv * inv) * inner_sum / width
-    grad_rows, block_output = after((grad_rows.astype(BF16), block_output))
+    grad_rows = grad_rows.astype(BF16)
     gain = jnp.sum(d_normed * x_rows * inv, axis=0)
     devices = lax.axis_size("fsdp")
 
     def owned(*parts):
         pieces = [part.reshape(devices, -1, inner).astype(BF16) for part in parts]
+        fill = -sum(piece.shape[1] for piece in pieces) % LANES
+        pieces.append(jnp.zeros((devices, fill, inner), BF16))
         pieces = row_major(jnp.concatenate(pieces, axis=1).reshape(-1, inner))
         return lax.psum_scatter(pieces, "fsdp", scatter_dimension=0, tiled=True)
 
-    early = owned(*after((grad_gate_part, grad_out_part), sent_rows, block_output))
-    late = owned(grad_x_part, grad_dt_part, grad_conv_part)
+    sums = owned(grad_conv_part, grad_gate_part, grad_out_part, grad_x_part, grad_dt_part)
     thin = jnp.concatenate(
         [
             d_rates * rates,
             jnp.stack(tap_grads),
             jnp.sum(d_conv, axis=(0, 1))[None],
-            jnp.sum(d_logits.astype(F32), axis=0)[None],
-            jnp.sum(d_mixed * act, axis=0)[None],
+            d_bias,
+            d_skips,
             gain.reshape(-1, inner),
         ],
         axis=0,
@@ -515,19 +633,12 @@
     thin = doubling_sum(thin, ("fsdp",))
     others = [thin] + [swap(thin, "context", k) for k in range(1, ctxs)]
     gain = total([part[channels:] for part in others]).reshape(1, width)
-    terms = []
-    for _ in range(3):
-        terms.append(gain.astype(BF16))
-        gain = gain - terms[-1].astype(F32)
-    half = grad_rows.shape[0] // 2
-    fill = jnp.zeros((SUB * 2 - len(terms), width), BF16)
-    early_rows = gather(grad_rows[:half], "tensor", 0).reshape(-1, half, width)
-    late_rows = gather(jnp.concatenate([grad_rows[half:]] + terms + [fill]), "tensor", 0)
-    late_rows = late_rows.reshape(-1, half + SUB * 2, width)
-    grad_gain = total(
-        [jnp.sum(late_rows[:, half + i].astype(F32), axis=0) for i in range(len(terms) - 1, -1, -1)]
-    )
-    grad_input = jnp.concatenate([early_rows, late_rows[:, :half]], axis=1).reshape(block_input.shape)
+    grad_gain = doubling_sum(gain, ("tensor",))[0]
+    count = grad_rows.shape[0]
+    grad_input = jnp.zeros((count * lax.axis_size("tensor"), width), BF16)
+    for k, part in enumerate(doubling_pieces(grad_rows, "tensor")):
+        grad_input = lax.dynamic_update_slice_in_dim(grad_input, part, (zplace ^ k) * count, 0)
+    grad_input = grad_input.reshape(block_input.shape)
 
     def side_by_side(parts, dim):
         size = parts[0].shape[dim]
@@ -538,18 +649,14 @@
         return out
 
     thin = side_by_side([part[:channels] for part in others], 1)
-    early, late = [
-        [sums] + [swap(sums, "context", k) for k in range(1, ctxs)] for sums in (early, late)
-    ]
-    grad_in = jnp.stack(
-        [
-            side_by_side([part[xcols + dtrows :].astype(F32) for part in late], 1),
-            side_by_side([part[:share].astype(F32) for part in early], 1),
-        ]
-    )
-    grad_out = side_by_side([part[share:].T.astype(F32) for part in early], 0)
-    grad_x = side_by_side([part[:xcols].T.astype(F32) for part in late], 0)
-    grad_dt = side_by_side([part[xcols : xcols + dtrows].astype(F32) for part in late], 1)
+    sums = [sums] + [swap(sums, "context", k) for k in range(1, ctxs)]
+    grad_in = side_by_side(
+        [part[: 2 * share].reshape(2, share, inner).astype(F32) for part in sums], 2
+    )
+    grad_out = side_by_side([part[2 * share : 3 * share].T.astype(F32) for part in sums], 0)
+    thin_at = 3 * share + xcols
+    grad_x = side_by_side([part[3 * share : thin_at].T.astype(F32) for part in sums], 0)
+    grad_dt = side_by_side([part[thin_at : thin_at + dtrows].astype(F32) for part in sums], 1)
     return (
         block_output.reshape(block_input.shape),
         grad_input,

time: 618 us -> 541 us (0.88)
  the two profiles are of different devices: /device:TPU:13 before, /device:TPU:0 now
where the time goes in v3:
time: 541 us; the launch traced here: 533 us
  waiting for transfers between devices  192 us (35%)
  Pallas kernels  93.9 us (17%)
  matrix products  86.4 us (16%)
  local copies, waits for them, and re-layouts  59.9 us (11%)
  other arithmetic  48.4 us (9%)
  starting transfers between devices  36.5 us (7%)
  between operations  15.6 us (3%)
    ppermute x39, waiting for transfers between devices, swap(): return lax.ppermute(array, axis, [(i, i ^ k) for i in range(size)])  179 us
    dot_general x18, matrix products, dot(): lax.dot_general(left, right, (((left_dim,), (right_dim,)), ((), ())), pre...  86.4 us
    pallas_call x1, Pallas kernels, adjoint(): pl.pallas_call(adjoint_kernel, grid=(count,), in_specs=[cols] + [by_row(C...  58.6 us
    ppermute x39, starting transfers between devices, swap(): return lax.ppermute(array, axis, [(i, i ^ k) for i in range(size)])  35.7 us
    pallas_call x1, Pallas kernels, scan(): pl.pallas_call(scan_kernel, grid=(tokens // CHUNK,), in_specs=[pl.BlockSp...  35.3 us
    unnamed x148, local copies, waits for them, and re-layouts  22.6 us
  transfers between devices with their start and end apart: 44, of which 21 were waited for; matrix products, arithmetic and copies ran while one was open for 29% of the time, Pallas kernels for 18%

profile of v3, /device:TPU:0, one launch (start us, length us, event | category | flops | bytes accessed | tf_op | source)
XLA Modules:
  0.0 533.1 jit_solution(5046645631281319474)
XLA Ops:
  7.3 3.2 fusion
  10.8 3.0 fusion.2
  15.3 2.6 collective-permute-start
  22.2 10.1 %collective-permute-done = bf16[584,512]{1,0:T(8,128)(2,1)S(1)} collective-permute-done((bf16[584,512]{1,0:T(8,128)(2,1)S(1)}, bf16[584,512]{1,0:T(8,128)(2,1)S(1)}, u32[]{:S(2)}, u32[]{:S(2)}) %collective-permute-start) | collective-permute-done | bytes 598048 | tf_op jit(solution)/shard_map/ppermute | solution.py:363
  32.2 14.2 %collective-permute-done.1 = bf16[584,512]{1,0:T(8,128)(2,1)} collective-permute-done((bf16[584,512]{1,0:T(8,128)(2,1)S(1)}, bf16[584,512]{1,0:T(8,128)(2,1)}, u32[]{:S(2)}, u32[]{:S(2)}) %collective-permute-start.1) | collective-permute-done | bytes 598048 | tf_op jit(solution)/shard_map/ppermute | solution.py:363
  51.1 5.3 fusion.60
  56.4 5.2 fusion.62
  62.3 5.0 fusion.33
  74.0 8.2 %all-gather.5.cloned.1.call-done = bf16[2048,512]{1,0:T(8,128)(2,1)} async-done(((bf16[512,512]{1,0:T(8,128)(2,1)}), bf16[2048,512]{1,0:T(8,128)(2,1)}) %all-gather.5.cloned.1.call-update) | async-done | bytes 2097168 | tf_op jit(solution)/shard_map/all_gather | solution.py:533
  86.8 2.4 collective-permute-start.6
  90.5 5.5 %collective-permute-done.6 = bf16[160,256]{1,0:T(8,128)(2,1)S(1)} collective-permute-done((bf16[160,256]{1,0:T(8,128)(2,1)S(1)}, bf16[160,256]{1,0:T(8,128)(2,1)S(1)}, u32[]{:S(2)}, u32[]{:S(2)}) %collective-permute-start.6) | collective-permute-done | bytes 81952 | tf_op jit(solution)/shard_map/ppermute | solution.py:363
  98.1 4.5 convolution_dynamic-update-slice_fusion.1
  105.7 5.4 %collective-permute-done.9 = bf16[160,256]{1,0:T(8,128)(2,1)S(1)} collective-permute-done((bf16[160,256]{1,0:T(8,128)(2,1)S(1)}, bf16[160,256]{1,0:T(8,128)(2,1)S(1)}, u32[]{:S(2)}, u32[]{:S(2)}) %collective-permute-start.9) | collective-permute-done | bytes 81952 | tf_op jit(solution)/shard_map/ppermute | solution.py:363
  111.2 4.5 convolution_dynamic-update-slice_fusion.gate_ref
  119.6 35.3 %scan.1 = (bf16[2048,512]{1,0:T(8,128)(2,1)S(1)}, f32[2048,512]{1,0:T(8,128)S(1)}, f32[2048,512]{1,0:T(8,128)S(1)}, f32[2048,512]{1,0:T(8,128)}, f32[32768,512]{1,0:T(8,128)}, /*index=5*/f32[16,512]{1,0:T(8,128)S(1)}) custom-call(bf16[160,2048]{1,0:T(8,128)(2,1)S(1)} %constant_dynamic-update-slice_fusion.8.proj_ref, ...), custom_call_target="tpu_custom_call" | custom-call | flops 40265318400 | bytes 134217728 | tf_op jit(solution)/shard_map/scan/pallas_call | solution.py:286
  155.6 6.7 %fusion.83 = f32[512,2048]{1,0:T(8,128)S(1)} fusion(bf16[1024,512]{1,0:T(8,128)(2,1)S(1)} %get-tuple-element.106, bf16[1024,2048]{1,0:T(8,128)(2,1)} %collective-permute-done.14), kind=kOutput, calls=%fused_computation.191 | convolution fusion | flops 2147483648 | bytes 9437184 | tf_op jit(solution)/shard_map/dot_general | solution.py:442
  162.3 6.1 %add_bitcast_fusion = bf16[2048,512]{0,1:T(8,128)(2,1)} fusion(f32[512,2048]{1,0:T(8,128)S(1)} %fusion.83, bf16[1024,512]{1,0:T(8,128)(2,1)S(1)} %get-tuple-element.105, bf16[1,1024,2048]{2,1,0:T(8,128)(2,1)} %param.25), kind=kOutput, calls=%fused_computation.60 | convolution fusion | flops 2149580800 | bytes 11534336 | tf_op jit(solution)/shard_map/dot_general | solution.py:442
  168.4 6.2 %fusion.42 = bf16[1024,2048]{1,0:T(8,128)(2,1)} fusion(bf16[2048,512]{0,1:T(8,128)(2,1)S(1)} %collective-permute-done.13, bf16[2048,512]{0,1:T(8,128)(2,1)S(1)} %copy-done.64, bf16[1024,512]{1,0:T(8,128)(2,1)S(1)} %collective-permute-done.12, bf16[1024,512]{1,0:T(8,128)(2,1)S(1)} %get-tuple-element.105), kind=kOutput, calls=%fused_computation.65 | convolution fusion | flops 4309647360 | bytes 10485760 | tf_op jit(solution)/shard_map/dot_general | solution.py:442
  176.6 4.5 bitcast_dynamic-update-slice_fusion.1
  181.2 4.8 bitcast_dynamic-update-slice_fusion
  186.1 4.7 multiply_convert_fusion.1
  190.8 58.6 %adjoint.1 = (bf16[2048,512]{1,0:T(8,128)(2,1)S(1)}, f32[2048,512]{1,0:T(8,128)S(1)}, f32[160,2048]{1,0:T(8,128)S(1)}, f32[16,512]{1,0:T(8,128)S(1)}, f32[1,512]{1,0:T(1,128)S(1)}, /*index=5*/f32[1,512]{1,0:T(1,128)S(1)}) custom-call(bf16[160,2048]{1,0:T(8,128)(2,1)S(1)} %constant_dynamic-update-slice_fusion.8.proj_ref, ...), custom_call_target="tpu_custom_call" | custom-call | flops 80530636800 | bytes 134217728 | tf_op jit(solution)/shard_map/adjoint/pallas_call | solution.py:328
  255.4 2.5 fusion.46
  262.1 2.4 collective-permute-start.18
  264.9 4.6 fusion.86
  273.4 6.0 %add_convert_fusion = bf16[2048,512]{1,0:T(8,128)(2,1)} fusion(f32[2048,512]{1,0:T(8,128)S(1)} %fusion.86, bf16[1024,2048]{1,0:T(8,128)(2,1)} %collective-permute-done.3, bf16[1024,512]{1,0:T(8,128)(2,1)S(1)} %get-tuple-element.102), kind=kOutput, calls=%fused_computation.52 | convolution fusion | flops 2149580800 | bytes 11534336 | tf_op jit(solution)/shard_map/dot_general | solution.py:442
  282.4 5.7 %collective-permute-done.21 = bf16[160,256]{1,0:T(8,128)(2,1)S(1)} collective-permute-done((bf16[160,256]{1,0:T(8,128)(2,1)S(1)}, bf16[160,256]{1,0:T(8,128)(2,1)S(1)}, u32[]{:S(2)}, u32[]{:S(2)}) %collective-permute-start.21) | collective-permute-done | bytes 81952 | tf_op jit(solution)/shard_map/ppermute | solution.py:363
  288.7 3.1 copy.32
  294.2 3.5 fusion.78
  297.8 4.0 multiply_reduce_fusion
  301.8 3.7 fusion.15
  305.8 5.4 %fusion.85 = f32[2048,512]{1,0:T(8,128)S(1)} fusion(bf16[1024,2048]{1,0:T(8,128)(2,1)} %fusion.2, bf16[1024,512]{1,0:T(8,128)(2,1)S(1)} %get-tuple-element.103), kind=kOutput, calls=%fused_computation.193 | convolution fusion | flops 2147483648 | bytes 9437184 | tf_op jit(solution)/shard_map/dot_general | solution.py:442
  311.2 4.7 add_convert_fusion.1
  326.6 3.4 collective-permute-done.26
  330.0 6.0 %collective-permute-done.25 = bf16[2048,512]{1,0:T(8,128)(2,1)S(1)} collective-permute-done((bf16[2048,512]{1,0:T(8,128)(2,1)}, bf16[2048,512]{1,0:T(8,128)(2,1)S(1)}, u32[]{:S(2)}, u32[]{:S(2)}) %collective-permute-start.25) | collective-permute-done | bytes 2097184 | tf_op jit(solution)/shard_map/ppermute | solution.py:363
  338.3 13.8 %fusion.37 = bf16[1024,2048]{1,0:T(8,128)(2,1)} fusion(bf16[2048,512]{1,0:T(8,128)(2,1)} %copy-done.66, bf16[2048,512]{1,0:T(8,128)(2,1)} %slice_dynamic-update-slice_fusion, bf16[2048,512]{1,0:T(8,128)(2,1)} %copy-done.67, bf16[2048,512]{1,0:T(8,128)(2,1)} %all-gather.5.cloned.1.call-done, bf16[1024,512]{1,0:T(8,128)(2,1)} %collective-permute-done.24, ...), kind=kOutput, calls=%fused_computation.64 | convolution fusion | flops 8642363392 | bytes 16777216 | tf_op jit(solution)/shard_map/dot_general | solution.py:442
  352.1 4.0 constant_dynamic-slice_fusion.1
  356.1 3.8 all-gather.9.cloned.1.call-done
  361.9 24.2 %collective-permute-done.28 = bf16[256,2048]{1,0:T(8,128)(2,1)S(1)} collective-permute-done((bf16[256,2048]{1,0:T(8,128)(2,1)}, bf16[256,2048]{1,0:T(8,128)(2,1)S(1)}, u32[]{:S(2)}, u32[]{:S(2)}) %collective-permute-start.28) | collective-permute-done | bytes 1048608 | tf_op jit(solution)/shard_map/ppermute | solution.py:363
  387.5 39.8 %collective-permute-done.27 = bf16[256,2048]{1,0:T(8,128)(2,1)S(1)} collective-permute-done((bf16[256,2048]{1,0:T(8,128)(2,1)}, bf16[256,2048]{1,0:T(8,128)(2,1)S(1)}, u32[]{:S(2)}, u32[]{:S(2)}) %collective-permute-start.27) | collective-permute-done | bytes 1048608 | tf_op jit(solution)/shard_map/ppermute | solution.py:363
  427.3 5.7 %collective-permute-done.29 = bf16[256,2048]{1,0:T(8,128)(2,1)S(1)} collective-permute-done((bf16[256,2048]{1,0:T(8,128)(2,1)S(1)}, bf16[256,2048]{1,0:T(8,128)(2,1)S(1)}, u32[]{:S(2)}, u32[]{:S(2)}) %collective-permute-start.29) | collective-permute-done | bytes 1048608 | tf_op jit(solution)/shard_map/ppermute | solution.py:363
  433.0 2.7 fusion.53
  436.2 3.6 bitcast_dynamic-update-slice_fusion.5
  443.4 2.8 collective-permute-done.33
  447.8 2.8 collective-permute-done.34
  452.1 31.3 %collective-permute-done.36 = f32[1,2048]{1,0:T(1,128)S(1)} collective-permute-done((f32[1,2048]{1,0:T(1,128)S(1)}, f32[1,2048]{1,0:T(1,128)S(1)}, u32[]{:S(2)}, u32[]{:S(2)}) %collective-permute-start.36) | collective-permute-done | bytes 8224 | tf_op jit(solution)/shard_map/ppermute | solution.py:363
  483.4 2.3 collective-permute-start.37
  490.9 16.9 %collective-permute-done.32 = bf16[256,2048]{1,0:T(8,128)(2,1)S(1)} collective-permute-done((bf16[256,2048]{1,0:T(8,128)(2,1)S(1)}, bf16[256,2048]{1,0:T(8,128)(2,1)S(1)}, u32[]{:S(2)}, u32[]{:S(2)}) %collective-permute-start.32) | collective-permute-done | bytes 1048608 | tf_op jit(solution)/shard_map/ppermute | solution.py:363
  (323 shorter events, 102.6 us)
Async XLA Ops:
  7.2 63.5 %copy-start = (bf16[1024,512]{1,0:T(8,128)(2,1)S(1)}, bf16[1024,512]{1,0:T(8,128)(2,1)}, u32[]{:S(2)}) copy-start(bf16[1024,512]{1,0:T(8,128)(2,1)} %param.24) | copy-start | bytes 3145732
  7.2 75.0 %all-gather.5.cloned.1.call-start = ((), (), s32[]{:S(2)}) async-start(), calls=%async_computation.2 | async-start | bytes 2621440 | tf_op jit(solution)/shard_map/all_gather | solution.py:533
  13.8 42.6 %collective-permute-start.3 = (bf16[1024,2048]{1,0:T(8,128)(2,1)}, bf16[1024,2048]{1,0:T(8,128)(2,1)}, u32[]{:S(2)}, u32[]{:S(2)}) collective-permute-start(bf16[1024,2048]{1,0:T(8,128)(2,1)} %fusion.2), channel_id=1, source_target_pairs={{0,4},{4,0},{1,5},{5,1},{2,6},{6,2},{3,7},{7,3},{8,12},{12,8},{9,1... | collective-permute-start | bytes 12582920 | tf_op jit(solution)/shard_map/ppermute | solution.py:363
  15.3 16.9 %collective-permute-start = (bf16[584,512]{1,0:T(8,128)(2,1)S(1)}, bf16[584,512]{1,0:T(8,128)(2,1)S(1)}, u32[]{:S(2)}, u32[]{:S(2)}) collective-permute-start(bf16[584,512]{1,0:T(8,128)(2,1)S(1)} %pad_maximum_fusion), channel_id=1, source_target_pairs={{0,8},{8,0},{16,24},{24,16},{1,9},{9,1},{17,25},{25,17},{2,10},{10... | collective-permute-start | bytes 1794056 | tf_op jit(solution)/shard_map/ppermute | solution.py:363
  17.9 28.5 %collective-permute-start.1 = (bf16[584,512]{1,0:T(8,128)(2,1)S(1)}, bf16[584,512]{1,0:T(8,128)(2,1)}, u32[]{:S(2)}, u32[]{:S(2)}) collective-permute-start(bf16[584,512]{1,0:T(8,128)(2,1)S(1)} %pad_maximum_fusion), channel_id=1, source_target_pairs={{0,16},{8,24},{16,0},{24,8},{1,17},{9,25},{17,1},{25,9},{2,18},{10... | collective-permute-start | bytes 1794056 | tf_op jit(solution)/shard_map/ppermute | solution.py:363
  19.4 27.0 %collective-permute-start.2 = (bf16[584,512]{1,0:T(8,128)(2,1)S(1)}, bf16[584,512]{1,0:T(8,128)(2,1)S(1)}, u32[]{:S(2)}, u32[]{:S(2)}) collective-permute-start(bf16[584,512]{1,0:T(8,128)(2,1)S(1)} %pad_maximum_fusion), channel_id=1, source_target_pairs={{0,24},{8,16},{16,8},{24,0},{1,25},{9,17},{17,9},{25,1},{2,26},{10... | collective-permute-start | bytes 1794056 | tf_op jit(solution)/shard_map/ppermute | solution.py:363
  22.0 40.3 %copy-start.49 = (f32[1,512]{1,0:T(1,128)}, f32[1,512]{1,0:T(1,128)S(1)}, u32[]{:S(2)}) copy-start(f32[1,512]{1,0:T(1,128)S(1)} %get-tuple-element.118) | copy-start | bytes 6148
  22.2 97.1 %copy-start.37 = (f32[1,2048]{1,0:T(1,128)}, f32[1,2048]{1,0:T(1,128)S(1)}, u32[]{:S(2)}) copy-start(f32[1,2048]{1,0:T(1,128)S(1)} %get-tuple-element.122) | copy-start | bytes 24580
  46.4 72.8 %all-gather.7.cloned.1.call-start = ((), (), s32[]{:S(2)}) async-start(), calls=%async_computation.3 | async-start | bytes 2621440 | tf_op jit(solution)/shard_map/all_gather | solution.py:535
  70.2 2.4 collective-permute-start.4
  70.2 85.4 %collective-permute-start.14 = (bf16[1024,2048]{1,0:T(8,128)(2,1)}, bf16[1024,2048]{1,0:T(8,128)(2,1)}, u32[]{:S(2)}, u32[]{:S(2)}) collective-permute-start(bf16[1024,2048]{1,0:T(8,128)(2,1)} %bitcast.18), channel_id=1, source_target_pairs={{0,4},{4,0},{1,5},{5,1},{2,6},{6,2},{3,7},{7,3},{8,12},{12,8},{9,1... | collective-permute-start | bytes 12582920 | tf_op jit(solution)/shard_map/ppermute | solution.py:363
  82.3 171.6 %reduce-scatter.3.cloned.1.call-start = ((), (), s32[]{:S(2)}) async-start(), calls=%async_computation.4 | async-start | bytes 5242880 | tf_op jit(solution)/shard_map/reduce_scatter | solution.py:567
  85.2 5.2 collective-permute-start.5
  86.8 9.2 %collective-permute-start.6 = (bf16[160,256]{1,0:T(8,128)(2,1)S(1)}, bf16[160,256]{1,0:T(8,128)(2,1)S(1)}, u32[]{:S(2)}, u32[]{:S(2)}) collective-permute-start(bf16[160,256]{1,0:T(8,128)(2,1)S(1)} %get-tuple-element.114), channel_id=1, source_target_pairs={{0,2},{1,3},{2,0},{3,1},{4,6},{5,7},{6,4},{7,5},{8,10},{9,11},{10,... | collective-permute-start | bytes 245768 | tf_op jit(solution)/shard_map/ppermute | solution.py:363
  89.2 6.8 %collective-permute-start.7 = (bf16[160,256]{1,0:T(8,128)(2,1)S(1)}, bf16[160,256]{1,0:T(8,128)(2,1)S(1)}, u32[]{:S(2)}, u32[]{:S(2)}) collective-permute-start(bf16[160,256]{1,0:T(8,128)(2,1)S(1)} %get-tuple-element.113), channel_id=1, source_target_pairs={{0,3},{1,2},{2,1},{3,0},{4,7},{5,6},{6,5},{7,4},{8,11},{9,10},{10,... | collective-permute-start | bytes 245768 | tf_op jit(solution)/shard_map/ppermute | solution.py:363
  96.1 9.6 %collective-permute-start.8 = (bf16[160,256]{1,0:T(8,128)(2,1)S(1)}, bf16[160,256]{1,0:T(8,128)(2,1)S(1)}, u32[]{:S(2)}, u32[]{:S(2)}) collective-permute-start(bf16[160,256]{1,0:T(8,128)(2,1)S(1)} %get-tuple-element.90), channel_id=1, source_target_pairs={{0,1},{1,0},{2,3},{3,2},{4,5},{5,4},{6,7},{7,6},{8,9},{9,8},{10,11... | collective-permute-start | bytes 245768 | tf_op jit(solution)/shard_map/ppermute | solution.py:363
  102.6 8.4 %collective-permute-start.9 = (bf16[160,256]{1,0:T(8,128)(2,1)S(1)}, bf16[160,256]{1,0:T(8,128)(2,1)S(1)}, u32[]{:S(2)}, u32[]{:S(2)}) collective-permute-start(bf16[160,256]{1,0:T(8,128)(2,1)S(1)} %get-tuple-element.90), channel_id=1, source_target_pairs={{0,2},{1,3},{2,0},{3,1},{4,6},{5,7},{6,4},{7,5},{8,10},{9,11},{10,... | collective-permute-start | bytes 245768 | tf_op jit(solution)/shard_map/ppermute | solution.py:363
  104.2 6.9 %collective-permute-start.10 = (bf16[160,256]{1,0:T(8,128)(2,1)S(1)}, bf16[160,256]{1,0:T(8,128)(2,1)S(1)}, u32[]{:S(2)}, u32[]{:S(2)}) collective-permute-start(bf16[160,256]{1,0:T(8,128)(2,1)S(1)} %get-tuple-element.90), channel_id=1, source_target_pairs={{0,3},{1,2},{2,1},{3,0},{4,7},{5,6},{6,5},{7,4},{8,11},{9,10},{10,... | collective-permute-start | bytes 245768 | tf_op jit(solution)/shard_map/ppermute | solution.py:363
  111.1 6.6 %collective-permute-start.11 = (bf16[160,1024]{1,0:T(8,128)(2,1)S(1)}, bf16[160,1024]{1,0:T(8,128)(2,1)S(1)}, u32[]{:S(2)}, u32[]{:S(2)}) collective-permute-start(bf16[160,1024]{1,0:T(8,128)(2,1)S(1)} %constant_dynamic-update-slice_fusion.10), channel_id=1, source_target_pairs={{0,4},{4,0},{1,5},{5,1},{2,6},{6,2},{3,7},{7,3},{8,12},{12,8},{9,1... | collective-permute-start | bytes 983048 | tf_op jit(solution)/shard_map/ppermute | solution.py:363
  119.3 49.2 %collective-permute-start.13 = (bf16[2048,512]{0,1:T(8,128)(2,1)}, bf16[2048,512]{0,1:T(8,128)(2,1)S(1)}, u32[]{:S(2)}, u32[]{:S(2)}) collective-permute-start(bf16[2048,512]{0,1:T(8,128)(2,1)} %all-gather.7.cloned.1.call-done), channel_id=1, source_target_pairs={{0,4},{4,0},{1,5},{5,1},{2,6},{6,2},{3,7},{7,3},{8,12},{12,8},{9,1... | collective-permute-start | bytes 6291464 | tf_op jit(solution)/shard_map/ppermute | solution.py:363
  155.0 13.4 %collective-permute-start.12 = (bf16[1024,512]{1,0:T(8,128)(2,1)S(1)}, bf16[1024,512]{1,0:T(8,128)(2,1)S(1)}, u32[]{:S(2)}, u32[]{:S(2)}) collective-permute-start(bf16[1024,512]{1,0:T(8,128)(2,1)S(1)} %get-tuple-element.106), channel_id=1, source_target_pairs={{0,4},{4,0},{1,5},{5,1},{2,6},{6,2},{3,7},{7,3},{8,12},{12,8},{9,1... | collective-permute-start | bytes 3145736 | tf_op jit(solution)/shard_map/ppermute | solution.py:363
  174.6 185.3 %all-gather.9.cloned.1.call-start = ((), (), s32[]{:S(2)}) async-start(), calls=%async_computation.6 | async-start | bytes 5242880 | tf_op jit(solution)/shard_map/all_gather | solution.py:578
  258.0 2.3 collective-permute-start.16
  260.4 9.0 %collective-permute-start.17 = (bf16[160,256]{1,0:T(8,128)(2,1)S(1)}, bf16[160,256]{1,0:T(8,128)(2,1)S(1)}, u32[]{:S(2)}, u32[]{:S(2)}) collective-permute-start(bf16[160,256]{1,0:T(8,128)(2,1)S(1)} %get-tuple-element.109), channel_id=1, source_target_pairs={{0,1},{1,0},{2,3},{3,2},{4,5},{5,4},{6,7},{7,6},{8,9},{9,8},{10,11... | collective-permute-start | bytes 245768 | tf_op jit(solution)/shard_map/ppermute | solution.py:363
  262.1 9.5 %collective-permute-start.18 = (bf16[160,256]{1,0:T(8,128)(2,1)S(1)}, bf16[160,256]{1,0:T(8,128)(2,1)S(1)}, u32[]{:S(2)}, u32[]{:S(2)}) collective-permute-start(bf16[160,256]{1,0:T(8,128)(2,1)S(1)} %get-tuple-element.111), channel_id=1, source_target_pairs={{0,2},{1,3},{2,0},{3,1},{4,6},{5,7},{6,4},{7,5},{8,10},{9,11},{10,... | collective-permute-start | bytes 245768 | tf_op jit(solution)/shard_map/ppermute | solution.py:363
  264.5 7.1 %collective-permute-start.19 = (bf16[160,256]{1,0:T(8,128)(2,1)S(1)}, bf16[160,256]{1,0:T(8,128)(2,1)S(1)}, u32[]{:S(2)}, u32[]{:S(2)}) collective-permute-start(bf16[160,256]{1,0:T(8,128)(2,1)S(1)} %get-tuple-element.110), channel_id=1, source_target_pairs={{0,3},{1,2},{2,1},{3,0},{4,7},{5,6},{6,5},{7,4},{8,11},{9,10},{10,... | collective-permute-start | bytes 245768 | tf_op jit(solution)/shard_map/ppermute | solution.py:363
  271.7 10.6 %collective-permute-start.20 = (bf16[160,256]{1,0:T(8,128)(2,1)S(1)}, bf16[160,256]{1,0:T(8,128)(2,1)S(1)}, u32[]{:S(2)}, u32[]{:S(2)}) collective-permute-start(bf16[160,256]{1,0:T(8,128)(2,1)S(1)} %get-tuple-element.88), channel_id=1, source_target_pairs={{0,1},{1,0},{2,3},{3,2},{4,5},{5,4},{6,7},{7,6},{8,9},{9,8},{10,11... | collective-permute-start | bytes 245768 | tf_op jit(solution)/shard_map/ppermute | solution.py:363
  279.5 210.3 %reduce-scatter.5.cloned.1.call-start = ((), (), s32[]{:S(2)}) async-start(), calls=%async_computation.5 | async-start | bytes 8519680 | tf_op jit(solution)/shard_map/reduce_scatter | solution.py:618
  279.5 8.6 %collective-permute-start.21 = (bf16[160,256]{1,0:T(8,128)(2,1)S(1)}, bf16[160,256]{1,0:T(8,128)(2,1)S(1)}, u32[]{:S(2)}, u32[]{:S(2)}) collective-permute-start(bf16[160,256]{1,0:T(8,128)(2,1)S(1)} %get-tuple-element.88), channel_id=1, source_target_pairs={{0,2},{1,3},{2,0},{3,1},{4,6},{5,7},{6,4},{7,5},{8,10},{9,11},{10,... | collective-permute-start | bytes 245768 | tf_op jit(solution)/shard_map/ppermute | solution.py:363
  281.1 7.0 %collective-permute-start.22 = (bf16[160,256]{1,0:T(8,128)(2,1)S(1)}, bf16[160,256]{1,0:T(8,128)(2,1)S(1)}, u32[]{:S(2)}, u32[]{:S(2)}) collective-permute-start(bf16[160,256]{1,0:T(8,128)(2,1)S(1)} %get-tuple-element.88), channel_id=1, source_target_pairs={{0,3},{1,2},{2,1},{3,0},{4,7},{5,6},{6,5},{7,4},{8,11},{9,10},{10,... | collective-permute-start | bytes 245768 | tf_op jit(solution)/shard_map/ppermute | solution.py:363
  288.1 3.8 collective-permute-start.23
  325.5 4.5 collective-permute-start.26
  326.0 10.0 %collective-permute-start.25 = (bf16[2048,512]{1,0:T(8,128)(2,1)}, bf16[2048,512]{1,0:T(8,128)(2,1)S(1)}, u32[]{:S(2)}, u32[]{:S(2)}) collective-permute-start(bf16[2048,512]{1,0:T(8,128)(2,1)} %all-gather.5.cloned.1.call-done), channel_id=1, source_target_pairs={{0,4},{4,0},{1,5},{5,1},{2,6},{6,2},{3,7},{7,3},{8,12},{12,8},{9,1... | collective-permute-start | bytes 6291464 | tf_op jit(solution)/shard_map/ppermute | solution.py:363
  326.1 9.9 %collective-permute-start.15 = (bf16[1024,512]{1,0:T(8,128)(2,1)S(1)}, bf16[1024,512]{1,0:T(8,128)(2,1)S(1)}, u32[]{:S(2)}, u32[]{:S(2)}) collective-permute-start(bf16[1024,512]{1,0:T(8,128)(2,1)S(1)} %copy-done.30), channel_id=1, source_target_pairs={{0,4},{4,0},{1,5},{5,1},{2,6},{6,2},{3,7},{7,3},{8,12},{12,8},{9,1... | collective-permute-start | bytes 3145736 | tf_op jit(solution)/shard_map/ppermute | solution.py:363
  326.5 11.8 %collective-permute-start.24 = (bf16[1024,512]{1,0:T(8,128)(2,1)}, bf16[1024,512]{1,0:T(8,128)(2,1)}, u32[]{:S(2)}, u32[]{:S(2)}) collective-permute-start(bf16[1024,512]{1,0:T(8,128)(2,1)} %copy-done.32), channel_id=1, source_target_pairs={{0,4},{4,0},{1,5},{5,1},{2,6},{6,2},{3,7},{7,3},{8,12},{12,8},{9,1... | collective-permute-start | bytes 3145736 | tf_op jit(solution)/shard_map/ppermute | solution.py:363
  352.1 80.9 %copy-start.45 = (f32[2048]{0:T(1024)S(1)}, f32[2048]{0:T(1024)}, u32[]{:S(2)}) copy-start(f32[2048]{0:T(1024)} %param.15) | copy-start | bytes 24580
  359.9 26.3 %collective-permute-start.28 = (bf16[256,2048]{1,0:T(8,128)(2,1)}, bf16[256,2048]{1,0:T(8,128)(2,1)S(1)}, u32[]{:S(2)}, u32[]{:S(2)}) collective-permute-start(bf16[256,2048]{1,0:T(8,128)(2,1)} %get-tuple-element.68), channel_id=1, source_target_pairs={{0,1},{1,0},{2,3},{3,2},{4,5},{5,4},{6,7},{7,6},{8,9},{9,8},{10,11... | collective-permute-start | bytes 3145736 | tf_op jit(solution)/shard_map/ppermute | solution.py:363
  359.9 67.5 %collective-permute-start.27 = (bf16[256,2048]{1,0:T(8,128)(2,1)}, bf16[256,2048]{1,0:T(8,128)(2,1)S(1)}, u32[]{:S(2)}, u32[]{:S(2)}) collective-permute-start(bf16[256,2048]{1,0:T(8,128)(2,1)} %get-tuple-element.66), channel_id=1, source_target_pairs={{0,1},{1,0},{2,3},{3,2},{4,5},{5,4},{6,7},{7,6},{8,9},{9,8},{10,11... | collective-permute-start | bytes 3145736 | tf_op jit(solution)/shard_map/ppermute | solution.py:363
  386.5 46.5 %collective-permute-start.29 = (bf16[256,2048]{1,0:T(8,128)(2,1)S(1)}, bf16[256,2048]{1,0:T(8,128)(2,1)S(1)}, u32[]{:S(2)}, u32[]{:S(2)}) collective-permute-start(bf16[256,2048]{1,0:T(8,128)(2,1)S(1)} %add_convert_fusion.2), channel_id=1, source_target_pairs={{0,2},{1,3},{2,0},{3,1},{4,6},{5,7},{6,4},{7,5},{8,10},{9,11},{10,... | collective-permute-start | bytes 3145736 | tf_op jit(solution)/shard_map/ppermute | solution.py:363
  439.8 45.9 %collective-permute-start.31 = (bf16[256,2048]{1,0:T(8,128)(2,1)}, bf16[256,2048]{1,0:T(8,128)(2,1)S(1)}, u32[]{:S(2)}, u32[]{:S(2)}) collective-permute-start(bf16[256,2048]{1,0:T(8,128)(2,1)} %get-tuple-element.86), channel_id=1, source_target_pairs={{0,2},{1,3},{2,0},{3,1},{4,6},{5,7},{6,4},{7,5},{8,10},{9,11},{10,... | collective-permute-start | bytes 3145736 | tf_op jit(solution)/shard_map/ppermute | solution.py:363
  439.8 49.0 %collective-permute-start.30 = (bf16[256,2048]{1,0:T(8,128)(2,1)}, bf16[256,2048]{1,0:T(8,128)(2,1)S(1)}, u32[]{:S(2)}, u32[]{:S(2)}) collective-permute-start(bf16[256,2048]{1,0:T(8,128)(2,1)} %get-tuple-element.86), channel_id=1, source_target_pairs={{0,1},{1,0},{2,3},{3,2},{4,5},{5,4},{6,7},{7,6},{8,9},{9,8},{10,11... | collective-permute-start | bytes 3145736 | tf_op jit(solution)/shard_map/ppermute | solution.py:363
  442.0 4.3 collective-permute-start.33
  446.3 4.3 collective-permute-start.34
  450.7 1.3 collective-permute-start.35
  452.0 31.4 %collective-permute-start.36 = (f32[1,2048]{1,0:T(1,128)S(1)}, f32[1,2048]{1,0:T(1,128)S(1)}, u32[]{:S(2)}, u32[]{:S(2)}) collective-permute-start(f32[1,2048]{1,0:T(1,128)S(1)} %bitcast.190), channel_id=1, source_target_pairs={{0,1},{1,0},{2,3},{3,2},{4,5},{5,4},{6,7},{7,6},{8,9},{9,8},{10,11... | collective-permute-start | bytes 24584 | tf_op jit(solution)/shard_map/ppermute | solution.py:363
  483.4 4.7 collective-permute-start.37
  485.7 22.0 %collective-permute-start.32 = (bf16[256,2048]{1,0:T(8,128)(2,1)S(1)}, bf16[256,2048]{1,0:T(8,128)(2,1)S(1)}, u32[]{:S(2)}, u32[]{:S(2)}) collective-permute-start(bf16[256,2048]{1,0:T(8,128)(2,1)S(1)} %collective-permute-done.31), channel_id=1, source_target_pairs={{0,1},{1,0},{2,3},{3,2},{4,5},{5,4},{6,7},{7,6},{8,9},{9,8},{10,11... | collective-permute-start | bytes 3145736 | tf_op jit(solution)/shard_map/ppermute | solution.py:363
  489.8 24.6 %collective-permute-start.38 = (bf16[1664,512]{1,0:T(8,128)(2,1)}, bf16[1664,512]{1,0:T(8,128)(2,1)}, u32[]{:S(2)}, u32[]{:S(2)}) collective-permute-start(bf16[1664,512]{1,0:T(8,128)(2,1)} %reduce-scatter.5.cloned.1.call-done), channel_id=1, source_target_pairs={{0,4},{4,0},{1,5},{5,1},{2,6},{6,2},{3,7},{7,3},{8,12},{12,8},{9,1... | collective-permute-start | bytes 5111816 | tf_op jit(solution)/shard_map/ppermute | solution.py:363
  (67 other events, 627.7 us)
Sparse Core Ops, SparseCore 0:
  46.6 35.6 all-gather.4
  84.1 35.1 all-gather.6
  174.7 76.9 reduce-scatter.2
  279.6 80.2 all-gather.8
  363.0 73.1 reduce-scatter.4

commit v4 on v3

--- a/solution.py
+++ b/solution.py
@@ -11,7 +11,7 @@
 LANES = 128
 SUB = 8
 CHUNK = 128
-VMEM_LIMIT = 40 << 20
+VMEM_LIMIT = 56 << 20
 GONE = 1e4
 LOG2E = 1.4426950408889634
 
@@ -523,27 +523,29 @@
         conv_output = conv_output + taps_w[k] * shifted[k] * same[k]
     conv_flat = conv_output.reshape(rows, inner)
     activated = jax.nn.silu(conv_flat).astype(BF16)
-    def all_sum(part):
+    def all_sum(part, *beside):
         halved = scatter_sum(part, "context", 1, F32)
+        halved = after(halved, *beside)
         summed = scatter_sum(halved, "tensor", 1, BF16).astype(BF16)
-        return gather(gather(summed, "tensor", 1), "context", 1), halved
-
-    projections, halved = all_sum(dot(w_x, activated, 1, 1))
+        return gather(gather(summed, "tensor", 1), "context", 1), halved, summed
+
+    projections, _, summed = all_sum(dot(w_x, activated, 1, 1))
     w_gate = after(
-        lax.all_gather(after(in_half[1], first), "fsdp", axis=0, tiled=True), halved
-    )
-    w_out = lax.all_gather(after(mine(out_proj, 0).T, w_gate), "fsdp", axis=0, tiled=True)
+        lax.all_gather(after(in_half[1], first), "fsdp", axis=0, tiled=True), summed
+    )
+    w_out = lax.all_gather(after(mine(out_proj, 0).T, conv_input), "fsdp", axis=0, tiled=True)
     own_cotangent = grad_output.reshape(seqs * piece, width)
     cotangent = [own_cotangent] + [
         swap(after(own_cotangent, conv_input), "context", k) for k in range(1, ctxs)
     ]
+    keep = jnp.broadcast_to(same[1].reshape(rows, 1), (rows, LANES))
+    projections, keep = after((projections, keep))
     dt_input = projections[:rank]
-    keep = jnp.broadcast_to(same[1].reshape(rows, 1), (rows, LANES))
-    w_out = after(w_out, projections)
     gate = whole_tokens([dot(part, w_gate) for part in normed])
     gated, sloped, steps, slope, history, last = scan(
         projections, activated, gate, keep, rates * LOG2E, w_dt, dt_b[None], skip[None]
     )
+    w_out = after(w_out, gated)
 
     def my_tokens(parts):
         return [parts[0]] + [swap(parts[k], "context", k) for k in range(1, ctxs)]
@@ -560,8 +562,8 @@
         1,
         1,
     ).astype(BF16)
-    w_out_late = after(w_out, branch)
-    d_gated = whole_tokens([dot(part, w_out_late) for part in cotangent])
+    later = [after(part, branch) for part in cotangent[1:]]
+    d_gated = whole_tokens([dot(part, w_out) for part in cotangent[:1] + later])
     d_mixed = d_gated * jax.nn.silu(gate)
     d_gate = (d_gated * sloped).astype(BF16)
     branch = lax.psum_scatter(branch, "tensor", scatter_dimension=0, tiled=True).astype(F32)
@@ -570,14 +572,16 @@
         projections, activated, steps, slope, d_mixed, keep, rates * LOG2E, w_dt, skip[None],
         history, last,
     )
-    grad_out_part = over_tokens(cotangent, gated_parts)
-    d_part, branch, grad_out_part = after((d_part, branch, grad_out_part))
+    gate_halves, conv_halves = all_halves(w_gate), all_halves(w_conv)
+    d_part, branch, gate_halves, conv_halves = after((d_part, branch, gate_halves, conv_halves))
     x_rows = piece_of(x_flat, "tensor", 0, zplace).astype(F32)
     output_rows = (x_rows + branch).astype(BF16)
-    d_part, output_rows = after((d_part, output_rows))
+    d_projections, halved, summed = all_sum(d_part, output_rows)
     block_output = lax.all_gather(output_rows[None], "tensor", axis=1, tiled=True)
-    d_projections, halved = all_sum(d_part)
     gate_parts = token_parts(d_gate)
+    late_gate, late_gated = after((gate_parts, gated_parts), halved)
+    grad_out_part = over_tokens(cotangent, late_gated)
+    grad_gate_part = over_tokens(normed, late_gate)
     grad_dt_part = dot(dt_input, d_logits)
     d_act = d_act + dot(d_projections, w_x, 0, 0)
     grad_x_part = dot(d_projections, activated)
@@ -592,7 +596,7 @@
     d_conv_input = d_conv_input.reshape(rows, inner).astype(BF16)
     conv_parts = token_parts(d_conv_input)
     left = jnp.concatenate(my_tokens(gate_parts) + my_tokens(conv_parts), axis=1)
-    right = jnp.concatenate(all_halves(w_gate) + all_halves(w_conv), axis=1)
+    right = jnp.concatenate(gate_halves + conv_halves, axis=1)
     partial = dot(left, right, 1, 1).astype(BF16)
     row_parts = [
         piece_of(partial, "tensor", 0, zplace ^ k) for k in range(lax.axis_size("tensor"))
@@ -600,13 +604,13 @@
     row_parts, block_output = after((row_parts, block_output))
     d_normed = halving_sum(row_parts, "tensor")
     grad_conv_part = over_tokens(normed, conv_parts)
-    grad_gate_part = over_tokens(normed, gate_parts)
     d_rows = piece_of(own_cotangent, "tensor", 0, zplace).astype(F32)
     inv = inverse_rms(x_rows)
     scaled = d_normed * norm_gain
     inner_sum = jnp.sum(scaled * x_rows, axis=-1, keepdims=True)
     grad_rows = d_rows + inv * scaled - x_rows * (inv * inv * inv) * inner_sum / width
-    grad_rows = grad_rows.astype(BF16)
+    grad_rows = after(grad_rows.astype(BF16))
+    row_pieces = doubling_pieces(grad_rows, "tensor")
     gain = jnp.sum(d_normed * x_rows * inv, axis=0)
     devices = lax.axis_size("fsdp")
 
@@ -617,7 +621,12 @@
         pieces = row_major(jnp.concatenate(pieces, axis=1).reshape(-1, inner))
         return lax.psum_scatter(pieces, "fsdp", scatter_dimension=0, tiled=True)
 
-    sums = owned(grad_conv_part, grad_gate_part, grad_out_part, grad_x_part, grad_dt_part)
+    sums = jnp.concatenate(
+        [
+            owned(*after((grad_conv_part, grad_x_part, grad_dt_part), d_normed)),
+            owned(grad_gate_part, grad_out_part),
+        ]
+    )
     thin = jnp.concatenate(
         [
             d_rates * rates,
@@ -630,16 +639,8 @@
         axis=0,
     )
     channels = states + taps + 3
-    thin = doubling_sum(thin, ("fsdp",))
+    thin = doubling_sum(after(thin, row_pieces[1]), ("fsdp",))
     others = [thin] + [swap(thin, "context", k) for k in range(1, ctxs)]
-    gain = total([part[channels:] for part in others]).reshape(1, width)
-    grad_gain = doubling_sum(gain, ("tensor",))[0]
-    count = grad_rows.shape[0]
-    grad_input = jnp.zeros((count * lax.axis_size("tensor"), width), BF16)
-    for k, part in enumerate(doubling_pieces(grad_rows, "tensor")):
-        grad_input = lax.dynamic_update_slice_in_dim(grad_input, part, (zplace ^ k) * count, 0)
-    grad_input = grad_input.reshape(block_input.shape)
-
     def side_by_side(parts, dim):
         size = parts[0].shape[dim]
         shape = parts[0].shape[:dim] + (size * ctxs,) + parts[0].shape[dim + 1 :]
@@ -650,13 +651,27 @@
 
     thin = side_by_side([part[:channels] for part in others], 1)
     sums = [sums] + [swap(sums, "context", k) for k in range(1, ctxs)]
+    conv_at = sums[0].shape[0] - 2 * share
     grad_in = side_by_side(
-        [part[: 2 * share].reshape(2, share, inner).astype(F32) for part in sums], 2
-    )
-    grad_out = side_by_side([part[2 * share : 3 * share].T.astype(F32) for part in sums], 0)
-    thin_at = 3 * share + xcols
-    grad_x = side_by_side([part[3 * share : thin_at].T.astype(F32) for part in sums], 0)
+        [
+            jnp.stack([part[:share], part[conv_at : conv_at + share]]).astype(F32)
+            for part in sums
+        ],
+        2,
+    )
+    grad_out = side_by_side([part[conv_at + share :].T.astype(F32) for part in sums], 0)
+    thin_at = share + xcols
+    grad_x = side_by_side([part[share:thin_at].T.astype(F32) for part in sums], 0)
     grad_dt = side_by_side([part[thin_at : thin_at + dtrows].astype(F32) for part in sums], 1)
+    gain = total([part[channels:] for part in others]).reshape(1, width)
+    grad_gain = doubling_sum(gain, ("tensor",))[0]
+    count = grad_rows.shape[0]
+    grad_input = jnp.zeros((count * lax.axis_size("tensor"), width), BF16)
+    row_pieces[-1] = after(row_pieces[-1], grad_in, grad_out, grad_x, grad_dt)
+    for k, part in enumerate(row_pieces):
+        grad_input = lax.dynamic_update_slice_in_dim(grad_input, part, (zplace ^ k) * count, 0)
+    grad_input = grad_input.reshape(block_input.shape)
+
     return (
         block_output.reshape(block_input.shape),
         grad_input,

time: 541 us -> 522 us (0.965)
  waiting for transfers between devices: 192 us -> 154 us
  starting transfers between devices: 36.5 us -> 47.8 us
  matrix products: 86.4 us -> 92.8 us
    ppermute x39, waiting for transfers between devices: 179 us -> 149 us  [swap(): return lax.ppermute(array, axis, [(i, i ^ k) for i in range(size)])]
    unnamed x148 -> x132, local copies, waits for them, and re-layouts: 22.6 us -> 8.28 us
    ppermute x39, starting transfers between devices: 35.7 us -> 46.5 us  [swap(): return lax.ppermute(array, axis, [(i, i ^ k) for i in range(size)])]
    concatenate x0 -> x3, other arithmetic: none -> 8.32 us  [the longest x2 7.06 us: owned(): pieces = row_major(jnp.concatenate(pieces, axis=1).reshape(-1, inner))]
    all_gather x1, waiting for transfers between devices: 8.22 us -> 0.01 us  [shards(): lax.all_gather(after(in_half[1], first), 'fsdp', axis=0, tiled=True)]
    dot_general x18, matrix products: 86.4 us -> 92.8 us  [dot(): lax.dot_general(left, right, (((left_dim,), (right_dim,)), ((), ())), pre...]
    dynamic_update_slice x3 -> x4, local copies, waits for them, and re-layouts: 3.16 us -> 9.28 us  [shards(): lax.dynamic_update_slice_in_dim(grad_input, part, (zplace ^ k) * count, 0)]
  transfers between devices with their start and end apart: 44 -> 45, of which waited for: 21 -> 17; matrix products, arithmetic and copies ran while one was open for 29% -> 35% of each run, Pallas kernels for 18% -> 19%
where the time goes in v4:
time: 522 us; the launch traced here: 514 us
  waiting for transfers between devices  154 us (30%)
  Pallas kernels  95.2 us (18%)
  matrix products  92.8 us (18%)
  local copies, waits for them, and re-layouts  55.7 us (11%)
  other arithmetic  53 us (10%)
  starting transfers between devices  47.8 us (9%)
  between operations  15.9 us (3%)
    ppermute x39, waiting for transfers between devices, swap(): return lax.ppermute(array, axis, [(i, i ^ k) for i in range(size)])  149 us
    dot_general x18, matrix products, dot(): lax.dot_general(left, right, (((left_dim,), (right_dim,)), ((), ())), pre...  92.8 us
    pallas_call x1, Pallas kernels, adjoint(): pl.pallas_call(adjoint_kernel, grid=(count,), in_specs=[cols] + [by_row(C...  58.8 us
    ppermute x39, starting transfers between devices, swap(): return lax.ppermute(array, axis, [(i, i ^ k) for i in range(size)])  46.5 us
    pallas_call x1, Pallas kernels, scan(): pl.pallas_call(scan_kernel, grid=(tokens // CHUNK,), in_specs=[pl.BlockSp...  36.3 us
  transfers between devices with their start and end apart: 45, of which 17 were waited for; matrix products, arithmetic and copies ran while one was open for 35% of the time, Pallas kernels for 19%

profile of v4, /device:TPU:0, one launch (start us, length us, event | category | flops | bytes accessed | tf_op | source)
XLA Modules:
  0.0 513.9 jit_solution(9125538260559846422)
XLA Ops:
  7.3 3.2 fusion
  10.8 3.0 fusion.2
  15.4 2.6 collective-permute-start
  25.0 7.3 %collective-permute-done = bf16[584,512]{1,0:T(8,128)(2,1)S(1)} collective-permute-done((bf16[584,512]{1,0:T(8,128)(2,1)S(1)}, bf16[584,512]{1,0:T(8,128)(2,1)S(1)}, u32[]{:S(2)}, u32[]{:S(2)}) %collective-permute-start) | collective-permute-done | bytes 598048 | tf_op jit(solution)/shard_map/ppermute | solution.py:363
  32.3 14.2 %collective-permute-done.1 = bf16[584,512]{1,0:T(8,128)(2,1)} collective-permute-done((bf16[584,512]{1,0:T(8,128)(2,1)S(1)}, bf16[584,512]{1,0:T(8,128)(2,1)}, u32[]{:S(2)}, u32[]{:S(2)}) %collective-permute-start.1) | collective-permute-done | bytes 598048 | tf_op jit(solution)/shard_map/ppermute | solution.py:363
  51.1 5.3 %fusion.59 = bf16[1,2048,512]{2,1,0:T(8,128)(2,1)S(1)} fusion(bf16[1,2048,512]{2,1,0:T(8,128)(2,1)S(1)} %broadcast_in_dim.58, s32[]{:T(128)S(6)} %select_n.45, bf16[1024,2048]{1,0:T(8,128)(2,1)} %fusion.2, bf16[2048,512]{1,0:T(8,128)(2,1)} %slice_dynamic-update-slice_fusion), kind=kOutput, calls=%fused_computation.94 | convolution fusion | flops 2148007936 | bytes 7340036 | tf_op jit(solution)/shard_map/dot_general | solution.py:442
  56.5 5.2 %fusion.61 = bf16[1,2048,512]{2,1,0:T(8,128)(2,1)S(1)} fusion(bf16[1,2048,512]{2,1,0:T(8,128)(2,1)S(1)} %fusion.59, s32[]{:T(128)S(6)} %select_n.46, bf16[1024,2048]{1,0:T(8,128)(2,1)} %collective-permute-done.3, bf16[2048,512]{1,0:T(8,128)(2,1)} %slice_dynamic-update-slice_fusion), kind=kOutput, calls=%fused_computation.96 | convolution fusion | flops 2148007936 | bytes 7340036 | tf_op jit(solution)/shard_map/dot_general | solution.py:442
  62.4 5.0 fusion.34
  72.5 2.6 collective-permute-start.6
  76.4 5.6 %collective-permute-done.6 = bf16[160,256]{1,0:T(8,128)(2,1)S(1)} collective-permute-done((bf16[160,256]{1,0:T(8,128)(2,1)S(1)}, bf16[160,256]{1,0:T(8,128)(2,1)S(1)}, u32[]{:S(2)}, u32[]{:S(2)}) %collective-permute-start.6) | collective-permute-done | bytes 81952 | tf_op jit(solution)/shard_map/ppermute | solution.py:363
  88.0 5.3 %convolution_dynamic-update-slice_fusion.2 = f32[2048,512]{1,0:T(8,128)S(1)} fusion(f32[2048,512]{1,0:T(8,128)S(1)} %reshape.210.clone, s32[]{:T(128)S(6)} %select_n.45, bf16[1024,2048]{1,0:T(8,128)(2,1)} %fusion.2, bf16[2048,512]{1,0:T(8,128)(2,1)} %all-gather.7.cloned.1.call-done), kind=kOutput, calls=%fused_computation.89 | convolution fusion | flops 2147483648 | bytes 8388612 | tf_op jit(solution)/shard_map/dot_general | solution.py:442
  94.0 5.2 %convolution_dynamic-update-slice_fusion.1.gate_ref = f32[2048,512]{1,0:T(8,128)S(1)} fusion(f32[2048,512]{1,0:T(8,128)S(1)} %convolution_dynamic-update-slice_fusion.2, s32[]{:T(128)S(6)} %select_n.46, bf16[1024,2048]{1,0:T(8,128)(2,1)} %collective-permute-done.3, bf16[2048,512]{1,0:T(8,128)(2,1)} %all-gather.7.cloned.1.call-done), kind=kOutput, calls=%fused_computation.88 | convolution fusion | flops 2147483648 | bytes 8388612 | tf_op jit(solution)/shard_map/dot_general | solution.py:442
  101.7 36.3 %scan.1 = (bf16[2048,512]{1,0:T(8,128)(2,1)}, f32[2048,512]{1,0:T(8,128)}, f32[2048,512]{1,0:T(8,128)}, f32[2048,512]{1,0:T(8,128)}, f32[32768,512]{1,0:T(8,128)}, /*index=5*/f32[16,512]{1,0:T(8,128)}) custom-call(bf16[160,2048]{1,0:T(8,128)(2,1)} %copy-done.15, bf16[2048,512]{1,0:T(8,128)(2,1)} %copy-done.4, f32[2048,512]{1,0:T(8,128)} %copy-done.6, ...), custom_call_target="tpu_custom_call" | custom-call | flops 40265318400 | bytes 134217728 | tf_op jit(solution)/shard_map/scan/pallas_call | solution.py:286
  141.1 2.5 reshape.210
  143.6 5.9 %bitcast_dynamic-update-slice_fusion = f32[2048,512]{1,0:T(8,128)} fusion(f32[2048,512]{1,0:T(8,128)} %reshape.210, s32[]{:T(128)S(6)} %select_n.45, bf16[2048,512]{0,1:T(8,128)(2,1)S(1)} %copy-done.61, bf16[1,1024,2048]{2,1,0:T(8,128)(2,1)} %param.25), kind=kOutput, calls=%fused_computation.82 | convolution fusion | flops 2147483648 | bytes 8388612 | tf_op jit(solution)/shard_map/dot_general | solution.py:442
  149.4 6.1 %fusion.43 = bf16[1024,2048]{1,0:T(8,128)(2,1)} fusion(bf16[2048,512]{0,1:T(8,128)(2,1)S(1)} %collective-permute-done.14, bf16[2048,512]{0,1:T(8,128)(2,1)S(1)} %copy-done.61, bf16[1024,512]{1,0:T(8,128)(2,1)S(1)} %collective-permute-done.13, bf16[1024,512]{1,0:T(8,128)(2,1)S(1)} %get-tuple-element.95), kind=kOutput, calls=%fused_computation.65 | convolution fusion | flops 4309647360 | bytes 10485760 | tf_op jit(solution)/shard_map/dot_general | solution.py:442
  156.0 6.0 %convolution_dynamic-update-slice_fusion = f32[2048,512]{1,0:T(8,128)} fusion(f32[2048,512]{1,0:T(8,128)} %bitcast_dynamic-update-slice_fusion, s32[]{:T(128)S(6)} %select_n.46, bf16[1024,2048]{1,0:T(8,128)(2,1)} %collective-permute-done.12, bf16[2048,512]{0,1:T(8,128)(2,1)S(1)} %copy-done.61), kind=kOutput, calls=%fused_computation.87 | convolution fusion | flops 2147483648 | bytes 8388612 | tf_op jit(solution)/shard_map/dot_general | solution.py:442
  162.0 6.2 %multiply_convert_fusion = (bf16[2048,512]{1,0:T(8,128)(2,1)S(1)}, f32[2048,512]{1,0:T(8,128)}) fusion(f32[2048,512]{1,0:T(8,128)} %convolution_dynamic-update-slice_fusion, f32[2048,512]{1,0:T(8,128)S(1)} %copy-done.12, f32[2048,512]{1,0:T(8,128)S(1)} %copy-done.7), kind=kLoop, calls=%fused_computation.62 | loop fusion | flops 7340032 | bytes 18874368 | tf_op jit(solution)/shard_map/convert_element_type | solution.py:568
  168.3 58.8 %adjoint.1 = (bf16[2048,512]{1,0:T(8,128)(2,1)}, f32[2048,512]{1,0:T(8,128)}, f32[160,2048]{1,0:T(8,128)}, f32[16,512]{1,0:T(8,128)}, f32[1,512]{1,0:T(1,128)}, /*index=5*/f32[1,512]{1,0:T(1,128)}) custom-call(bf16[160,2048]{1,0:T(8,128)(2,1)} %copy-done.15, bf16[2048,512]{1,0:T(8,128)(2,1)} %copy-done.4, f32[2048,512]{1,0:T(8,128)} %get-tuple-element.71.steps_ref, ...), custom_call_target="tpu_custom_call" | custom-call | flops 80530636800 | bytes 134217728 | tf_op jit(solution)/shard_map/adjoint/pallas_call | solution.py:328
  227.1 4.4 reduce-scatter.4.cloned.1.call-done
  233.0 2.5 fusion.47
  243.8 4.8 fusion.77
  248.6 6.2 %add_convert_fusion = bf16[2048,512]{1,0:T(8,128)(2,1)} fusion(f32[2048,512]{1,0:T(8,128)S(1)} %fusion.77, bf16[1024,2048]{1,0:T(8,128)(2,1)} %collective-permute-done.3, bf16[1024,512]{1,0:T(8,128)(2,1)} %get-tuple-element.94), kind=kOutput, calls=%fused_computation.57 | convolution fusion | flops 2149580800 | bytes 11534336 | tf_op jit(solution)/shard_map/dot_general | solution.py:442
  254.8 4.6 fusion.69
  259.6 3.4 collective-permute-start.22
  263.0 5.9 %fusion.30 = bf16[2048,512]{0,1:T(8,128)(2,1)} fusion(f32[512,2048]{1,0:T(8,128)S(1)} %fusion.69, bf16[1024,2048]{1,0:T(8,128)(2,1)} %collective-permute-done.12, bf16[1024,512]{1,0:T(8,128)(2,1)S(1)} %copy-done.23), kind=kOutput, calls=%fused_computation.38 | convolution fusion | flops 2149580800 | bytes 11534336 | tf_op jit(solution)/shard_map/dot_general | solution.py:442
  268.9 2.9 copy.34
  275.6 11.3 %collective-permute-done.23 = bf16[160,256]{1,0:T(8,128)(2,1)S(1)} collective-permute-done((bf16[160,256]{1,0:T(8,128)(2,1)S(1)}, bf16[160,256]{1,0:T(8,128)(2,1)S(1)}, u32[]{:S(2)}, u32[]{:S(2)}) %collective-permute-start.23) | collective-permute-done | bytes 81952 | tf_op jit(solution)/shard_map/ppermute | solution.py:363
  287.1 3.9 pad_maximum_fusion
  291.9 5.4 %fusion.73 = (f32[512]{0:T(512)S(1)}, f32[2048,512]{1,0:T(8,128)S(1)}) fusion(f32[1,2048,512]{2,1,0:T(8,128)} %get-tuple-element.117, f32[2048,512]{1,0:T(8,128)} %get-tuple-element.75, bf16[160,2048]{1,0:T(8,128)(2,1)S(1)} %constant_dynamic-update-slice_fusion.2, bf16[160,512]{1,0:T(8,128)(2,1)S(1)} %copy-done.26), kind=kOutput, calls=%fused_computation.187 | convolution fusion | flops 346029568 | bytes 13404160 | tf_op jit(solution)/shard_map/dot_general | solution.py:442
  297.4 4.1 multiply_reduce_fusion
  301.5 3.7 fusion.15
  310.0 13.8 %fusion.38 = bf16[1024,2048]{1,0:T(8,128)(2,1)} fusion(bf16[2048,512]{1,0:T(8,128)(2,1)} %collective-permute-done.17, bf16[2048,512]{1,0:T(8,128)(2,1)} %slice_dynamic-update-slice_fusion, bf16[2048,512]{1,0:T(8,128)(2,1)} %collective-permute-done.16, bf16[2048,512]{1,0:T(8,128)(2,1)} %all-gather.7.cloned.1.call-done, bf16[1024,512]{1,0:T(8,128)(2,1)} %copy-done.62, ...), kind=kOutput, calls=%fused_computation.64 | convolution fusion | flops 8642363392 | bytes 16777216 | tf_op jit(solution)/shard_map/dot_general | solution.py:442
  323.8 4.1 constant_dynamic-slice_fusion.1
  327.9 6.9 %collective-permute-start.28 = (bf16[256,2048]{1,0:T(8,128)(2,1)}, bf16[256,2048]{1,0:T(8,128)(2,1)S(1)}, u32[]{:S(2)}, u32[]{:S(2)}) collective-permute-start(bf16[256,2048]{1,0:T(8,128)(2,1)} %get-tuple-element.88), channel_id=1, source_target_pairs={{0,1},{1,0},{2,3},{3,2},{4,5},{5,4},{6,7},{7,6},{8,9},{9,8},{10,11... | collective-permute-start | bytes 3145736 | tf_op jit(solution)/shard_map/ppermute | solution.py:363
  336.9 5.1 fusion.75
  342.7 16.3 %collective-permute-done.28 = bf16[256,2048]{1,0:T(8,128)(2,1)S(1)} collective-permute-done((bf16[256,2048]{1,0:T(8,128)(2,1)}, bf16[256,2048]{1,0:T(8,128)(2,1)S(1)}, u32[]{:S(2)}, u32[]{:S(2)}) %collective-permute-start.28) | collective-permute-done | bytes 1048608 | tf_op jit(solution)/shard_map/ppermute | solution.py:363
  359.3 2.4 collective-permute-start.29
  362.3 4.7 convolution_add_fusion
  367.0 34.3 %collective-permute-done.27 = bf16[256,2048]{1,0:T(8,128)(2,1)S(1)} collective-permute-done((bf16[256,2048]{1,0:T(8,128)(2,1)S(1)}, bf16[256,2048]{1,0:T(8,128)(2,1)S(1)}, u32[]{:S(2)}, u32[]{:S(2)}) %collective-permute-start.27) | collective-permute-done | bytes 1048608 | tf_op jit(solution)/shard_map/ppermute | solution.py:363
  401.3 6.2 %collective-permute-done.29 = bf16[256,2048]{1,0:T(8,128)(2,1)S(1)} collective-permute-done((bf16[256,2048]{1,0:T(8,128)(2,1)S(1)}, bf16[256,2048]{1,0:T(8,128)(2,1)S(1)}, u32[]{:S(2)}, u32[]{:S(2)}) %collective-permute-start.29) | collective-permute-done | bytes 1048608 | tf_op jit(solution)/shard_map/ppermute | solution.py:363
  407.5 2.5 fusion.54
  410.0 3.2 maximum_maximum_fusion
  413.2 3.3 fusion.51
  419.4 2.5 reshape.224
  427.7 34.6 %collective-permute-done.30 = bf16[256,2048]{1,0:T(8,128)(2,1)} collective-permute-done((bf16[256,2048]{1,0:T(8,128)(2,1)}, bf16[256,2048]{1,0:T(8,128)(2,1)}, u32[]{:S(2)}, u32[]{:S(2)}) %collective-permute-start.30) | collective-permute-done | bytes 1048608 | tf_op jit(solution)/shard_map/ppermute | solution.py:363
  474.8 13.3 %collective-permute-done.37 = f32[1,2048]{1,0:T(1,128)S(1)} collective-permute-done((f32[1,2048]{1,0:T(1,128)S(1)}, f32[1,2048]{1,0:T(1,128)S(1)}, u32[]{:S(2)}, u32[]{:S(2)}) %collective-permute-start.37) | collective-permute-done | bytes 8224 | tf_op jit(solution)/shard_map/ppermute | solution.py:363
  502.1 2.4 bitcast_dynamic-update-slice_fusion.1
  (313 shorter events, 93.0 us)
Async XLA Ops:
  7.2 80.2 %all-gather.7.cloned.1.call-start = ((), (), s32[]{:S(2)}) async-start(), calls=%async_computation.4 | async-start | bytes 2621440 | tf_op jit(solution)/shard_map/all_gather | solution.py:534
  13.8 42.6 %collective-permute-start.3 = (bf16[1024,2048]{1,0:T(8,128)(2,1)}, bf16[1024,2048]{1,0:T(8,128)(2,1)}, u32[]{:S(2)}, u32[]{:S(2)}) collective-permute-start(bf16[1024,2048]{1,0:T(8,128)(2,1)} %fusion.2), channel_id=1, source_target_pairs={{0,4},{4,0},{1,5},{5,1},{2,6},{6,2},{3,7},{7,3},{8,12},{12,8},{9,1... | collective-permute-start | bytes 12582920 | tf_op jit(solution)/shard_map/ppermute | solution.py:363
  15.4 17.0 %collective-permute-start = (bf16[584,512]{1,0:T(8,128)(2,1)S(1)}, bf16[584,512]{1,0:T(8,128)(2,1)S(1)}, u32[]{:S(2)}, u32[]{:S(2)}) collective-permute-start(bf16[584,512]{1,0:T(8,128)(2,1)S(1)} %pad_maximum_fusion.2), channel_id=1, source_target_pairs={{0,8},{8,0},{16,24},{24,16},{1,9},{9,1},{17,25},{25,17},{2,10},{10... | collective-permute-start | bytes 1794056 | tf_op jit(solution)/shard_map/ppermute | solution.py:363
  18.0 28.5 %collective-permute-start.1 = (bf16[584,512]{1,0:T(8,128)(2,1)S(1)}, bf16[584,512]{1,0:T(8,128)(2,1)}, u32[]{:S(2)}, u32[]{:S(2)}) collective-permute-start(bf16[584,512]{1,0:T(8,128)(2,1)S(1)} %pad_maximum_fusion.2), channel_id=1, source_target_pairs={{0,16},{8,24},{16,0},{24,8},{1,17},{9,25},{17,1},{25,9},{2,18},{10... | collective-permute-start | bytes 1794056 | tf_op jit(solution)/shard_map/ppermute | solution.py:363
  19.5 27.0 %collective-permute-start.2 = (bf16[584,512]{1,0:T(8,128)(2,1)S(1)}, bf16[584,512]{1,0:T(8,128)(2,1)S(1)}, u32[]{:S(2)}, u32[]{:S(2)}) collective-permute-start(bf16[584,512]{1,0:T(8,128)(2,1)S(1)} %pad_maximum_fusion.2), channel_id=1, source_target_pairs={{0,24},{8,16},{16,8},{24,0},{1,25},{9,17},{17,9},{25,1},{2,26},{10... | collective-permute-start | bytes 1794056 | tf_op jit(solution)/shard_map/ppermute | solution.py:363
  25.0 74.3 %copy-start.31 = (f32[1,2048]{1,0:T(1,128)}, f32[1,2048]{1,0:T(1,128)S(1)}, u32[]{:S(2)}) copy-start(f32[1,2048]{1,0:T(1,128)S(1)} %get-tuple-element.152) | copy-start | bytes 24580
  46.5 91.6 %all-gather.5.cloned.1.call-start = ((), (), s32[]{:S(2)}) async-start(), calls=%async_computation.3 | async-start | bytes 2621440 | tf_op jit(solution)/shard_map/all_gather | solution.py:536
  68.3 2.4 collective-permute-start.4
  70.9 5.5 %collective-permute-start.5 = (bf16[160,256]{1,0:T(8,128)(2,1)S(1)}, bf16[160,256]{1,0:T(8,128)(2,1)S(1)}, u32[]{:S(2)}, u32[]{:S(2)}) collective-permute-start(bf16[160,256]{1,0:T(8,128)(2,1)S(1)} %get-tuple-element.142), channel_id=1, source_target_pairs={{0,1},{1,0},{2,3},{3,2},{4,5},{5,4},{6,7},{7,6},{8,9},{9,8},{10,11... | collective-permute-start | bytes 245768 | tf_op jit(solution)/shard_map/ppermute | solution.py:363
  72.5 9.5 %collective-permute-start.6 = (bf16[160,256]{1,0:T(8,128)(2,1)S(1)}, bf16[160,256]{1,0:T(8,128)(2,1)S(1)}, u32[]{:S(2)}, u32[]{:S(2)}) collective-permute-start(bf16[160,256]{1,0:T(8,128)(2,1)S(1)} %get-tuple-element.144), channel_id=1, source_target_pairs={{0,2},{1,3},{2,0},{3,1},{4,6},{5,7},{6,4},{7,5},{8,10},{9,11},{10,... | collective-permute-start | bytes 245768 | tf_op jit(solution)/shard_map/ppermute | solution.py:363
  75.1 6.9 %collective-permute-start.7 = (bf16[160,256]{1,0:T(8,128)(2,1)S(1)}, bf16[160,256]{1,0:T(8,128)(2,1)}, u32[]{:S(2)}, u32[]{:S(2)}) collective-permute-start(bf16[160,256]{1,0:T(8,128)(2,1)S(1)} %get-tuple-element.143), channel_id=1, source_target_pairs={{0,3},{1,2},{2,1},{3,0},{4,7},{5,6},{6,5},{7,4},{8,11},{9,10},{10,... | collective-permute-start | bytes 245768 | tf_op jit(solution)/shard_map/ppermute | solution.py:363
  76.1 79.9 %collective-permute-start.12 = (bf16[1024,2048]{1,0:T(8,128)(2,1)}, bf16[1024,2048]{1,0:T(8,128)(2,1)}, u32[]{:S(2)}, u32[]{:S(2)}) collective-permute-start(bf16[1024,2048]{1,0:T(8,128)(2,1)} %bitcast.19), channel_id=1, source_target_pairs={{0,4},{4,0},{1,5},{5,1},{2,6},{6,2},{3,7},{7,3},{8,12},{12,8},{9,1... | collective-permute-start | bytes 12582920 | tf_op jit(solution)/shard_map/ppermute | solution.py:363
  76.1 155.4 %reduce-scatter.4.cloned.1.call-start = ((), (), s32[]{:S(2)}) async-start(), calls=%async_computation.5 | async-start | bytes 5242880 | tf_op jit(solution)/shard_map/reduce_scatter | solution.py:569
  83.0 10.3 %collective-permute-start.8 = (bf16[160,256]{1,0:T(8,128)(2,1)S(1)}, bf16[160,256]{1,0:T(8,128)(2,1)S(1)}, u32[]{:S(2)}, u32[]{:S(2)}) collective-permute-start(bf16[160,256]{1,0:T(8,128)(2,1)S(1)} %get-tuple-element.115), channel_id=1, source_target_pairs={{0,1},{1,0},{2,3},{3,2},{4,5},{5,4},{6,7},{7,6},{8,9},{9,8},{10,11... | collective-permute-start | bytes 245768 | tf_op jit(solution)/shard_map/ppermute | solution.py:363
  84.9 8.9 %collective-permute-start.9 = (bf16[160,256]{1,0:T(8,128)(2,1)S(1)}, bf16[160,256]{1,0:T(8,128)(2,1)S(1)}, u32[]{:S(2)}, u32[]{:S(2)}) collective-permute-start(bf16[160,256]{1,0:T(8,128)(2,1)S(1)} %get-tuple-element.115), channel_id=1, source_target_pairs={{0,2},{1,3},{2,0},{3,1},{4,6},{5,7},{6,4},{7,5},{8,10},{9,11},{10,... | collective-permute-start | bytes 245768 | tf_op jit(solution)/shard_map/ppermute | solution.py:363
  86.3 7.5 %collective-permute-start.10 = (bf16[160,256]{1,0:T(8,128)(2,1)S(1)}, bf16[160,256]{1,0:T(8,128)(2,1)S(1)}, u32[]{:S(2)}, u32[]{:S(2)}) collective-permute-start(bf16[160,256]{1,0:T(8,128)(2,1)S(1)} %get-tuple-element.115), channel_id=1, source_target_pairs={{0,3},{1,2},{2,1},{3,0},{4,7},{5,6},{6,5},{7,4},{8,11},{9,10},{10,... | collective-permute-start | bytes 245768 | tf_op jit(solution)/shard_map/ppermute | solution.py:363
  93.9 5.4 %collective-permute-start.11 = (bf16[160,1024]{1,0:T(8,128)(2,1)S(1)}, bf16[160,1024]{1,0:T(8,128)(2,1)S(1)}, u32[]{:S(2)}, u32[]{:S(2)}) collective-permute-start(bf16[160,1024]{1,0:T(8,128)(2,1)S(1)} %constant_dynamic-update-slice_fusion.10), channel_id=1, source_target_pairs={{0,4},{4,0},{1,5},{5,1},{2,6},{6,2},{3,7},{7,3},{8,12},{12,8},{9,1... | collective-permute-start | bytes 983048 | tf_op jit(solution)/shard_map/ppermute | solution.py:363
  138.1 11.3 %collective-permute-start.14 = (bf16[2048,512]{0,1:T(8,128)(2,1)}, bf16[2048,512]{0,1:T(8,128)(2,1)S(1)}, u32[]{:S(2)}, u32[]{:S(2)}) collective-permute-start(bf16[2048,512]{0,1:T(8,128)(2,1)} %all-gather.5.cloned.1.call-done), channel_id=1, source_target_pairs={{0,4},{4,0},{1,5},{5,1},{2,6},{6,2},{3,7},{7,3},{8,12},{12,8},{9,1... | collective-permute-start | bytes 6291464 | tf_op jit(solution)/shard_map/ppermute | solution.py:363
  140.4 9.0 %collective-permute-start.13 = (bf16[1024,512]{1,0:T(8,128)(2,1)S(1)}, bf16[1024,512]{1,0:T(8,128)(2,1)S(1)}, u32[]{:S(2)}, u32[]{:S(2)}) collective-permute-start(bf16[1024,512]{1,0:T(8,128)(2,1)S(1)} %get-tuple-element.96), channel_id=1, source_target_pairs={{0,4},{4,0},{1,5},{5,1},{2,6},{6,2},{3,7},{7,3},{8,12},{12,8},{9,1... | collective-permute-start | bytes 3145736 | tf_op jit(solution)/shard_map/ppermute | solution.py:363
  140.5 92.4 %collective-permute-start.17 = (bf16[2048,512]{1,0:T(8,128)(2,1)}, bf16[2048,512]{1,0:T(8,128)(2,1)}, u32[]{:S(2)}, u32[]{:S(2)}) collective-permute-start(bf16[2048,512]{1,0:T(8,128)(2,1)} %slice_dynamic-update-slice_fusion), channel_id=1, source_target_pairs={{0,4},{4,0},{1,5},{5,1},{2,6},{6,2},{3,7},{7,3},{8,12},{12,8},{9,1... | collective-permute-start | bytes 6291464 | tf_op jit(solution)/shard_map/ppermute | solution.py:363
  141.0 92.0 %collective-permute-start.16 = (bf16[2048,512]{1,0:T(8,128)(2,1)}, bf16[2048,512]{1,0:T(8,128)(2,1)}, u32[]{:S(2)}, u32[]{:S(2)}) collective-permute-start(bf16[2048,512]{1,0:T(8,128)(2,1)} %all-gather.7.cloned.1.call-done), channel_id=1, source_target_pairs={{0,4},{4,0},{1,5},{5,1},{2,6},{6,2},{3,7},{7,3},{8,12},{12,8},{9,1... | collective-permute-start | bytes 6291464 | tf_op jit(solution)/shard_map/ppermute | solution.py:363
  155.5 172.4 %all-gather.9.cloned.1.call-start = ((), (), s32[]{:S(2)}) async-start(), calls=%async_computation.8 | async-start | bytes 5242880 | tf_op jit(solution)/shard_map/all_gather | solution.py:580
  235.5 188.7 %reduce-scatter.8.cloned.1.call-start = ((), (), s32[]{:S(2)}) async-start(), calls=%async_computation.7 | async-start | bytes 5242880 | tf_op jit(solution)/shard_map/reduce_scatter | solution.py:622
  237.0 2.2 collective-permute-start.18
  238.2 68.6 %collective-permute-start.15 = (bf16[1024,512]{1,0:T(8,128)(2,1)}, bf16[1024,512]{1,0:T(8,128)(2,1)}, u32[]{:S(2)}, u32[]{:S(2)}) collective-permute-start(bf16[1024,512]{1,0:T(8,128)(2,1)} %get-tuple-element.94), channel_id=1, source_target_pairs={{0,4},{4,0},{1,5},{5,1},{2,6},{6,2},{3,7},{7,3},{8,12},{12,8},{9,1... | collective-permute-start | bytes 3145736 | tf_op jit(solution)/shard_map/ppermute | solution.py:363
  239.3 20.1 %collective-permute-start.19 = (bf16[160,256]{1,0:T(8,128)(2,1)S(1)}, bf16[160,256]{1,0:T(8,128)(2,1)S(1)}, u32[]{:S(2)}, u32[]{:S(2)}) collective-permute-start(bf16[160,256]{1,0:T(8,128)(2,1)S(1)} %get-tuple-element.139), channel_id=1, source_target_pairs={{0,1},{1,0},{2,3},{3,2},{4,5},{5,4},{6,7},{7,6},{8,9},{9,8},{10,11... | collective-permute-start | bytes 245768 | tf_op jit(solution)/shard_map/ppermute | solution.py:363
  240.8 18.6 %collective-permute-start.20 = (bf16[160,256]{1,0:T(8,128)(2,1)S(1)}, bf16[160,256]{1,0:T(8,128)(2,1)S(1)}, u32[]{:S(2)}, u32[]{:S(2)}) collective-permute-start(bf16[160,256]{1,0:T(8,128)(2,1)S(1)} %get-tuple-element.141), channel_id=1, source_target_pairs={{0,2},{1,3},{2,0},{3,1},{4,6},{5,7},{6,4},{7,5},{8,10},{9,11},{10,... | collective-permute-start | bytes 245768 | tf_op jit(solution)/shard_map/ppermute | solution.py:363
  242.5 17.0 %collective-permute-start.21 = (bf16[160,256]{1,0:T(8,128)(2,1)S(1)}, bf16[160,256]{1,0:T(8,128)(2,1)S(1)}, u32[]{:S(2)}, u32[]{:S(2)}) collective-permute-start(bf16[160,256]{1,0:T(8,128)(2,1)S(1)} %get-tuple-element.140), channel_id=1, source_target_pairs={{0,3},{1,2},{2,1},{3,0},{4,7},{5,6},{6,5},{7,4},{8,11},{9,10},{10,... | collective-permute-start | bytes 245768 | tf_op jit(solution)/shard_map/ppermute | solution.py:363
  259.6 16.0 %collective-permute-start.22 = (bf16[160,256]{1,0:T(8,128)(2,1)S(1)}, bf16[160,256]{1,0:T(8,128)(2,1)S(1)}, u32[]{:S(2)}, u32[]{:S(2)}) collective-permute-start(bf16[160,256]{1,0:T(8,128)(2,1)S(1)} %get-tuple-element.113), channel_id=1, source_target_pairs={{0,1},{1,0},{2,3},{3,2},{4,5},{5,4},{6,7},{7,6},{8,9},{9,8},{10,11... | collective-permute-start | bytes 245768 | tf_op jit(solution)/shard_map/ppermute | solution.py:363
  271.8 15.1 %collective-permute-start.23 = (bf16[160,256]{1,0:T(8,128)(2,1)S(1)}, bf16[160,256]{1,0:T(8,128)(2,1)S(1)}, u32[]{:S(2)}, u32[]{:S(2)}) collective-permute-start(bf16[160,256]{1,0:T(8,128)(2,1)S(1)} %get-tuple-element.113), channel_id=1, source_target_pairs={{0,2},{1,3},{2,0},{3,1},{4,6},{5,7},{6,4},{7,5},{8,10},{9,11},{10,... | collective-permute-start | bytes 245768 | tf_op jit(solution)/shard_map/ppermute | solution.py:363
  274.1 12.8 %collective-permute-start.24 = (bf16[160,256]{1,0:T(8,128)(2,1)S(1)}, bf16[160,256]{1,0:T(8,128)(2,1)S(1)}, u32[]{:S(2)}, u32[]{:S(2)}) collective-permute-start(bf16[160,256]{1,0:T(8,128)(2,1)S(1)} %get-tuple-element.113), channel_id=1, source_target_pairs={{0,3},{1,2},{2,1},{3,0},{4,7},{5,6},{6,5},{7,4},{8,11},{9,10},{10,... | collective-permute-start | bytes 245768 | tf_op jit(solution)/shard_map/ppermute | solution.py:363
  286.9 4.5 collective-permute-start.25
  291.0 180.0 %reduce-scatter.6.cloned.1.call-start = ((), (), s32[]{:S(2)}) async-start(), calls=%async_computation.6 | async-start | bytes 3276800 | tf_op jit(solution)/shard_map/reduce_scatter | solution.py:622
  306.3 2.7 collective-permute-start.26
  327.9 31.0 %collective-permute-start.28 = (bf16[256,2048]{1,0:T(8,128)(2,1)}, bf16[256,2048]{1,0:T(8,128)(2,1)S(1)}, u32[]{:S(2)}, u32[]{:S(2)}) collective-permute-start(bf16[256,2048]{1,0:T(8,128)(2,1)} %get-tuple-element.88), channel_id=1, source_target_pairs={{0,1},{1,0},{2,3},{3,2},{4,5},{5,4},{6,7},{7,6},{8,9},{9,8},{10,11... | collective-permute-start | bytes 3145736 | tf_op jit(solution)/shard_map/ppermute | solution.py:363
  342.0 59.3 %collective-permute-start.27 = (bf16[256,2048]{1,0:T(8,128)(2,1)S(1)}, bf16[256,2048]{1,0:T(8,128)(2,1)S(1)}, u32[]{:S(2)}, u32[]{:S(2)}) collective-permute-start(bf16[256,2048]{1,0:T(8,128)(2,1)S(1)} %copy-done.24), channel_id=1, source_target_pairs={{0,1},{1,0},{2,3},{3,2},{4,5},{5,4},{6,7},{7,6},{8,9},{9,8},{10,11... | collective-permute-start | bytes 3145736 | tf_op jit(solution)/shard_map/ppermute | solution.py:363
  359.3 48.1 %collective-permute-start.29 = (bf16[256,2048]{1,0:T(8,128)(2,1)S(1)}, bf16[256,2048]{1,0:T(8,128)(2,1)S(1)}, u32[]{:S(2)}, u32[]{:S(2)}) collective-permute-start(bf16[256,2048]{1,0:T(8,128)(2,1)S(1)} %add_convert_fusion.1), channel_id=1, source_target_pairs={{0,2},{1,3},{2,0},{3,1},{4,6},{5,7},{6,4},{7,5},{8,10},{9,11},{10,... | collective-permute-start | bytes 3145736 | tf_op jit(solution)/shard_map/ppermute | solution.py:363
  362.2 45.2 %copy-start.11 = (bf16[256,2048]{1,0:T(8,128)(2,1)S(1)}, bf16[256,2048]{1,0:T(8,128)(2,1)}, u32[]{:S(2)}) copy-start(bf16[256,2048]{1,0:T(8,128)(2,1)} %get-tuple-element.85) | copy-start | bytes 3145732
  362.2 45.2 %copy-start.36 = (f32[2048]{0:T(1024)S(1)}, f32[2048]{0:T(1024)}, u32[]{:S(2)}) copy-start(f32[2048]{0:T(1024)} %param.15) | copy-start | bytes 24580
  416.5 45.8 %collective-permute-start.30 = (bf16[256,2048]{1,0:T(8,128)(2,1)}, bf16[256,2048]{1,0:T(8,128)(2,1)}, u32[]{:S(2)}, u32[]{:S(2)}) collective-permute-start(bf16[256,2048]{1,0:T(8,128)(2,1)} %fusion.51), channel_id=1, source_target_pairs={{0,1},{1,0},{2,3},{3,2},{4,5},{5,4},{6,7},{7,6},{8,9},{9,8},{10,11... | collective-permute-start | bytes 3145736 | tf_op jit(solution)/shard_map/ppermute | solution.py:363
  416.5 47.5 %collective-permute-start.31 = (bf16[256,2048]{1,0:T(8,128)(2,1)}, bf16[256,2048]{1,0:T(8,128)(2,1)}, u32[]{:S(2)}, u32[]{:S(2)}) collective-permute-start(bf16[256,2048]{1,0:T(8,128)(2,1)} %fusion.51), channel_id=1, source_target_pairs={{0,2},{1,3},{2,0},{3,1},{4,6},{5,7},{6,4},{7,5},{8,10},{9,11},{10,... | collective-permute-start | bytes 3145736 | tf_op jit(solution)/shard_map/ppermute | solution.py:363
  462.3 4.3 collective-permute-start.34
  464.1 38.1 %collective-permute-start.32 = (bf16[256,2048]{1,0:T(8,128)(2,1)}, bf16[256,2048]{1,0:T(8,128)(2,1)}, u32[]{:S(2)}, u32[]{:S(2)}) collective-permute-start(bf16[256,2048]{1,0:T(8,128)(2,1)} %collective-permute-done.31), channel_id=1, source_target_pairs={{0,1},{1,0},{2,3},{3,2},{4,5},{5,4},{6,7},{7,6},{8,9},{9,8},{10,11... | collective-permute-start | bytes 3145736 | tf_op jit(solution)/shard_map/ppermute | solution.py:363
  466.6 4.3 collective-permute-start.35
  470.9 1.9 collective-permute-start.36
  472.3 22.7 %collective-permute-start.33 = (bf16[1664,512]{1,0:T(8,128)(2,1)S(1)}, bf16[1664,512]{1,0:T(8,128)(2,1)S(1)}, u32[]{:S(2)}, u32[]{:S(2)}) collective-permute-start(bf16[1664,512]{1,0:T(8,128)(2,1)S(1)} %pad_maximum_fusion.1), channel_id=1, source_target_pairs={{0,4},{4,0},{1,5},{5,1},{2,6},{6,2},{3,7},{7,3},{8,12},{12,8},{9,1... | collective-permute-start | bytes 5111816 | tf_op jit(solution)/shard_map/ppermute | solution.py:363
  472.9 15.2 %collective-permute-start.37 = (f32[1,2048]{1,0:T(1,128)S(1)}, f32[1,2048]{1,0:T(1,128)S(1)}, u32[]{:S(2)}, u32[]{:S(2)}) collective-permute-start(f32[1,2048]{1,0:T(1,128)S(1)} %bitcast.183), channel_id=1, source_target_pairs={{0,1},{1,0},{2,3},{3,2},{4,5},{5,4},{6,7},{7,6},{8,9},{9,8},{10,11... | collective-permute-start | bytes 24584 | tf_op jit(solution)/shard_map/ppermute | solution.py:363
  488.1 4.6 collective-permute-start.38
  (62 other events, 706.3 us)
Sparse Core Ops, SparseCore 0:
  46.6 35.6 all-gather.6
  84.1 35.1 all-gather.4
  155.7 75.7 reduce-scatter.3
  235.6 90.7 all-gather.8
  330.1 52.9 reduce-scatter.7
  413.3 39.0 reduce-scatter.5

commit v5 on v4

--- a/solution.py
+++ b/solution.py
@@ -11,6 +11,7 @@
 LANES = 128
 SUB = 8
 CHUNK = 128
+PARTS = 2
 VMEM_LIMIT = 56 << 20
 GONE = 1e4
 LOG2E = 1.4426950408889634
@@ -195,6 +196,7 @@
     chunk, width = act_ref.shape
     halves, groups = rate_ref.shape[0] // SUB, width // LANES
     states, rank = rate_ref.shape[0], w_dt_ref.shape[0]
+    size = chunk // PARTS
 
     @pl.when(pl.program_id(0) == 0)
     def _():
@@ -205,48 +207,61 @@
         now_ref[...] = last_ref[...]
 
     step_rows(steps_ref[...], act_ref[...].astype(jnp.float32), keep_ref, fade_ref, fed_ref)
-    coef_ref[...] = proj_ref[rank:, :].astype(jnp.float32)
-    in_ref, out_ref = coef_ref.at[:states], coef_ref.at[states:]
+    for part in range(PARTS):
+        coef = proj_ref[rank:, :].astype(jnp.float32)
+        coef_ref[part] = pltpu.roll(coef, -part * size % chunk, 1) if part else coef
     rate = blocks(rate_ref, halves, groups)
-    flow = blocks(flow_ref, halves, groups)
-    d_rate = blocks(d_rate_ref, halves, groups)
-    now = blocks(now_ref, halves, groups)
     bits = sublane_bits()
-    for base in range(chunk - SUB, -SUB, -SUB):
-        fade = [fade_ref[base : base + SUB, span(g)] for g in range(groups)]
-        fed = [fed_ref[base : base + SUB, span(g)] for g in range(groups)]
-        up = [up_ref[base : base + SUB, span(g)] for g in range(groups)]
-        weighted = [[] for _ in range(groups)]
-        slopes = [[] for _ in range(groups)]
-        for r in range(SUB - 1, -1, -1):
-            t = base + r
-            in_col, out_col = column(in_ref, halves, t), column(out_ref, halves, t)
-            in_parts = [[] for _ in range(halves)]
-            out_parts = [[] for _ in range(halves)]
+
+    def tokens(step, carry):
+        flow, d_rate, now = jax.tree.map(lambda v: v, carry)
+        part = PARTS - 1 - step
+        in_ref, out_ref = coef_ref.at[part, :states], coef_ref.at[part, states:]
+        for base in range(size - SUB, -SUB, -SUB):
+            here = pl.ds(pl.multiple_of(part * size + base, SUB), SUB)
+            fade = [fade_ref[here, span(g)] for g in range(groups)]
+            fed = [fed_ref[here, span(g)] for g in range(groups)]
+            up = [up_ref[here, span(g)] for g in range(groups)]
+            weighted = [[] for _ in range(groups)]
+            slopes = [[] for _ in range(groups)]
+            for r in range(SUB - 1, -1, -1):
+                t = base + r
+                in_col, out_col = column(in_ref, halves, t), column(out_ref, halves, t)
+                in_parts = [[] for _ in range(halves)]
+                out_parts = [[] for _ in range(halves)]
+                first = (part * size + t) * states
+                for g in range(groups):
+                    fade_row, fed_row, up_row = row(fade[g], r), row(fed[g], r), row(up[g], r)
+                    by_in, by_rate = [], []
+                    for i in range(halves):
+                        place = pl.ds(pl.multiple_of(first + i * SUB, SUB), SUB)
+                        before = h_ref[place, span(g)]
+                        factor = jnp.exp2(fade_row * rate[i][g])
+                        adjoint = out_col[i] * up_row + flow[i][g]
+                        out_parts[i].append(now[i][g] * up_row)
+                        in_parts[i].append(adjoint * fed_row)
+                        flow[i][g] = factor * adjoint
+                        pulled = flow[i][g] * before
+                        by_in.append(adjoint * in_col[i])
+                        by_rate.append(pulled * rate[i][g])
+                        d_rate[i][g] = d_rate[i][g] + pulled * fade_row
+                        now[i][g] = before
+                    fold(weighted[g], total(by_in), bits, True)
+                    fold(slopes[g], total(by_rate), bits, True)
+                place = pl.ds(pl.multiple_of(first, states), states)
+                for ref, parts in ((in_part_ref, in_parts), (out_part_ref, out_parts)):
+                    ref[place, :] = jnp.concatenate([total(p) for p in parts]).astype(jnp.bfloat16)
             for g in range(groups):
-                fade_row, fed_row, up_row = row(fade[g], r), row(fed[g], r), row(up[g], r)
-                by_in, by_rate = [], []
-                for i in range(halves):
-                    place = (t * halves + i) * SUB
-                    before = h_ref[place : place + SUB, span(g)]
-                    factor = jnp.exp2(fade_row * rate[i][g])
-                    adjoint = out_col[i] * up_row + flow[i][g]
-                    out_parts[i].append(now[i][g] * up_row)
-                    in_parts[i].append(adjoint * fed_row)
-                    flow[i][g] = factor * adjoint
-                    pulled = flow[i][g] * before
-                    by_in.append(adjoint * in_col[i])
-                    by_rate.append(pulled * rate[i][g])
-                    d_rate[i][g] = d_rate[i][g] + pulled * fade_row
-                    now[i][g] = before
-                fold(weighted[g], total(by_in), bits, True)
-                fold(slopes[g], total(by_rate), bits, True)
-            place = slice(t * states, (t + 1) * states)
-            for ref, parts in ((in_part_ref, in_parts), (out_part_ref, out_parts)):
-                ref[place, :] = jnp.concatenate([total(part) for part in parts]).astype(jnp.bfloat16)
-        for g in range(groups):
-            weighted_ref[base : base + SUB, span(g)] = weighted[g][0][1]
-            pulled_ref[base : base + SUB, span(g)] = slopes[g][0][1]
+                weighted_ref[here, span(g)] = weighted[g][0][1]
+                pulled_ref[here, span(g)] = slopes[g][0][1]
+        return flow, d_rate, now
+
+    flow, d_rate, now = lax.fori_loop(
+        0,
+        PARTS,
+        tokens,
+        tuple(blocks(ref, halves, groups) for ref in (flow_ref, d_rate_ref, now_ref)),
+    )
     put_blocks(flow_ref, flow)
     put_blocks(d_rate_ref, d_rate)
     put_blocks(now_ref, now)
@@ -344,7 +359,7 @@
         scratch_shapes=[scratch(states, width)] * 2
         + [pltpu.VMEM((CHUNK * states, LANES), jnp.bfloat16)] * 2
         + [scratch(CHUNK, width)] * 4
-        + [scratch(2 * states, CHUNK)],
+        + [scratch(PARTS, 2 * states, CHUNK)],
         compiler_params=pltpu.CompilerParams(
             dimension_semantics=("arbitrary",), vmem_limit_bytes=VMEM_LIMIT
         ),
@@ -529,7 +544,8 @@
         summed = scatter_sum(halved, "tensor", 1, BF16).astype(BF16)
         return gather(gather(summed, "tensor", 1), "context", 1), halved, summed
 
-    projections, _, summed = all_sum(dot(w_x, activated, 1, 1))
+    keep = jnp.broadcast_to(same[1].reshape(rows, 1), (rows, LANES))
+    projections, _, summed = all_sum(dot(w_x, activated, 1, 1), keep)
     w_gate = after(
         lax.all_gather(after(in_half[1], first), "fsdp", axis=0, tiled=True), summed
     )
@@ -538,8 +554,6 @@
     cotangent = [own_cotangent] + [
         swap(after(own_cotangent, conv_input), "context", k) for k in range(1, ctxs)
     ]
-    keep = jnp.broadcast_to(same[1].reshape(rows, 1), (rows, LANES))
-    projections, keep = after((projections, keep))
     dt_input = projections[:rank]
     gate = whole_tokens([dot(part, w_gate) for part in normed])
     gated, sloped, steps, slope, history, last = scan(
@@ -614,17 +628,17 @@
     gain = jnp.sum(d_normed * x_rows * inv, axis=0)
     devices = lax.axis_size("fsdp")
 
-    def owned(*parts):
+    def owned(parts, hold=()):
         pieces = [part.reshape(devices, -1, inner).astype(BF16) for part in parts]
         fill = -sum(piece.shape[1] for piece in pieces) % LANES
         pieces.append(jnp.zeros((devices, fill, inner), BF16))
         pieces = row_major(jnp.concatenate(pieces, axis=1).reshape(-1, inner))
-        return lax.psum_scatter(pieces, "fsdp", scatter_dimension=0, tiled=True)
+        return lax.psum_scatter(after(pieces, hold), "fsdp", scatter_dimension=0, tiled=True)
 
     sums = jnp.concatenate(
         [
-            owned(*after((grad_conv_part, grad_x_part, grad_dt_part), d_normed)),
-            owned(grad_gate_part, grad_out_part),
+            owned((grad_conv_part, grad_x_part, grad_dt_part), d_normed),
+            owned((grad_gate_part, grad_out_part)),
         ]
     )
     thin = jnp.concatenate(

time: 522 us -> 518 us (level)
    unnamed x132 -> x128, local copies, waits for them, and re-layouts: 8.28 us -> 10.5 us
  transfers between devices with their start and end apart: 45 -> 45, of which waited for: 17 -> 17; matrix products, arithmetic and copies ran while one was open for 35% -> 35% of each run, Pallas kernels for 19% -> 18%
where the time goes in v5:
time: 518 us; the launch traced here: 510 us
  waiting for transfers between devices  152 us (29%)
  Pallas kernels  93.6 us (18%)
  matrix products  89 us (17%)
  other arithmetic  55.5 us (11%)
  local copies, waits for them, and re-layouts  55.3 us (11%)
  starting transfers between devices  48 us (9%)
  between operations  16 us (3%)
    ppermute x39, waiting for transfers between devices, swap(): return lax.ppermute(array, axis, [(i, i ^ k) for i in range(size)])  146 us
    dot_general x18, matrix products, dot(): lax.dot_general(left, right, (((left_dim,), (right_dim,)), ((), ())), pre...  89 us
    pallas_call x1, Pallas kernels, adjoint(): pl.pallas_call(adjoint_kernel, grid=(count,), in_specs=[cols] + [by_row(C...  57.4 us
    ppermute x39, starting transfers between devices, swap(): return lax.ppermute(array, axis, [(i, i ^ k) for i in range(size)])  46.8 us
    pallas_call x1, Pallas kernels, scan(): pl.pallas_call(scan_kernel, grid=(tokens // CHUNK,), in_specs=[pl.BlockSp...  36.2 us
    unnamed x128, local copies, waits for them, and re-layouts  10.5 us
  transfers between devices with their start and end apart: 45, of which 17 were waited for; matrix products, arithmetic and copies ran while one was open for 35% of the time, Pallas kernels for 18%

profile of v5, /device:TPU:0, one launch (start us, length us, event | category | flops | bytes accessed | tf_op | source)
XLA Modules:
  0.0 509.8 jit_solution(13116262075471830492)
XLA Ops:
  7.3 3.2 fusion
  10.8 3.0 fusion.2
  15.3 2.6 collective-permute-start
  25.0 7.3 %collective-permute-done = bf16[584,512]{1,0:T(8,128)(2,1)S(1)} collective-permute-done((bf16[584,512]{1,0:T(8,128)(2,1)S(1)}, bf16[584,512]{1,0:T(8,128)(2,1)S(1)}, u32[]{:S(2)}, u32[]{:S(2)}) %collective-permute-start) | collective-permute-done | bytes 598048 | tf_op jit(solution)/shard_map/ppermute | solution.py:378
  32.3 14.2 %collective-permute-done.1 = bf16[584,512]{1,0:T(8,128)(2,1)} collective-permute-done((bf16[584,512]{1,0:T(8,128)(2,1)S(1)}, bf16[584,512]{1,0:T(8,128)(2,1)}, u32[]{:S(2)}, u32[]{:S(2)}) %collective-permute-start.1) | collective-permute-done | bytes 598048 | tf_op jit(solution)/shard_map/ppermute | solution.py:378
  51.0 5.3 %fusion.61 = bf16[1,2048,512]{2,1,0:T(8,128)(2,1)S(1)} fusion(bf16[1,2048,512]{2,1,0:T(8,128)(2,1)S(1)} %broadcast_in_dim.58, s32[]{:T(128)S(6)} %select_n.45, bf16[1024,2048]{1,0:T(8,128)(2,1)} %fusion.2, bf16[2048,512]{1,0:T(8,128)(2,1)} %slice_dynamic-update-slice_fusion), kind=kOutput, calls=%fused_computation.97 | convolution fusion | flops 2148007936 | bytes 7340036 | tf_op jit(solution)/shard_map/dot_general | solution.py:457
  56.4 5.2 %fusion.63 = bf16[1,2048,512]{2,1,0:T(8,128)(2,1)S(1)} fusion(bf16[1,2048,512]{2,1,0:T(8,128)(2,1)S(1)} %fusion.61, s32[]{:T(128)S(6)} %select_n.46, bf16[1024,2048]{1,0:T(8,128)(2,1)} %collective-permute-done.3, bf16[2048,512]{1,0:T(8,128)(2,1)} %slice_dynamic-update-slice_fusion), kind=kOutput, calls=%fused_computation.99 | convolution fusion | flops 2148007936 | bytes 7340036 | tf_op jit(solution)/shard_map/dot_general | solution.py:457
  62.3 5.0 fusion.34
  73.5 2.6 collective-permute-start.6
  76.7 6.3 %collective-permute-done.6 = bf16[160,256]{1,0:T(8,128)(2,1)S(1)} collective-permute-done((bf16[160,256]{1,0:T(8,128)(2,1)S(1)}, bf16[160,256]{1,0:T(8,128)(2,1)S(1)}, u32[]{:S(2)}, u32[]{:S(2)}) %collective-permute-start.6) | collective-permute-done | bytes 81952 | tf_op jit(solution)/shard_map/ppermute | solution.py:378
  88.0 5.3 %convolution_dynamic-update-slice_fusion.2 = f32[2048,512]{1,0:T(8,128)S(1)} fusion(f32[2048,512]{1,0:T(8,128)S(1)} %reshape.211.clone, s32[]{:T(128)S(6)} %select_n.45, bf16[1024,2048]{1,0:T(8,128)(2,1)} %fusion.2, bf16[2048,512]{1,0:T(8,128)(2,1)} %all-gather.7.cloned.1.call-done), kind=kOutput, calls=%fused_computation.92 | convolution fusion | flops 2147483648 | bytes 8388612 | tf_op jit(solution)/shard_map/dot_general | solution.py:457
  93.5 5.2 %convolution_dynamic-update-slice_fusion.1.gate_ref = f32[2048,512]{1,0:T(8,128)S(1)} fusion(f32[2048,512]{1,0:T(8,128)S(1)} %convolution_dynamic-update-slice_fusion.2, s32[]{:T(128)S(6)} %select_n.46, bf16[1024,2048]{1,0:T(8,128)(2,1)} %collective-permute-done.3, bf16[2048,512]{1,0:T(8,128)(2,1)} %all-gather.7.cloned.1.call-done), kind=kOutput, calls=%fused_computation.91 | convolution fusion | flops 2147483648 | bytes 8388612 | tf_op jit(solution)/shard_map/dot_general | solution.py:457
  100.9 36.2 %scan.1 = (bf16[2048,512]{1,0:T(8,128)(2,1)}, f32[2048,512]{1,0:T(8,128)}, f32[2048,512]{1,0:T(8,128)}, f32[2048,512]{1,0:T(8,128)}, f32[32768,512]{1,0:T(8,128)}, /*index=5*/f32[16,512]{1,0:T(8,128)}) custom-call(bf16[160,2048]{1,0:T(8,128)(2,1)} %copy-done.15, bf16[2048,512]{1,0:T(8,128)(2,1)} %copy-done.8, f32[2048,512]{1,0:T(8,128)} %copy-done.6, ...), custom_call_target="tpu_custom_call" | custom-call | flops 40265318400 | bytes 134217728 | tf_op jit(solution)/shard_map/scan/pallas_call | solution.py:301
  140.1 2.5 reshape.211
  142.7 5.9 %bitcast_dynamic-update-slice_fusion = f32[2048,512]{1,0:T(8,128)} fusion(f32[2048,512]{1,0:T(8,128)} %reshape.211, s32[]{:T(128)S(6)} %select_n.45, bf16[2048,512]{0,1:T(8,128)(2,1)S(1)} %copy-done.59, bf16[1,1024,2048]{2,1,0:T(8,128)(2,1)} %param.25), kind=kOutput, calls=%fused_computation.85 | convolution fusion | flops 2147483648 | bytes 8388612 | tf_op jit(solution)/shard_map/dot_general | solution.py:457
  148.5 6.1 %fusion.43 = bf16[1024,2048]{1,0:T(8,128)(2,1)} fusion(bf16[2048,512]{0,1:T(8,128)(2,1)S(1)} %collective-permute-done.14, bf16[2048,512]{0,1:T(8,128)(2,1)S(1)} %copy-done.59, bf16[1024,512]{1,0:T(8,128)(2,1)S(1)} %collective-permute-done.13, bf16[1024,512]{1,0:T(8,128)(2,1)S(1)} %get-tuple-element.89), kind=kOutput, calls=%fused_computation.67 | convolution fusion | flops 4309647360 | bytes 10485760 | tf_op jit(solution)/shard_map/dot_general | solution.py:457
  155.1 6.0 %convolution_dynamic-update-slice_fusion = f32[2048,512]{1,0:T(8,128)} fusion(f32[2048,512]{1,0:T(8,128)} %bitcast_dynamic-update-slice_fusion, s32[]{:T(128)S(6)} %select_n.46, bf16[1024,2048]{1,0:T(8,128)(2,1)} %collective-permute-done.12, bf16[2048,512]{0,1:T(8,128)(2,1)S(1)} %copy-done.59), kind=kOutput, calls=%fused_computation.90 | convolution fusion | flops 2147483648 | bytes 8388612 | tf_op jit(solution)/shard_map/dot_general | solution.py:457
  161.1 6.2 %multiply_convert_fusion.1 = (bf16[2048,512]{1,0:T(8,128)(2,1)S(1)}, f32[2048,512]{1,0:T(8,128)}) fusion(f32[2048,512]{1,0:T(8,128)} %convolution_dynamic-update-slice_fusion, f32[2048,512]{1,0:T(8,128)S(1)} %copy-done.13, f32[2048,512]{1,0:T(8,128)S(1)} %copy-done.7), kind=kLoop, calls=%fused_computation.64 | loop fusion | flops 7340032 | bytes 18874368 | tf_op jit(solution)/shard_map/convert_element_type | solution.py:582
  167.4 57.4 %adjoint.1 = (bf16[2048,512]{1,0:T(8,128)(2,1)}, f32[2048,512]{1,0:T(8,128)}, f32[160,2048]{1,0:T(8,128)}, f32[16,512]{1,0:T(8,128)}, f32[1,512]{1,0:T(1,128)}, /*index=5*/f32[1,512]{1,0:T(1,128)}) custom-call(bf16[160,2048]{1,0:T(8,128)(2,1)} %copy-done.15, bf16[2048,512]{1,0:T(8,128)(2,1)} %copy-done.8, f32[2048,512]{1,0:T(8,128)} %get-tuple-element.67.steps_ref, ...), custom_call_target="tpu_custom_call" | custom-call | flops 80530636800 | bytes 134217728 | tf_op jit(solution)/shard_map/adjoint/pallas_call | solution.py:343
  224.8 6.1 %reduce-scatter.4.cloned.1.call-done = bf16[256,2048]{1,0:T(8,128)(2,1)} async-done(((bf16[1024,2048]{1,0:T(8,128)(2,1)}), bf16[256,2048]{1,0:T(8,128)(2,1)}) %reduce-scatter.4.cloned.1.call-update) | async-done | bytes 1048592 | tf_op jit(solution)/shard_map/reduce_scatter | solution.py:583
  232.4 2.6 fusion.47
  243.2 4.8 fusion.83
  248.1 6.2 %add_convert_fusion = bf16[2048,512]{1,0:T(8,128)(2,1)} fusion(f32[2048,512]{1,0:T(8,128)S(1)} %fusion.83, bf16[1024,2048]{1,0:T(8,128)(2,1)} %collective-permute-done.3, bf16[1024,512]{1,0:T(8,128)(2,1)} %get-tuple-element.88), kind=kOutput, calls=%fused_computation.57 | convolution fusion | flops 2149580800 | bytes 11534336 | tf_op jit(solution)/shard_map/dot_general | solution.py:457
  254.2 4.6 fusion.73
  259.0 3.4 collective-permute-start.22
  262.4 5.9 %fusion.30 = bf16[2048,512]{0,1:T(8,128)(2,1)} fusion(f32[512,2048]{1,0:T(8,128)S(1)} %fusion.73, bf16[1024,2048]{1,0:T(8,128)(2,1)} %collective-permute-done.12, bf16[1024,512]{1,0:T(8,128)(2,1)S(1)} %copy-done.25), kind=kOutput, calls=%fused_computation.38 | convolution fusion | flops 2149580800 | bytes 11534336 | tf_op jit(solution)/shard_map/dot_general | solution.py:457
  268.3 2.9 copy.34
  271.2 2.3 collective-permute-start.23
  275.1 11.3 %collective-permute-done.23 = bf16[160,256]{1,0:T(8,128)(2,1)S(1)} collective-permute-done((bf16[160,256]{1,0:T(8,128)(2,1)S(1)}, bf16[160,256]{1,0:T(8,128)(2,1)S(1)}, u32[]{:S(2)}, u32[]{:S(2)}) %collective-permute-start.23) | collective-permute-done | bytes 81952 | tf_op jit(solution)/shard_map/ppermute | solution.py:378
  286.6 3.9 pad_maximum_fusion
  292.9 3.5 fusion.77
  296.5 4.0 multiply_reduce_fusion
  300.6 3.7 fusion.15
  309.1 13.8 %fusion.38 = bf16[1024,2048]{1,0:T(8,128)(2,1)} fusion(bf16[2048,512]{1,0:T(8,128)(2,1)} %collective-permute-done.17, bf16[2048,512]{1,0:T(8,128)(2,1)} %slice_dynamic-update-slice_fusion, bf16[2048,512]{1,0:T(8,128)(2,1)} %collective-permute-done.16, bf16[2048,512]{1,0:T(8,128)(2,1)} %all-gather.7.cloned.1.call-done, bf16[1024,512]{1,0:T(8,128)(2,1)} %copy-done.60, ...), kind=kOutput, calls=%fused_computation.66 | convolution fusion | flops 8642363392 | bytes 16777216 | tf_op jit(solution)/shard_map/dot_general | solution.py:457
  323.0 4.1 constant_dynamic-slice_fusion.1
  327.1 6.9 %collective-permute-start.28 = (bf16[256,2048]{1,0:T(8,128)(2,1)}, bf16[256,2048]{1,0:T(8,128)(2,1)S(1)}, u32[]{:S(2)}, u32[]{:S(2)}) collective-permute-start(bf16[256,2048]{1,0:T(8,128)(2,1)} %get-tuple-element.84), channel_id=1, source_target_pairs={{0,1},{1,0},{2,3},{3,2},{4,5},{5,4},{6,7},{7,6},{8,9},{9,8},{10,11... | collective-permute-start | bytes 3145736 | tf_op jit(solution)/shard_map/ppermute | solution.py:378
  336.1 5.0 fusion.82
  341.8 16.3 %collective-permute-done.28 = bf16[256,2048]{1,0:T(8,128)(2,1)S(1)} collective-permute-done((bf16[256,2048]{1,0:T(8,128)(2,1)}, bf16[256,2048]{1,0:T(8,128)(2,1)S(1)}, u32[]{:S(2)}, u32[]{:S(2)}) %collective-permute-start.28) | collective-permute-done | bytes 1048608 | tf_op jit(solution)/shard_map/ppermute | solution.py:378
  360.9 4.7 add_convert_fusion.1
  367.0 3.2 maximum_maximum_fusion
  370.2 30.2 %collective-permute-done.27 = bf16[256,2048]{1,0:T(8,128)(2,1)S(1)} collective-permute-done((bf16[256,2048]{1,0:T(8,128)(2,1)S(1)}, bf16[256,2048]{1,0:T(8,128)(2,1)S(1)}, u32[]{:S(2)}, u32[]{:S(2)}) %collective-permute-start.27) | collective-permute-done | bytes 1048608 | tf_op jit(solution)/shard_map/ppermute | solution.py:378
  400.4 6.3 %collective-permute-done.29 = bf16[256,2048]{1,0:T(8,128)(2,1)S(1)} collective-permute-done((bf16[256,2048]{1,0:T(8,128)(2,1)S(1)}, bf16[256,2048]{1,0:T(8,128)(2,1)S(1)}, u32[]{:S(2)}, u32[]{:S(2)}) %collective-permute-start.29) | collective-permute-done | bytes 1048608 | tf_op jit(solution)/shard_map/ppermute | solution.py:378
  406.7 2.5 fusion.54
  409.3 3.2 fusion.51
  415.3 2.5 reshape.225
  423.7 34.6 %collective-permute-done.30 = bf16[256,2048]{1,0:T(8,128)(2,1)} collective-permute-done((bf16[256,2048]{1,0:T(8,128)(2,1)}, bf16[256,2048]{1,0:T(8,128)(2,1)}, u32[]{:S(2)}, u32[]{:S(2)}) %collective-permute-start.30) | collective-permute-done | bytes 1048608 | tf_op jit(solution)/shard_map/ppermute | solution.py:378
  470.8 13.3 %collective-permute-done.37 = f32[1,2048]{1,0:T(1,128)S(1)} collective-permute-done((f32[1,2048]{1,0:T(1,128)S(1)}, f32[1,2048]{1,0:T(1,128)S(1)}, u32[]{:S(2)}, u32[]{:S(2)}) %collective-permute-start.37) | collective-permute-done | bytes 8224 | tf_op jit(solution)/shard_map/ppermute | solution.py:378
  498.1 2.4 bitcast_dynamic-update-slice_fusion.1
  (310 shorter events, 94.1 us)
Async XLA Ops:
  7.2 80.3 %all-gather.7.cloned.1.call-start = ((), (), s32[]{:S(2)}) async-start(), calls=%async_computation.4 | async-start | bytes 2621440 | tf_op jit(solution)/shard_map/all_gather | solution.py:550
  13.8 42.5 %collective-permute-start.3 = (bf16[1024,2048]{1,0:T(8,128)(2,1)}, bf16[1024,2048]{1,0:T(8,128)(2,1)}, u32[]{:S(2)}, u32[]{:S(2)}) collective-permute-start(bf16[1024,2048]{1,0:T(8,128)(2,1)} %fusion.2), channel_id=1, source_target_pairs={{0,4},{4,0},{1,5},{5,1},{2,6},{6,2},{3,7},{7,3},{8,12},{12,8},{9,1... | collective-permute-start | bytes 12582920 | tf_op jit(solution)/shard_map/ppermute | solution.py:378
  15.3 17.0 %collective-permute-start = (bf16[584,512]{1,0:T(8,128)(2,1)S(1)}, bf16[584,512]{1,0:T(8,128)(2,1)S(1)}, u32[]{:S(2)}, u32[]{:S(2)}) collective-permute-start(bf16[584,512]{1,0:T(8,128)(2,1)S(1)} %pad_maximum_fusion.2), channel_id=1, source_target_pairs={{0,8},{8,0},{16,24},{24,16},{1,9},{9,1},{17,25},{25,17},{2,10},{10... | collective-permute-start | bytes 1794056 | tf_op jit(solution)/shard_map/ppermute | solution.py:378
  17.9 28.5 %collective-permute-start.1 = (bf16[584,512]{1,0:T(8,128)(2,1)S(1)}, bf16[584,512]{1,0:T(8,128)(2,1)}, u32[]{:S(2)}, u32[]{:S(2)}) collective-permute-start(bf16[584,512]{1,0:T(8,128)(2,1)S(1)} %pad_maximum_fusion.2), channel_id=1, source_target_pairs={{0,16},{8,24},{16,0},{24,8},{1,17},{9,25},{17,1},{25,9},{2,18},{10... | collective-permute-start | bytes 1794056 | tf_op jit(solution)/shard_map/ppermute | solution.py:378
  19.5 27.0 %collective-permute-start.2 = (bf16[584,512]{1,0:T(8,128)(2,1)S(1)}, bf16[584,512]{1,0:T(8,128)(2,1)S(1)}, u32[]{:S(2)}, u32[]{:S(2)}) collective-permute-start(bf16[584,512]{1,0:T(8,128)(2,1)S(1)} %pad_maximum_fusion.2), channel_id=1, source_target_pairs={{0,24},{8,16},{16,8},{24,0},{1,25},{9,17},{17,9},{25,1},{2,26},{10... | collective-permute-start | bytes 1794056 | tf_op jit(solution)/shard_map/ppermute | solution.py:378
  22.5 39.7 %copy-start.47 = (f32[1,512]{1,0:T(1,128)}, f32[1,512]{1,0:T(1,128)S(1)}, u32[]{:S(2)}) copy-start(f32[1,512]{1,0:T(1,128)S(1)} %get-tuple-element.146) | copy-start | bytes 6148
  25.0 45.5 %copy-start.29 = (f32[1,2048]{1,0:T(1,128)}, f32[1,2048]{1,0:T(1,128)S(1)}, u32[]{:S(2)}) copy-start(f32[1,2048]{1,0:T(1,128)S(1)} %get-tuple-element.148) | copy-start | bytes 24580
  46.5 90.7 %all-gather.5.cloned.1.call-start = ((), (), s32[]{:S(2)}) async-start(), calls=%async_computation.3 | async-start | bytes 2621440 | tf_op jit(solution)/shard_map/all_gather | solution.py:552
  68.2 2.2 collective-permute-start.4
  71.9 4.8 collective-permute-start.5
  73.5 9.5 %collective-permute-start.6 = (bf16[160,256]{1,0:T(8,128)(2,1)S(1)}, bf16[160,256]{1,0:T(8,128)(2,1)S(1)}, u32[]{:S(2)}, u32[]{:S(2)}) collective-permute-start(bf16[160,256]{1,0:T(8,128)(2,1)S(1)} %get-tuple-element.140), channel_id=1, source_target_pairs={{0,2},{1,3},{2,0},{3,1},{4,6},{5,7},{6,4},{7,5},{8,10},{9,11},{10,... | collective-permute-start | bytes 245768 | tf_op jit(solution)/shard_map/ppermute | solution.py:378
  76.1 6.9 %collective-permute-start.7 = (bf16[160,256]{1,0:T(8,128)(2,1)S(1)}, bf16[160,256]{1,0:T(8,128)(2,1)S(1)}, u32[]{:S(2)}, u32[]{:S(2)}) collective-permute-start(bf16[160,256]{1,0:T(8,128)(2,1)S(1)} %get-tuple-element.139), channel_id=1, source_target_pairs={{0,3},{1,2},{2,1},{3,0},{4,7},{5,6},{6,5},{7,4},{8,11},{9,10},{10,... | collective-permute-start | bytes 245768 | tf_op jit(solution)/shard_map/ppermute | solution.py:378
  76.3 78.8 %collective-permute-start.12 = (bf16[1024,2048]{1,0:T(8,128)(2,1)}, bf16[1024,2048]{1,0:T(8,128)(2,1)}, u32[]{:S(2)}, u32[]{:S(2)}) collective-permute-start(bf16[1024,2048]{1,0:T(8,128)(2,1)} %bitcast.19), channel_id=1, source_target_pairs={{0,4},{4,0},{1,5},{5,1},{2,6},{6,2},{3,7},{7,3},{8,12},{12,8},{9,1... | collective-permute-start | bytes 12582920 | tf_op jit(solution)/shard_map/ppermute | solution.py:378
  76.4 154.5 %reduce-scatter.4.cloned.1.call-start = ((), (), s32[]{:S(2)}) async-start(), calls=%async_computation.5 | async-start | bytes 5242880 | tf_op jit(solution)/shard_map/reduce_scatter | solution.py:583
  83.0 10.3 %collective-permute-start.8 = (bf16[160,256]{1,0:T(8,128)(2,1)S(1)}, bf16[160,256]{1,0:T(8,128)(2,1)S(1)}, u32[]{:S(2)}, u32[]{:S(2)}) collective-permute-start(bf16[160,256]{1,0:T(8,128)(2,1)S(1)} %get-tuple-element.111), channel_id=1, source_target_pairs={{0,1},{1,0},{2,3},{3,2},{4,5},{5,4},{6,7},{7,6},{8,9},{9,8},{10,11... | collective-permute-start | bytes 245768 | tf_op jit(solution)/shard_map/ppermute | solution.py:378
  84.6 8.7 %collective-permute-start.9 = (bf16[160,256]{1,0:T(8,128)(2,1)S(1)}, bf16[160,256]{1,0:T(8,128)(2,1)S(1)}, u32[]{:S(2)}, u32[]{:S(2)}) collective-permute-start(bf16[160,256]{1,0:T(8,128)(2,1)S(1)} %get-tuple-element.111), channel_id=1, source_target_pairs={{0,2},{1,3},{2,0},{3,1},{4,6},{5,7},{6,4},{7,5},{8,10},{9,11},{10,... | collective-permute-start | bytes 245768 | tf_op jit(solution)/shard_map/ppermute | solution.py:378
  86.2 7.2 %collective-permute-start.10 = (bf16[160,256]{1,0:T(8,128)(2,1)S(1)}, bf16[160,256]{1,0:T(8,128)(2,1)S(1)}, u32[]{:S(2)}, u32[]{:S(2)}) collective-permute-start(bf16[160,256]{1,0:T(8,128)(2,1)S(1)} %get-tuple-element.111), channel_id=1, source_target_pairs={{0,3},{1,2},{2,1},{3,0},{4,7},{5,6},{6,5},{7,4},{8,11},{9,10},{10,... | collective-permute-start | bytes 245768 | tf_op jit(solution)/shard_map/ppermute | solution.py:378
  93.4 5.4 %collective-permute-start.11 = (bf16[160,1024]{1,0:T(8,128)(2,1)S(1)}, bf16[160,1024]{1,0:T(8,128)(2,1)S(1)}, u32[]{:S(2)}, u32[]{:S(2)}) collective-permute-start(bf16[160,1024]{1,0:T(8,128)(2,1)S(1)} %constant_dynamic-update-slice_fusion.10), channel_id=1, source_target_pairs={{0,4},{4,0},{1,5},{5,1},{2,6},{6,2},{3,7},{7,3},{8,12},{12,8},{9,1... | collective-permute-start | bytes 983048 | tf_op jit(solution)/shard_map/ppermute | solution.py:378
  137.2 11.4 %collective-permute-start.14 = (bf16[2048,512]{0,1:T(8,128)(2,1)}, bf16[2048,512]{0,1:T(8,128)(2,1)S(1)}, u32[]{:S(2)}, u32[]{:S(2)}) collective-permute-start(bf16[2048,512]{0,1:T(8,128)(2,1)} %all-gather.5.cloned.1.call-done), channel_id=1, source_target_pairs={{0,4},{4,0},{1,5},{5,1},{2,6},{6,2},{3,7},{7,3},{8,12},{12,8},{9,1... | collective-permute-start | bytes 6291464 | tf_op jit(solution)/shard_map/ppermute | solution.py:378
  139.5 9.0 %collective-permute-start.13 = (bf16[1024,512]{1,0:T(8,128)(2,1)S(1)}, bf16[1024,512]{1,0:T(8,128)(2,1)S(1)}, u32[]{:S(2)}, u32[]{:S(2)}) collective-permute-start(bf16[1024,512]{1,0:T(8,128)(2,1)S(1)} %get-tuple-element.90), channel_id=1, source_target_pairs={{0,4},{4,0},{1,5},{5,1},{2,6},{6,2},{3,7},{7,3},{8,12},{12,8},{9,1... | collective-permute-start | bytes 3145736 | tf_op jit(solution)/shard_map/ppermute | solution.py:378
  139.6 92.7 %collective-permute-start.17 = (bf16[2048,512]{1,0:T(8,128)(2,1)}, bf16[2048,512]{1,0:T(8,128)(2,1)}, u32[]{:S(2)}, u32[]{:S(2)}) collective-permute-start(bf16[2048,512]{1,0:T(8,128)(2,1)} %slice_dynamic-update-slice_fusion), channel_id=1, source_target_pairs={{0,4},{4,0},{1,5},{5,1},{2,6},{6,2},{3,7},{7,3},{8,12},{12,8},{9,1... | collective-permute-start | bytes 6291464 | tf_op jit(solution)/shard_map/ppermute | solution.py:378
  140.1 92.3 %collective-permute-start.16 = (bf16[2048,512]{1,0:T(8,128)(2,1)}, bf16[2048,512]{1,0:T(8,128)(2,1)}, u32[]{:S(2)}, u32[]{:S(2)}) collective-permute-start(bf16[2048,512]{1,0:T(8,128)(2,1)} %all-gather.7.cloned.1.call-done), channel_id=1, source_target_pairs={{0,4},{4,0},{1,5},{5,1},{2,6},{6,2},{3,7},{7,3},{8,12},{12,8},{9,1... | collective-permute-start | bytes 6291464 | tf_op jit(solution)/shard_map/ppermute | solution.py:378
  154.6 172.4 %all-gather.9.cloned.1.call-start = ((), (), s32[]{:S(2)}) async-start(), calls=%async_computation.8 | async-start | bytes 5242880 | tf_op jit(solution)/shard_map/all_gather | solution.py:594
  235.0 185.2 %reduce-scatter.8.cloned.1.call-start = ((), (), s32[]{:S(2)}) async-start(), calls=%async_computation.7 | async-start | bytes 5242880 | tf_op jit(solution)/shard_map/reduce_scatter | solution.py:636
  236.4 2.2 collective-permute-start.18
  237.7 68.3 %collective-permute-start.15 = (bf16[1024,512]{1,0:T(8,128)(2,1)}, bf16[1024,512]{1,0:T(8,128)(2,1)}, u32[]{:S(2)}, u32[]{:S(2)}) collective-permute-start(bf16[1024,512]{1,0:T(8,128)(2,1)} %get-tuple-element.88), channel_id=1, source_target_pairs={{0,4},{4,0},{1,5},{5,1},{2,6},{6,2},{3,7},{7,3},{8,12},{12,8},{9,1... | collective-permute-start | bytes 3145736 | tf_op jit(solution)/shard_map/ppermute | solution.py:378
  238.7 20.2 %collective-permute-start.19 = (bf16[160,256]{1,0:T(8,128)(2,1)S(1)}, bf16[160,256]{1,0:T(8,128)(2,1)S(1)}, u32[]{:S(2)}, u32[]{:S(2)}) collective-permute-start(bf16[160,256]{1,0:T(8,128)(2,1)S(1)} %get-tuple-element.135), channel_id=1, source_target_pairs={{0,1},{1,0},{2,3},{3,2},{4,5},{5,4},{6,7},{7,6},{8,9},{9,8},{10,11... | collective-permute-start | bytes 245768 | tf_op jit(solution)/shard_map/ppermute | solution.py:378
  240.3 18.6 %collective-permute-start.20 = (bf16[160,256]{1,0:T(8,128)(2,1)S(1)}, bf16[160,256]{1,0:T(8,128)(2,1)S(1)}, u32[]{:S(2)}, u32[]{:S(2)}) collective-permute-start(bf16[160,256]{1,0:T(8,128)(2,1)S(1)} %get-tuple-element.137), channel_id=1, source_target_pairs={{0,2},{1,3},{2,0},{3,1},{4,6},{5,7},{6,4},{7,5},{8,10},{9,11},{10,... | collective-permute-start | bytes 245768 | tf_op jit(solution)/shard_map/ppermute | solution.py:378
  241.9 17.0 %collective-permute-start.21 = (bf16[160,256]{1,0:T(8,128)(2,1)S(1)}, bf16[160,256]{1,0:T(8,128)(2,1)S(1)}, u32[]{:S(2)}, u32[]{:S(2)}) collective-permute-start(bf16[160,256]{1,0:T(8,128)(2,1)S(1)} %get-tuple-element.136), channel_id=1, source_target_pairs={{0,3},{1,2},{2,1},{3,0},{4,7},{5,6},{6,5},{7,4},{8,11},{9,10},{10,... | collective-permute-start | bytes 245768 | tf_op jit(solution)/shard_map/ppermute | solution.py:378
  259.0 16.0 %collective-permute-start.22 = (bf16[160,256]{1,0:T(8,128)(2,1)S(1)}, bf16[160,256]{1,0:T(8,128)(2,1)S(1)}, u32[]{:S(2)}, u32[]{:S(2)}) collective-permute-start(bf16[160,256]{1,0:T(8,128)(2,1)S(1)} %get-tuple-element.109), channel_id=1, source_target_pairs={{0,1},{1,0},{2,3},{3,2},{4,5},{5,4},{6,7},{7,6},{8,9},{9,8},{10,11... | collective-permute-start | bytes 245768 | tf_op jit(solution)/shard_map/ppermute | solution.py:378
  271.2 15.1 %collective-permute-start.23 = (bf16[160,256]{1,0:T(8,128)(2,1)S(1)}, bf16[160,256]{1,0:T(8,128)(2,1)S(1)}, u32[]{:S(2)}, u32[]{:S(2)}) collective-permute-start(bf16[160,256]{1,0:T(8,128)(2,1)S(1)} %get-tuple-element.109), channel_id=1, source_target_pairs={{0,2},{1,3},{2,0},{3,1},{4,6},{5,7},{6,4},{7,5},{8,10},{9,11},{10,... | collective-permute-start | bytes 245768 | tf_op jit(solution)/shard_map/ppermute | solution.py:378
  273.6 12.8 %collective-permute-start.24 = (bf16[160,256]{1,0:T(8,128)(2,1)S(1)}, bf16[160,256]{1,0:T(8,128)(2,1)S(1)}, u32[]{:S(2)}, u32[]{:S(2)}) collective-permute-start(bf16[160,256]{1,0:T(8,128)(2,1)S(1)} %get-tuple-element.109), channel_id=1, source_target_pairs={{0,3},{1,2},{2,1},{3,0},{4,7},{5,6},{6,5},{7,4},{8,11},{9,10},{10,... | collective-permute-start | bytes 245768 | tf_op jit(solution)/shard_map/ppermute | solution.py:378
  286.4 4.5 collective-permute-start.25
  290.5 176.5 %reduce-scatter.6.cloned.1.call-start = ((), (), s32[]{:S(2)}) async-start(), calls=%async_computation.6 | async-start | bytes 3276800 | tf_op jit(solution)/shard_map/reduce_scatter | solution.py:636
  305.5 2.7 collective-permute-start.26
  327.1 31.0 %collective-permute-start.28 = (bf16[256,2048]{1,0:T(8,128)(2,1)}, bf16[256,2048]{1,0:T(8,128)(2,1)S(1)}, u32[]{:S(2)}, u32[]{:S(2)}) collective-permute-start(bf16[256,2048]{1,0:T(8,128)(2,1)} %get-tuple-element.84), channel_id=1, source_target_pairs={{0,1},{1,0},{2,3},{3,2},{4,5},{5,4},{6,7},{7,6},{8,9},{9,8},{10,11... | collective-permute-start | bytes 3145736 | tf_op jit(solution)/shard_map/ppermute | solution.py:378
  341.1 59.3 %collective-permute-start.27 = (bf16[256,2048]{1,0:T(8,128)(2,1)S(1)}, bf16[256,2048]{1,0:T(8,128)(2,1)S(1)}, u32[]{:S(2)}, u32[]{:S(2)}) collective-permute-start(bf16[256,2048]{1,0:T(8,128)(2,1)S(1)} %copy-done.26), channel_id=1, source_target_pairs={{0,1},{1,0},{2,3},{3,2},{4,5},{5,4},{6,7},{7,6},{8,9},{9,8},{10,11... | collective-permute-start | bytes 3145736 | tf_op jit(solution)/shard_map/ppermute | solution.py:378
  358.5 48.1 %collective-permute-start.29 = (bf16[256,2048]{1,0:T(8,128)(2,1)S(1)}, bf16[256,2048]{1,0:T(8,128)(2,1)S(1)}, u32[]{:S(2)}, u32[]{:S(2)}) collective-permute-start(bf16[256,2048]{1,0:T(8,128)(2,1)S(1)} %add_convert_fusion.2), channel_id=1, source_target_pairs={{0,2},{1,3},{2,0},{3,1},{4,6},{5,7},{6,4},{7,5},{8,10},{9,11},{10,... | collective-permute-start | bytes 3145736 | tf_op jit(solution)/shard_map/ppermute | solution.py:378
  412.5 45.7 %collective-permute-start.30 = (bf16[256,2048]{1,0:T(8,128)(2,1)}, bf16[256,2048]{1,0:T(8,128)(2,1)}, u32[]{:S(2)}, u32[]{:S(2)}) collective-permute-start(bf16[256,2048]{1,0:T(8,128)(2,1)} %fusion.51), channel_id=1, source_target_pairs={{0,1},{1,0},{2,3},{3,2},{4,5},{5,4},{6,7},{7,6},{8,9},{9,8},{10,11... | collective-permute-start | bytes 3145736 | tf_op jit(solution)/shard_map/ppermute | solution.py:378
  412.5 47.5 %collective-permute-start.31 = (bf16[256,2048]{1,0:T(8,128)(2,1)}, bf16[256,2048]{1,0:T(8,128)(2,1)}, u32[]{:S(2)}, u32[]{:S(2)}) collective-permute-start(bf16[256,2048]{1,0:T(8,128)(2,1)} %fusion.51), channel_id=1, source_target_pairs={{0,2},{1,3},{2,0},{3,1},{4,6},{5,7},{6,4},{7,5},{8,10},{9,11},{10,... | collective-permute-start | bytes 3145736 | tf_op jit(solution)/shard_map/ppermute | solution.py:378
  422.0 45.0 %copy-start.11 = (bf16[1024,512]{1,0:T(8,128)(2,1)S(1)}, bf16[1024,512]{1,0:T(8,128)(2,1)}, u32[]{:S(2)}) copy-start(bf16[1024,512]{1,0:T(8,128)(2,1)} %reduce-scatter.8.cloned.1.call-done) | copy-start | bytes 3145732
  458.2 4.3 collective-permute-start.34
  460.0 38.1 %collective-permute-start.32 = (bf16[256,2048]{1,0:T(8,128)(2,1)}, bf16[256,2048]{1,0:T(8,128)(2,1)}, u32[]{:S(2)}, u32[]{:S(2)}) collective-permute-start(bf16[256,2048]{1,0:T(8,128)(2,1)} %collective-permute-done.31), channel_id=1, source_target_pairs={{0,1},{1,0},{2,3},{3,2},{4,5},{5,4},{6,7},{7,6},{8,9},{9,8},{10,11... | collective-permute-start | bytes 3145736 | tf_op jit(solution)/shard_map/ppermute | solution.py:378
  462.5 4.3 collective-permute-start.35
  466.9 1.9 collective-permute-start.36
  468.3 22.7 %collective-permute-start.33 = (bf16[1664,512]{1,0:T(8,128)(2,1)S(1)}, bf16[1664,512]{1,0:T(8,128)(2,1)S(1)}, u32[]{:S(2)}, u32[]{:S(2)}) collective-permute-start(bf16[1664,512]{1,0:T(8,128)(2,1)S(1)} %pad_maximum_fusion.1), channel_id=1, source_target_pairs={{0,4},{4,0},{1,5},{5,1},{2,6},{6,2},{3,7},{7,3},{8,12},{12,8},{9,1... | collective-permute-start | bytes 5111816 | tf_op jit(solution)/shard_map/ppermute | solution.py:378
  468.8 15.2 %collective-permute-start.37 = (f32[1,2048]{1,0:T(1,128)S(1)}, f32[1,2048]{1,0:T(1,128)S(1)}, u32[]{:S(2)}, u32[]{:S(2)}) collective-permute-start(f32[1,2048]{1,0:T(1,128)S(1)} %bitcast.189), channel_id=1, source_target_pairs={{0,1},{1,0},{2,3},{3,2},{4,5},{5,4},{6,7},{7,6},{8,9},{9,8},{10,11... | collective-permute-start | bytes 24584 | tf_op jit(solution)/shard_map/ppermute | solution.py:378
  484.1 4.6 collective-permute-start.38
  (60 other events, 595.3 us)
Sparse Core Ops, SparseCore 0:
  46.6 35.6 all-gather.6
  84.1 35.1 all-gather.4
  154.8 76.0 reduce-scatter.3
  235.1 90.7 all-gather.8
  329.0 52.9 reduce-scatter.7
  409.4 39.1 reduce-scatter.5

commit v6 on v5

--- a/solution.py
+++ b/solution.py
@@ -426,8 +426,7 @@
     return collect(*shares(array, axis, dim, kind), axis)
 
 
-def halving_sum(pieces, axis):
-    k = 1
+def halving_sum(pieces, axis, k=1):
     while len(pieces) > 1:
         came = [swap(piece.astype(BF16), axis, k) for piece in pieces[1::2]]
         pieces = [own.astype(F32) + part.astype(F32) for own, part in zip(pieces[::2], came)]
@@ -593,8 +592,7 @@
     d_projections, halved, summed = all_sum(d_part, output_rows)
     block_output = lax.all_gather(output_rows[None], "tensor", axis=1, tiled=True)
     gate_parts = token_parts(d_gate)
-    late_gate, late_gated = after((gate_parts, gated_parts), halved)
-    grad_out_part = over_tokens(cotangent, late_gated)
+    late_gate = after(gate_parts, halved)
     grad_gate_part = over_tokens(normed, late_gate)
     grad_dt_part = dot(dt_input, d_logits)
     d_act = d_act + dot(d_projections, w_x, 0, 0)
@@ -616,7 +614,10 @@
         piece_of(partial, "tensor", 0, zplace ^ k) for k in range(lax.axis_size("tensor"))
     ]
     row_parts, block_output = after((row_parts, block_output))
-    d_normed = halving_sum(row_parts, "tensor")
+    came = [swap(part, "tensor", 1) for part in row_parts[1::2]]
+    row_parts = [own.astype(F32) + part.astype(F32) for own, part in zip(row_parts[::2], came)]
+    d_normed = halving_sum(row_parts, "tensor", 2)
+    grad_out_part = over_tokens(cotangent, after(gated_parts, came[1]))
     grad_conv_part = over_tokens(normed, conv_parts)
     d_rows = piece_of(own_cotangent, "tensor", 0, zplace).astype(F32)
     inv = inverse_rms(x_rows)
@@ -637,8 +638,8 @@
 
     sums = jnp.concatenate(
         [
-            owned((grad_conv_part, grad_x_part, grad_dt_part), d_normed),
-            owned((grad_gate_part, grad_out_part)),
+            owned((grad_conv_part, grad_out_part, grad_x_part, grad_dt_part), d_normed),
+            owned((grad_gate_part,)),
         ]
     )
     thin = jnp.concatenate(
@@ -665,17 +666,12 @@
 
     thin = side_by_side([part[:channels] for part in others], 1)
     sums = [sums] + [swap(sums, "context", k) for k in range(1, ctxs)]
-    conv_at = sums[0].shape[0] - 2 * share
     grad_in = side_by_side(
-        [
-            jnp.stack([part[:share], part[conv_at : conv_at + share]]).astype(F32)
-            for part in sums
-        ],
-        2,
-    )
-    grad_out = side_by_side([part[conv_at + share :].T.astype(F32) for part in sums], 0)
-    thin_at = share + xcols
-    grad_x = side_by_side([part[share:thin_at].T.astype(F32) for part in sums], 0)
+        [jnp.stack([part[:share], part[-share:]]).astype(F32) for part in sums], 2
+    )
+    grad_out = side_by_side([part[share : 2 * share].T.astype(F32) for part in sums], 0)
+    thin_at = 2 * share + xcols
+    grad_x = side_by_side([part[2 * share : thin_at].T.astype(F32) for part in sums], 0)
     grad_dt = side_by_side([part[thin_at : thin_at + dtrows].astype(F32) for part in sums], 1)
     gain = total([part[channels:] for part in others]).reshape(1, width)
     grad_gain = doubling_sum(gain, ("tensor",))[0]

time: 518 us -> 512 us (0.988)
    ppermute x39, waiting for transfers between devices: 146 us -> 136 us  [swap(): return lax.ppermute(array, axis, [(i, i ^ k) for i in range(size)])]
    all_gather x1, waiting for transfers between devices: 0.01 us -> 6.73 us  [shards(): lax.all_gather(output_rows[None], 'tensor', axis=1, tiled=True)]
    concatenate x3 -> x1, other arithmetic: 8.32 us -> 2.82 us  [shards(): jnp.concatenate([owned((grad_conv_part, grad_out_part, grad_x_part, grad_...]
    unnamed x128 -> x137, local copies, waits for them, and re-layouts: 10.5 us -> 13.1 us
  transfers between devices with their start and end apart: 45 -> 45, of which waited for: 17 -> 22; matrix products, arithmetic and copies ran while one was open for 35% -> 35% of each run, Pallas kernels for 18% -> 19%
where the time goes in v6:
time: 512 us; the launch traced here: 504 us
  waiting for transfers between devices  150 us (29%)
  Pallas kernels  93.8 us (18%)
  matrix products  88.2 us (17%)
  local copies, waits for them, and re-layouts  56 us (11%)
  other arithmetic  50.5 us (10%)
  starting transfers between devices  49.8 us (10%)
  between operations  16 us (3%)
    ppermute x39, waiting for transfers between devices, swap(): return lax.ppermute(array, axis, [(i, i ^ k) for i in range(size)])  136 us
    dot_general x18, matrix products, dot(): lax.dot_general(left, right, (((left_dim,), (right_dim,)), ((), ())), pre...  88.2 us
    pallas_call x1, Pallas kernels, adjoint(): pl.pallas_call(adjoint_kernel, grid=(count,), in_specs=[cols] + [by_row(C...  57.4 us
    ppermute x39, starting transfers between devices, swap(): return lax.ppermute(array, axis, [(i, i ^ k) for i in range(size)])  48.8 us
    pallas_call x1, Pallas kernels, scan(): pl.pallas_call(scan_kernel, grid=(tokens // CHUNK,), in_specs=[pl.BlockSp...  36.4 us
    unnamed x137, local copies, waits for them, and re-layouts  13.1 us
  transfers between devices with their start and end apart: 45, of which 22 were waited for; matrix products, arithmetic and copies ran while one was open for 35% of the time, Pallas kernels for 19%

profile of v6, /device:TPU:0, one launch (start us, length us, event | category | flops | bytes accessed | tf_op | source)
XLA Modules:
  0.0 504.2 jit_solution(4485667161796876020)
XLA Ops:
  7.3 3.2 fusion
  10.8 3.0 fusion.2
  15.3 2.6 collective-permute-start
  25.0 7.3 %collective-permute-done = bf16[584,512]{1,0:T(8,128)(2,1)S(1)} collective-permute-done((bf16[584,512]{1,0:T(8,128)(2,1)S(1)}, bf16[584,512]{1,0:T(8,128)(2,1)S(1)}, u32[]{:S(2)}, u32[]{:S(2)}) %collective-permute-start) | collective-permute-done | bytes 598048 | tf_op jit(solution)/shard_map/ppermute | solution.py:378
  32.3 14.2 %collective-permute-done.1 = bf16[584,512]{1,0:T(8,128)(2,1)} collective-permute-done((bf16[584,512]{1,0:T(8,128)(2,1)S(1)}, bf16[584,512]{1,0:T(8,128)(2,1)}, u32[]{:S(2)}, u32[]{:S(2)}) %collective-permute-start.1) | collective-permute-done | bytes 598048 | tf_op jit(solution)/shard_map/ppermute | solution.py:378
  51.0 5.3 %fusion.61 = bf16[1,2048,512]{2,1,0:T(8,128)(2,1)S(1)} fusion(bf16[1,2048,512]{2,1,0:T(8,128)(2,1)S(1)} %broadcast_in_dim.58, s32[]{:T(128)S(6)} %select_n.45, bf16[1024,2048]{1,0:T(8,128)(2,1)} %fusion.2, bf16[2048,512]{1,0:T(8,128)(2,1)} %slice_dynamic-update-slice_fusion), kind=kOutput, calls=%fused_computation.95 | convolution fusion | flops 2148007936 | bytes 7340036 | tf_op jit(solution)/shard_map/dot_general | solution.py:456
  56.4 5.2 %fusion.63 = bf16[1,2048,512]{2,1,0:T(8,128)(2,1)S(1)} fusion(bf16[1,2048,512]{2,1,0:T(8,128)(2,1)S(1)} %fusion.61, s32[]{:T(128)S(6)} %select_n.46, bf16[1024,2048]{1,0:T(8,128)(2,1)} %collective-permute-done.3, bf16[2048,512]{1,0:T(8,128)(2,1)} %slice_dynamic-update-slice_fusion), kind=kOutput, calls=%fused_computation.97 | convolution fusion | flops 2148007936 | bytes 7340036 | tf_op jit(solution)/shard_map/dot_general | solution.py:456
  62.3 5.0 fusion.34
  73.4 2.6 collective-permute-start.6
  76.6 6.3 %collective-permute-done.6 = bf16[160,256]{1,0:T(8,128)(2,1)S(1)} collective-permute-done((bf16[160,256]{1,0:T(8,128)(2,1)S(1)}, bf16[160,256]{1,0:T(8,128)(2,1)S(1)}, u32[]{:S(2)}, u32[]{:S(2)}) %collective-permute-start.6) | collective-permute-done | bytes 81952 | tf_op jit(solution)/shard_map/ppermute | solution.py:378
  88.0 5.3 %convolution_dynamic-update-slice_fusion.2 = f32[2048,512]{1,0:T(8,128)S(1)} fusion(f32[2048,512]{1,0:T(8,128)S(1)} %reshape.208.clone, s32[]{:T(128)S(6)} %select_n.45, bf16[1024,2048]{1,0:T(8,128)(2,1)} %fusion.2, bf16[2048,512]{1,0:T(8,128)(2,1)} %all-gather.7.cloned.1.call-done), kind=kOutput, calls=%fused_computation.90 | convolution fusion | flops 2147483648 | bytes 8388612 | tf_op jit(solution)/shard_map/dot_general | solution.py:456
  93.4 5.2 %convolution_dynamic-update-slice_fusion.1.gate_ref = f32[2048,512]{1,0:T(8,128)S(1)} fusion(f32[2048,512]{1,0:T(8,128)S(1)} %convolution_dynamic-update-slice_fusion.2, s32[]{:T(128)S(6)} %select_n.46, bf16[1024,2048]{1,0:T(8,128)(2,1)} %collective-permute-done.3, bf16[2048,512]{1,0:T(8,128)(2,1)} %all-gather.7.cloned.1.call-done), kind=kOutput, calls=%fused_computation.89 | convolution fusion | flops 2147483648 | bytes 8388612 | tf_op jit(solution)/shard_map/dot_general | solution.py:456
  100.9 36.4 %scan.1 = (bf16[2048,512]{1,0:T(8,128)(2,1)}, f32[2048,512]{1,0:T(8,128)}, f32[2048,512]{1,0:T(8,128)}, f32[2048,512]{1,0:T(8,128)}, f32[32768,512]{1,0:T(8,128)}, /*index=5*/f32[16,512]{1,0:T(8,128)}) custom-call(bf16[160,2048]{1,0:T(8,128)(2,1)} %copy-done.18, bf16[2048,512]{1,0:T(8,128)(2,1)} %copy-done.8, f32[2048,512]{1,0:T(8,128)} %copy-done.6, ...), custom_call_target="tpu_custom_call" | custom-call | flops 40265318400 | bytes 134217728 | tf_op jit(solution)/shard_map/scan/pallas_call | solution.py:301
  142.8 5.9 %bitcast_dynamic-update-slice_fusion = f32[2048,512]{1,0:T(8,128)} fusion(f32[2048,512]{1,0:T(8,128)} %reshape.208, s32[]{:T(128)S(6)} %select_n.45, bf16[2048,512]{0,1:T(8,128)(2,1)S(1)} %copy-done.63, bf16[1,1024,2048]{2,1,0:T(8,128)(2,1)} %param.25), kind=kOutput, calls=%fused_computation.83 | convolution fusion | flops 2147483648 | bytes 8388612 | tf_op jit(solution)/shard_map/dot_general | solution.py:456
  148.7 6.1 %fusion.43 = bf16[1024,2048]{1,0:T(8,128)(2,1)} fusion(bf16[2048,512]{0,1:T(8,128)(2,1)S(1)} %collective-permute-done.14, bf16[2048,512]{0,1:T(8,128)(2,1)S(1)} %copy-done.63, bf16[1024,512]{1,0:T(8,128)(2,1)S(1)} %collective-permute-done.13, bf16[1024,512]{1,0:T(8,128)(2,1)S(1)} %get-tuple-element.85), kind=kOutput, calls=%fused_computation.66 | convolution fusion | flops 4309647360 | bytes 10485760 | tf_op jit(solution)/shard_map/dot_general | solution.py:456
  155.3 6.0 %convolution_dynamic-update-slice_fusion = f32[2048,512]{1,0:T(8,128)} fusion(f32[2048,512]{1,0:T(8,128)} %bitcast_dynamic-update-slice_fusion, s32[]{:T(128)S(6)} %select_n.46, bf16[1024,2048]{1,0:T(8,128)(2,1)} %collective-permute-done.12, bf16[2048,512]{0,1:T(8,128)(2,1)S(1)} %copy-done.63), kind=kOutput, calls=%fused_computation.88 | convolution fusion | flops 2147483648 | bytes 8388612 | tf_op jit(solution)/shard_map/dot_general | solution.py:456
  161.3 6.2 %multiply_convert_fusion.1 = (bf16[2048,512]{1,0:T(8,128)(2,1)S(1)}, f32[2048,512]{1,0:T(8,128)}) fusion(f32[2048,512]{1,0:T(8,128)} %convolution_dynamic-update-slice_fusion, f32[2048,512]{1,0:T(8,128)S(1)} %copy-done.16, f32[2048,512]{1,0:T(8,128)S(1)} %copy-done.7), kind=kLoop, calls=%fused_computation.63 | loop fusion | flops 7340032 | bytes 18874368 | tf_op jit(solution)/shard_map/convert_element_type | solution.py:581
  167.5 57.4 %adjoint.1 = (bf16[2048,512]{1,0:T(8,128)(2,1)}, f32[2048,512]{1,0:T(8,128)}, f32[160,2048]{1,0:T(8,128)}, f32[16,512]{1,0:T(8,128)}, f32[1,512]{1,0:T(1,128)}, /*index=5*/f32[1,512]{1,0:T(1,128)}) custom-call(bf16[160,2048]{1,0:T(8,128)(2,1)} %copy-done.18, bf16[2048,512]{1,0:T(8,128)(2,1)} %copy-done.8, f32[2048,512]{1,0:T(8,128)} %get-tuple-element.67.steps_ref, ...), custom_call_target="tpu_custom_call" | custom-call | flops 80530636800 | bytes 134217728 | tf_op jit(solution)/shard_map/adjoint/pallas_call | solution.py:343
  224.9 6.1 %reduce-scatter.4.cloned.1.call-done = bf16[256,2048]{1,0:T(8,128)(2,1)} async-done(((bf16[1024,2048]{1,0:T(8,128)(2,1)}), bf16[256,2048]{1,0:T(8,128)(2,1)}) %reduce-scatter.4.cloned.1.call-update) | async-done | bytes 1048592 | tf_op jit(solution)/shard_map/reduce_scatter | solution.py:582
  246.1 3.8 collective-permute-done.21
  250.0 11.9 %collective-permute-start.22 = (bf16[160,256]{1,0:T(8,128)(2,1)S(1)}, bf16[160,256]{1,0:T(8,128)(2,1)S(1)}, u32[]{:S(2)}, u32[]{:S(2)}) collective-permute-start(bf16[160,256]{1,0:T(8,128)(2,1)S(1)} %get-tuple-element.109), channel_id=1, source_target_pairs={{0,1},{1,0},{2,3},{3,2},{4,5},{5,4},{6,7},{7,6},{8,9},{9,8},{10,11... | collective-permute-start | bytes 245768 | tf_op jit(solution)/shard_map/ppermute | solution.py:378
  262.4 3.2 collective-permute-start.23
  267.1 3.7 collective-permute-done.22
  270.8 5.7 %collective-permute-done.23 = bf16[160,256]{1,0:T(8,128)(2,1)S(1)} collective-permute-done((bf16[160,256]{1,0:T(8,128)(2,1)S(1)}, bf16[160,256]{1,0:T(8,128)(2,1)S(1)}, u32[]{:S(2)}, u32[]{:S(2)}) %collective-permute-start.23) | collective-permute-done | bytes 81952 | tf_op jit(solution)/shard_map/ppermute | solution.py:378
  281.7 4.0 multiply_reduce_fusion
  285.8 3.7 fusion.15
  291.1 4.6 fusion.86
  295.6 6.3 %add_convert_fusion = bf16[2048,512]{1,0:T(8,128)(2,1)} fusion(f32[2048,512]{1,0:T(8,128)S(1)} %fusion.86, bf16[1024,2048]{1,0:T(8,128)(2,1)} %collective-permute-done.3, bf16[1024,512]{1,0:T(8,128)(2,1)} %get-tuple-element.90), kind=kOutput, calls=%fused_computation.56 | convolution fusion | flops 2149580800 | bytes 11534336 | tf_op jit(solution)/shard_map/dot_general | solution.py:456
  302.0 13.4 %fusion.38 = bf16[1024,2048]{1,0:T(8,128)(2,1)} fusion(bf16[2048,512]{1,0:T(8,128)(2,1)} %collective-permute-done.17, bf16[2048,512]{1,0:T(8,128)(2,1)} %slice_dynamic-update-slice_fusion, bf16[2048,512]{1,0:T(8,128)(2,1)} %collective-permute-done.16, bf16[2048,512]{1,0:T(8,128)(2,1)} %all-gather.7.cloned.1.call-done, ...), kind=kOutput, calls=%fused_computation.65 | convolution fusion | flops 8642363392 | bytes 16777216 | tf_op jit(solution)/shard_map/dot_general | solution.py:456
  315.4 4.1 constant_dynamic-slice_fusion.1
  319.5 6.7 %all-gather.9.cloned.1.call-done = bf16[1024,2048]{1,0:T(8,128)(2,1)} async-done(((bf16[256,2048]{1,0:T(8,128)(2,1)}), bf16[1024,2048]{1,0:T(8,128)(2,1)}) %all-gather.9.cloned.1.call-update) | async-done | bytes 4194320 | tf_op jit(solution)/shard_map/all_gather | solution.py:593
  326.2 4.6 fusion.85
  330.8 4.6 add_convert_fusion.1
  338.9 13.6 %collective-permute-done.28 = bf16[256,2048]{1,0:T(8,128)(2,1)S(1)} collective-permute-done((bf16[256,2048]{1,0:T(8,128)(2,1)}, bf16[256,2048]{1,0:T(8,128)(2,1)S(1)}, u32[]{:S(2)}, u32[]{:S(2)}) %collective-permute-start.28) | collective-permute-done | bytes 1048608 | tf_op jit(solution)/shard_map/ppermute | solution.py:378
  353.8 2.9 collective-permute-start.29
  356.7 4.6 fusion.76
  361.3 6.0 %fusion.30 = bf16[2048,512]{0,1:T(8,128)(2,1)} fusion(f32[512,2048]{1,0:T(8,128)S(1)} %fusion.76, bf16[1024,2048]{1,0:T(8,128)(2,1)} %collective-permute-done.12, bf16[1024,512]{1,0:T(8,128)(2,1)S(1)} %copy-done.27), kind=kOutput, calls=%fused_computation.37 | convolution fusion | flops 2149580800 | bytes 11534336 | tf_op jit(solution)/shard_map/dot_general | solution.py:456
  367.3 3.1 copy.34
  373.3 3.3 fusion.67
  378.0 16.4 %collective-permute-done.27 = bf16[256,2048]{1,0:T(8,128)(2,1)} collective-permute-done((bf16[256,2048]{1,0:T(8,128)(2,1)}, bf16[256,2048]{1,0:T(8,128)(2,1)}, u32[]{:S(2)}, u32[]{:S(2)}) %collective-permute-start.27) | collective-permute-done | bytes 1048608 | tf_op jit(solution)/shard_map/ppermute | solution.py:378
  394.4 7.0 %collective-permute-done.29 = bf16[256,2048]{1,0:T(8,128)(2,1)} collective-permute-done((bf16[256,2048]{1,0:T(8,128)(2,1)}, bf16[256,2048]{1,0:T(8,128)(2,1)}, u32[]{:S(2)}, u32[]{:S(2)}) %collective-permute-start.29) | collective-permute-done | bytes 1048608 | tf_op jit(solution)/shard_map/ppermute | solution.py:378
  401.4 3.1 fusion.54
  407.0 2.9 collective-permute-start.31
  410.1 2.6 reshape.222
  413.7 37.9 %collective-permute-done.30 = bf16[256,2048]{1,0:T(8,128)(2,1)S(1)} collective-permute-done((bf16[256,2048]{1,0:T(8,128)(2,1)S(1)}, bf16[256,2048]{1,0:T(8,128)(2,1)S(1)}, u32[]{:S(2)}, u32[]{:S(2)}) %collective-permute-start.30) | collective-permute-done | bytes 1048608 | tf_op jit(solution)/shard_map/ppermute | solution.py:378
  454.6 2.8 collective-permute-done.34
  463.2 2.8 pad_maximum_fusion
  467.8 8.5 %collective-permute-done.37 = f32[1,2048]{1,0:T(1,128)S(1)} collective-permute-done((f32[1,2048]{1,0:T(1,128)S(1)}, f32[1,2048]{1,0:T(1,128)S(1)}, u32[]{:S(2)}, u32[]{:S(2)}) %collective-permute-start.37) | collective-permute-done | bytes 8224 | tf_op jit(solution)/shard_map/ppermute | solution.py:378
  (315 shorter events, 101.2 us)
Async XLA Ops:
  7.2 80.2 %all-gather.7.cloned.1.call-start = ((), (), s32[]{:S(2)}) async-start(), calls=%async_computation.4 | async-start | bytes 2621440 | tf_op jit(solution)/shard_map/all_gather | solution.py:549
  13.8 42.5 %collective-permute-start.3 = (bf16[1024,2048]{1,0:T(8,128)(2,1)}, bf16[1024,2048]{1,0:T(8,128)(2,1)}, u32[]{:S(2)}, u32[]{:S(2)}) collective-permute-start(bf16[1024,2048]{1,0:T(8,128)(2,1)} %fusion.2), channel_id=1, source_target_pairs={{0,4},{4,0},{1,5},{5,1},{2,6},{6,2},{3,7},{7,3},{8,12},{12,8},{9,1... | collective-permute-start | bytes 12582920 | tf_op jit(solution)/shard_map/ppermute | solution.py:378
  15.3 17.0 %collective-permute-start = (bf16[584,512]{1,0:T(8,128)(2,1)S(1)}, bf16[584,512]{1,0:T(8,128)(2,1)S(1)}, u32[]{:S(2)}, u32[]{:S(2)}) collective-permute-start(bf16[584,512]{1,0:T(8,128)(2,1)S(1)} %pad_maximum_fusion.1), channel_id=1, source_target_pairs={{0,8},{8,0},{16,24},{24,16},{1,9},{9,1},{17,25},{25,17},{2,10},{10... | collective-permute-start | bytes 1794056 | tf_op jit(solution)/shard_map/ppermute | solution.py:378
  17.9 28.5 %collective-permute-start.1 = (bf16[584,512]{1,0:T(8,128)(2,1)S(1)}, bf16[584,512]{1,0:T(8,128)(2,1)}, u32[]{:S(2)}, u32[]{:S(2)}) collective-permute-start(bf16[584,512]{1,0:T(8,128)(2,1)S(1)} %pad_maximum_fusion.1), channel_id=1, source_target_pairs={{0,16},{8,24},{16,0},{24,8},{1,17},{9,25},{17,1},{25,9},{2,18},{10... | collective-permute-start | bytes 1794056 | tf_op jit(solution)/shard_map/ppermute | solution.py:378
  19.5 27.0 %collective-permute-start.2 = (bf16[584,512]{1,0:T(8,128)(2,1)S(1)}, bf16[584,512]{1,0:T(8,128)(2,1)S(1)}, u32[]{:S(2)}, u32[]{:S(2)}) collective-permute-start(bf16[584,512]{1,0:T(8,128)(2,1)S(1)} %pad_maximum_fusion.1), channel_id=1, source_target_pairs={{0,24},{8,16},{16,8},{24,0},{1,25},{9,17},{17,9},{25,1},{2,26},{10... | collective-permute-start | bytes 1794056 | tf_op jit(solution)/shard_map/ppermute | solution.py:378
  22.5 39.7 %copy-start.51 = (f32[1,512]{1,0:T(1,128)}, f32[1,512]{1,0:T(1,128)S(1)}, u32[]{:S(2)}) copy-start(f32[1,512]{1,0:T(1,128)S(1)} %get-tuple-element.146) | copy-start | bytes 6148
  22.5 39.7 %copy-start.53 = (f32[1,512]{1,0:T(1,128)}, f32[1,512]{1,0:T(1,128)S(1)}, u32[]{:S(2)}) copy-start(f32[1,512]{1,0:T(1,128)S(1)} %get-tuple-element.147) | copy-start | bytes 6148
  25.0 45.5 %copy-start.33 = (f32[1,2048]{1,0:T(1,128)}, f32[1,2048]{1,0:T(1,128)S(1)}, u32[]{:S(2)}) copy-start(f32[1,2048]{1,0:T(1,128)S(1)} %get-tuple-element.148) | copy-start | bytes 24580
  46.5 90.8 %all-gather.5.cloned.1.call-start = ((), (), s32[]{:S(2)}) async-start(), calls=%async_computation.3 | async-start | bytes 2621440 | tf_op jit(solution)/shard_map/all_gather | solution.py:551
  68.2 2.2 collective-permute-start.4
  71.9 4.8 collective-permute-start.5
  73.4 9.5 %collective-permute-start.6 = (bf16[160,256]{1,0:T(8,128)(2,1)S(1)}, bf16[160,256]{1,0:T(8,128)(2,1)S(1)}, u32[]{:S(2)}, u32[]{:S(2)}) collective-permute-start(bf16[160,256]{1,0:T(8,128)(2,1)S(1)} %get-tuple-element.140), channel_id=1, source_target_pairs={{0,2},{1,3},{2,0},{3,1},{4,6},{5,7},{6,4},{7,5},{8,10},{9,11},{10,... | collective-permute-start | bytes 245768 | tf_op jit(solution)/shard_map/ppermute | solution.py:378
  76.0 6.9 %collective-permute-start.7 = (bf16[160,256]{1,0:T(8,128)(2,1)S(1)}, bf16[160,256]{1,0:T(8,128)(2,1)S(1)}, u32[]{:S(2)}, u32[]{:S(2)}) collective-permute-start(bf16[160,256]{1,0:T(8,128)(2,1)S(1)} %get-tuple-element.139), channel_id=1, source_target_pairs={{0,3},{1,2},{2,1},{3,0},{4,7},{5,6},{6,5},{7,4},{8,11},{9,10},{10,... | collective-permute-start | bytes 245768 | tf_op jit(solution)/shard_map/ppermute | solution.py:378
  76.3 79.0 %collective-permute-start.12 = (bf16[1024,2048]{1,0:T(8,128)(2,1)}, bf16[1024,2048]{1,0:T(8,128)(2,1)}, u32[]{:S(2)}, u32[]{:S(2)}) collective-permute-start(bf16[1024,2048]{1,0:T(8,128)(2,1)} %bitcast.19), channel_id=1, source_target_pairs={{0,4},{4,0},{1,5},{5,1},{2,6},{6,2},{3,7},{7,3},{8,12},{12,8},{9,1... | collective-permute-start | bytes 12582920 | tf_op jit(solution)/shard_map/ppermute | solution.py:378
  76.3 154.7 %reduce-scatter.4.cloned.1.call-start = ((), (), s32[]{:S(2)}) async-start(), calls=%async_computation.5 | async-start | bytes 5242880 | tf_op jit(solution)/shard_map/reduce_scatter | solution.py:582
  83.0 10.3 %collective-permute-start.8 = (bf16[160,256]{1,0:T(8,128)(2,1)S(1)}, bf16[160,256]{1,0:T(8,128)(2,1)S(1)}, u32[]{:S(2)}, u32[]{:S(2)}) collective-permute-start(bf16[160,256]{1,0:T(8,128)(2,1)S(1)} %get-tuple-element.111), channel_id=1, source_target_pairs={{0,1},{1,0},{2,3},{3,2},{4,5},{5,4},{6,7},{7,6},{8,9},{9,8},{10,11... | collective-permute-start | bytes 245768 | tf_op jit(solution)/shard_map/ppermute | solution.py:378
  84.6 8.7 %collective-permute-start.9 = (bf16[160,256]{1,0:T(8,128)(2,1)S(1)}, bf16[160,256]{1,0:T(8,128)(2,1)S(1)}, u32[]{:S(2)}, u32[]{:S(2)}) collective-permute-start(bf16[160,256]{1,0:T(8,128)(2,1)S(1)} %get-tuple-element.111), channel_id=1, source_target_pairs={{0,2},{1,3},{2,0},{3,1},{4,6},{5,7},{6,4},{7,5},{8,10},{9,11},{10,... | collective-permute-start | bytes 245768 | tf_op jit(solution)/shard_map/ppermute | solution.py:378
  86.1 7.2 %collective-permute-start.10 = (bf16[160,256]{1,0:T(8,128)(2,1)S(1)}, bf16[160,256]{1,0:T(8,128)(2,1)S(1)}, u32[]{:S(2)}, u32[]{:S(2)}) collective-permute-start(bf16[160,256]{1,0:T(8,128)(2,1)S(1)} %get-tuple-element.111), channel_id=1, source_target_pairs={{0,3},{1,2},{2,1},{3,0},{4,7},{5,6},{6,5},{7,4},{8,11},{9,10},{10,... | collective-permute-start | bytes 245768 | tf_op jit(solution)/shard_map/ppermute | solution.py:378
  93.3 5.4 %collective-permute-start.11 = (bf16[160,1024]{1,0:T(8,128)(2,1)S(1)}, bf16[160,1024]{1,0:T(8,128)(2,1)S(1)}, u32[]{:S(2)}, u32[]{:S(2)}) collective-permute-start(bf16[160,1024]{1,0:T(8,128)(2,1)S(1)} %constant_dynamic-update-slice_fusion.10), channel_id=1, source_target_pairs={{0,4},{4,0},{1,5},{5,1},{2,6},{6,2},{3,7},{7,3},{8,12},{12,8},{9,1... | collective-permute-start | bytes 983048 | tf_op jit(solution)/shard_map/ppermute | solution.py:378
  137.3 11.3 %collective-permute-start.14 = (bf16[2048,512]{0,1:T(8,128)(2,1)}, bf16[2048,512]{0,1:T(8,128)(2,1)S(1)}, u32[]{:S(2)}, u32[]{:S(2)}) collective-permute-start(bf16[2048,512]{0,1:T(8,128)(2,1)} %all-gather.5.cloned.1.call-done), channel_id=1, source_target_pairs={{0,4},{4,0},{1,5},{5,1},{2,6},{6,2},{3,7},{7,3},{8,12},{12,8},{9,1... | collective-permute-start | bytes 6291464 | tf_op jit(solution)/shard_map/ppermute | solution.py:378
  139.6 9.0 %collective-permute-start.13 = (bf16[1024,512]{1,0:T(8,128)(2,1)S(1)}, bf16[1024,512]{1,0:T(8,128)(2,1)S(1)}, u32[]{:S(2)}, u32[]{:S(2)}) collective-permute-start(bf16[1024,512]{1,0:T(8,128)(2,1)S(1)} %get-tuple-element.86), channel_id=1, source_target_pairs={{0,4},{4,0},{1,5},{5,1},{2,6},{6,2},{3,7},{7,3},{8,12},{12,8},{9,1... | collective-permute-start | bytes 3145736 | tf_op jit(solution)/shard_map/ppermute | solution.py:378
  139.8 92.7 %collective-permute-start.17 = (bf16[2048,512]{1,0:T(8,128)(2,1)}, bf16[2048,512]{1,0:T(8,128)(2,1)}, u32[]{:S(2)}, u32[]{:S(2)}) collective-permute-start(bf16[2048,512]{1,0:T(8,128)(2,1)} %slice_dynamic-update-slice_fusion), channel_id=1, source_target_pairs={{0,4},{4,0},{1,5},{5,1},{2,6},{6,2},{3,7},{7,3},{8,12},{12,8},{9,1... | collective-permute-start | bytes 6291464 | tf_op jit(solution)/shard_map/ppermute | solution.py:378
  140.2 92.3 %collective-permute-start.16 = (bf16[2048,512]{1,0:T(8,128)(2,1)}, bf16[2048,512]{1,0:T(8,128)(2,1)}, u32[]{:S(2)}, u32[]{:S(2)}) collective-permute-start(bf16[2048,512]{1,0:T(8,128)(2,1)} %all-gather.7.cloned.1.call-done), channel_id=1, source_target_pairs={{0,4},{4,0},{1,5},{5,1},{2,6},{6,2},{3,7},{7,3},{8,12},{12,8},{9,1... | collective-permute-start | bytes 6291464 | tf_op jit(solution)/shard_map/ppermute | solution.py:378
  154.8 171.4 %all-gather.9.cloned.1.call-start = ((), (), s32[]{:S(2)}) async-start(), calls=%async_computation.8 | async-start | bytes 5242880 | tf_op jit(solution)/shard_map/all_gather | solution.py:593
  234.5 2.8 collective-permute-start.18
  237.1 224.7 %reduce-scatter.8.cloned.1.call-start = ((), (), s32[]{:S(2)}) async-start(), calls=%async_computation.7 | async-start | bytes 2621440 | tf_op jit(solution)/shard_map/reduce_scatter | solution.py:637
  238.9 6.0 %collective-permute-start.19 = (bf16[160,256]{1,0:T(8,128)(2,1)S(1)}, bf16[160,256]{1,0:T(8,128)(2,1)S(1)}, u32[]{:S(2)}, u32[]{:S(2)}) collective-permute-start(bf16[160,256]{1,0:T(8,128)(2,1)S(1)} %get-tuple-element.135), channel_id=1, source_target_pairs={{0,1},{1,0},{2,3},{3,2},{4,5},{5,4},{6,7},{7,6},{8,9},{9,8},{10,11... | collective-permute-start | bytes 245768 | tf_op jit(solution)/shard_map/ppermute | solution.py:378
  240.5 5.7 %collective-permute-start.20 = (bf16[160,256]{1,0:T(8,128)(2,1)S(1)}, bf16[160,256]{1,0:T(8,128)(2,1)S(1)}, u32[]{:S(2)}, u32[]{:S(2)}) collective-permute-start(bf16[160,256]{1,0:T(8,128)(2,1)S(1)} %get-tuple-element.137), channel_id=1, source_target_pairs={{0,2},{1,3},{2,0},{3,1},{4,6},{5,7},{6,4},{7,5},{8,10},{9,11},{10,... | collective-permute-start | bytes 245768 | tf_op jit(solution)/shard_map/ppermute | solution.py:378
  242.2 7.7 %collective-permute-start.21 = (bf16[160,256]{1,0:T(8,128)(2,1)S(1)}, bf16[160,256]{1,0:T(8,128)(2,1)S(1)}, u32[]{:S(2)}, u32[]{:S(2)}) collective-permute-start(bf16[160,256]{1,0:T(8,128)(2,1)S(1)} %get-tuple-element.136), channel_id=1, source_target_pairs={{0,3},{1,2},{2,1},{3,0},{4,7},{5,6},{6,5},{7,4},{8,11},{9,10},{10,... | collective-permute-start | bytes 245768 | tf_op jit(solution)/shard_map/ppermute | solution.py:378
  244.9 57.1 %collective-permute-start.15 = (bf16[1024,512]{1,0:T(8,128)(2,1)}, bf16[1024,512]{1,0:T(8,128)(2,1)}, u32[]{:S(2)}, u32[]{:S(2)}) collective-permute-start(bf16[1024,512]{1,0:T(8,128)(2,1)} %get-tuple-element.90), channel_id=1, source_target_pairs={{0,4},{4,0},{1,5},{5,1},{2,6},{6,2},{3,7},{7,3},{8,12},{12,8},{9,1... | collective-permute-start | bytes 3145736 | tf_op jit(solution)/shard_map/ppermute | solution.py:378
  250.0 20.7 %collective-permute-start.22 = (bf16[160,256]{1,0:T(8,128)(2,1)S(1)}, bf16[160,256]{1,0:T(8,128)(2,1)S(1)}, u32[]{:S(2)}, u32[]{:S(2)}) collective-permute-start(bf16[160,256]{1,0:T(8,128)(2,1)S(1)} %get-tuple-element.109), channel_id=1, source_target_pairs={{0,1},{1,0},{2,3},{3,2},{4,5},{5,4},{6,7},{7,6},{8,9},{9,8},{10,11... | collective-permute-start | bytes 245768 | tf_op jit(solution)/shard_map/ppermute | solution.py:378
  262.4 14.1 %collective-permute-start.23 = (bf16[160,256]{1,0:T(8,128)(2,1)S(1)}, bf16[160,256]{1,0:T(8,128)(2,1)S(1)}, u32[]{:S(2)}, u32[]{:S(2)}) collective-permute-start(bf16[160,256]{1,0:T(8,128)(2,1)S(1)} %get-tuple-element.109), channel_id=1, source_target_pairs={{0,2},{1,3},{2,0},{3,1},{4,6},{5,7},{6,4},{7,5},{8,10},{9,11},{10,... | collective-permute-start | bytes 245768 | tf_op jit(solution)/shard_map/ppermute | solution.py:378
  265.6 11.5 %collective-permute-start.24 = (bf16[160,256]{1,0:T(8,128)(2,1)S(1)}, bf16[160,256]{1,0:T(8,128)(2,1)S(1)}, u32[]{:S(2)}, u32[]{:S(2)}) collective-permute-start(bf16[160,256]{1,0:T(8,128)(2,1)S(1)} %get-tuple-element.109), channel_id=1, source_target_pairs={{0,3},{1,2},{2,1},{3,0},{4,7},{5,6},{6,5},{7,4},{8,11},{9,10},{10,... | collective-permute-start | bytes 245768 | tf_op jit(solution)/shard_map/ppermute | solution.py:378
  277.1 1.7 collective-permute-start.25
  289.7 12.3 %collective-permute-start.26 = (bf16[1024,512]{1,0:T(8,128)(2,1)S(1)}, bf16[1024,512]{1,0:T(8,128)(2,1)}, u32[]{:S(2)}, u32[]{:S(2)}) collective-permute-start(bf16[1024,512]{1,0:T(8,128)(2,1)S(1)} %get-tuple-element.125), channel_id=1, source_target_pairs={{0,4},{4,0},{1,5},{5,1},{2,6},{6,2},{3,7},{7,3},{8,12},{12,8},{9,1... | collective-permute-start | bytes 3145736 | tf_op jit(solution)/shard_map/ppermute | solution.py:378
  301.9 161.3 %reduce-scatter.6.cloned.1.call-start = ((), (), s32[]{:S(2)}) async-start(), calls=%async_computation.6 | async-start | bytes 5898240 | tf_op jit(solution)/shard_map/reduce_scatter | solution.py:637
  326.2 26.2 %collective-permute-start.28 = (bf16[256,2048]{1,0:T(8,128)(2,1)}, bf16[256,2048]{1,0:T(8,128)(2,1)S(1)}, u32[]{:S(2)}, u32[]{:S(2)}) collective-permute-start(bf16[256,2048]{1,0:T(8,128)(2,1)} %get-tuple-element.84), channel_id=1, source_target_pairs={{0,1},{1,0},{2,3},{3,2},{4,5},{5,4},{6,7},{7,6},{8,9},{9,8},{10,11... | collective-permute-start | bytes 3145736 | tf_op jit(solution)/shard_map/ppermute | solution.py:378
  336.9 57.5 %collective-permute-start.27 = (bf16[256,2048]{1,0:T(8,128)(2,1)}, bf16[256,2048]{1,0:T(8,128)(2,1)}, u32[]{:S(2)}, u32[]{:S(2)}) collective-permute-start(bf16[256,2048]{1,0:T(8,128)(2,1)} %get-tuple-element.82), channel_id=1, source_target_pairs={{0,1},{1,0},{2,3},{3,2},{4,5},{5,4},{6,7},{7,6},{8,9},{9,8},{10,11... | collective-permute-start | bytes 3145736 | tf_op jit(solution)/shard_map/ppermute | solution.py:378
  353.8 47.6 %collective-permute-start.29 = (bf16[256,2048]{1,0:T(8,128)(2,1)}, bf16[256,2048]{1,0:T(8,128)(2,1)}, u32[]{:S(2)}, u32[]{:S(2)}) collective-permute-start(bf16[256,2048]{1,0:T(8,128)(2,1)} %add_convert_fusion.2), channel_id=1, source_target_pairs={{0,2},{1,3},{2,0},{3,1},{4,6},{5,7},{6,4},{7,5},{8,10},{9,11},{10,... | collective-permute-start | bytes 3145736 | tf_op jit(solution)/shard_map/ppermute | solution.py:378
  406.9 44.8 %collective-permute-start.30 = (bf16[256,2048]{1,0:T(8,128)(2,1)S(1)}, bf16[256,2048]{1,0:T(8,128)(2,1)S(1)}, u32[]{:S(2)}, u32[]{:S(2)}) collective-permute-start(bf16[256,2048]{1,0:T(8,128)(2,1)S(1)} %fusion.51), channel_id=1, source_target_pairs={{0,1},{1,0},{2,3},{3,2},{4,5},{5,4},{6,7},{7,6},{8,9},{9,8},{10,11... | collective-permute-start | bytes 3145736 | tf_op jit(solution)/shard_map/ppermute | solution.py:378
  407.0 46.6 %collective-permute-start.31 = (bf16[256,2048]{1,0:T(8,128)(2,1)S(1)}, bf16[256,2048]{1,0:T(8,128)(2,1)}, u32[]{:S(2)}, u32[]{:S(2)}) collective-permute-start(bf16[256,2048]{1,0:T(8,128)(2,1)S(1)} %fusion.51), channel_id=1, source_target_pairs={{0,2},{1,3},{2,0},{3,1},{4,6},{5,7},{6,4},{7,5},{8,10},{9,11},{10,... | collective-permute-start | bytes 3145736 | tf_op jit(solution)/shard_map/ppermute | solution.py:378
  451.7 5.7 %collective-permute-start.34 = (f32[27,512]{1,0:T(8,128)S(1)}, f32[27,512]{1,0:T(8,128)S(1)}, u32[]{:S(2)}, u32[]{:S(2)}) collective-permute-start(f32[27,512]{1,0:T(8,128)S(1)} %concatenate.35), channel_id=1, source_target_pairs={{0,8},{8,0},{16,24},{24,16},{1,9},{9,1},{17,25},{25,17},{2,10},{10... | collective-permute-start | bytes 165896 | tf_op jit(solution)/shard_map/ppermute | solution.py:378
  453.5 39.0 %collective-permute-start.32 = (bf16[256,2048]{1,0:T(8,128)(2,1)}, bf16[256,2048]{1,0:T(8,128)(2,1)}, u32[]{:S(2)}, u32[]{:S(2)}) collective-permute-start(bf16[256,2048]{1,0:T(8,128)(2,1)} %collective-permute-done.31), channel_id=1, source_target_pairs={{0,1},{1,0},{2,3},{3,2},{4,5},{5,4},{6,7},{7,6},{8,9},{9,8},{10,11... | collective-permute-start | bytes 3145736 | tf_op jit(solution)/shard_map/ppermute | solution.py:378
  457.4 4.3 collective-permute-start.35
  461.7 4.3 collective-permute-start.36
  466.0 20.4 %collective-permute-start.33 = (bf16[1664,512]{1,0:T(8,128)(2,1)}, bf16[1664,512]{1,0:T(8,128)(2,1)}, u32[]{:S(2)}, u32[]{:S(2)}) collective-permute-start(bf16[1664,512]{1,0:T(8,128)(2,1)} %pad_maximum_fusion), channel_id=1, source_target_pairs={{0,4},{4,0},{1,5},{5,1},{2,6},{6,2},{3,7},{7,3},{8,12},{12,8},{9,1... | collective-permute-start | bytes 5111816 | tf_op jit(solution)/shard_map/ppermute | solution.py:378
  466.1 10.2 %collective-permute-start.37 = (f32[1,2048]{1,0:T(1,128)S(1)}, f32[1,2048]{1,0:T(1,128)S(1)}, u32[]{:S(2)}, u32[]{:S(2)}) collective-permute-start(f32[1,2048]{1,0:T(1,128)S(1)} %bitcast.187), channel_id=1, source_target_pairs={{0,1},{1,0},{2,3},{3,2},{4,5},{5,4},{6,7},{7,6},{8,9},{9,8},{10,11... | collective-permute-start | bytes 24584 | tf_op jit(solution)/shard_map/ppermute | solution.py:378
  476.3 4.6 collective-permute-start.38
  (63 other events, 657.8 us)
Sparse Core Ops, SparseCore 0:
  46.6 35.6 all-gather.6
  84.1 35.1 all-gather.4
  154.9 76.0 reduce-scatter.3
  237.2 88.9 all-gather.8
  329.3 35.6 reduce-scatter.7
  404.7 58.4 reduce-scatter.5

commit v7 on v6

--- a/solution.py
+++ b/solution.py
@@ -12,7 +12,7 @@
 SUB = 8
 CHUNK = 128
 PARTS = 2
-VMEM_LIMIT = 56 << 20
+VMEM_LIMIT = 50 << 20
 GONE = 1e4
 LOG2E = 1.4426950408889634
 

time: 512 us -> 507 us (level)
  starting transfers between devices: 49.8 us -> 44.3 us
    all_gather x1, waiting for transfers between devices: 6.73 us -> 12.3 us  [shards(): lax.all_gather(output_rows[None], 'tensor', axis=1, tiled=True)]
    ppermute x39, starting transfers between devices: 48.8 us -> 43.3 us  [swap(): return lax.ppermute(array, axis, [(i, i ^ k) for i in range(size)])]
    unnamed x137 -> x125, local copies, waits for them, and re-layouts: 13.1 us -> 12.8 us
  transfers between devices with their start and end apart: 45 -> 45, of which waited for: 22 -> 22; matrix products, arithmetic and copies ran while one was open for 35% -> 35% of each run, Pallas kernels for 19% -> 18%
where the time goes in v7:
time: 507 us; the launch traced here: 499 us
  waiting for transfers between devices  154 us (30%)
  Pallas kernels  92 us (18%)
  matrix products  88.2 us (17%)
  local copies, waits for them, and re-layouts  54.6 us (11%)
  other arithmetic  50.3 us (10%)
  starting transfers between devices  44.3 us (9%)
  between operations  15.9 us (3%)
    ppermute x39, waiting for transfers between devices, swap(): return lax.ppermute(array, axis, [(i, i ^ k) for i in range(size)])  136 us
    dot_general x18, matrix products, dot(): lax.dot_general(left, right, (((left_dim,), (right_dim,)), ((), ())), pre...  88.2 us
    pallas_call x1, Pallas kernels, adjoint(): pl.pallas_call(adjoint_kernel, grid=(count,), in_specs=[cols] + [by_row(C...  56.6 us
    ppermute x39, starting transfers between devices, swap(): return lax.ppermute(array, axis, [(i, i ^ k) for i in range(size)])  43.3 us
    pallas_call x1, Pallas kernels, scan(): pl.pallas_call(scan_kernel, grid=(tokens // CHUNK,), in_specs=[pl.BlockSp...  35.4 us
    unnamed x125, local copies, waits for them, and re-layouts  12.8 us
    all_gather x1, waiting for transfers between devices, shards(): lax.all_gather(output_rows[None], 'tensor', axis=1, tiled=True)  12.3 us
  transfers between devices with their start and end apart: 45, of which 22 were waited for; matrix products, arithmetic and copies ran while one was open for 35% of the time, Pallas kernels for 18%

profile of v7, /device:TPU:0, one launch (start us, length us, event | category | flops | bytes accessed | tf_op | source)
XLA Modules:
  0.0 499.4 jit_solution(4470902879975097010)
XLA Ops:
  7.3 3.2 fusion
  10.8 3.0 fusion.2
  15.3 2.6 collective-permute-start
  23.3 9.0 %collective-permute-done = bf16[584,512]{1,0:T(8,128)(2,1)S(1)} collective-permute-done((bf16[584,512]{1,0:T(8,128)(2,1)S(1)}, bf16[584,512]{1,0:T(8,128)(2,1)S(1)}, u32[]{:S(2)}, u32[]{:S(2)}) %collective-permute-start) | collective-permute-done | bytes 598048 | tf_op jit(solution)/shard_map/ppermute | solution.py:378
  32.3 14.2 %collective-permute-done.1 = bf16[584,512]{1,0:T(8,128)(2,1)} collective-permute-done((bf16[584,512]{1,0:T(8,128)(2,1)S(1)}, bf16[584,512]{1,0:T(8,128)(2,1)}, u32[]{:S(2)}, u32[]{:S(2)}) %collective-permute-start.1) | collective-permute-done | bytes 598048 | tf_op jit(solution)/shard_map/ppermute | solution.py:378
  51.0 5.3 %fusion.61 = bf16[1,2048,512]{2,1,0:T(8,128)(2,1)S(1)} fusion(bf16[1,2048,512]{2,1,0:T(8,128)(2,1)S(1)} %broadcast_in_dim.58, s32[]{:T(128)S(6)} %select_n.45, bf16[1024,2048]{1,0:T(8,128)(2,1)} %fusion.2, bf16[2048,512]{1,0:T(8,128)(2,1)} %slice_dynamic-update-slice_fusion), kind=kOutput, calls=%fused_computation.95 | convolution fusion | flops 2148007936 | bytes 7340036 | tf_op jit(solution)/shard_map/dot_general | solution.py:456
  56.4 5.2 %fusion.63 = bf16[1,2048,512]{2,1,0:T(8,128)(2,1)S(1)} fusion(bf16[1,2048,512]{2,1,0:T(8,128)(2,1)S(1)} %fusion.61, s32[]{:T(128)S(6)} %select_n.46, bf16[1024,2048]{1,0:T(8,128)(2,1)} %collective-permute-done.3, bf16[2048,512]{1,0:T(8,128)(2,1)} %slice_dynamic-update-slice_fusion), kind=kOutput, calls=%fused_computation.97 | convolution fusion | flops 2148007936 | bytes 7340036 | tf_op jit(solution)/shard_map/dot_general | solution.py:456
  62.3 5.0 %fusion.34 = (bf16[2048,512]{1,0:T(8,128)(2,1)S(1)}, f32[1,2048,512]{2,1,0:T(8,128)}) fusion(f32[2048]{0:T(1024)S(1)} %bitcast.186, f32[1,2051,512]{2,1,0:T(8,128)S(1)} %pad_convert_fusion, f32[512]{0:T(512)S(1)} %bitcast.198, f32[2048]{0:T(1024)S(1)} %bitcast.188, f32[512]{0:T(512)S(1)} %bitcast.194, f32[2048]{0:T(1024)S(1)} %bitcast.183, ...), kind=kLoop, calls=%fused_computation.49 | loop fusion | flops 16777216 | bytes 23103488 | tf_op jit(solution)/shard_map/convert_element_type | solution.py:539
  73.4 2.6 collective-permute-start.6
  76.6 6.3 %collective-permute-done.6 = bf16[160,256]{1,0:T(8,128)(2,1)S(1)} collective-permute-done((bf16[160,256]{1,0:T(8,128)(2,1)S(1)}, bf16[160,256]{1,0:T(8,128)(2,1)S(1)}, u32[]{:S(2)}, u32[]{:S(2)}) %collective-permute-start.6) | collective-permute-done | bytes 81952 | tf_op jit(solution)/shard_map/ppermute | solution.py:378
  88.0 5.3 %convolution_dynamic-update-slice_fusion.2 = f32[2048,512]{1,0:T(8,128)S(1)} fusion(f32[2048,512]{1,0:T(8,128)S(1)} %reshape.208.clone, s32[]{:T(128)S(6)} %select_n.45, bf16[1024,2048]{1,0:T(8,128)(2,1)} %fusion.2, bf16[2048,512]{1,0:T(8,128)(2,1)} %all-gather.7.cloned.1.call-done), kind=kOutput, calls=%fused_computation.90 | convolution fusion | flops 2147483648 | bytes 8388612 | tf_op jit(solution)/shard_map/dot_general | solution.py:456
  93.4 5.3 %convolution_dynamic-update-slice_fusion.1.gate_ref = f32[2048,512]{1,0:T(8,128)S(1)} fusion(f32[2048,512]{1,0:T(8,128)S(1)} %convolution_dynamic-update-slice_fusion.2, s32[]{:T(128)S(6)} %select_n.46, bf16[1024,2048]{1,0:T(8,128)(2,1)} %collective-permute-done.3, bf16[2048,512]{1,0:T(8,128)(2,1)} %all-gather.7.cloned.1.call-done), kind=kOutput, calls=%fused_computation.89 | convolution fusion | flops 2147483648 | bytes 8388612 | tf_op jit(solution)/shard_map/dot_general | solution.py:456
  100.7 35.4 %scan.1 = (bf16[2048,512]{1,0:T(8,128)(2,1)S(1)}, f32[2048,512]{1,0:T(8,128)}, f32[2048,512]{1,0:T(8,128)}, f32[2048,512]{1,0:T(8,128)}, f32[32768,512]{1,0:T(8,128)}, /*index=5*/f32[16,512]{1,0:T(8,128)S(1)}) custom-call(bf16[160,2048]{1,0:T(8,128)(2,1)S(1)} %constant_dynamic-update-slice_fusion.8.proj_ref, bf16[2048,512]{1,0:T(8,128)(2,1)} %copy-done.10, ...), custom_call_target="tpu_custom_call" | custom-call | flops 40265318400 | bytes 134217728 | tf_op jit(solution)/shard_map/scan/pallas_call | solution.py:301
  137.4 2.5 reshape.208
  139.9 5.9 %bitcast_dynamic-update-slice_fusion = f32[2048,512]{1,0:T(8,128)} fusion(f32[2048,512]{1,0:T(8,128)} %reshape.208, s32[]{:T(128)S(6)} %select_n.45, bf16[2048,512]{0,1:T(8,128)(2,1)S(1)} %copy-done.56, bf16[1,1024,2048]{2,1,0:T(8,128)(2,1)} %param.25), kind=kOutput, calls=%fused_computation.83 | convolution fusion | flops 2147483648 | bytes 8388612 | tf_op jit(solution)/shard_map/dot_general | solution.py:456
  145.8 6.1 %fusion.43 = bf16[1024,2048]{1,0:T(8,128)(2,1)} fusion(bf16[2048,512]{0,1:T(8,128)(2,1)S(1)} %collective-permute-done.14, bf16[2048,512]{0,1:T(8,128)(2,1)S(1)} %copy-done.56, bf16[1024,512]{1,0:T(8,128)(2,1)S(1)} %collective-permute-done.13, bf16[1024,512]{1,0:T(8,128)(2,1)S(1)} %get-tuple-element.85), kind=kOutput, calls=%fused_computation.66 | convolution fusion | flops 4309647360 | bytes 10485760 | tf_op jit(solution)/shard_map/dot_general | solution.py:456
  153.5 6.5 %convolution_dynamic-update-slice_fusion = f32[2048,512]{1,0:T(8,128)} fusion(f32[2048,512]{1,0:T(8,128)} %bitcast_dynamic-update-slice_fusion, s32[]{:T(128)S(6)} %select_n.46, bf16[1024,2048]{1,0:T(8,128)(2,1)} %collective-permute-done.12, bf16[2048,512]{0,1:T(8,128)(2,1)S(1)} %copy-done.57), kind=kOutput, calls=%fused_computation.88 | convolution fusion | flops 2147483648 | bytes 8388612 | tf_op jit(solution)/shard_map/dot_general | solution.py:456
  160.0 7.0 %multiply_convert_fusion.1 = (bf16[2048,512]{1,0:T(8,128)(2,1)}, f32[2048,512]{1,0:T(8,128)}) fusion(f32[2048,512]{1,0:T(8,128)} %convolution_dynamic-update-slice_fusion, f32[2048,512]{1,0:T(8,128)S(1)} %copy-done.18, f32[2048,512]{1,0:T(8,128)S(1)} %copy-done.9), kind=kLoop, calls=%fused_computation.63 | loop fusion | flops 7340032 | bytes 18874368 | tf_op jit(solution)/shard_map/convert_element_type | solution.py:581
  166.9 56.6 %adjoint.1 = (bf16[2048,512]{1,0:T(8,128)(2,1)}, f32[2048,512]{1,0:T(8,128)}, f32[160,2048]{1,0:T(8,128)S(1)}, f32[16,512]{1,0:T(8,128)S(1)}, f32[1,512]{1,0:T(1,128)S(1)}, /*index=5*/f32[1,512]{1,0:T(1,128)S(1)}) custom-call(bf16[160,2048]{1,0:T(8,128)(2,1)S(1)} %constant_dynamic-update-slice_fusion.8.proj_ref, bf16[2048,512]{1,0:T(8,128)(2,1)} %copy-done.10, ...), custom_call_target="tpu_custom_call" | custom-call | flops 80530636800 | bytes 134217728 | tf_op jit(solution)/shard_map/adjoint/pallas_call | solution.py:343
  223.6 4.6 reduce-scatter.4.cloned.1.call-done
  230.5 2.6 fusion.47
  240.8 3.6 collective-permute-done.21
  244.5 5.7 %collective-permute-start.22 = (bf16[160,256]{1,0:T(8,128)(2,1)S(1)}, bf16[160,256]{1,0:T(8,128)(2,1)S(1)}, u32[]{:S(2)}, u32[]{:S(2)}) collective-permute-start(bf16[160,256]{1,0:T(8,128)(2,1)S(1)} %get-tuple-element.109), channel_id=1, source_target_pairs={{0,1},{1,0},{2,3},{3,2},{4,5},{5,4},{6,7},{7,6},{8,9},{9,8},{10,11... | collective-permute-start | bytes 245768 | tf_op jit(solution)/shard_map/ppermute | solution.py:378
  250.6 4.2 collective-permute-start.23
  256.4 2.7 collective-permute-done.22
  259.1 6.7 %collective-permute-done.23 = bf16[160,256]{1,0:T(8,128)(2,1)S(1)} collective-permute-done((bf16[160,256]{1,0:T(8,128)(2,1)S(1)}, bf16[160,256]{1,0:T(8,128)(2,1)S(1)}, u32[]{:S(2)}, u32[]{:S(2)}) %collective-permute-start.23) | collective-permute-done | bytes 81952 | tf_op jit(solution)/shard_map/ppermute | solution.py:378
  271.2 4.0 multiply_reduce_fusion
  275.3 3.7 fusion.15
  280.7 4.6 fusion.86
  285.3 6.0 %add_convert_fusion = bf16[2048,512]{1,0:T(8,128)(2,1)} fusion(f32[2048,512]{1,0:T(8,128)S(1)} %fusion.86, bf16[1024,2048]{1,0:T(8,128)(2,1)} %collective-permute-done.3, bf16[1024,512]{1,0:T(8,128)(2,1)S(1)} %get-tuple-element.90), kind=kOutput, calls=%fused_computation.56 | convolution fusion | flops 2149580800 | bytes 11534336 | tf_op jit(solution)/shard_map/dot_general | solution.py:456
  291.4 13.8 %fusion.38 = bf16[1024,2048]{1,0:T(8,128)(2,1)} fusion(bf16[2048,512]{1,0:T(8,128)(2,1)} %collective-permute-done.17, bf16[2048,512]{1,0:T(8,128)(2,1)} %slice_dynamic-update-slice_fusion, bf16[2048,512]{1,0:T(8,128)(2,1)} %collective-permute-done.16, bf16[2048,512]{1,0:T(8,128)(2,1)} %all-gather.7.cloned.1.call-done, ...), kind=kOutput, calls=%fused_computation.65 | convolution fusion | flops 8642363392 | bytes 16777216 | tf_op jit(solution)/shard_map/dot_general | solution.py:456
  305.2 4.1 constant_dynamic-slice_fusion.1
  309.2 12.3 %all-gather.9.cloned.1.call-done = bf16[1024,2048]{1,0:T(8,128)(2,1)} async-done(((bf16[256,2048]{1,0:T(8,128)(2,1)}), bf16[1024,2048]{1,0:T(8,128)(2,1)}) %all-gather.9.cloned.1.call-update) | async-done | bytes 4194320 | tf_op jit(solution)/shard_map/all_gather | solution.py:593
  321.6 4.6 fusion.85
  326.1 4.9 add_convert_fusion.1
  334.5 13.3 %collective-permute-done.28 = bf16[256,2048]{1,0:T(8,128)(2,1)S(1)} collective-permute-done((bf16[256,2048]{1,0:T(8,128)(2,1)}, bf16[256,2048]{1,0:T(8,128)(2,1)S(1)}, u32[]{:S(2)}, u32[]{:S(2)}) %collective-permute-start.28) | collective-permute-done | bytes 1048608 | tf_op jit(solution)/shard_map/ppermute | solution.py:378
  349.8 4.9 fusion.76
  354.7 6.0 %fusion.30 = bf16[2048,512]{0,1:T(8,128)(2,1)} fusion(f32[512,2048]{1,0:T(8,128)S(1)} %fusion.76, bf16[1024,2048]{1,0:T(8,128)(2,1)} %collective-permute-done.12, bf16[1024,512]{1,0:T(8,128)(2,1)S(1)} %copy-done.26), kind=kOutput, calls=%fused_computation.37 | convolution fusion | flops 2149580800 | bytes 11534336 | tf_op jit(solution)/shard_map/dot_general | solution.py:456
  360.7 3.1 copy.34
  370.2 18.1 %collective-permute-done.27 = bf16[256,2048]{1,0:T(8,128)(2,1)} collective-permute-done((bf16[256,2048]{1,0:T(8,128)(2,1)}, bf16[256,2048]{1,0:T(8,128)(2,1)}, u32[]{:S(2)}, u32[]{:S(2)}) %collective-permute-start.27) | collective-permute-done | bytes 1048608 | tf_op jit(solution)/shard_map/ppermute | solution.py:378
  388.4 7.5 %collective-permute-done.29 = bf16[256,2048]{1,0:T(8,128)(2,1)} collective-permute-done((bf16[256,2048]{1,0:T(8,128)(2,1)}, bf16[256,2048]{1,0:T(8,128)(2,1)}, u32[]{:S(2)}, u32[]{:S(2)}) %collective-permute-start.29) | collective-permute-done | bytes 1048608 | tf_op jit(solution)/shard_map/ppermute | solution.py:378
  395.8 3.2 fusion.54
  399.0 3.2 fusion.51
  402.3 3.2 collective-permute-start.31
  405.6 2.5 reshape.222
  410.5 36.2 %collective-permute-done.30 = bf16[256,2048]{1,0:T(8,128)(2,1)S(1)} collective-permute-done((bf16[256,2048]{1,0:T(8,128)(2,1)}, bf16[256,2048]{1,0:T(8,128)(2,1)S(1)}, u32[]{:S(2)}, u32[]{:S(2)}) %collective-permute-start.30) | collective-permute-done | bytes 1048608 | tf_op jit(solution)/shard_map/ppermute | solution.py:378
  457.8 2.8 pad_maximum_fusion
  462.4 9.1 %collective-permute-done.37 = f32[1,2048]{1,0:T(1,128)S(1)} collective-permute-done((f32[1,2048]{1,0:T(1,128)S(1)}, f32[1,2048]{1,0:T(1,128)S(1)}, u32[]{:S(2)}, u32[]{:S(2)}) %collective-permute-start.37) | collective-permute-done | bytes 8224 | tf_op jit(solution)/shard_map/ppermute | solution.py:378
  (303 shorter events, 95.4 us)
Async XLA Ops:
  7.2 80.2 %all-gather.7.cloned.1.call-start = ((), (), s32[]{:S(2)}) async-start(), calls=%async_computation.4 | async-start | bytes 2621440 | tf_op jit(solution)/shard_map/all_gather | solution.py:549
  13.8 42.5 %collective-permute-start.3 = (bf16[1024,2048]{1,0:T(8,128)(2,1)}, bf16[1024,2048]{1,0:T(8,128)(2,1)}, u32[]{:S(2)}, u32[]{:S(2)}) collective-permute-start(bf16[1024,2048]{1,0:T(8,128)(2,1)} %fusion.2), channel_id=1, source_target_pairs={{0,4},{4,0},{1,5},{5,1},{2,6},{6,2},{3,7},{7,3},{8,12},{12,8},{9,1... | collective-permute-start | bytes 12582920 | tf_op jit(solution)/shard_map/ppermute | solution.py:378
  15.3 17.0 %collective-permute-start = (bf16[584,512]{1,0:T(8,128)(2,1)S(1)}, bf16[584,512]{1,0:T(8,128)(2,1)S(1)}, u32[]{:S(2)}, u32[]{:S(2)}) collective-permute-start(bf16[584,512]{1,0:T(8,128)(2,1)S(1)} %pad_maximum_fusion.1), channel_id=1, source_target_pairs={{0,8},{8,0},{16,24},{24,16},{1,9},{9,1},{17,25},{25,17},{2,10},{10... | collective-permute-start | bytes 1794056 | tf_op jit(solution)/shard_map/ppermute | solution.py:378
  17.9 28.5 %collective-permute-start.1 = (bf16[584,512]{1,0:T(8,128)(2,1)S(1)}, bf16[584,512]{1,0:T(8,128)(2,1)}, u32[]{:S(2)}, u32[]{:S(2)}) collective-permute-start(bf16[584,512]{1,0:T(8,128)(2,1)S(1)} %pad_maximum_fusion.1), channel_id=1, source_target_pairs={{0,16},{8,24},{16,0},{24,8},{1,17},{9,25},{17,1},{25,9},{2,18},{10... | collective-permute-start | bytes 1794056 | tf_op jit(solution)/shard_map/ppermute | solution.py:378
  19.5 27.0 %collective-permute-start.2 = (bf16[584,512]{1,0:T(8,128)(2,1)S(1)}, bf16[584,512]{1,0:T(8,128)(2,1)S(1)}, u32[]{:S(2)}, u32[]{:S(2)}) collective-permute-start(bf16[584,512]{1,0:T(8,128)(2,1)S(1)} %pad_maximum_fusion.1), channel_id=1, source_target_pairs={{0,24},{8,16},{16,8},{24,0},{1,25},{9,17},{17,9},{25,1},{2,26},{10... | collective-permute-start | bytes 1794056 | tf_op jit(solution)/shard_map/ppermute | solution.py:378
  21.9 40.3 %copy-start.46 = (f32[1,512]{1,0:T(1,128)}, f32[1,512]{1,0:T(1,128)S(1)}, u32[]{:S(2)}) copy-start(f32[1,512]{1,0:T(1,128)S(1)} %get-tuple-element.146) | copy-start | bytes 6148
  21.9 40.3 %copy-start.48 = (f32[1,512]{1,0:T(1,128)}, f32[1,512]{1,0:T(1,128)S(1)}, u32[]{:S(2)}) copy-start(f32[1,512]{1,0:T(1,128)S(1)} %get-tuple-element.147) | copy-start | bytes 6148
  23.2 47.2 %copy-start.30 = (f32[1,2048]{1,0:T(1,128)}, f32[1,2048]{1,0:T(1,128)S(1)}, u32[]{:S(2)}) copy-start(f32[1,2048]{1,0:T(1,128)S(1)} %get-tuple-element.148) | copy-start | bytes 24580
  46.5 89.6 %all-gather.5.cloned.1.call-start = ((), (), s32[]{:S(2)}) async-start(), calls=%async_computation.3 | async-start | bytes 2621440 | tf_op jit(solution)/shard_map/all_gather | solution.py:551
  68.2 2.2 collective-permute-start.4
  71.8 4.8 collective-permute-start.5
  73.4 9.5 %collective-permute-start.6 = (bf16[160,256]{1,0:T(8,128)(2,1)S(1)}, bf16[160,256]{1,0:T(8,128)(2,1)S(1)}, u32[]{:S(2)}, u32[]{:S(2)}) collective-permute-start(bf16[160,256]{1,0:T(8,128)(2,1)S(1)} %get-tuple-element.140), channel_id=1, source_target_pairs={{0,2},{1,3},{2,0},{3,1},{4,6},{5,7},{6,4},{7,5},{8,10},{9,11},{10,... | collective-permute-start | bytes 245768 | tf_op jit(solution)/shard_map/ppermute | solution.py:378
  76.0 6.9 %collective-permute-start.7 = (bf16[160,256]{1,0:T(8,128)(2,1)S(1)}, bf16[160,256]{1,0:T(8,128)(2,1)S(1)}, u32[]{:S(2)}, u32[]{:S(2)}) collective-permute-start(bf16[160,256]{1,0:T(8,128)(2,1)S(1)} %get-tuple-element.139), channel_id=1, source_target_pairs={{0,3},{1,2},{2,1},{3,0},{4,7},{5,6},{6,5},{7,4},{8,11},{9,10},{10,... | collective-permute-start | bytes 245768 | tf_op jit(solution)/shard_map/ppermute | solution.py:378
  76.3 76.1 %collective-permute-start.12 = (bf16[1024,2048]{1,0:T(8,128)(2,1)}, bf16[1024,2048]{1,0:T(8,128)(2,1)}, u32[]{:S(2)}, u32[]{:S(2)}) collective-permute-start(bf16[1024,2048]{1,0:T(8,128)(2,1)} %bitcast.19), channel_id=1, source_target_pairs={{0,4},{4,0},{1,5},{5,1},{2,6},{6,2},{3,7},{7,3},{8,12},{12,8},{9,1... | collective-permute-start | bytes 12582920 | tf_op jit(solution)/shard_map/ppermute | solution.py:378
  76.3 151.8 %reduce-scatter.4.cloned.1.call-start = ((), (), s32[]{:S(2)}) async-start(), calls=%async_computation.5 | async-start | bytes 5242880 | tf_op jit(solution)/shard_map/reduce_scatter | solution.py:582
  83.0 10.3 %collective-permute-start.8 = (bf16[160,256]{1,0:T(8,128)(2,1)S(1)}, bf16[160,256]{1,0:T(8,128)(2,1)S(1)}, u32[]{:S(2)}, u32[]{:S(2)}) collective-permute-start(bf16[160,256]{1,0:T(8,128)(2,1)S(1)} %get-tuple-element.111), channel_id=1, source_target_pairs={{0,1},{1,0},{2,3},{3,2},{4,5},{5,4},{6,7},{7,6},{8,9},{9,8},{10,11... | collective-permute-start | bytes 245768 | tf_op jit(solution)/shard_map/ppermute | solution.py:378
  84.6 8.7 %collective-permute-start.9 = (bf16[160,256]{1,0:T(8,128)(2,1)S(1)}, bf16[160,256]{1,0:T(8,128)(2,1)S(1)}, u32[]{:S(2)}, u32[]{:S(2)}) collective-permute-start(bf16[160,256]{1,0:T(8,128)(2,1)S(1)} %get-tuple-element.111), channel_id=1, source_target_pairs={{0,2},{1,3},{2,0},{3,1},{4,6},{5,7},{6,4},{7,5},{8,10},{9,11},{10,... | collective-permute-start | bytes 245768 | tf_op jit(solution)/shard_map/ppermute | solution.py:378
  86.1 7.2 %collective-permute-start.10 = (bf16[160,256]{1,0:T(8,128)(2,1)S(1)}, bf16[160,256]{1,0:T(8,128)(2,1)S(1)}, u32[]{:S(2)}, u32[]{:S(2)}) collective-permute-start(bf16[160,256]{1,0:T(8,128)(2,1)S(1)} %get-tuple-element.111), channel_id=1, source_target_pairs={{0,3},{1,2},{2,1},{3,0},{4,7},{5,6},{6,5},{7,4},{8,11},{9,10},{10,... | collective-permute-start | bytes 245768 | tf_op jit(solution)/shard_map/ppermute | solution.py:378
  93.4 5.5 %collective-permute-start.11 = (bf16[160,1024]{1,0:T(8,128)(2,1)S(1)}, bf16[160,1024]{1,0:T(8,128)(2,1)S(1)}, u32[]{:S(2)}, u32[]{:S(2)}) collective-permute-start(bf16[160,1024]{1,0:T(8,128)(2,1)S(1)} %constant_dynamic-update-slice_fusion.10), channel_id=1, source_target_pairs={{0,4},{4,0},{1,5},{5,1},{2,6},{6,2},{3,7},{7,3},{8,12},{12,8},{9,1... | collective-permute-start | bytes 983048 | tf_op jit(solution)/shard_map/ppermute | solution.py:378
  136.1 9.7 %collective-permute-start.14 = (bf16[2048,512]{0,1:T(8,128)(2,1)}, bf16[2048,512]{0,1:T(8,128)(2,1)S(1)}, u32[]{:S(2)}, u32[]{:S(2)}) collective-permute-start(bf16[2048,512]{0,1:T(8,128)(2,1)} %all-gather.5.cloned.1.call-done), channel_id=1, source_target_pairs={{0,4},{4,0},{1,5},{5,1},{2,6},{6,2},{3,7},{7,3},{8,12},{12,8},{9,1... | collective-permute-start | bytes 6291464 | tf_op jit(solution)/shard_map/ppermute | solution.py:378
  136.8 9.0 %collective-permute-start.13 = (bf16[1024,512]{1,0:T(8,128)(2,1)S(1)}, bf16[1024,512]{1,0:T(8,128)(2,1)S(1)}, u32[]{:S(2)}, u32[]{:S(2)}) collective-permute-start(bf16[1024,512]{1,0:T(8,128)(2,1)S(1)} %get-tuple-element.86), channel_id=1, source_target_pairs={{0,4},{4,0},{1,5},{5,1},{2,6},{6,2},{3,7},{7,3},{8,12},{12,8},{9,1... | collective-permute-start | bytes 3145736 | tf_op jit(solution)/shard_map/ppermute | solution.py:378
  136.9 92.7 %collective-permute-start.17 = (bf16[2048,512]{1,0:T(8,128)(2,1)}, bf16[2048,512]{1,0:T(8,128)(2,1)}, u32[]{:S(2)}, u32[]{:S(2)}) collective-permute-start(bf16[2048,512]{1,0:T(8,128)(2,1)} %slice_dynamic-update-slice_fusion), channel_id=1, source_target_pairs={{0,4},{4,0},{1,5},{5,1},{2,6},{6,2},{3,7},{7,3},{8,12},{12,8},{9,1... | collective-permute-start | bytes 6291464 | tf_op jit(solution)/shard_map/ppermute | solution.py:378
  137.4 92.3 %collective-permute-start.16 = (bf16[2048,512]{1,0:T(8,128)(2,1)}, bf16[2048,512]{1,0:T(8,128)(2,1)}, u32[]{:S(2)}, u32[]{:S(2)}) collective-permute-start(bf16[2048,512]{1,0:T(8,128)(2,1)} %all-gather.7.cloned.1.call-done), channel_id=1, source_target_pairs={{0,4},{4,0},{1,5},{5,1},{2,6},{6,2},{3,7},{7,3},{8,12},{12,8},{9,1... | collective-permute-start | bytes 6291464 | tf_op jit(solution)/shard_map/ppermute | solution.py:378
  151.9 169.6 %all-gather.9.cloned.1.call-start = ((), (), s32[]{:S(2)}) async-start(), calls=%async_computation.8 | async-start | bytes 5242880 | tf_op jit(solution)/shard_map/all_gather | solution.py:593
  230.5 2.8 collective-permute-start.18
  233.1 223.7 %reduce-scatter.8.cloned.1.call-start = ((), (), s32[]{:S(2)}) async-start(), calls=%async_computation.7 | async-start | bytes 2621440 | tf_op jit(solution)/shard_map/reduce_scatter | solution.py:637
  233.5 6.3 %collective-permute-start.19 = (bf16[160,256]{1,0:T(8,128)(2,1)S(1)}, bf16[160,256]{1,0:T(8,128)(2,1)S(1)}, u32[]{:S(2)}, u32[]{:S(2)}) collective-permute-start(bf16[160,256]{1,0:T(8,128)(2,1)S(1)} %get-tuple-element.135), channel_id=1, source_target_pairs={{0,1},{1,0},{2,3},{3,2},{4,5},{5,4},{6,7},{7,6},{8,9},{9,8},{10,11... | collective-permute-start | bytes 245768 | tf_op jit(solution)/shard_map/ppermute | solution.py:378
  235.1 5.7 %collective-permute-start.20 = (bf16[160,256]{1,0:T(8,128)(2,1)S(1)}, bf16[160,256]{1,0:T(8,128)(2,1)S(1)}, u32[]{:S(2)}, u32[]{:S(2)}) collective-permute-start(bf16[160,256]{1,0:T(8,128)(2,1)S(1)} %get-tuple-element.137), channel_id=1, source_target_pairs={{0,2},{1,3},{2,0},{3,1},{4,6},{5,7},{6,4},{7,5},{8,10},{9,11},{10,... | collective-permute-start | bytes 245768 | tf_op jit(solution)/shard_map/ppermute | solution.py:378
  236.8 7.6 %collective-permute-start.21 = (bf16[160,256]{1,0:T(8,128)(2,1)S(1)}, bf16[160,256]{1,0:T(8,128)(2,1)S(1)}, u32[]{:S(2)}, u32[]{:S(2)}) collective-permute-start(bf16[160,256]{1,0:T(8,128)(2,1)S(1)} %get-tuple-element.136), channel_id=1, source_target_pairs={{0,3},{1,2},{2,1},{3,0},{4,7},{5,6},{6,5},{7,4},{8,11},{9,10},{10,... | collective-permute-start | bytes 245768 | tf_op jit(solution)/shard_map/ppermute | solution.py:378
  239.7 51.6 %collective-permute-start.15 = (bf16[1024,512]{1,0:T(8,128)(2,1)S(1)}, bf16[1024,512]{1,0:T(8,128)(2,1)}, u32[]{:S(2)}, u32[]{:S(2)}) collective-permute-start(bf16[1024,512]{1,0:T(8,128)(2,1)S(1)} %get-tuple-element.90), channel_id=1, source_target_pairs={{0,4},{4,0},{1,5},{5,1},{2,6},{6,2},{3,7},{7,3},{8,12},{12,8},{9,1... | collective-permute-start | bytes 3145736 | tf_op jit(solution)/shard_map/ppermute | solution.py:378
  244.5 14.6 %collective-permute-start.22 = (bf16[160,256]{1,0:T(8,128)(2,1)S(1)}, bf16[160,256]{1,0:T(8,128)(2,1)S(1)}, u32[]{:S(2)}, u32[]{:S(2)}) collective-permute-start(bf16[160,256]{1,0:T(8,128)(2,1)S(1)} %get-tuple-element.109), channel_id=1, source_target_pairs={{0,1},{1,0},{2,3},{3,2},{4,5},{5,4},{6,7},{7,6},{8,9},{9,8},{10,11... | collective-permute-start | bytes 245768 | tf_op jit(solution)/shard_map/ppermute | solution.py:378
  250.6 15.1 %collective-permute-start.23 = (bf16[160,256]{1,0:T(8,128)(2,1)S(1)}, bf16[160,256]{1,0:T(8,128)(2,1)S(1)}, u32[]{:S(2)}, u32[]{:S(2)}) collective-permute-start(bf16[160,256]{1,0:T(8,128)(2,1)S(1)} %get-tuple-element.109), channel_id=1, source_target_pairs={{0,2},{1,3},{2,0},{3,1},{4,6},{5,7},{6,4},{7,5},{8,10},{9,11},{10,... | collective-permute-start | bytes 245768 | tf_op jit(solution)/shard_map/ppermute | solution.py:378
  254.9 11.8 %collective-permute-start.24 = (bf16[160,256]{1,0:T(8,128)(2,1)S(1)}, bf16[160,256]{1,0:T(8,128)(2,1)S(1)}, u32[]{:S(2)}, u32[]{:S(2)}) collective-permute-start(bf16[160,256]{1,0:T(8,128)(2,1)S(1)} %get-tuple-element.109), channel_id=1, source_target_pairs={{0,3},{1,2},{2,1},{3,0},{4,7},{5,6},{6,5},{7,4},{8,11},{9,10},{10,... | collective-permute-start | bytes 245768 | tf_op jit(solution)/shard_map/ppermute | solution.py:378
  266.7 1.7 collective-permute-start.25
  280.5 10.8 %collective-permute-start.26 = (bf16[1024,512]{1,0:T(8,128)(2,1)}, bf16[1024,512]{1,0:T(8,128)(2,1)}, u32[]{:S(2)}, u32[]{:S(2)}) collective-permute-start(bf16[1024,512]{1,0:T(8,128)(2,1)} %get-tuple-element.125), channel_id=1, source_target_pairs={{0,4},{4,0},{1,5},{5,1},{2,6},{6,2},{3,7},{7,3},{8,12},{12,8},{9,1... | collective-permute-start | bytes 3145736 | tf_op jit(solution)/shard_map/ppermute | solution.py:378
  291.3 166.5 %reduce-scatter.6.cloned.1.call-start = ((), (), s32[]{:S(2)}) async-start(), calls=%async_computation.6 | async-start | bytes 5898240 | tf_op jit(solution)/shard_map/reduce_scatter | solution.py:637
  321.5 26.3 %collective-permute-start.28 = (bf16[256,2048]{1,0:T(8,128)(2,1)}, bf16[256,2048]{1,0:T(8,128)(2,1)S(1)}, u32[]{:S(2)}, u32[]{:S(2)}) collective-permute-start(bf16[256,2048]{1,0:T(8,128)(2,1)} %get-tuple-element.84), channel_id=1, source_target_pairs={{0,1},{1,0},{2,3},{3,2},{4,5},{5,4},{6,7},{7,6},{8,9},{9,8},{10,11... | collective-permute-start | bytes 3145736 | tf_op jit(solution)/shard_map/ppermute | solution.py:378
  332.5 55.9 %collective-permute-start.27 = (bf16[256,2048]{1,0:T(8,128)(2,1)}, bf16[256,2048]{1,0:T(8,128)(2,1)}, u32[]{:S(2)}, u32[]{:S(2)}) collective-permute-start(bf16[256,2048]{1,0:T(8,128)(2,1)} %get-tuple-element.82), channel_id=1, source_target_pairs={{0,1},{1,0},{2,3},{3,2},{4,5},{5,4},{6,7},{7,6},{8,9},{9,8},{10,11... | collective-permute-start | bytes 3145736 | tf_op jit(solution)/shard_map/ppermute | solution.py:378
  349.2 46.6 %collective-permute-start.29 = (bf16[256,2048]{1,0:T(8,128)(2,1)}, bf16[256,2048]{1,0:T(8,128)(2,1)}, u32[]{:S(2)}, u32[]{:S(2)}) collective-permute-start(bf16[256,2048]{1,0:T(8,128)(2,1)} %add_convert_fusion.2), channel_id=1, source_target_pairs={{0,2},{1,3},{2,0},{3,1},{4,6},{5,7},{6,4},{7,5},{8,10},{9,11},{10,... | collective-permute-start | bytes 3145736 | tf_op jit(solution)/shard_map/ppermute | solution.py:378
  402.3 44.4 %collective-permute-start.30 = (bf16[256,2048]{1,0:T(8,128)(2,1)}, bf16[256,2048]{1,0:T(8,128)(2,1)S(1)}, u32[]{:S(2)}, u32[]{:S(2)}) collective-permute-start(bf16[256,2048]{1,0:T(8,128)(2,1)} %fusion.51), channel_id=1, source_target_pairs={{0,1},{1,0},{2,3},{3,2},{4,5},{5,4},{6,7},{7,6},{8,9},{9,8},{10,11... | collective-permute-start | bytes 3145736 | tf_op jit(solution)/shard_map/ppermute | solution.py:378
  402.3 46.5 %collective-permute-start.31 = (bf16[256,2048]{1,0:T(8,128)(2,1)}, bf16[256,2048]{1,0:T(8,128)(2,1)}, u32[]{:S(2)}, u32[]{:S(2)}) collective-permute-start(bf16[256,2048]{1,0:T(8,128)(2,1)} %fusion.51), channel_id=1, source_target_pairs={{0,2},{1,3},{2,0},{3,1},{4,6},{5,7},{6,4},{7,5},{8,10},{9,11},{10,... | collective-permute-start | bytes 3145736 | tf_op jit(solution)/shard_map/ppermute | solution.py:378
  446.7 5.6 %collective-permute-start.34 = (f32[27,512]{1,0:T(8,128)S(1)}, f32[27,512]{1,0:T(8,128)S(1)}, u32[]{:S(2)}, u32[]{:S(2)}) collective-permute-start(f32[27,512]{1,0:T(8,128)S(1)} %concatenate.35), channel_id=1, source_target_pairs={{0,8},{8,0},{16,24},{24,16},{1,9},{9,1},{17,25},{25,17},{2,10},{10... | collective-permute-start | bytes 165896 | tf_op jit(solution)/shard_map/ppermute | solution.py:378
  448.8 38.9 %collective-permute-start.32 = (bf16[256,2048]{1,0:T(8,128)(2,1)}, bf16[256,2048]{1,0:T(8,128)(2,1)}, u32[]{:S(2)}, u32[]{:S(2)}) collective-permute-start(bf16[256,2048]{1,0:T(8,128)(2,1)} %collective-permute-done.31), channel_id=1, source_target_pairs={{0,1},{1,0},{2,3},{3,2},{4,5},{5,4},{6,7},{7,6},{8,9},{9,8},{10,11... | collective-permute-start | bytes 3145736 | tf_op jit(solution)/shard_map/ppermute | solution.py:378
  452.4 4.3 collective-permute-start.35
  456.7 3.9 collective-permute-start.36
  460.6 20.9 %collective-permute-start.33 = (bf16[1664,512]{1,0:T(8,128)(2,1)}, bf16[1664,512]{1,0:T(8,128)(2,1)}, u32[]{:S(2)}, u32[]{:S(2)}) collective-permute-start(bf16[1664,512]{1,0:T(8,128)(2,1)} %pad_maximum_fusion), channel_id=1, source_target_pairs={{0,4},{4,0},{1,5},{5,1},{2,6},{6,2},{3,7},{7,3},{8,12},{12,8},{9,1... | collective-permute-start | bytes 5111816 | tf_op jit(solution)/shard_map/ppermute | solution.py:378
  460.7 10.8 %collective-permute-start.37 = (f32[1,2048]{1,0:T(1,128)S(1)}, f32[1,2048]{1,0:T(1,128)S(1)}, u32[]{:S(2)}, u32[]{:S(2)}) collective-permute-start(f32[1,2048]{1,0:T(1,128)S(1)} %bitcast.190), channel_id=1, source_target_pairs={{0,1},{1,0},{2,3},{3,2},{4,5},{5,4},{6,7},{7,6},{8,9},{9,8},{10,11... | collective-permute-start | bytes 24584 | tf_op jit(solution)/shard_map/ppermute | solution.py:378
  471.5 4.6 collective-permute-start.38
  (57 other events, 591.3 us)
Sparse Core Ops, SparseCore 0:
  46.6 35.6 all-gather.6
  84.1 35.1 all-gather.4
  152.0 76.0 reduce-scatter.3
  233.2 88.2 all-gather.8
  324.6 34.9 reduce-scatter.7
  399.1 58.6 reduce-scatter.5
